TPU v7x, 512 devices: a whole 4x4x16 slice. The times are simulated.
512 devices in a mesh: blk: 64 (over y, z_lo, core), col: 8 (over x, z_hi).
Axes of the slice: x: 4, y: 4, z: 16 (z_hi: 2, z_lo: 8; z = z_hi * 8 + z_lo), core: 2. Of those that a mesh axis runs over, the one named last changes fastest.
Arguments:
- node_feats: bfloat16 [256, 131072], P('col', 'blk'), may hold values from -6 to 6
- tile_dst: int32 [3584], P('blk'), may hold values from 0 to 15
- tile_src: int32 [3584], P('blk'), may hold values from 0 to 47, as said below
- tile_cnt: int32 [3584, 128, 128], P('blk'), may hold values from 0 to 3, as said below
- send_blk: int32 [64, 8, 4], P('blk'), may hold values from 0 to 15
- self_weight: bfloat16 [256, 256], replicated, may hold values from -0.375 to 0.375
- neigh_weight: bfloat16 [256, 256], replicated, may hold values from -0.75 to 0.75
- bias: float32 [256], replicated, may hold values from -4 to 4
- cotangent: bfloat16 [256, 131072], P('col', 'blk'), may hold values from -6 to 6
Outputs:
- grad_feats: bfloat16 [256, 131072], P('col', 'blk')
- grad_self: float32 [256, 256], P('col')
- grad_neigh: float32 [256, 256], P('col')
- grad_bias: float32 [256], P('col')
Inputs may be any that keep to these rules, and one draw needn't show every extreme that they name: `tile_src`: of each device's 56 entries, the first 32 are 16 + a permutation of 0 to 32 - 1 (every received slot is read by one tile); the others are own blocks below 16. `tile_cnt`: edge counts; some rows of a tile are empty.
All inputs are finite; a program needn't handle non-finite values.
Results may differ from a plain program's by a relative error of at most 0.006.
Values may be sent and summed in bfloat16 or wider, within the bound.
No kernel may reach another device: no remote copies, remote signals or barrier semaphores. Data moves between devices by JAX's collectives and lax.ppermute only.
A program may use at most 64 MiB of HBM per device.

v0:
```python
import jax
import jax.numpy as jnp
from jax import lax
from jax.sharding import PartitionSpec as P


def shifted(block, axis, distance):
    devices = range(lax.axis_size(axis))
    route = [((i - distance) % len(devices), i) for i in devices]
    return lax.ppermute(block, axis, route)


def gelu_slope(pre_act):
    inner = 0.7978845608 * (pre_act + 0.044715 * pre_act * pre_act * pre_act)
    tanh_value = jnp.tanh(inner)
    return 0.5 * (1.0 + tanh_value) + 0.5 * pre_act * (
        1.0 - tanh_value * tanh_value
    ) * 0.7978845608 * (1.0 + 3.0 * 0.044715 * pre_act * pre_act)


def per_device(
    node_feats, tile_dst, tile_src, tile_cnt, send_blk, self_weight, neigh_weight, bias, cotangent
):
    highest = lax.Precision.HIGHEST
    local_dim, local_rows = node_feats.shape
    block_rows = tile_cnt.shape[1]
    own_blocks = local_rows // block_rows
    num_offsets = send_blk.shape[1]
    slot_cap = send_blk.shape[2]
    slot_total = num_offsets * slot_cap
    col_index = lax.axis_index("col")
    first_feat = col_index * local_dim
    feat_blocks = node_feats.reshape(local_dim, own_blocks, block_rows)
    send_table = send_blk[0].reshape(slot_total)
    outgoing = jnp.take(feat_blocks, send_table, axis=1).reshape(
        local_dim, num_offsets, slot_cap, block_rows
    )
    distances = [(index // 2 + 1) * (1 - 2 * (index % 2)) for index in range(num_offsets)]
    arrived = [shifted(outgoing[:, index], "blk", distances[index]) for index in range(num_offsets)]
    received = jnp.stack(arrived, axis=1).reshape(local_dim, slot_total, block_rows)
    source_buffer = jnp.concatenate([feat_blocks, received], axis=1)
    count_half = tile_cnt.astype(jnp.bfloat16)
    picked = jnp.take(source_buffer, tile_src, axis=1)
    products = jnp.einsum("ctj,tij->cti", picked, count_half, preferred_element_type=jnp.float32)
    dest_onehot = (tile_dst[:, None] == jnp.arange(own_blocks, dtype=jnp.int32)[None, :]).astype(
        jnp.float32
    )
    agg_raw = jnp.einsum("cti,tb->cbi", products, dest_onehot, precision=highest)
    degree = jnp.einsum(
        "ti,tb->bi", jnp.sum(tile_cnt, axis=2).astype(jnp.float32), dest_onehot, precision=highest
    )
    floor_degree = jnp.maximum(degree, 1.0)
    aggregate = (agg_raw / floor_degree[None]).astype(jnp.bfloat16).reshape(local_dim, local_rows)
    self_rows = lax.dynamic_slice_in_dim(self_weight, first_feat, local_dim, 0)
    neigh_rows = lax.dynamic_slice_in_dim(neigh_weight, first_feat, local_dim, 0)
    contract_first = (((0,), (0,)), ((), ()))
    self_part = self_rows
    neigh_part = neigh_rows
    pre_act = lax.psum_scatter(
        lax.dot_general(self_part, node_feats, contract_first, preferred_element_type=jnp.float32)
        + lax.dot_general(
            neigh_part, aggregate, contract_first, preferred_element_type=jnp.float32
        ),
        "col",
        scatter_dimension=0,
        tiled=True,
    )
    pre_act = pre_act + lax.dynamic_slice_in_dim(bias, first_feat, local_dim, 0)[:, None]
    grad_pre = (cotangent.astype(jnp.float32) * gelu_slope(pre_act)).astype(jnp.bfloat16)
    contract_last = (((1,), (1,)), ((), ()))
    grad_part = lax.all_gather(grad_pre, "col", axis=0, tiled=True)
    self_part = self_rows
    neigh_part = neigh_rows
    self_acc = jnp.dot(self_part, grad_part, preferred_element_type=jnp.float32)
    neigh_acc = jnp.dot(neigh_part, grad_part, preferred_element_type=jnp.float32)
    self_piece = lax.dot_general(
        node_feats, grad_part, contract_last, preferred_element_type=jnp.float32
    )
    neigh_piece = lax.dot_general(
        aggregate, grad_part, contract_last, preferred_element_type=jnp.float32
    )
    self_grad = self_piece
    neigh_grad = neigh_piece
    self_acc, neigh_acc, self_grad, neigh_grad = (self_acc, neigh_acc, self_grad, neigh_grad)
    bias_local = jnp.sum(grad_pre.astype(jnp.float32), axis=1)
    grad_self, grad_neigh, grad_bias = lax.psum((self_grad, neigh_grad, bias_local), "blk")
    scaled = (neigh_acc.reshape(local_dim, own_blocks, block_rows) / floor_degree[None]).astype(
        jnp.bfloat16
    )
    scaled_tiles = jnp.take(scaled, tile_dst, axis=1)
    contrib = jnp.einsum(
        "cti,tij->ctj", scaled_tiles, count_half, preferred_element_type=jnp.float32
    )
    source_onehot = (
        tile_src[:, None] == jnp.arange(own_blocks + slot_total, dtype=jnp.int32)[None, :]
    ).astype(jnp.float32)
    spread = jnp.einsum("ctj,ts->csj", contrib, source_onehot, precision=highest)
    back_local = spread[:, :own_blocks]
    returning = spread[:, own_blocks:].reshape(local_dim, num_offsets, slot_cap, block_rows)
    back_parts = [
        shifted(returning[:, index], "blk", -distances[index]) for index in range(num_offsets)
    ]
    came_back = jnp.stack(back_parts, axis=1).reshape(local_dim, slot_total, block_rows)
    send_onehot = (send_table[:, None] == jnp.arange(own_blocks, dtype=jnp.int32)[None, :]).astype(
        jnp.float32
    )
    back_remote = jnp.einsum("csj,sb->cbj", came_back, send_onehot, precision=highest)
    grad_feats = (self_acc + (back_local + back_remote).reshape(local_dim, local_rows)).astype(
        jnp.bfloat16
    )
    return (grad_feats, grad_self, grad_neigh, grad_bias)


def solution(mesh):
    placed = (
        P("col", "blk"),
        P("blk"),
        P("blk"),
        P("blk", None, None),
        P("blk", None, None),
        P(),
        P(),
        P(),
        P("col", "blk"),
    )
    return jax.shard_map(
        per_device,
        mesh=mesh,
        in_specs=placed,
        out_specs=(P("col", "blk"), P("col", None), P("col", None), P("col")),
        check_vma=False,
    )
```

profile of v0, /device:TPU:6, one launch (start us, length us, event | category | flops | bytes accessed | tf_op | source)
XLA Modules:
  0.0 1108.9 jit_solution(5263001337863859142)
XLA Ops:
  10.4 14.3 %collective-permute-start.7 = (bf16[32,4,128]{2,0,1:T(8,128)(2,1)S(1)}, bf16[32,4,128]{2,0,1:T(8,128)(2,1)S(1)}, u32[]{:S(2)}, u32[]{:S(2)}) collective-permute-start(bf16[32,4,128]{2,0,1:T(8,128)(2,1)S(1)} %get-tuple-element.17), channel_id=1, source_target_pairs={{32,0},{40,8},{48,16},{56,24},{64,32},{72,40},{80,48},{88,56},{96,... | collective-permute-start | bytes 98312 | tf_op jit(solution)/shard_map/ppermute | solution.py:10
  24.6 1.9 collective-permute-start.6
  26.5 10.6 collective-permute-start.5
  37.2 1.9 collective-permute-start.4
  39.1 4.5 collective-permute-start
  43.6 3.1 reduce_sum.18
  48.0 5.5 collective-permute-done
  53.5 4.8 collective-permute-start.1
  58.3 1.6 collective-permute-done.1
  59.9 1.9 collective-permute-start.2
  61.8 12.6 %collective-permute-done.2 = bf16[32,4,128]{2,0,1:T(8,128)(2,1)S(1)} collective-permute-done((bf16[32,4,128]{2,0,1:T(8,128)(2,1)S(1)}, bf16[32,4,128]{2,0,1:T(8,128)(2,1)S(1)}, u32[]{:S(2)}, u32[]{:S(2)}) %collective-permute-start.2) | collective-permute-done | bytes 32800 | tf_op jit(solution)/shard_map/ppermute | solution.py:10
  74.4 1.9 collective-permute-start.3
  76.3 3.9 collective-permute-done.3
  81.0 3.1 convolution_bitcast_fusion.1
  85.1 2.5 convolution_add_fusion
  88.3 142.6 %reduce-scatter.2.cloned.1.call-done = f32[32,2048]{1,0:T(8,128)} async-done(((f32[256,2048]{1,0:T(8,128)}), f32[32,2048]{1,0:T(8,128)}) %reduce-scatter.2.cloned.1.call-update) | async-done | bytes 262160 | tf_op jit(solution)/shard_map/reduce_scatter | solution.py:59
  230.9 2.5 convert_reduce_fusion
  233.6 83.4 %all-gather.2.cloned.1.call-done = bf16[256,2048]{1,0:T(8,128)(2,1)} async-done(((bf16[32,2048]{1,0:T(8,128)(2,1)}), bf16[256,2048]{1,0:T(8,128)(2,1)}) %all-gather.2.cloned.1.call-update) | async-done | bytes 1048592 | tf_op jit(solution)/shard_map/all_gather | solution.py:71
  319.2 2.7 convolution_bitcast_fusion
  323.2 1.9 collective-permute-start.15
  325.1 1.9 collective-permute-start.13
  327.0 11.5 %collective-permute-start.12 = (f32[32,4,128]{2,1,0:T(4,128)S(1)}, f32[32,4,128]{2,1,0:T(4,128)S(1)}, u32[]{:S(2)}, u32[]{:S(2)}) collective-permute-start(f32[32,4,128]{2,1,0:T(4,128)S(1)} %get-tuple-element.11), channel_id=1, source_target_pairs={{24,0},{32,8},{40,16},{48,24},{56,32},{64,40},{72,48},{80,56},{88,... | collective-permute-start | bytes 196616 | tf_op jit(solution)/shard_map/ppermute | solution.py:10
  338.5 1.9 collective-permute-start.11
  340.4 11.1 %collective-permute-start.8 = (f32[32,4,128]{2,1,0:T(4,128)S(1)}, f32[32,4,128]{2,1,0:T(4,128)S(1)}, u32[]{:S(2)}, u32[]{:S(2)}) collective-permute-start(f32[32,4,128]{2,1,0:T(4,128)S(1)} %get-tuple-element.15), channel_id=1, source_target_pairs={{8,0},{16,8},{24,16},{32,24},{40,32},{48,40},{56,48},{64,56},{72,6... | collective-permute-start | bytes 196616 | tf_op jit(solution)/shard_map/ppermute | solution.py:10
  353.6 1.9 collective-permute-start.9
  355.6 12.5 %collective-permute-done.9 = f32[32,4,128]{2,1,0:T(4,128)S(1)} collective-permute-done((f32[32,4,128]{2,1,0:T(4,128)S(1)}, f32[32,4,128]{2,1,0:T(4,128)S(1)}, u32[]{:S(2)}, u32[]{:S(2)}) %collective-permute-start.9) | collective-permute-done | bytes 65568 | tf_op jit(solution)/shard_map/ppermute | solution.py:10
  368.1 1.9 collective-permute-start.10
  370.0 4.2 collective-permute-done.10
  374.2 1.9 collective-permute-start.14
  376.2 5.0 collective-permute-done.14
  381.8 1.7 fusion
  383.4 715.1 %all-reduce.3.cloned.1.call-done = (f32[32,256]{1,0:T(8,128)}, f32[32,256]{1,0:T(8,128)}, f32[32]{0:T(128)}) async-done(((f32[32,256]{1,0:T(8,128)}, f32[32,256]{1,0:T(8,128)}, f32[32]{0:T(128)}), (f32[32,256]{1,0:T(8,128)}, f32[32,256]{1,0:T(8,128)}, f32[32]{0:T(128)})) %all-reduce.3.cloned.1.call-update) | async-done | bytes 65680 | tf_op jit(solution)/shard_map/psum | solution.py:86
  (78 shorter events, 17.1 us)
Async XLA Ops:
  7.2 2.4 copy-start
  7.2 223.7 %reduce-scatter.2.cloned.1.call-start = ((), (), s32[]{:S(2)}) async-start(), calls=%async_computation.1 | async-start | bytes 2359296 | tf_op jit(solution)/shard_map/reduce_scatter | solution.py:59
  10.3 36.4 %copy-start.4 = (s32[56]{0:T(128)S(1)}, s32[56]{0:T(128)}, u32[]{:S(2)}) copy-start(s32[56]{0:T(128)} %param.10) | copy-start | bytes 676
  10.4 69.9 %collective-permute-start.7 = (bf16[32,4,128]{2,0,1:T(8,128)(2,1)S(1)}, bf16[32,4,128]{2,0,1:T(8,128)(2,1)S(1)}, u32[]{:S(2)}, u32[]{:S(2)}) collective-permute-start(bf16[32,4,128]{2,0,1:T(8,128)(2,1)S(1)} %get-tuple-element.17), channel_id=1, source_target_pairs={{32,0},{40,8},{48,16},{56,24},{64,32},{72,40},{80,48},{88,56},{96,... | collective-permute-start | bytes 98312 | tf_op jit(solution)/shard_map/ppermute | solution.py:10
  24.6 55.6 %collective-permute-start.6 = (bf16[32,4,128]{2,0,1:T(8,128)(2,1)S(1)}, bf16[32,4,128]{2,0,1:T(8,128)(2,1)S(1)}, u32[]{:S(2)}, u32[]{:S(2)}) collective-permute-start(bf16[32,4,128]{2,0,1:T(8,128)(2,1)S(1)} %get-tuple-element.18), channel_id=1, source_target_pairs={{480,0},{488,8},{496,16},{504,24},{0,32},{8,40},{16,48},{24,56},{3... | collective-permute-start | bytes 98312 | tf_op jit(solution)/shard_map/ppermute | solution.py:10
  26.5 53.7 %collective-permute-start.5 = (bf16[32,4,128]{2,0,1:T(8,128)(2,1)S(1)}, bf16[32,4,128]{2,0,1:T(8,128)(2,1)S(1)}, u32[]{:S(2)}, u32[]{:S(2)}) collective-permute-start(bf16[32,4,128]{2,0,1:T(8,128)(2,1)S(1)} %get-tuple-element.19), channel_id=1, source_target_pairs={{24,0},{32,8},{40,16},{48,24},{56,32},{64,40},{72,48},{80,56},{88,... | collective-permute-start | bytes 98312 | tf_op jit(solution)/shard_map/ppermute | solution.py:10
  37.2 43.0 %collective-permute-start.4 = (bf16[32,4,128]{2,0,1:T(8,128)(2,1)S(1)}, bf16[32,4,128]{2,0,1:T(8,128)(2,1)S(1)}, u32[]{:S(2)}, u32[]{:S(2)}) collective-permute-start(bf16[32,4,128]{2,0,1:T(8,128)(2,1)S(1)} %get-tuple-element.20), channel_id=1, source_target_pairs={{488,0},{496,8},{504,16},{0,24},{8,32},{16,40},{24,48},{32,56},{40... | collective-permute-start | bytes 98312 | tf_op jit(solution)/shard_map/ppermute | solution.py:10
  39.1 14.4 %collective-permute-start = (bf16[32,4,128]{2,0,1:T(8,128)(2,1)S(1)}, bf16[32,4,128]{2,0,1:T(8,128)(2,1)S(1)}, u32[]{:S(2)}, u32[]{:S(2)}) collective-permute-start(bf16[32,4,128]{2,0,1:T(8,128)(2,1)S(1)} %get-tuple-element.24), channel_id=1, source_target_pairs={{504,0},{0,8},{8,16},{16,24},{24,32},{32,40},{40,48},{48,56},{56,6... | collective-permute-start | bytes 98312 | tf_op jit(solution)/shard_map/ppermute | solution.py:10
  43.6 4.4 copy-start.3
  53.5 6.4 collective-permute-start.1
  59.9 14.5 %collective-permute-start.2 = (bf16[32,4,128]{2,0,1:T(8,128)(2,1)S(1)}, bf16[32,4,128]{2,0,1:T(8,128)(2,1)S(1)}, u32[]{:S(2)}, u32[]{:S(2)}) collective-permute-start(bf16[32,4,128]{2,0,1:T(8,128)(2,1)S(1)} %get-tuple-element.22), channel_id=1, source_target_pairs={{496,0},{504,8},{0,16},{8,24},{16,32},{24,40},{32,48},{40,56},{48,... | collective-permute-start | bytes 98312 | tf_op jit(solution)/shard_map/ppermute | solution.py:10
  74.4 5.8 collective-permute-start.3
  87.6 0.7 copy-start.5
  87.6 143.3 %copy-start.2 = (bf16[32,2048]{1,0:T(8,128)(2,1)S(1)}, bf16[32,2048]{1,0:T(8,128)(2,1)}, u32[]{:S(2)}) copy-start(bf16[32,2048]{1,0:T(8,128)(2,1)} %param.17) | copy-start | bytes 393220
  87.6 229.4 %all-gather.2.cloned.1.call-start = ((), (), s32[]{:S(2)}) async-start(), calls=%async_computation.2 | async-start | bytes 1179648 | tf_op jit(solution)/shard_map/all_gather | solution.py:71
  233.4 865.1 %all-reduce.3.cloned.1.call-start = ((), (), s32[]{:S(2)}) async-start(), calls=%async_computation.3 | async-start | bytes 132096 | tf_op jit(solution)/shard_map/psum | solution.py:86
  321.9 29.7 %copy-start.1 = (bf16[256,2048]{1,0:T(8,128)(2,1)S(1)}, bf16[256,2048]{1,0:T(8,128)(2,1)}, u32[]{:S(2)}) copy-start(bf16[256,2048]{1,0:T(8,128)(2,1)} %all-gather.2.cloned.1.call-done) | copy-start | bytes 3145732
  323.2 58.1 %collective-permute-start.15 = (f32[32,4,128]{2,1,0:T(4,128)S(1)}, f32[32,4,128]{2,1,0:T(4,128)S(1)}, u32[]{:S(2)}, u32[]{:S(2)}) collective-permute-start(f32[32,4,128]{2,1,0:T(4,128)S(1)} %get-tuple-element.9), channel_id=1, source_target_pairs={{480,0},{488,8},{496,16},{504,24},{0,32},{8,40},{16,48},{24,56},{3... | collective-permute-start | bytes 196616 | tf_op jit(solution)/shard_map/ppermute | solution.py:10
  325.1 51.1 %collective-permute-start.13 = (f32[32,4,128]{2,1,0:T(4,128)S(1)}, f32[32,4,128]{2,1,0:T(4,128)S(1)}, u32[]{:S(2)}, u32[]{:S(2)}) collective-permute-start(f32[32,4,128]{2,1,0:T(4,128)S(1)} %get-tuple-element.10), channel_id=1, source_target_pairs={{488,0},{496,8},{504,16},{0,24},{8,32},{16,40},{24,48},{32,56},{40... | collective-permute-start | bytes 196616 | tf_op jit(solution)/shard_map/ppermute | solution.py:10
  327.0 49.2 %collective-permute-start.12 = (f32[32,4,128]{2,1,0:T(4,128)S(1)}, f32[32,4,128]{2,1,0:T(4,128)S(1)}, u32[]{:S(2)}, u32[]{:S(2)}) collective-permute-start(f32[32,4,128]{2,1,0:T(4,128)S(1)} %get-tuple-element.11), channel_id=1, source_target_pairs={{24,0},{32,8},{40,16},{48,24},{56,32},{64,40},{72,48},{80,56},{88,... | collective-permute-start | bytes 196616 | tf_op jit(solution)/shard_map/ppermute | solution.py:10
  338.5 37.7 %collective-permute-start.11 = (f32[32,4,128]{2,1,0:T(4,128)S(1)}, f32[32,4,128]{2,1,0:T(4,128)S(1)}, u32[]{:S(2)}, u32[]{:S(2)}) collective-permute-start(f32[32,4,128]{2,1,0:T(4,128)S(1)} %get-tuple-element.12), channel_id=1, source_target_pairs={{496,0},{504,8},{0,16},{8,24},{16,32},{24,40},{32,48},{40,56},{48,... | collective-permute-start | bytes 196616 | tf_op jit(solution)/shard_map/ppermute | solution.py:10
  340.4 13.2 %collective-permute-start.8 = (f32[32,4,128]{2,1,0:T(4,128)S(1)}, f32[32,4,128]{2,1,0:T(4,128)S(1)}, u32[]{:S(2)}, u32[]{:S(2)}) collective-permute-start(f32[32,4,128]{2,1,0:T(4,128)S(1)} %get-tuple-element.15), channel_id=1, source_target_pairs={{8,0},{16,8},{24,16},{32,24},{40,32},{48,40},{56,48},{64,56},{72,6... | collective-permute-start | bytes 196616 | tf_op jit(solution)/shard_map/ppermute | solution.py:10
  353.6 14.4 %collective-permute-start.9 = (f32[32,4,128]{2,1,0:T(4,128)S(1)}, f32[32,4,128]{2,1,0:T(4,128)S(1)}, u32[]{:S(2)}, u32[]{:S(2)}) collective-permute-start(f32[32,4,128]{2,1,0:T(4,128)S(1)} %get-tuple-element.14), channel_id=1, source_target_pairs={{504,0},{0,8},{8,16},{16,24},{24,32},{32,40},{40,48},{48,56},{56,6... | collective-permute-start | bytes 196616 | tf_op jit(solution)/shard_map/ppermute | solution.py:10
  368.1 6.1 collective-permute-start.10
  374.2 7.1 collective-permute-start.14
Sparse Core Ops, SparseCore 0:
  87.7 143.1 reduce-scatter.1
  235.2 81.7 all-gather.1
  353.8 744.7 all-reduce.2
where the time goes:
time: 1110 us
  waiting for transfers between devices  986 us (89%)
  starting transfers between devices  76 us (7%)
  matrix products  17.3 us (2%)
  between operations  14.2 us (1%)
    psum x1, waiting for transfers between devices, per_device(): lax.psum((self_grad, neigh_grad, bias_local), 'blk')  715 us
    reduce_scatter x1, waiting for transfers between devices, per_device(): lax.psum_scatter(lax.dot_general(self_part, node_feats, contract_first, p...  143 us
    all_gather x1, waiting for transfers between devices, per_device(): grad_part = lax.all_gather(grad_pre, 'col', axis=0, tiled=True)  83.4 us
    ppermute x16, starting transfers between devices, shifted(): return lax.ppermute(block, axis, route)  75.9 us
    ppermute x16, waiting for transfers between devices, shifted(): return lax.ppermute(block, axis, route)  45.2 us
  transfers between devices with their start and end apart: 19, of which 10 were waited for; matrix products, arithmetic and copies ran while one was open for 1% of the time, Pallas kernels for 0%

commit v1 on v0

v1 whole, which is shorter than its diff:
```python
import jax
import jax.numpy as jnp
from jax import lax
from jax.sharding import PartitionSpec as P

GROUP = 8


def gelu_slope(pre_act):
    inner = 0.7978845608 * (pre_act + 0.044715 * pre_act * pre_act * pre_act)
    tanh_value = jnp.tanh(inner)
    return 0.5 * (1.0 + tanh_value) + 0.5 * pre_act * (
        1.0 - tanh_value * tanh_value
    ) * 0.7978845608 * (1.0 + 3.0 * 0.044715 * pre_act * pre_act)


def halo_groups(devices, shift):
    return [
        [(first + shift + i) % devices for i in range(GROUP)]
        for first in range(0, devices, GROUP)
    ]


def offset_to_index(distance):
    k = 2 * (jnp.abs(distance) - 1) + (distance < 0).astype(jnp.int32)
    return jnp.clip(k, 0, 7)


def swap(rows, shift):
    devices = lax.axis_size("blk")
    return lax.all_to_all(
        rows, "blk", 0, 0, axis_index_groups=halo_groups(devices, shift), tiled=False
    )


def per_device(
    node_feats, tile_dst, tile_src, tile_cnt, send_blk, self_weight, neigh_weight, bias, cotangent
):
    highest = lax.Precision.HIGHEST
    dim, nodes = node_feats.shape
    width = tile_cnt.shape[1]
    blocks = nodes // width
    slot_cap = send_blk.shape[2]
    slots = send_blk.shape[1] * slot_cap
    cols = lax.axis_size("col")
    per_col = blocks // cols
    full = cols * dim
    bf16 = jnp.bfloat16

    def by_block(value):
        return value.reshape(dim, blocks, width).transpose(1, 0, 2)

    def to_full(value):
        return value.transpose(0, 2, 1, 3).reshape(full, per_col * width)

    def from_full(value):
        return value.reshape(cols, dim, per_col, width).transpose(0, 2, 1, 3)

    col = lax.axis_index("col")
    blk = lax.axis_index("blk")
    peers = jnp.arange(GROUP, dtype=jnp.int32)
    place_a = blk % GROUP
    place_b = (blk + GROUP // 2) % GROUP
    out_a = offset_to_index(peers - place_a)
    out_b = offset_to_index(peers - place_b)
    back_a = offset_to_index(place_a - peers)
    back_b = offset_to_index(place_b - peers)
    kinds = jnp.arange(2 * (GROUP // 2), dtype=jnp.int32)
    distance = (kinds // 2 + 1) * (1 - 2 * (kinds % 2))
    from_a = place_a - distance
    in_a = (from_a >= 0) & (from_a < GROUP)
    came_row = jnp.where(in_a, from_a, GROUP + jnp.clip(place_b - distance, 0, GROUP - 1))
    ahead_a = place_a + distance
    ahead_in_a = (ahead_a >= 0) & (ahead_a < GROUP)
    ret_row = jnp.where(ahead_in_a, ahead_a, GROUP + jnp.clip(place_b + distance, 0, GROUP - 1))

    table = send_blk[0]
    feats = by_block(node_feats)
    send_a = jnp.take(feats, table[out_a].reshape(-1), axis=0)
    send_b = jnp.take(feats, table[out_b].reshape(-1), axis=0)
    shape = (GROUP, slot_cap, dim, width)
    got_b = swap(send_b.reshape(shape), GROUP // 2)
    got_a = swap(send_a.reshape(shape), 0)
    sources = jnp.concatenate(
        [
            feats,
            got_a.reshape(GROUP * slot_cap, dim, width),
            got_b.reshape(GROUP * slot_cap, dim, width),
        ],
        axis=0,
    )
    slot = jnp.maximum(tile_src - blocks, 0)
    remote = blocks + came_row[slot // slot_cap] * slot_cap + slot % slot_cap
    source = jnp.where(tile_src < blocks, tile_src, remote)
    counts = tile_cnt.astype(bf16)
    picked = jnp.take(sources, source, axis=0)
    products = jnp.einsum("tcj,tij->tci", picked, counts, preferred_element_type=jnp.float32)
    dest = (tile_dst[:, None] == jnp.arange(blocks, dtype=jnp.int32)[None, :]).astype(jnp.float32)
    agg_raw = jnp.einsum("tci,tb->bci", products, dest, precision=highest)
    degree = jnp.einsum(
        "ti,tb->bi", jnp.sum(tile_cnt, axis=2).astype(jnp.float32), dest, precision=highest
    )
    floor_degree = jnp.maximum(degree, 1.0)
    aggregate = (agg_raw / floor_degree[:, None, :]).astype(bf16)

    def split(value):
        return value.reshape(cols, 1, per_col, dim, width)

    mixed = jnp.concatenate([split(feats), split(aggregate), split(by_block(cotangent))], axis=1)
    mixed = lax.all_to_all(mixed, "col", 0, 0, tiled=False)
    x_full = to_full(mixed[:, 0])
    agg_full = to_full(mixed[:, 1])
    cot_full = to_full(mixed[:, 2])
    first = (((0,), (0,)), ((), ()))
    last = (((1,), (1,)), ((), ()))
    pre_act = (
        lax.dot_general(self_weight, x_full, first, preferred_element_type=jnp.float32)
        + lax.dot_general(neigh_weight, agg_full, first, preferred_element_type=jnp.float32)
        + bias[:, None]
    )
    dz = (cot_full.astype(jnp.float32) * gelu_slope(pre_act)).astype(bf16)
    my_degree = lax.dynamic_slice_in_dim(floor_degree, col * per_col, per_col, 0).reshape(1, -1)
    scaled = (jnp.dot(neigh_weight, dz, preferred_element_type=jnp.float32) / my_degree).astype(bf16)
    own = jnp.dot(self_weight, dz, preferred_element_type=jnp.float32).astype(bf16)
    home = jnp.concatenate([from_full(scaled)[:, None], from_full(own)[:, None]], axis=1)
    home = lax.all_to_all(home, "col", 0, 0, tiled=False)

    weight_part = jnp.concatenate(
        [
            lax.dot_general(x_full, dz, last, preferred_element_type=jnp.float32).reshape(cols, dim, full),
            lax.dot_general(agg_full, dz, last, preferred_element_type=jnp.float32).reshape(cols, dim, full),
            jnp.broadcast_to(
                jnp.sum(dz.astype(jnp.float32), axis=1)[None, None, :], (cols, 16, full)
            ),
        ],
        axis=1,
    ).astype(bf16)
    weight = jnp.sum(
        lax.all_to_all(weight_part, "col", 0, 0, tiled=False).astype(jnp.float32), axis=0
    )

    def total(value, groups):
        count = len(groups[0])
        copies = jnp.broadcast_to(value.astype(bf16)[None], (count,) + value.shape)
        return jnp.sum(
            lax.all_to_all(
                copies, "blk", 0, 0, axis_index_groups=groups, tiled=False
            ).astype(jnp.float32),
            axis=0,
        )

    devices = lax.axis_size("blk")
    spread = [[16 * y + 2 * z + c for y in range(devices // 16) for c in range(2)] for z in range(8)]
    along = [[16 * y + 2 * z + c for z in range(8)] for y in range(devices // 16) for c in range(2)]
    weight = total(total(weight, spread), along)
    grad_self = weight[:dim]
    grad_neigh = weight[dim : 2 * dim]
    grad_bias = lax.dynamic_slice_in_dim(weight[2 * dim], col * dim, dim, 0)

    scaled_blocks = home[:, 0].reshape(blocks, dim, width)
    own_blocks = home[:, 1].reshape(blocks, dim, width)
    scaled_tiles = jnp.take(scaled_blocks, tile_dst, axis=0)
    contrib = jnp.einsum("tci,tij->tcj", scaled_tiles, counts, preferred_element_type=jnp.float32)
    tile_of_slot = jnp.argmax(
        tile_src[None, :slots] == blocks + jnp.arange(slots, dtype=jnp.int32)[:, None], axis=1
    ).astype(jnp.int32).reshape(-1, slot_cap)
    away = contrib[:slots].astype(bf16)
    ret_b = swap(jnp.take(away, tile_of_slot[back_b].reshape(-1), axis=0).reshape(shape), GROUP // 2)
    ret_a = swap(jnp.take(away, tile_of_slot[back_a].reshape(-1), axis=0).reshape(shape), 0)
    returned = jnp.concatenate([ret_a, ret_b], axis=0)[ret_row].reshape(slots, dim, width)
    local = (
        tile_src[slots:, None] == jnp.arange(blocks, dtype=jnp.int32)[None, :]
    ).astype(jnp.float32)
    back_local = jnp.einsum("tcj,ts->scj", contrib[slots:], local, precision=highest)
    sent = (
        table.reshape(-1)[:, None] == jnp.arange(blocks, dtype=jnp.int32)[None, :]
    ).astype(bf16)
    back_remote = jnp.einsum("tcj,ts->scj", returned, sent, preferred_element_type=jnp.float32)
    grad_feats = (own_blocks.astype(jnp.float32) + back_local + back_remote).astype(bf16)
    grad_feats = grad_feats.transpose(1, 0, 2).reshape(dim, nodes)
    return grad_feats, grad_self, grad_neigh, grad_bias


def solution(mesh):
    placed = (
        P("col", "blk"),
        P("blk"),
        P("blk"),
        P("blk", None, None),
        P("blk", None, None),
        P(),
        P(),
        P(),
        P("col", "blk"),
    )
    return jax.shard_map(
        per_device,
        mesh=mesh,
        in_specs=placed,
        out_specs=(P("col", "blk"), P("col", None), P("col", None), P("col")),
        check_vma=False,
    )
```

time: 1110 us -> 215 us (0.19)
  waiting for transfers between devices: 986 us -> 81.8 us
  between operations: 14.2 us -> 1.23 us
  starting transfers between devices: 76 us -> 88.7 us
    psum x1 -> x0, waiting for transfers between devices: 715 us -> none  [per_device(): lax.psum((self_grad, neigh_grad, bias_local), 'blk')]
    reduce_scatter x1 -> x0, waiting for transfers between devices: 143 us -> none  [per_device(): lax.psum_scatter(lax.dot_general(self_part, node_feats, contract_first, p...]
    all_to_all x0 -> x9, starting transfers between devices: none -> 88.7 us  [the longest x4 53.8 us: swap(): lax.all_to_all(rows, 'blk', 0, 0, axis_index_groups=halo_groups(devices,...]
    all_gather x1 -> x0, waiting for transfers between devices: 83.4 us -> none  [per_device(): grad_part = lax.all_gather(grad_pre, 'col', axis=0, tiled=True)]
    all_to_all x0 -> x9, waiting for transfers between devices: none -> 81.8 us  [the longest x4 21.9 us: swap(): lax.all_to_all(rows, 'blk', 0, 0, axis_index_groups=halo_groups(devices,...]
    ppermute x16 -> x0, starting transfers between devices: 75.9 us -> none  [shifted(): return lax.ppermute(block, axis, route)]
    ppermute x16 -> x0, waiting for transfers between devices: 45.2 us -> none  [shifted(): return lax.ppermute(block, axis, route)]
  transfers between devices with their start and end apart: 19 -> 9, of which waited for: 10 -> 9; matrix products, arithmetic and copies ran while one was open for 1% -> 11% of each run, Pallas kernels for 0% -> 0%
where the time goes in v1:
time: 215 us; the launch traced here: 211 us
  starting transfers between devices  88.7 us (41%)
  waiting for transfers between devices  81.8 us (38%)
  local copies, waits for them, and re-layouts  16 us (7%)
  other arithmetic  13.9 us (6%)
  matrix products  9.07 us (4%)
    all_to_all x4, starting transfers between devices, swap(): lax.all_to_all(rows, 'blk', 0, 0, axis_index_groups=halo_groups(devices,...  53.8 us
    all_to_all x4, waiting for transfers between devices, swap(): lax.all_to_all(rows, 'blk', 0, 0, axis_index_groups=halo_groups(devices,...  21.9 us
    all_to_all x2, waiting for transfers between devices, total(): lax.all_to_all(copies, 'blk', 0, 0, axis_index_groups=groups, tiled=False)  20.6 us
    all_to_all x1, waiting for transfers between devices, per_device(): mixed = lax.all_to_all(mixed, 'col', 0, 0, tiled=False)  14.6 us
    all_to_all x1, waiting for transfers between devices, per_device(): lax.all_to_all(weight_part, 'col', 0, 0, tiled=False).astype(jnp.float32)  13.5 us
    all_to_all x1, starting transfers between devices, per_device(): mixed = lax.all_to_all(mixed, 'col', 0, 0, tiled=False)  12.8 us
    all_to_all x1, waiting for transfers between devices, per_device(): home = lax.all_to_all(home, 'col', 0, 0, tiled=False)  11.1 us
    all_to_all x2, starting transfers between devices, total(): lax.all_to_all(copies, 'blk', 0, 0, axis_index_groups=groups, tiled=False)  10.5 us
  transfers between devices with their start and end apart: 9, of which 9 were waited for; matrix products, arithmetic and copies ran while one was open for 11% of the time, Pallas kernels for 0%

profile of v1, /device:TPU:6, one launch (start us, length us, event | category | flops | bytes accessed | tf_op | source)
XLA Modules:
  0.0 210.8 jit_solution(3854272145955060979)
XLA Ops:
  0.7 0.8 copy.126
  2.8 0.9 copy_bitcast_fusion.2
  4.4 0.8 broadcast_select_fusion.2
  5.2 15.7 %all-to-all-start.1 = ((bf16[8,4,32,128]{3,2,1,0:T(8,128)(2,1)}), bf16[8,4,32,128]{3,2,1,0:T(8,128)(2,1)S(1)}, u32[]{:S(2)}, u32[]{:S(2)}) async-start(bf16[8,4,32,128]{3,2,1,0:T(8,128)(2,1)} %bitcast.16), calls=%async_computation.1 | async-start | bytes 524288 | tf_op jit(solution)/shard_map/all_to_all | solution.py:31
  21.5 0.8 broadcast_select_fusion.3
  22.3 5.9 %all-to-all-done.1 = bf16[8,4,32,128]{3,2,1,0:T(8,128)(2,1)S(1)} async-done(((bf16[8,4,32,128]{3,2,1,0:T(8,128)(2,1)}), bf16[8,4,32,128]{3,2,1,0:T(8,128)(2,1)S(1)}, u32[]{:S(2)}, u32[]{:S(2)}) %all-to-all-start.1) | async-done | bytes 262176 | tf_op jit(solution)/shard_map/all_to_all | solution.py:31
  28.2 4.8 %all-to-all-start = ((bf16[8,4,32,128]{3,2,1,0:T(8,128)(2,1)}), bf16[8,4,32,128]{3,2,1,0:T(8,128)(2,1)S(1)}, u32[]{:S(2)}, u32[]{:S(2)}) async-start(bf16[8,4,32,128]{3,2,1,0:T(8,128)(2,1)} %bitcast.13), calls=%async_computation | async-start | bytes 524288 | tf_op jit(solution)/shard_map/all_to_all | solution.py:31
  33.0 3.1 %reduce_sum.51 = s32[56,128]{1,0:T(8,128)S(1)} reduce(s32[56,128,128]{2,1,0:T(8,128)} %param.16, s32[]{:T(128)} %constant.156.clone.1), dimensions={2}, to_apply=%region_0.2 | reduce | flops 910336 | bytes 3698692 | tf_op jit(solution)/shard_map/reduce_sum | solution.py:101
  36.9 5.2 %compare_and_fusion.5 = (pred[56]{0:T(512)(128)(4,1)S(1)}, s32[56]{0:T(128)S(1)}) fusion(s32[56]{0:T(128)S(1)} %copy-done.4, s32[]{:T(128)} %bitcast.10, s32[]{:T(128)} %bitcast.9, s32[]{:T(128)} %bitcast.8, s32[]{:T(128)} %bitcast.7, s32[]{:T(128)} %bitcast.6, s32[]{:T(128)} %bitcast.5, s32[]{:T(128)} %bitcast.4, s32[]{:T(128)} %bitcast.3), kind=kLoop, calls=%fused_computation.136 | loop fusion | flops 2352 | bytes 536 | tf_op jit(solution)/shard_map/jit(_take)/and | solution.py:96
  43.5 3.1 %fusion.11 = f32[56,32,128]{2,1,0:T(8,128)S(1)} fusion(s32[56,128,128]{2,1,0:T(8,128)} %param.16, bf16[56,32,128]{2,1,0:T(8,128)(2,1)S(1)} %gather_fusion.2, pred[56]{0:T(512)(128)(4,1)S(1)} %get-tuple-element.8), kind=kOutput, calls=%fused_computation.30 | convolution fusion | flops 59867136 | bytes 5046328 | tf_op jit(solution)/shard_map/tcj,tij->tci/dot_general | solution.py:97
  46.7 0.9 fusion.4
  47.7 0.8 copy.131
  48.5 12.8 %all-to-all-start.2 = ((bf16[8,3,2,32,128]{4,3,2,1,0:T(8,128)(2,1)}), bf16[8,3,2,32,128]{4,3,2,1,0:T(8,128)(2,1)S(1)}, u32[]{:S(2)}, u32[]{:S(2)}) async-start(bf16[8,3,2,32,128]{4,3,2,1,0:T(8,128)(2,1)} %copy.131), calls=%async_computation.2 | async-start | bytes 786432 | tf_op jit(solution)/shard_map/all_to_all | solution.py:110
  62.1 14.6 %all-to-all-done.2 = bf16[8,3,2,32,128]{4,3,2,1,0:T(8,128)(2,1)S(1)} async-done(((bf16[8,3,2,32,128]{4,3,2,1,0:T(8,128)(2,1)}), bf16[8,3,2,32,128]{4,3,2,1,0:T(8,128)(2,1)S(1)}, u32[]{:S(2)}, u32[]{:S(2)}) %all-to-all-start.2) | async-done | bytes 393248 | tf_op jit(solution)/shard_map/all_to_all | solution.py:110
  79.2 0.9 copy.138
  80.1 5.7 %all-to-all-start.3 = ((bf16[8,2,2,32,128]{4,2,3,1,0:T(2,128)(2,1)}), bf16[8,2,2,32,128]{4,2,3,1,0:T(2,128)(2,1)S(1)}, u32[]{:S(2)}, u32[]{:S(2)}) async-start(bf16[8,2,2,32,128]{4,2,3,1,0:T(2,128)(2,1)} %copy.138), calls=%async_computation.3 | async-start | bytes 524288 | tf_op jit(solution)/shard_map/all_to_all | solution.py:126
  87.6 0.8 pad_maximum_fusion.3
  88.3 11.1 %all-to-all-done.3 = bf16[8,2,2,32,128]{4,2,3,1,0:T(2,128)(2,1)S(1)} async-done(((bf16[8,2,2,32,128]{4,2,3,1,0:T(2,128)(2,1)}), bf16[8,2,2,32,128]{4,2,3,1,0:T(2,128)(2,1)S(1)}, u32[]{:S(2)}, u32[]{:S(2)}) %all-to-all-start.3) | async-done | bytes 262176 | tf_op jit(solution)/shard_map/all_to_all | solution.py:126
  99.5 5.8 %all-to-all-start.6 = ((bf16[8,80,256]{2,1,0:T(8,128)(2,1)}), bf16[8,80,256]{2,1,0:T(8,128)(2,1)S(1)}, u32[]{:S(2)}, u32[]{:S(2)}) async-start(bf16[8,80,256]{2,1,0:T(8,128)(2,1)} %pad_maximum_fusion.3), calls=%async_computation.6 | async-start | bytes 655360 | tf_op jit(solution)/shard_map/all_to_all | solution.py:139
  106.3 13.5 %all-to-all-done.6 = bf16[8,80,256]{2,1,0:T(8,128)(2,1)S(1)} async-done(((bf16[8,80,256]{2,1,0:T(8,128)(2,1)}), bf16[8,80,256]{2,1,0:T(8,128)(2,1)S(1)}, u32[]{:S(2)}, u32[]{:S(2)}) %all-to-all-start.6) | async-done | bytes 327712 | tf_op jit(solution)/shard_map/all_to_all | solution.py:139
  119.8 0.8 broadcast_in_dim.90
  120.6 4.0 %all-to-all-start.7 = ((bf16[8,80,256]{2,1,0:T(8,128)(2,1)}), bf16[8,80,256]{2,1,0:T(8,128)(2,1)S(1)}, u32[]{:S(2)}, u32[]{:S(2)}) async-start(bf16[8,80,256]{2,1,0:T(8,128)(2,1)} %broadcast_in_dim.90), calls=%async_computation.7 | async-start | bytes 655360 | tf_op jit(solution)/shard_map/all_to_all | solution.py:146
  124.6 2.7 %fusion.9 = f32[56,32,128]{2,1,0:T(8,128)S(1)} fusion(s32[56,128,128]{2,1,0:T(8,128)} %param.16, bf16[56,32,128]{2,1,0:T(8,128)(2,1)S(1)} %gather_fusion.3, pred[56]{0:T(512)(128)(4,1)S(1)} %compare_and_fusion.4), kind=kOutput, calls=%fused_computation.28 | convolution fusion | flops 59867136 | bytes 5046328 | tf_op jit(solution)/shard_map/tci,tij->tcj/dot_general | solution.py:163
  127.9 0.8 broadcast_select_fusion
  128.7 4.1 %all-to-all-done.7 = bf16[8,80,256]{2,1,0:T(8,128)(2,1)S(1)} async-done(((bf16[8,80,256]{2,1,0:T(8,128)(2,1)}), bf16[8,80,256]{2,1,0:T(8,128)(2,1)S(1)}, u32[]{:S(2)}, u32[]{:S(2)}) %all-to-all-start.7) | async-done | bytes 327712 | tf_op jit(solution)/shard_map/all_to_all | solution.py:146
  132.8 29.9 %all-to-all-start.5 = ((bf16[8,4,32,128]{3,2,1,0:T(8,128)(2,1)}), bf16[8,4,32,128]{3,2,1,0:T(8,128)(2,1)S(1)}, u32[]{:S(2)}, u32[]{:S(2)}) async-start(bf16[8,4,32,128]{3,2,1,0:T(8,128)(2,1)} %bitcast.42), calls=%async_computation.5 | async-start | bytes 524288 | tf_op jit(solution)/shard_map/all_to_all | solution.py:31
  163.3 0.8 broadcast_select_fusion.1
  164.2 5.9 %all-to-all-done.5 = bf16[8,4,32,128]{3,2,1,0:T(8,128)(2,1)S(1)} async-done(((bf16[8,4,32,128]{3,2,1,0:T(8,128)(2,1)}), bf16[8,4,32,128]{3,2,1,0:T(8,128)(2,1)S(1)}, u32[]{:S(2)}, u32[]{:S(2)}) %all-to-all-start.5) | async-done | bytes 262176 | tf_op jit(solution)/shard_map/all_to_all | solution.py:31
  170.0 3.4 %all-to-all-start.4 = ((bf16[8,4,32,128]{3,2,1,0:T(8,128)(2,1)}), bf16[8,4,32,128]{3,2,1,0:T(8,128)(2,1)S(1)}, u32[]{:S(2)}, u32[]{:S(2)}) async-start(bf16[8,4,32,128]{3,2,1,0:T(8,128)(2,1)} %bitcast.40), calls=%async_computation.4 | async-start | bytes 524288 | tf_op jit(solution)/shard_map/all_to_all | solution.py:31
  173.5 9.6 %all-to-all-done.4 = bf16[8,4,32,128]{3,2,1,0:T(8,128)(2,1)S(1)} async-done(((bf16[8,4,32,128]{3,2,1,0:T(8,128)(2,1)}), bf16[8,4,32,128]{3,2,1,0:T(8,128)(2,1)S(1)}, u32[]{:S(2)}, u32[]{:S(2)}) %all-to-all-start.4) | async-done | bytes 262176 | tf_op jit(solution)/shard_map/all_to_all | solution.py:31
  183.8 6.5 %all-to-all-start.8 = ((bf16[8,80,256]{2,1,0:T(8,128)(2,1)}), bf16[8,80,256]{2,1,0:T(8,128)(2,1)S(1)}, u32[]{:S(2)}, u32[]{:S(2)}) async-start(bf16[8,80,256]{2,1,0:T(8,128)(2,1)} %broadcast_in_dim.91), calls=%async_computation.8 | async-start | bytes 655360 | tf_op jit(solution)/shard_map/all_to_all | solution.py:146
  193.0 16.5 %all-to-all-done.8 = bf16[8,80,256]{2,1,0:T(8,128)(2,1)S(1)} async-done(((bf16[8,80,256]{2,1,0:T(8,128)(2,1)}), bf16[8,80,256]{2,1,0:T(8,128)(2,1)S(1)}, u32[]{:S(2)}, u32[]{:S(2)}) %all-to-all-start.8) | async-done | bytes 327712 | tf_op jit(solution)/shard_map/all_to_all | solution.py:146
  (103 shorter events, 16.5 us)
Async XLA Ops:
  0.6 77.0 %copy-start = (bf16[256,256]{1,0:T(8,128)(2,1)S(1)}, bf16[256,256]{1,0:T(8,128)(2,1)}, u32[]{:S(2)}) copy-start(bf16[256,256]{1,0:T(8,128)(2,1)} %param.19) | copy-start | bytes 393220
  1.5 34.6 %copy-start.2 = (bf16[32,2048]{1,0:T(8,128)(2,1)S(1)}, bf16[32,2048]{1,0:T(8,128)(2,1)}, u32[]{:S(2)}) copy-start(bf16[32,2048]{1,0:T(8,128)(2,1)} %param.21) | copy-start | bytes 393220
  3.8 33.1 %copy-start.4 = (s32[56]{0:T(128)S(1)}, s32[56]{0:T(128)}, u32[]{:S(2)}) copy-start(s32[56]{0:T(128)} %param.15) | copy-start | bytes 676
  3.8 38.3 %copy-start.5 = (s32[56]{0:T(128)S(1)}, s32[56]{0:T(128)}, u32[]{:S(2)}) copy-start(s32[56]{0:T(128)} %param.14) | copy-start | bytes 676
  5.2 23.0 %all-to-all-start.1 = ((bf16[8,4,32,128]{3,2,1,0:T(8,128)(2,1)}), bf16[8,4,32,128]{3,2,1,0:T(8,128)(2,1)S(1)}, u32[]{:S(2)}, u32[]{:S(2)}) async-start(bf16[8,4,32,128]{3,2,1,0:T(8,128)(2,1)} %bitcast.16), calls=%async_computation.1 | async-start | bytes 524288 | tf_op jit(solution)/shard_map/all_to_all | solution.py:31
  28.2 14.6 %all-to-all-start = ((bf16[8,4,32,128]{3,2,1,0:T(8,128)(2,1)}), bf16[8,4,32,128]{3,2,1,0:T(8,128)(2,1)S(1)}, u32[]{:S(2)}, u32[]{:S(2)}) async-start(bf16[8,4,32,128]{3,2,1,0:T(8,128)(2,1)} %bitcast.13), calls=%async_computation | async-start | bytes 524288 | tf_op jit(solution)/shard_map/all_to_all | solution.py:31
  46.6 30.8 %copy-start.1 = (bf16[256,256]{1,0:T(8,128)(2,1)S(1)}, bf16[256,256]{1,0:T(8,128)(2,1)}, u32[]{:S(2)}) copy-start(bf16[256,256]{1,0:T(8,128)(2,1)} %param.18) | copy-start | bytes 393220
  46.7 31.0 %copy-start.6 = (f32[256]{0:T(256)S(1)}, f32[256]{0:T(256)}, u32[]{:S(2)}) copy-start(f32[256]{0:T(256)} %param.20) | copy-start | bytes 3076
  48.5 28.3 %all-to-all-start.2 = ((bf16[8,3,2,32,128]{4,3,2,1,0:T(8,128)(2,1)}), bf16[8,3,2,32,128]{4,3,2,1,0:T(8,128)(2,1)S(1)}, u32[]{:S(2)}, u32[]{:S(2)}) async-start(bf16[8,3,2,32,128]{4,3,2,1,0:T(8,128)(2,1)} %copy.131), calls=%async_computation.2 | async-start | bytes 786432 | tf_op jit(solution)/shard_map/all_to_all | solution.py:110
  80.1 19.3 %all-to-all-start.3 = ((bf16[8,2,2,32,128]{4,2,3,1,0:T(2,128)(2,1)}), bf16[8,2,2,32,128]{4,2,3,1,0:T(2,128)(2,1)S(1)}, u32[]{:S(2)}, u32[]{:S(2)}) async-start(bf16[8,2,2,32,128]{4,2,3,1,0:T(2,128)(2,1)} %copy.138), calls=%async_computation.3 | async-start | bytes 524288 | tf_op jit(solution)/shard_map/all_to_all | solution.py:126
  99.5 20.3 %all-to-all-start.6 = ((bf16[8,80,256]{2,1,0:T(8,128)(2,1)}), bf16[8,80,256]{2,1,0:T(8,128)(2,1)S(1)}, u32[]{:S(2)}, u32[]{:S(2)}) async-start(bf16[8,80,256]{2,1,0:T(8,128)(2,1)} %pad_maximum_fusion.3), calls=%async_computation.6 | async-start | bytes 655360 | tf_op jit(solution)/shard_map/all_to_all | solution.py:139
  120.6 12.2 %all-to-all-start.7 = ((bf16[8,80,256]{2,1,0:T(8,128)(2,1)}), bf16[8,80,256]{2,1,0:T(8,128)(2,1)S(1)}, u32[]{:S(2)}, u32[]{:S(2)}) async-start(bf16[8,80,256]{2,1,0:T(8,128)(2,1)} %broadcast_in_dim.90), calls=%async_computation.7 | async-start | bytes 655360 | tf_op jit(solution)/shard_map/all_to_all | solution.py:146
  127.3 63.2 %copy-start.3 = (s32[1,8,4]{1,2,0:T(4,128)S(1)}, s32[1,8,4]{1,2,0:T(4,128)}, u32[]{:S(2)}) copy-start(s32[1,8,4]{1,2,0:T(4,128)} %param.17) | copy-start | bytes 388
  132.8 37.2 %all-to-all-start.5 = ((bf16[8,4,32,128]{3,2,1,0:T(8,128)(2,1)}), bf16[8,4,32,128]{3,2,1,0:T(8,128)(2,1)S(1)}, u32[]{:S(2)}, u32[]{:S(2)}) async-start(bf16[8,4,32,128]{3,2,1,0:T(8,128)(2,1)} %bitcast.42), calls=%async_computation.5 | async-start | bytes 524288 | tf_op jit(solution)/shard_map/all_to_all | solution.py:31
  170.0 13.1 %all-to-all-start.4 = ((bf16[8,4,32,128]{3,2,1,0:T(8,128)(2,1)}), bf16[8,4,32,128]{3,2,1,0:T(8,128)(2,1)S(1)}, u32[]{:S(2)}, u32[]{:S(2)}) async-start(bf16[8,4,32,128]{3,2,1,0:T(8,128)(2,1)} %bitcast.40), calls=%async_computation.4 | async-start | bytes 524288 | tf_op jit(solution)/shard_map/all_to_all | solution.py:31
  183.8 25.7 %all-to-all-start.8 = ((bf16[8,80,256]{2,1,0:T(8,128)(2,1)}), bf16[8,80,256]{2,1,0:T(8,128)(2,1)S(1)}, u32[]{:S(2)}, u32[]{:S(2)}) async-start(bf16[8,80,256]{2,1,0:T(8,128)(2,1)} %broadcast_in_dim.91), calls=%async_computation.8 | async-start | bytes 655360 | tf_op jit(solution)/shard_map/all_to_all | solution.py:146

commit v2 on v0

v2 whole, which is shorter than its diff:
```python
import functools

import jax
import jax.numpy as jnp
from jax import lax
from jax.experimental import pallas as pl
from jax.experimental.pallas import tpu as pltpu
from jax.sharding import PartitionSpec as P

GROUP = 8
Y, Z_LO, CORE, X, Z_HI = 4, 8, 2, 4, 2
BF16 = jnp.bfloat16
F32 = jnp.float32
FIRST = (((0,), (0,)), ((), ()))
LAST = (((1,), (1,)), ((), ()))
VMEM = pl.BlockSpec(memory_space=pltpu.VMEM)
SMEM = pl.BlockSpec(memory_space=pltpu.SMEM)


def gelu_slope(pre_act):
    inner = 0.7978845608 * (pre_act + 0.044715 * pre_act * pre_act * pre_act)
    tanh_value = jnp.tanh(inner)
    return 0.5 * (1.0 + tanh_value) + 0.5 * pre_act * (
        1.0 - tanh_value * tanh_value
    ) * 0.7978845608 * (1.0 + 3.0 * 0.044715 * pre_act * pre_act)


def dot(left, right, dims=(((1,), (0,)), ((), ()))):
    return lax.dot_general(left, right, dims, preferred_element_type=F32)


def call(body, out_shape, in_specs, scratch=(), cost=(1e7, 1e6)):
    outs = jax.tree.map(lambda _: VMEM, out_shape)
    return pl.pallas_call(
        body,
        out_shape=out_shape,
        in_specs=in_specs,
        out_specs=outs,
        scratch_shapes=scratch,
        compiler_params=pltpu.CompilerParams(vmem_limit_bytes=32 * 2**20),
        cost_estimate=pl.CostEstimate(
            flops=int(cost[0]), bytes_accessed=int(cost[1]), transcendentals=0
        ),
    )


def places():
    blk = lax.axis_index("blk")
    return lax.rem(blk, GROUP), lax.rem(blk + GROUP // 2, GROUP)


def kind_of(distance):
    k = 2 * (jnp.abs(distance) - 1) + jnp.where(distance < 0, 1, 0)
    return jnp.clip(k, 0, 7)


def offset_of(kind):
    return (kind // 2 + 1) * (1 - 2 * lax.rem(kind, 2))


def inside(place):
    return jnp.logical_and(place >= 0, place < GROUP)


def bounded(place):
    return jnp.clip(place, 0, GROUP - 1)


def pack_kernel(width, x_ref, cot_ref, send_ref, a_ref, b_ref, xc_ref):
    place_a, place_b = places()
    cap = send_ref.shape[1]
    for ref, place in ((b_ref, place_b), (a_ref, place_a)):
        for peer in range(GROUP):
            kind = kind_of(peer - place)
            for m in range(cap):
                start = pl.multiple_of(send_ref[kind, m] * width, width)
                ref[peer, m] = x_ref[:, pl.ds(start, width)]
    for block in range(x_ref.shape[1] // width):
        cols = slice(block * width, (block + 1) * width)
        xc_ref[block // 2, 0, block % 2] = x_ref[:, cols]
        xc_ref[block // 2, 1, block % 2] = cot_ref[:, cols]


def local_kernel(slots, chunk, x_ref, dst_ref, src_ref, cnt_ref, half_ref, acc_ref):
    step = pl.program_id(0)
    width = cnt_ref.shape[1]
    dim = x_ref.shape[0]
    half_ref[...] = cnt_ref[...].astype(F32).astype(BF16)

    @pl.when(step == 0)
    def _():
        acc_ref[...] = jnp.zeros_like(acc_ref)

    @pl.when(step * chunk >= slots)
    def _():
        ones = jnp.ones((16, width), BF16)
        for i in range(chunk):
            tile = step * chunk + i
            start = pl.multiple_of(src_ref[tile] * width, width)
            rows = jnp.concatenate([x_ref[:, pl.ds(start, width)], ones], axis=0)
            dst = dst_ref[tile]
            acc_ref[dst] += dot(rows, half_ref[i], LAST)[: dim + 8]


def aggregate_kernel(slots, a_ref, b_ref, dst_ref, src_ref, half_ref, acc_in, agg_ref, deg_ref, acc_ref):
    place_a, place_b = places()
    cap, dim, width = a_ref.shape[1:]
    blocks = acc_in.shape[0]
    ones = jnp.ones((16, width), BF16)
    acc_ref[...] = acc_in[...]
    for tile in range(slots):
        slot = src_ref[tile] - blocks
        kind = slot // cap
        m = lax.rem(slot, cap)
        row_a = place_a - offset_of(kind)
        row_b = place_b - offset_of(kind)
        got = jnp.where(inside(row_a), a_ref[bounded(row_a), m], b_ref[bounded(row_b), m])
        rows = jnp.concatenate([got, ones], axis=0)
        dst = dst_ref[tile]
        acc_ref[dst] += dot(rows, half_ref[tile], LAST)[: dim + 8]
    for block in range(blocks):
        degree = jnp.maximum(acc_ref[block, dim : dim + 8], 1.0)
        deg_ref[block] = degree
        agg_ref[block // 2, block % 2] = (acc_ref[block, :dim] / degree[:1]).astype(BF16)


def node_kernel(
    xc_ref, agg_ref, deg_ref, wt_ref, neigh_ref, own_w_ref, bias_ref, home_ref, dz_ref, xa_ref
):
    cols, _, per_col, dim, width = xc_ref.shape
    full = cols * dim
    col = lax.axis_index("col")
    for p in range(per_col):
        lanes = slice(p * width, (p + 1) * width)
        x = xc_ref[:, 0, p].reshape(full, width)
        cot = xc_ref[:, 1, p].reshape(full, width)
        xa = jnp.concatenate([x, agg_ref[:, p].reshape(full, width)], axis=0)
        xa_ref[:, lanes] = xa
        pre = dot(wt_ref[...], xa) + bias_ref[...]
        dz = (cot.astype(F32) * gelu_slope(pre)).astype(BF16)
        dz_ref[:, lanes] = dz
        degree = deg_ref[col * per_col + p][:1]
        scaled = (dot(neigh_ref[...], dz) / degree).astype(BF16)
        home_ref[:, 0, p] = scaled.reshape(cols, dim, width)
        own = dot(own_w_ref[...], dz).astype(BF16)
        home_ref[:, 1, p] = own.reshape(cols, dim, width)


def weight_kernel(dim, xa_ref, dz_ref, part_ref):
    full = dz_ref.shape[0]
    grads = dot(xa_ref[...], dz_ref[...], LAST)
    total = dot(jnp.ones((16, dz_ref.shape[1]), BF16), dz_ref[...], LAST)
    tail = jnp.concatenate([total[:8, :128], total[8:, 128:]], axis=0).astype(BF16)
    for which in range(2):
        for quarter in range(4):
            for x in range(X):
                rows = [
                    grads[start : start + 8]
                    for z in range(Z_HI)
                    for start in [which * full + (x * Z_HI + z) * dim + quarter * 8]
                ]
                piece = (which * 4 + quarter) * X + x
                part_ref[piece, :, :full] = jnp.concatenate(rows, axis=0).astype(BF16)
                part_ref[piece, :, full:] = tail


def contribution_kernel(slots, home_ref, dst_ref, src_ref, half_ref, a_ref, b_ref, hold_ref):
    place_a, place_b = places()
    blocks = home_ref.shape[0] * home_ref.shape[2]
    cap = a_ref.shape[1]
    for tile in range(slots):
        dst = dst_ref[tile]
        value = dot(home_ref[dst // 2, 0, lax.rem(dst, 2)], half_ref[tile])
        hold_ref[src_ref[tile] - blocks] = value.astype(BF16)
    for ref, place in ((b_ref, place_b), (a_ref, place_a)):
        for peer in range(GROUP):
            kind = kind_of(place - peer)
            for m in range(cap):
                ref[peer, m] = hold_ref[kind * cap + m]


def local_back_kernel(slots, home_ref, dst_ref, src_ref, half_ref, acc_ref):
    per = home_ref.shape[2]
    for block in range(acc_ref.shape[0]):
        acc_ref[block] = home_ref[block // per, 1, block % per].astype(F32)
    for tile in range(slots, half_ref.shape[0]):
        dst = dst_ref[tile]
        src = src_ref[tile]
        acc_ref[src] += dot(home_ref[dst // 2, 0, lax.rem(dst, 2)], half_ref[tile])


def finish_kernel(acc_in, a_ref, b_ref, send_ref, out_ref, acc_ref):
    place_a, place_b = places()
    kinds, cap = send_ref.shape
    width = acc_in.shape[2]
    acc_ref[...] = acc_in[...]
    for kind in range(kinds):
        offset = (kind // 2 + 1) * (1 - 2 * (kind % 2))
        row_a = place_a + offset
        row_b = place_b + offset
        for m in range(cap):
            got = jnp.where(inside(row_a), a_ref[bounded(row_a), m], b_ref[bounded(row_b), m])
            acc_ref[send_ref[kind, m]] += got.astype(F32)
    for block in range(acc_ref.shape[0]):
        out_ref[:, block * width : (block + 1) * width] = acc_ref[block].astype(BF16)


def rank(y, z_lo, core, x, z_hi):
    return ((y * Z_LO + z_lo) * CORE + core) * X * Z_HI + x * Z_HI + z_hi


def swap(rows, shift):
    devices = lax.axis_size("blk")
    groups = [
        [(first + shift + i) % devices for i in range(GROUP)] for first in range(0, devices, GROUP)
    ]
    return lax.all_to_all(rows, "blk", 0, 0, axis_index_groups=groups, tiled=False)


def over_col(rows):
    return lax.all_to_all(rows, "col", 0, 0, tiled=False)


def per_device(
    node_feats, tile_dst, tile_src, tile_cnt, send_blk, self_weight, neigh_weight, bias, cotangent
):
    dim, nodes = node_feats.shape
    tiles, width = tile_cnt.shape[:2]
    blocks = nodes // width
    table = send_blk[0]
    kinds, cap = table.shape
    slots = kinds * cap
    cols = X * Z_HI
    per_col = blocks // cols
    full = cols * dim
    chunk = 8
    halo = jax.ShapeDtypeStruct((GROUP, cap, dim, width), BF16)
    pairs = jax.ShapeDtypeStruct((cols, 2, per_col, dim, width), BF16)
    ranged = jax.ShapeDtypeStruct((cols, per_col, dim, width), BF16)

    send_a, send_b, xc = call(
        functools.partial(pack_kernel, width),
        (halo, halo, pairs),
        [VMEM, VMEM, SMEM],
    )(node_feats, cotangent, table)
    got_b = swap(send_b, GROUP // 2)
    got_a = swap(send_a, 0)
    xc, got_a = lax.optimization_barrier((xc, got_a))
    xc = over_col(xc)
    whole = lambda shape: pl.BlockSpec(shape, lambda i: (0,) * len(shape))
    half, acc = pl.pallas_call(
        functools.partial(local_kernel, slots, chunk),
        grid=(tiles // chunk,),
        out_shape=(
            jax.ShapeDtypeStruct(tile_cnt.shape, BF16),
            jax.ShapeDtypeStruct((blocks, dim + 8, width), F32),
        ),
        in_specs=[
            whole((dim, nodes)),
            SMEM,
            SMEM,
            pl.BlockSpec((chunk, width, width), lambda i: (i, 0, 0)),
        ],
        out_specs=(
            pl.BlockSpec((chunk, width, width), lambda i: (i, 0, 0)),
            whole((blocks, dim + 8, width)),
        ),
        compiler_params=pltpu.CompilerParams(vmem_limit_bytes=32 * 2**20),
        cost_estimate=pl.CostEstimate(
            flops=60000000, bytes_accessed=6000000, transcendentals=0
        ),
    )(node_feats, tile_dst, tile_src, tile_cnt)
    weight_t = jnp.concatenate([self_weight.T, neigh_weight.T], axis=1)
    bias_col = bias[:, None]
    agg, degree = call(
        functools.partial(aggregate_kernel, slots),
        (ranged, jax.ShapeDtypeStruct((blocks, 8, width), F32)),
        [VMEM, VMEM, SMEM, SMEM, VMEM, VMEM],
        [pltpu.VMEM((blocks, dim + 8, width), F32)],
    )(got_a, got_b, tile_dst, tile_src, half, acc)
    agg, xc = lax.optimization_barrier((agg, xc))
    agg = over_col(agg)
    home, dz, xa = call(
        node_kernel,
        (
            pairs,
            jax.ShapeDtypeStruct((full, per_col * width), BF16),
            jax.ShapeDtypeStruct((2 * full, per_col * width), BF16),
        ),
        [VMEM] * 7,
    )(xc, agg, degree, weight_t, neigh_weight, self_weight, bias_col)
    home = over_col(home)
    part = call(
        functools.partial(weight_kernel, dim),
        jax.ShapeDtypeStruct((Y * CORE * X, 16, full + 128), BF16),
        [VMEM] * 2,
    )(xa, dz)
    part, home = lax.optimization_barrier((part, home))

    both = ("blk", "col")
    flat = [
        [rank(y, l, c, x, h) for y in range(Y) for c in range(CORE) for x in range(X)]
        for l in range(Z_LO)
        for h in range(Z_HI)
    ]
    line = [
        [rank(y, l, c, x, h) for h in range(Z_HI) for l in range(Z_LO)]
        for y in range(Y)
        for c in range(CORE)
        for x in range(X)
    ]
    plane = [[(y * Z_LO + l) * CORE + c for y in range(Y) for c in range(CORE)] for l in range(Z_LO)]
    part = lax.all_to_all(part, both, 0, 0, axis_index_groups=flat, tiled=False)
    away_a, away_b = call(
        functools.partial(contribution_kernel, slots),
        (halo, halo),
        [VMEM, SMEM, SMEM, VMEM],
        [pltpu.VMEM((slots, dim, width), BF16)],
    )(home, tile_dst, tile_src, half)
    away_b, part = lax.optimization_barrier((away_b, part))
    back_b = swap(away_b, GROUP // 2)
    away_a, back_b = lax.optimization_barrier((away_a, back_b))
    back_a = swap(away_a, 0)
    part = jnp.sum(part.astype(F32), axis=0)
    tail = jnp.concatenate([part[0:4, full:], part[8:12, full:]], axis=0)
    ends = [jnp.concatenate([part[8 * h : 8 * h + 8, :full], tail], axis=1) for h in range(Z_HI)]
    part = jnp.broadcast_to(jnp.stack(ends)[:, None], (Z_HI, Z_LO, 8, full + 128))
    part = part.reshape(Z_HI * Z_LO, 8, full + 128)
    part, back_a = lax.optimization_barrier((part, back_a))
    part = jnp.sum(lax.all_to_all(part, both, 0, 0, axis_index_groups=line, tiled=False), axis=0)
    grad_bias = jnp.concatenate([part[0, full:], part[4, full:]])
    grad_bias = lax.dynamic_slice_in_dim(grad_bias, lax.axis_index("col") * dim, dim, 0)
    part = jnp.broadcast_to(part[None, :, :full], (Y * CORE, 8, full))
    part = lax.all_to_all(part, "blk", 0, 0, axis_index_groups=plane, tiled=False)
    part = part.reshape(2, dim, full)
    grad_self, grad_neigh = part[0], part[1]

    acc = call(
        functools.partial(local_back_kernel, slots),
        jax.ShapeDtypeStruct((blocks, dim, width), F32),
        [VMEM, SMEM, SMEM, VMEM],
    )(home, tile_dst, tile_src, half)
    grad_feats = call(
        finish_kernel,
        jax.ShapeDtypeStruct((dim, nodes), BF16),
        [VMEM, VMEM, VMEM, SMEM],
        [pltpu.VMEM((blocks, dim, width), F32)],
    )(acc, back_a, back_b, table)
    return grad_feats, grad_self, grad_neigh, grad_bias


def solution(mesh):
    placed = (
        P("col", "blk"),
        P("blk"),
        P("blk"),
        P("blk", None, None),
        P("blk", None, None),
        P(),
        P(),
        P(),
        P("col", "blk"),
    )
    return jax.shard_map(
        per_device,
        mesh=mesh,
        in_specs=placed,
        out_specs=(P("col", "blk"), P("col", None), P("col", None), P("col")),
        check_vma=False,
    )
```

time: 1110 us -> 202 us (0.18)
  waiting for transfers between devices: 986 us -> 80.5 us
  blocking collectives: 0 us -> 34.4 us
  matrix products: 17.3 us -> 0 us
  starting transfers between devices: 76 us -> 61 us
  between operations: 14.2 us -> 0.8 us
  Pallas kernels: 0 us -> 12 us
    psum x1 -> x0, waiting for transfers between devices: 715 us -> none  [per_device(): lax.psum((self_grad, neigh_grad, bias_local), 'blk')]
    reduce_scatter x1 -> x0, waiting for transfers between devices: 143 us -> none  [per_device(): lax.psum_scatter(lax.dot_general(self_part, node_feats, contract_first, p...]
    all_gather x1 -> x0, waiting for transfers between devices: 83.4 us -> none  [per_device(): grad_part = lax.all_gather(grad_pre, 'col', axis=0, tiled=True)]
    all_to_all x0 -> x8, waiting for transfers between devices: none -> 80.5 us  [the longest x3 37.5 us: over_col(): return lax.all_to_all(rows, 'col', 0, 0, tiled=False)]
    ppermute x16 -> x0, starting transfers between devices: 75.9 us -> none  [shifted(): return lax.ppermute(block, axis, route)]
    all_to_all x0 -> x8, starting transfers between devices: none -> 61 us  [the longest x3 27.4 us: over_col(): return lax.all_to_all(rows, 'col', 0, 0, tiled=False)]
    ppermute x16 -> x0, waiting for transfers between devices: 45.2 us -> none  [shifted(): return lax.ppermute(block, axis, route)]
    all_to_all x0 -> x2, blocking collectives: none -> 34.4 us  [swap(): lax.all_to_all(rows, 'blk', 0, 0, axis_index_groups=groups, tiled=False)]
  transfers between devices with their start and end apart: 19 -> 8, of which waited for: 10 -> 8; matrix products, arithmetic and copies ran while one was open for 1% -> 1% of each run, Pallas kernels for 0% -> 4%
where the time goes in v2:
time: 202 us; the launch traced here: 198 us
  waiting for transfers between devices  80.5 us (40%)
  starting transfers between devices  61 us (30%)
  blocking collectives  34.4 us (17%)
  Pallas kernels  12 us (6%)
  local copies, waits for them, and re-layouts  9.72 us (5%)
    all_to_all x3, waiting for transfers between devices, over_col(): return lax.all_to_all(rows, 'col', 0, 0, tiled=False)  37.5 us
    all_to_all x2, blocking collectives, swap(): lax.all_to_all(rows, 'blk', 0, 0, axis_index_groups=groups, tiled=False)  34.4 us
    all_to_all x3, starting transfers between devices, over_col(): return lax.all_to_all(rows, 'col', 0, 0, tiled=False)  27.4 us
    all_to_all x2, waiting for transfers between devices, swap(): lax.all_to_all(rows, 'blk', 0, 0, axis_index_groups=groups, tiled=False)  17 us
    all_to_all x2, starting transfers between devices, swap(): lax.all_to_all(rows, 'blk', 0, 0, axis_index_groups=groups, tiled=False)  16.8 us
    all_to_all x1, waiting for transfers between devices, per_device(): lax.all_to_all(part, both, 0, 0, axis_index_groups=line, tiled=False)  13.8 us
    all_to_all x1, waiting for transfers between devices, per_device(): part = lax.all_to_all(part, both, 0, 0, axis_index_groups=flat, tiled=False)  7.1 us
    all_to_all x1, starting transfers between devices, per_device(): lax.all_to_all(part, both, 0, 0, axis_index_groups=line, tiled=False)  6.81 us
  transfers between devices with their start and end apart: 8, of which 8 were waited for; matrix products, arithmetic and copies ran while one was open for 1% of the time, Pallas kernels for 4%

profile of v2, /device:TPU:6, one launch (start us, length us, event | category | flops | bytes accessed | tf_op | source)
XLA Modules:
  0.0 198.5 jit_solution(7714840371003484028)
XLA Ops:
  0.6 0.8 copy.22.send_ref
  1.4 0.9 copy-done.1
  2.3 0.9 copy-done.5
  3.2 1.6 shard_map.120
  4.8 15.4 %all_to_all.50.a_ref = bf16[8,4,32,128]{3,2,1,0:T(8,128)(2,1)S(1)} all-to-all(bf16[8,4,32,128]{3,2,1,0:T(8,128)(2,1)S(1)} %get-tuple-element.29), channel_id=1, replica_groups={{0,8,16,24,32,40,48,56},{64,72,80,88,96,104,112,120},{128,136,144,152,1..., dimensions={0} | all-to-all | bytes 524288 | tf_op jit(solution)/shard_map/all_to_all | solution.py:217
  20.2 12.2 %all-to-all-start.1 = ((bf16[8,4,32,128]{3,2,1,0:T(8,128)(2,1)}), bf16[8,4,32,128]{3,2,1,0:T(8,128)(2,1)S(1)}, u32[]{:S(2)}, u32[]{:S(2)}) async-start(bf16[8,4,32,128]{3,2,1,0:T(8,128)(2,1)} %get-tuple-element.31), calls=%async_computation.1 | async-start | bytes 524288 | tf_op jit(solution)/shard_map/all_to_all | solution.py:217
  32.4 7.4 %all-to-all-done.1.b_ref = bf16[8,4,32,128]{3,2,1,0:T(8,128)(2,1)S(1)} async-done(((bf16[8,4,32,128]{3,2,1,0:T(8,128)(2,1)}), bf16[8,4,32,128]{3,2,1,0:T(8,128)(2,1)S(1)}, u32[]{:S(2)}, u32[]{:S(2)}) %all-to-all-start.1) | async-done | bytes 262176 | tf_op jit(solution)/shard_map/all_to_all | solution.py:217
  39.8 14.2 %all-to-all-start.2 = ((bf16[8,2,2,32,128]{4,3,2,1,0:T(8,128)(2,1)}), bf16[8,2,2,32,128]{4,3,2,1,0:T(8,128)(2,1)S(1)}, u32[]{:S(2)}, u32[]{:S(2)}) async-start(bf16[8,2,2,32,128]{4,3,2,1,0:T(8,128)(2,1)} %get-tuple-element.35), calls=%async_computation.2 | async-start | bytes 524288 | tf_op jit(solution)/shard_map/all_to_all | solution.py:221
  54.0 2.0 %copy-done = s32[56,128,128]{2,1,0:T(8,128)S(1)} copy-done((s32[56,128,128]{2,1,0:T(8,128)S(1)}, s32[56,128,128]{2,1,0:T(8,128)}, u32[]{:S(2)}) %copy-start) | copy-done | bytes 3670040
  56.1 0.9 copy-done.2
  58.3 1.8 shard_map.121
  60.1 2.0 shard_map.122
  62.1 5.7 %all-to-all-done.2.xc_ref = bf16[8,2,2,32,128]{4,3,2,1,0:T(8,128)(2,1)S(1)} async-done(((bf16[8,2,2,32,128]{4,3,2,1,0:T(8,128)(2,1)}), bf16[8,2,2,32,128]{4,3,2,1,0:T(8,128)(2,1)S(1)}, u32[]{:S(2)}, u32[]{:S(2)}) %all-to-all-start.2) | async-done | bytes 262176 | tf_op jit(solution)/shard_map/all_to_all | solution.py:221
  67.8 8.7 %all-to-all-start.3 = ((bf16[8,2,32,128]{3,2,1,0:T(8,128)(2,1)}), bf16[8,2,32,128]{3,2,1,0:T(8,128)(2,1)S(1)}, u32[]{:S(2)}, u32[]{:S(2)}) async-start(bf16[8,2,32,128]{3,2,1,0:T(8,128)(2,1)} %get-tuple-element.37), calls=%async_computation.3 | async-start | bytes 262144 | tf_op jit(solution)/shard_map/all_to_all | solution.py:221
  76.9 14.3 %all-to-all-done.3.agg_ref = bf16[8,2,32,128]{3,2,1,0:T(8,128)(2,1)S(1)} async-done(((bf16[8,2,32,128]{3,2,1,0:T(8,128)(2,1)}), bf16[8,2,32,128]{3,2,1,0:T(8,128)(2,1)S(1)}, u32[]{:S(2)}, u32[]{:S(2)}) %all-to-all-start.3) | async-done | bytes 131104 | tf_op jit(solution)/shard_map/all_to_all | solution.py:221
  91.2 1.5 shard_map.123
  92.7 4.5 %all-to-all-start.4 = ((bf16[8,2,2,32,128]{4,3,2,1,0:T(8,128)(2,1)}), bf16[8,2,2,32,128]{4,3,2,1,0:T(8,128)(2,1)S(1)}, u32[]{:S(2)}, u32[]{:S(2)}) async-start(bf16[8,2,2,32,128]{4,3,2,1,0:T(8,128)(2,1)} %get-tuple-element.41), calls=%async_computation.4 | async-start | bytes 524288 | tf_op jit(solution)/shard_map/all_to_all | solution.py:221
  97.2 1.1 shard_map.124
  98.3 17.5 %all-to-all-done.4.home_ref = bf16[8,2,2,32,128]{4,3,2,1,0:T(8,128)(2,1)S(1)} async-done(((bf16[8,2,2,32,128]{4,3,2,1,0:T(8,128)(2,1)}), bf16[8,2,2,32,128]{4,3,2,1,0:T(8,128)(2,1)S(1)}, u32[]{:S(2)}, u32[]{:S(2)}) %all-to-all-start.4) | async-done | bytes 262176 | tf_op jit(solution)/shard_map/all_to_all | solution.py:221
  115.8 6.3 %all-to-all-start.5 = ((bf16[32,16,384]{2,1,0:T(8,128)(2,1)}), bf16[32,16,384]{2,1,0:T(8,128)(2,1)S(1)}, u32[]{:S(2)}, u32[]{:S(2)}) async-start(bf16[32,16,384]{2,1,0:T(8,128)(2,1)} %shard_map.124), calls=%async_computation.5 | async-start | bytes 786432 | tf_op jit(solution)/shard_map/all_to_all | solution.py:313
  122.1 1.7 shard_map.126
  123.8 7.1 %all-to-all-done.5 = bf16[32,16,384]{2,1,0:T(8,128)(2,1)S(1)} async-done(((bf16[32,16,384]{2,1,0:T(8,128)(2,1)}), bf16[32,16,384]{2,1,0:T(8,128)(2,1)S(1)}, u32[]{:S(2)}, u32[]{:S(2)}) %all-to-all-start.5) | async-done | bytes 393248 | tf_op jit(solution)/shard_map/all_to_all | solution.py:313
  130.9 18.9 %all_to_all.51.b_ref = bf16[8,4,32,128]{3,2,1,0:T(8,128)(2,1)S(1)} all-to-all(bf16[8,4,32,128]{3,2,1,0:T(8,128)(2,1)S(1)} %get-tuple-element.47), channel_id=1, replica_groups={{32,40,48,56,64,72,80,88},{96,104,112,120,128,136,144,152},{160,168,176..., dimensions={0} | all-to-all | bytes 524288 | tf_op jit(solution)/shard_map/all_to_all | solution.py:217
  149.8 4.7 %all-to-all-start.7 = ((bf16[8,4,32,128]{3,2,1,0:T(8,128)(2,1)}), bf16[8,4,32,128]{3,2,1,0:T(8,128)(2,1)S(1)}, u32[]{:S(2)}, u32[]{:S(2)}) async-start(bf16[8,4,32,128]{3,2,1,0:T(8,128)(2,1)} %get-tuple-element.48), calls=%async_computation.7 | async-start | bytes 524288 | tf_op jit(solution)/shard_map/all_to_all | solution.py:217
  154.6 9.6 %all-to-all-done.7.a_ref = bf16[8,4,32,128]{3,2,1,0:T(8,128)(2,1)S(1)} async-done(((bf16[8,4,32,128]{3,2,1,0:T(8,128)(2,1)}), bf16[8,4,32,128]{3,2,1,0:T(8,128)(2,1)S(1)}, u32[]{:S(2)}, u32[]{:S(2)}) %all-to-all-start.7) | async-done | bytes 262176 | tf_op jit(solution)/shard_map/all_to_all | solution.py:217
  164.2 0.7 broadcast_in_dim.7
  164.9 6.8 %all-to-all-start.8 = ((f32[16,8,384]{2,1,0:T(8,128)}), f32[16,8,384]{2,1,0:T(8,128)S(1)}, u32[]{:S(2)}, u32[]{:S(2)}) async-start(f32[16,8,384]{2,1,0:T(8,128)} %bitcast.6), calls=%async_computation.8 | async-start | bytes 393216 | tf_op jit(solution)/shard_map/all_to_all | solution.py:330
  171.7 0.9 shard_map.125.acc_in
  172.6 1.4 shard_map.127
  174.1 13.8 %all-to-all-done.8 = f32[16,8,384]{2,1,0:T(8,128)S(1)} async-done(((f32[16,8,384]{2,1,0:T(8,128)}), f32[16,8,384]{2,1,0:T(8,128)S(1)}, u32[]{:S(2)}, u32[]{:S(2)}) %all-to-all-start.8) | async-done | bytes 196640 | tf_op jit(solution)/shard_map/all_to_all | solution.py:330
  188.6 3.7 %all-to-all-start.9 = ((f32[8,8,256]{2,1,0:T(8,128)}), f32[8,8,256]{2,1,0:T(8,128)S(1)}, u32[]{:S(2)}, u32[]{:S(2)}) async-start(f32[8,8,256]{2,1,0:T(8,128)} %broadcast_in_dim.8), calls=%async_computation.9 | async-start | bytes 131072 | tf_op jit(solution)/shard_map/all_to_all | solution.py:334
  192.8 5.0 %all-to-all-done.9 = f32[8,8,256]{2,1,0:T(8,128)S(1)} async-done(((f32[8,8,256]{2,1,0:T(8,128)}), f32[8,8,256]{2,1,0:T(8,128)S(1)}, u32[]{:S(2)}, u32[]{:S(2)}) %all-to-all-start.9) | async-done | bytes 65568 | tf_op jit(solution)/shard_map/all_to_all | solution.py:334
  (34 shorter events, 3.7 us)
Async XLA Ops:
  1.4 0.9 copy-start.1
  2.3 0.9 copy-start.5
  20.2 19.6 %all-to-all-start.1 = ((bf16[8,4,32,128]{3,2,1,0:T(8,128)(2,1)}), bf16[8,4,32,128]{3,2,1,0:T(8,128)(2,1)S(1)}, u32[]{:S(2)}, u32[]{:S(2)}) async-start(bf16[8,4,32,128]{3,2,1,0:T(8,128)(2,1)} %get-tuple-element.31), calls=%async_computation.1 | async-start | bytes 524288 | tf_op jit(solution)/shard_map/all_to_all | solution.py:217
  32.4 44.1 %copy-start.3 = (bf16[256,256]{1,0:T(8,128)(2,1)S(1)}, bf16[256,256]{1,0:T(8,128)(2,1)}, u32[]{:S(2)}) copy-start(bf16[256,256]{1,0:T(8,128)(2,1)} %neigh_ref.1) | copy-start | bytes 393220
  32.4 44.2 %copy-start.4 = (bf16[256,256]{1,0:T(8,128)(2,1)S(1)}, bf16[256,256]{1,0:T(8,128)(2,1)}, u32[]{:S(2)}) copy-start(bf16[256,256]{1,0:T(8,128)(2,1)} %own_w_ref.1) | copy-start | bytes 393220
  39.8 28.0 %all-to-all-start.2 = ((bf16[8,2,2,32,128]{4,3,2,1,0:T(8,128)(2,1)}), bf16[8,2,2,32,128]{4,3,2,1,0:T(8,128)(2,1)S(1)}, u32[]{:S(2)}, u32[]{:S(2)}) async-start(bf16[8,2,2,32,128]{4,3,2,1,0:T(8,128)(2,1)} %get-tuple-element.35), calls=%async_computation.2 | async-start | bytes 524288 | tf_op jit(solution)/shard_map/all_to_all | solution.py:221
  54.0 2.0 %copy-start = (s32[56,128,128]{2,1,0:T(8,128)S(1)}, s32[56,128,128]{2,1,0:T(8,128)}, u32[]{:S(2)}) copy-start(s32[56,128,128]{2,1,0:T(8,128)} %cnt_ref.1) | copy-start | bytes 11010052
  56.1 0.9 copy-start.2
  57.0 0.7 copy-start.6
  57.6 0.7 copy-start.8
  58.3 18.4 %copy-start.10 = (f32[256]{0:T(256)S(1)}, f32[256]{0:T(256)}, u32[]{:S(2)}) copy-start(f32[256]{0:T(256)} %param.16) | copy-start | bytes 3076
  60.1 62.0 %copy-start.7 = (s32[56]{0:T(128)S(1)}, s32[56]{0:T(128)}, u32[]{:S(2)}) copy-start(s32[56]{0:T(128)} %dst_ref.7) | copy-start | bytes 676
  60.1 62.0 %copy-start.9 = (s32[56]{0:T(128)S(1)}, s32[56]{0:T(128)}, u32[]{:S(2)}) copy-start(s32[56]{0:T(128)} %src_ref.7) | copy-start | bytes 676
  67.8 23.4 %all-to-all-start.3 = ((bf16[8,2,32,128]{3,2,1,0:T(8,128)(2,1)}), bf16[8,2,32,128]{3,2,1,0:T(8,128)(2,1)S(1)}, u32[]{:S(2)}, u32[]{:S(2)}) async-start(bf16[8,2,32,128]{3,2,1,0:T(8,128)(2,1)} %get-tuple-element.37), calls=%async_computation.3 | async-start | bytes 262144 | tf_op jit(solution)/shard_map/all_to_all | solution.py:221
  92.7 23.1 %all-to-all-start.4 = ((bf16[8,2,2,32,128]{4,3,2,1,0:T(8,128)(2,1)}), bf16[8,2,2,32,128]{4,3,2,1,0:T(8,128)(2,1)S(1)}, u32[]{:S(2)}, u32[]{:S(2)}) async-start(bf16[8,2,2,32,128]{4,3,2,1,0:T(8,128)(2,1)} %get-tuple-element.41), calls=%async_computation.4 | async-start | bytes 524288 | tf_op jit(solution)/shard_map/all_to_all | solution.py:221
  115.8 15.1 %all-to-all-start.5 = ((bf16[32,16,384]{2,1,0:T(8,128)(2,1)}), bf16[32,16,384]{2,1,0:T(8,128)(2,1)S(1)}, u32[]{:S(2)}, u32[]{:S(2)}) async-start(bf16[32,16,384]{2,1,0:T(8,128)(2,1)} %shard_map.124), calls=%async_computation.5 | async-start | bytes 786432 | tf_op jit(solution)/shard_map/all_to_all | solution.py:313
  149.8 14.4 %all-to-all-start.7 = ((bf16[8,4,32,128]{3,2,1,0:T(8,128)(2,1)}), bf16[8,4,32,128]{3,2,1,0:T(8,128)(2,1)S(1)}, u32[]{:S(2)}, u32[]{:S(2)}) async-start(bf16[8,4,32,128]{3,2,1,0:T(8,128)(2,1)} %get-tuple-element.48), calls=%async_computation.7 | async-start | bytes 524288 | tf_op jit(solution)/shard_map/all_to_all | solution.py:217
  164.9 23.0 %all-to-all-start.8 = ((f32[16,8,384]{2,1,0:T(8,128)}), f32[16,8,384]{2,1,0:T(8,128)S(1)}, u32[]{:S(2)}, u32[]{:S(2)}) async-start(f32[16,8,384]{2,1,0:T(8,128)} %bitcast.6), calls=%async_computation.8 | async-start | bytes 393216 | tf_op jit(solution)/shard_map/all_to_all | solution.py:330
  188.6 9.3 %all-to-all-start.9 = ((f32[8,8,256]{2,1,0:T(8,128)}), f32[8,8,256]{2,1,0:T(8,128)S(1)}, u32[]{:S(2)}, u32[]{:S(2)}) async-start(f32[8,8,256]{2,1,0:T(8,128)} %broadcast_in_dim.8), calls=%async_computation.9 | async-start | bytes 131072 | tf_op jit(solution)/shard_map/all_to_all | solution.py:334

commit v3 on v2

--- a/solution.py
+++ b/solution.py
@@ -66,7 +66,7 @@
     return jnp.clip(place, 0, GROUP - 1)
 
 
-def pack_kernel(width, x_ref, cot_ref, send_ref, a_ref, b_ref, xc_ref):
+def pack_kernel(width, x_ref, send_ref, a_ref, b_ref):
     place_a, place_b = places()
     cap = send_ref.shape[1]
     for ref, place in ((b_ref, place_b), (a_ref, place_a)):
@@ -75,10 +75,30 @@
             for m in range(cap):
                 start = pl.multiple_of(send_ref[kind, m] * width, width)
                 ref[peer, m] = x_ref[:, pl.ds(start, width)]
-    for block in range(x_ref.shape[1] // width):
-        cols = slice(block * width, (block + 1) * width)
-        xc_ref[block // 2, 0, block % 2] = x_ref[:, cols]
-        xc_ref[block // 2, 1, block % 2] = cot_ref[:, cols]
+
+
+def column():
+    col = lax.axis_index("col")
+    return col // Z_HI, lax.rem(col, Z_HI)
+
+
+def split_kernel(width, x_ref, cot_ref, keep_ref, away_ref):
+    z_hi = column()[1]
+    per = keep_ref.shape[2]
+    for x in range(X):
+        for out, z in ((keep_ref, z_hi), (away_ref, 1 - z_hi)):
+            for p in range(per):
+                start = pl.multiple_of(((x * Z_HI + z) * per + p) * width, width)
+                out[x, 0, p] = x_ref[:, pl.ds(start, width)]
+                out[x, 1, p] = cot_ref[:, pl.ds(start, width)]
+
+
+def relay_kernel(keep_ref, got_ref, *outs):
+    x = column()[0]
+    for step, out in enumerate(outs, start=1):
+        to = lax.rem(x + step, X)
+        out[0] = keep_ref[to]
+        out[1] = got_ref[to]
 
 
 def local_kernel(slots, chunk, x_ref, dst_ref, src_ref, cnt_ref, half_ref, acc_ref):
@@ -125,25 +145,54 @@
 
 
 def node_kernel(
-    xc_ref, agg_ref, deg_ref, wt_ref, neigh_ref, own_w_ref, bias_ref, home_ref, dz_ref, xa_ref
+    keep_ref,
+    got_ref,
+    one_ref,
+    two_ref,
+    three_ref,
+    agg_ref,
+    deg_ref,
+    wt_ref,
+    neigh_ref,
+    own_w_ref,
+    bias_ref,
+    scaled_ref,
+    keep_own_ref,
+    away_own_ref,
+    dz_ref,
+    xa_ref,
+    cot_ref,
+    own_ref,
 ):
-    cols, _, per_col, dim, width = xc_ref.shape
+    _, per_col, dim, width = scaled_ref.shape
+    cols = X * Z_HI
     full = cols * dim
-    col = lax.axis_index("col")
+    x, z_hi = column()
+    arrived = [(keep_ref[x], got_ref[x])]
+    arrived += [(ref[0], ref[1]) for ref in (one_ref, two_ref, three_ref)]
+    for step, pair in enumerate(arrived):
+        source = lax.rem(x + X - step, X)
+        for z, piece in ((z_hi, pair[0]), (1 - z_hi, pair[1])):
+            rows = pl.ds(pl.multiple_of((source * Z_HI + z) * dim, dim), dim)
+            for p in range(per_col):
+                lanes = slice(p * width, (p + 1) * width)
+                xa_ref[rows, lanes] = piece[0, p]
+                cot_ref[rows, lanes] = piece[1, p]
     for p in range(per_col):
         lanes = slice(p * width, (p + 1) * width)
-        x = xc_ref[:, 0, p].reshape(full, width)
-        cot = xc_ref[:, 1, p].reshape(full, width)
-        xa = jnp.concatenate([x, agg_ref[:, p].reshape(full, width)], axis=0)
-        xa_ref[:, lanes] = xa
-        pre = dot(wt_ref[...], xa) + bias_ref[...]
-        dz = (cot.astype(F32) * gelu_slope(pre)).astype(BF16)
+        xa_ref[full:, lanes] = agg_ref[:, p].reshape(full, width)
+        pre = dot(wt_ref[...], xa_ref[:, lanes]) + bias_ref[...]
+        dz = (cot_ref[:, lanes].astype(F32) * gelu_slope(pre)).astype(BF16)
         dz_ref[:, lanes] = dz
-        degree = deg_ref[col * per_col + p][:1]
+        degree = deg_ref[(x * Z_HI + z_hi) * per_col + p][:1]
         scaled = (dot(neigh_ref[...], dz) / degree).astype(BF16)
-        home_ref[:, 0, p] = scaled.reshape(cols, dim, width)
-        own = dot(own_w_ref[...], dz).astype(BF16)
-        home_ref[:, 1, p] = own.reshape(cols, dim, width)
+        scaled_ref[:, p] = scaled.reshape(cols, dim, width)
+        own_ref[:, lanes] = dot(own_w_ref[...], dz).astype(BF16)
+    for to in range(X):
+        for out, z in ((keep_own_ref, z_hi), (away_own_ref, 1 - z_hi)):
+            rows = pl.ds(pl.multiple_of((to * Z_HI + z) * dim, dim), dim)
+            for p in range(per_col):
+                out[to, p] = own_ref[rows, p * width : (p + 1) * width]
 
 
 def weight_kernel(dim, xa_ref, dz_ref, part_ref):
@@ -164,13 +213,37 @@
                 part_ref[piece, :, full:] = tail
 
 
+def fold_kernel(part_ref, mine_ref, other_ref):
+    full = part_ref.shape[2] - 128
+    z_hi = column()[1]
+    total = part_ref[0].astype(F32)
+    for i in range(1, part_ref.shape[0]):
+        total += part_ref[i].astype(F32)
+    tail = jnp.concatenate([total[0:4, full:], total[8:12, full:]], axis=0)
+    low, high = total[:8, :full], total[8:, :full]
+    mine_ref[:, :full] = jnp.where(z_hi == 0, low, high)
+    other_ref[:, :full] = jnp.where(z_hi == 0, high, low)
+    mine_ref[:, full:] = tail
+    other_ref[:, full:] = tail
+
+
+def order_kernel(near_ref, far_ref, self_ref, neigh_ref):
+    blk = lax.axis_index("blk")
+    mine = blk // (Z_LO * CORE) * CORE + lax.rem(blk, CORE)
+    for piece in range(Y * CORE):
+        offset = jnp.bitwise_xor(mine, piece)
+        rows = jnp.where(lax.rem(offset, 2) == 0, near_ref[offset // 2], far_ref[offset // 2])
+        out = self_ref if piece < 4 else neigh_ref
+        out[piece % 4 * 8 : piece % 4 * 8 + 8] = rows
+
+
 def contribution_kernel(slots, home_ref, dst_ref, src_ref, half_ref, a_ref, b_ref, hold_ref):
     place_a, place_b = places()
-    blocks = home_ref.shape[0] * home_ref.shape[2]
+    blocks = home_ref.shape[0] * home_ref.shape[1]
     cap = a_ref.shape[1]
     for tile in range(slots):
         dst = dst_ref[tile]
-        value = dot(home_ref[dst // 2, 0, lax.rem(dst, 2)], half_ref[tile])
+        value = dot(home_ref[dst // 2, lax.rem(dst, 2)], half_ref[tile])
         hold_ref[src_ref[tile] - blocks] = value.astype(BF16)
     for ref, place in ((b_ref, place_b), (a_ref, place_a)):
         for peer in range(GROUP):
@@ -180,20 +253,29 @@
 
 
 def local_back_kernel(slots, home_ref, dst_ref, src_ref, half_ref, acc_ref):
-    per = home_ref.shape[2]
-    for block in range(acc_ref.shape[0]):
-        acc_ref[block] = home_ref[block // per, 1, block % per].astype(F32)
+    acc_ref[...] = jnp.zeros_like(acc_ref)
     for tile in range(slots, half_ref.shape[0]):
         dst = dst_ref[tile]
         src = src_ref[tile]
-        acc_ref[src] += dot(home_ref[dst // 2, 0, lax.rem(dst, 2)], half_ref[tile])
-
-
-def finish_kernel(acc_in, a_ref, b_ref, send_ref, out_ref, acc_ref):
+        acc_ref[src] += dot(home_ref[dst // 2, lax.rem(dst, 2)], half_ref[tile])
+
+
+def finish_kernel(
+    acc_in, a_ref, b_ref, keep_ref, got_ref, one_ref, two_ref, three_ref, send_ref, out_ref, acc_ref
+):
     place_a, place_b = places()
+    x, z_hi = column()
     kinds, cap = send_ref.shape
     width = acc_in.shape[2]
-    acc_ref[...] = acc_in[...]
+    per = keep_ref.shape[1]
+    arrived = [(keep_ref[x], got_ref[x])]
+    arrived += [(ref[0], ref[1]) for ref in (one_ref, two_ref, three_ref)]
+    for step, pair in enumerate(arrived):
+        source = lax.rem(x + X - step, X)
+        for z, piece in ((z_hi, pair[0]), (1 - z_hi, pair[1])):
+            for p in range(per):
+                block = (source * Z_HI + z) * per + p
+                acc_ref[block] = acc_in[block] + piece[p].astype(F32)
     for kind in range(kinds):
         offset = (kind // 2 + 1) * (1 - 2 * (kind % 2))
         row_a = place_a + offset
@@ -219,6 +301,24 @@
 
 def over_col(rows):
     return lax.all_to_all(rows, "col", 0, 0, tiled=False)
+
+
+def flip_z(rows):
+    return lax.ppermute(rows, "col", [(c, c ^ 1) for c in range(X * Z_HI)])
+
+
+def turn_x(keep, got):
+    shape = jax.ShapeDtypeStruct((2,) + keep.shape[1:], BF16)
+    sent = call(relay_kernel, (shape,) * (X - 1), [VMEM] * 2)(keep, got)
+    cols = X * Z_HI
+    return [
+        lax.ppermute(piece, "col", [(c, (c + Z_HI * step) % cols) for c in range(cols)])
+        for step, piece in enumerate(sent, start=1)
+    ]
+
+
+def across(rows, bit):
+    return lax.ppermute(rows, "blk", [(e, e ^ bit) for e in range(Y * Z_LO * CORE)])
 
 
 def per_device(
@@ -235,18 +335,20 @@
     full = cols * dim
     chunk = 8
     halo = jax.ShapeDtypeStruct((GROUP, cap, dim, width), BF16)
-    pairs = jax.ShapeDtypeStruct((cols, 2, per_col, dim, width), BF16)
     ranged = jax.ShapeDtypeStruct((cols, per_col, dim, width), BF16)
-
-    send_a, send_b, xc = call(
-        functools.partial(pack_kernel, width),
-        (halo, halo, pairs),
-        [VMEM, VMEM, SMEM],
-    )(node_feats, cotangent, table)
+    half_x = jax.ShapeDtypeStruct((X, 2, per_col, dim, width), BF16)
+    half_own = jax.ShapeDtypeStruct((X, per_col, dim, width), BF16)
+
+    send_a, send_b = call(
+        functools.partial(pack_kernel, width), (halo, halo), [VMEM, SMEM]
+    )(node_feats, table)
     got_b = swap(send_b, GROUP // 2)
+    keep, away = call(
+        functools.partial(split_kernel, width), (half_x, half_x), [VMEM] * 2
+    )(node_feats, cotangent)
+    got = flip_z(away)
+    send_a, got_b = lax.optimization_barrier((send_a, got_b))
     got_a = swap(send_a, 0)
-    xc, got_a = lax.optimization_barrier((xc, got_a))
-    xc = over_col(xc)
     whole = lambda shape: pl.BlockSpec(shape, lambda i: (0,) * len(shape))
     half, acc = pl.pallas_call(
         functools.partial(local_kernel, slots, chunk),
@@ -278,74 +380,70 @@
         [VMEM, VMEM, SMEM, SMEM, VMEM, VMEM],
         [pltpu.VMEM((blocks, dim + 8, width), F32)],
     )(got_a, got_b, tile_dst, tile_src, half, acc)
-    agg, xc = lax.optimization_barrier((agg, xc))
+    got, agg = lax.optimization_barrier((got, agg))
     agg = over_col(agg)
-    home, dz, xa = call(
+    turned = turn_x(keep, got)
+    scaled, keep_own, away_own, dz, xa = call(
         node_kernel,
         (
-            pairs,
+            ranged,
+            half_own,
+            half_own,
             jax.ShapeDtypeStruct((full, per_col * width), BF16),
             jax.ShapeDtypeStruct((2 * full, per_col * width), BF16),
         ),
-        [VMEM] * 7,
-    )(xc, agg, degree, weight_t, neigh_weight, self_weight, bias_col)
-    home = over_col(home)
+        [VMEM] * 11,
+        [pltpu.VMEM((full, per_col * width), BF16)] * 2,
+    )(keep, got, *turned, agg, degree, weight_t, neigh_weight, self_weight, bias_col)
+    scaled = over_col(scaled)
     part = call(
         functools.partial(weight_kernel, dim),
         jax.ShapeDtypeStruct((Y * CORE * X, 16, full + 128), BF16),
         [VMEM] * 2,
     )(xa, dz)
-    part, home = lax.optimization_barrier((part, home))
-
-    both = ("blk", "col")
+    part, scaled, away_own = lax.optimization_barrier((part, scaled, away_own))
+
     flat = [
         [rank(y, l, c, x, h) for y in range(Y) for c in range(CORE) for x in range(X)]
         for l in range(Z_LO)
         for h in range(Z_HI)
     ]
-    line = [
-        [rank(y, l, c, x, h) for h in range(Z_HI) for l in range(Z_LO)]
-        for y in range(Y)
-        for c in range(CORE)
-        for x in range(X)
-    ]
-    plane = [[(y * Z_LO + l) * CORE + c for y in range(Y) for c in range(CORE)] for l in range(Z_LO)]
-    part = lax.all_to_all(part, both, 0, 0, axis_index_groups=flat, tiled=False)
+    part = lax.all_to_all(part, ("blk", "col"), 0, 0, axis_index_groups=flat, tiled=False)
+    got_own = flip_z(away_own)
     away_a, away_b = call(
         functools.partial(contribution_kernel, slots),
         (halo, halo),
         [VMEM, SMEM, SMEM, VMEM],
         [pltpu.VMEM((slots, dim, width), BF16)],
-    )(home, tile_dst, tile_src, half)
+    )(scaled, tile_dst, tile_src, half)
     away_b, part = lax.optimization_barrier((away_b, part))
     back_b = swap(away_b, GROUP // 2)
     away_a, back_b = lax.optimization_barrier((away_a, back_b))
     back_a = swap(away_a, 0)
-    part = jnp.sum(part.astype(F32), axis=0)
-    tail = jnp.concatenate([part[0:4, full:], part[8:12, full:]], axis=0)
-    ends = [jnp.concatenate([part[8 * h : 8 * h + 8, :full], tail], axis=1) for h in range(Z_HI)]
-    part = jnp.broadcast_to(jnp.stack(ends)[:, None], (Z_HI, Z_LO, 8, full + 128))
-    part = part.reshape(Z_HI * Z_LO, 8, full + 128)
-    part, back_a = lax.optimization_barrier((part, back_a))
-    part = jnp.sum(lax.all_to_all(part, both, 0, 0, axis_index_groups=line, tiled=False), axis=0)
-    grad_bias = jnp.concatenate([part[0, full:], part[4, full:]])
+    piece = jax.ShapeDtypeStruct((8, full + 128), F32)
+    mine, other = call(fold_kernel, (piece, piece), [VMEM])(part)
+    mine += flip_z(other)
+    for bit in (CORE, 2 * CORE, 4 * CORE):
+        mine += across(mine, bit)
+    grad_bias = jnp.concatenate([mine[0, full:], mine[4, full:]])
     grad_bias = lax.dynamic_slice_in_dim(grad_bias, lax.axis_index("col") * dim, dim, 0)
-    part = jnp.broadcast_to(part[None, :, :full], (Y * CORE, 8, full))
-    part = lax.all_to_all(part, "blk", 0, 0, axis_index_groups=plane, tiled=False)
-    part = part.reshape(2, dim, full)
-    grad_self, grad_neigh = part[0], part[1]
-
+    rows = mine[None, :, :full]
+    for bit in (CORE * Z_LO, 2 * CORE * Z_LO):
+        rows = jnp.concatenate([rows, across(rows, bit)], axis=0)
+    grad = jax.ShapeDtypeStruct((dim, full), F32)
+    grad_self, grad_neigh = call(order_kernel, (grad, grad), [VMEM] * 2)(rows, across(rows, 1))
     acc = call(
         functools.partial(local_back_kernel, slots),
         jax.ShapeDtypeStruct((blocks, dim, width), F32),
         [VMEM, SMEM, SMEM, VMEM],
-    )(home, tile_dst, tile_src, half)
+    )(scaled, tile_dst, tile_src, half)
+    turned = turn_x(keep_own, got_own)
     grad_feats = call(
         finish_kernel,
         jax.ShapeDtypeStruct((dim, nodes), BF16),
-        [VMEM, VMEM, VMEM, SMEM],
+        [VMEM] * 8 + [SMEM],
         [pltpu.VMEM((blocks, dim, width), F32)],
-    )(acc, back_a, back_b, table)
+    )(acc, back_a, back_b, keep_own, got_own, *turned, table)
     return grad_feats, grad_self, grad_neigh, grad_bias
 
 

time: 202 us -> 229 us (1.13)
  starting transfers between devices: 61 us -> 104 us
  waiting for transfers between devices: 80.5 us -> 51.5 us
  blocking collectives: 34.4 us -> 45.7 us
    ppermute x0 -> x15, starting transfers between devices: none -> 57 us  [the longest x6 21.7 us: across(): lax.ppermute(rows, 'blk', [(e, e ^ bit) for e in range(Y * Z_LO * CORE)])]
    ppermute x0 -> x15, waiting for transfers between devices: none -> 32.2 us  [the longest x3 19.3 us: flip_z(): return lax.ppermute(rows, 'col', [(c, c ^ 1) for c in range(X * Z_HI)])]
    all_to_all x3 -> x2, waiting for transfers between devices: 37.5 us -> 12.3 us  [over_col(): return lax.all_to_all(rows, 'col', 0, 0, tiled=False)]
    all_to_all x3 -> x1, waiting for transfers between devices: 26 us -> 7.1 us  [per_device(): lax.all_to_all(part, ('blk', 'col'), 0, 0, axis_index_groups=flat, tiled=...]
    all_to_all x2, waiting for transfers between devices: 17 us -> 0.01 us  [swap(): lax.all_to_all(rows, 'blk', 0, 0, axis_index_groups=groups, tiled=False)]
    all_to_all x2, blocking collectives: 34.4 us -> 45.7 us  [swap(): lax.all_to_all(rows, 'blk', 0, 0, axis_index_groups=groups, tiled=False)]
    all_to_all x3 -> x1, starting transfers between devices: 16.8 us -> 7.33 us  [per_device(): lax.all_to_all(part, ('blk', 'col'), 0, 0, axis_index_groups=flat, tiled=...]
    all_to_all x2, starting transfers between devices: 16.8 us -> 11.3 us  [swap(): lax.all_to_all(rows, 'blk', 0, 0, axis_index_groups=groups, tiled=False)]
  transfers between devices with their start and end apart: 8 -> 20, of which waited for: 8 -> 10; matrix products, arithmetic and copies ran while one was open for 1% -> 0% of each run, Pallas kernels for 4% -> 4%
where the time goes in v3:
time: 229 us; the launch traced here: 224 us
  starting transfers between devices  104 us (45%)
  waiting for transfers between devices  51.5 us (22%)
  blocking collectives  45.7 us (20%)
  Pallas kernels  12.7 us (6%)
  local copies, waits for them, and re-layouts  9.88 us (4%)
    all_to_all x2, blocking collectives, swap(): lax.all_to_all(rows, 'blk', 0, 0, axis_index_groups=groups, tiled=False)  45.7 us
    all_to_all x2, starting transfers between devices, over_col(): return lax.all_to_all(rows, 'col', 0, 0, tiled=False)  27.9 us
    ppermute x6, starting transfers between devices, across(): lax.ppermute(rows, 'blk', [(e, e ^ bit) for e in range(Y * Z_LO * CORE)])  21.7 us
    ppermute x3, waiting for transfers between devices, flip_z(): return lax.ppermute(rows, 'col', [(c, c ^ 1) for c in range(X * Z_HI)])  19.3 us
    ppermute x3, starting transfers between devices, flip_z(): return lax.ppermute(rows, 'col', [(c, c ^ 1) for c in range(X * Z_HI)])  17.9 us
    ppermute x6, starting transfers between devices, turn_x(): lax.ppermute(piece, 'col', [(c, (c + Z_HI * step) % cols) for c in range(...  17.4 us
    all_to_all x2, waiting for transfers between devices, over_col(): return lax.all_to_all(rows, 'col', 0, 0, tiled=False)  12.3 us
    all_to_all x2, starting transfers between devices, swap(): lax.all_to_all(rows, 'blk', 0, 0, axis_index_groups=groups, tiled=False)  11.3 us
  transfers between devices with their start and end apart: 20, of which 10 were waited for; matrix products, arithmetic and copies ran while one was open for 0% of the time, Pallas kernels for 4%

profile of v3, /device:TPU:6, one launch (start us, length us, event | category | flops | bytes accessed | tf_op | source)
XLA Modules:
  0.0 224.5 jit_solution(6694158098280181359)
XLA Ops:
  3.8 22.7 %all_to_all.35.b_ref = bf16[8,4,32,128]{3,2,1,0:T(8,128)(2,1)S(1)} all-to-all(bf16[8,4,32,128]{3,2,1,0:T(8,128)(2,1)S(1)} %get-tuple-element.43), channel_id=1, replica_groups={{32,40,48,56,64,72,80,88},{96,104,112,120,128,136,144,152},{160,168,176..., dimensions={0} | all-to-all | bytes 524288 | tf_op jit(solution)/shard_map/all_to_all | solution.py:299
  26.5 5.0 %all-to-all-start.1 = ((bf16[8,4,32,128]{3,2,1,0:T(8,128)(2,1)}), bf16[8,4,32,128]{3,2,1,0:T(8,128)(2,1)S(1)}, u32[]{:S(2)}, u32[]{:S(2)}) async-start(bf16[8,4,32,128]{3,2,1,0:T(8,128)(2,1)} %get-tuple-element.44), calls=%async_computation.1 | async-start | bytes 524288 | tf_op jit(solution)/shard_map/all_to_all | solution.py:299
  33.3 10.5 %collective-permute-start = (bf16[4,2,2,32,128]{4,3,2,1,0:T(8,128)(2,1)S(1)}, bf16[4,2,2,32,128]{4,3,2,1,0:T(8,128)(2,1)S(1)}, u32[]{:S(2)}, u32[]{:S(2)}) collective-permute-start(bf16[4,2,2,32,128]{4,3,2,1,0:T(8,128)(2,1)S(1)} %get-tuple-element.41), channel_id=1, source_target_pairs={{0,1},{1,0},{2,3},{3,2},{4,5},{5,4},{6,7},{7,6},{8,9},{9,8},{10,11... | collective-permute-start | bytes 393224 | tf_op jit(solution)/shard_map/ppermute | solution.py:307
  43.9 2.0 copy-done
  47.2 1.8 shard_map.122
  49.1 2.0 shard_map.123
  51.0 13.7 %all-to-all-start.2 = ((bf16[8,2,32,128]{3,2,1,0:T(8,128)(2,1)}), bf16[8,2,32,128]{3,2,1,0:T(8,128)(2,1)S(1)}, u32[]{:S(2)}, u32[]{:S(2)}) async-start(bf16[8,2,32,128]{3,2,1,0:T(8,128)(2,1)} %get-tuple-element.53), calls=%async_computation.2 | async-start | bytes 262144 | tf_op jit(solution)/shard_map/all_to_all | solution.py:303
  65.1 1.9 collective-permute-start.1
  67.1 4.8 %collective-permute-start.2 = (bf16[2,2,2,32,128]{4,3,2,1,0:T(8,128)(2,1)S(1)}, bf16[2,2,2,32,128]{4,3,2,1,0:T(8,128)(2,1)S(1)}, u32[]{:S(2)}, u32[]{:S(2)}) collective-permute-start(bf16[2,2,2,32,128]{4,3,2,1,0:T(8,128)(2,1)S(1)} %get-tuple-element.51), channel_id=1, source_target_pairs={{0,4},{1,5},{2,6},{3,7},{4,0},{5,1},{6,2},{7,3},{8,12},{9,13},{10,... | collective-permute-start | bytes 196616 | tf_op jit(solution)/shard_map/ppermute | solution.py:315
  71.9 1.9 collective-permute-start.3
  74.7 4.5 %collective-permute-done.3.three_ref = bf16[2,2,2,32,128]{4,3,2,1,0:T(8,128)(2,1)S(1)} collective-permute-done((bf16[2,2,2,32,128]{4,3,2,1,0:T(8,128)(2,1)S(1)}, bf16[2,2,2,32,128]{4,3,2,1,0:T(8,128)(2,1)S(1)}, u32[]{:S(2)}, u32[]{:S(2)}) %collective-permute-start.3) | collective-permute-done | bytes 65568 | tf_op jit(solution)/shard_map/ppermute | solution.py:315
  82.9 14.3 %all-to-all-start.3 = ((bf16[8,2,32,128]{3,2,1,0:T(8,128)(2,1)}), bf16[8,2,32,128]{3,2,1,0:T(8,128)(2,1)S(1)}, u32[]{:S(2)}, u32[]{:S(2)}) async-start(bf16[8,2,32,128]{3,2,1,0:T(8,128)(2,1)} %get-tuple-element.57), calls=%async_computation.3 | async-start | bytes 262144 | tf_op jit(solution)/shard_map/all_to_all | solution.py:303
  98.3 12.3 %all-to-all-done.3.home_ref = bf16[8,2,32,128]{3,2,1,0:T(8,128)(2,1)S(1)} async-done(((bf16[8,2,32,128]{3,2,1,0:T(8,128)(2,1)}), bf16[8,2,32,128]{3,2,1,0:T(8,128)(2,1)S(1)}, u32[]{:S(2)}, u32[]{:S(2)}) %all-to-all-start.3) | async-done | bytes 131104 | tf_op jit(solution)/shard_map/all_to_all | solution.py:303
  110.5 7.3 %all-to-all-start.4 = ((bf16[32,16,384]{2,1,0:T(8,128)(2,1)}), bf16[32,16,384]{2,1,0:T(8,128)(2,1)S(1)}, u32[]{:S(2)}, u32[]{:S(2)}) async-start(bf16[32,16,384]{2,1,0:T(8,128)(2,1)} %shard_map.126), calls=%async_computation.4 | async-start | bytes 786432 | tf_op jit(solution)/shard_map/all_to_all | solution.py:411
  117.9 1.7 shard_map.128
  119.5 7.1 %all-to-all-done.4.part_ref = bf16[32,16,384]{2,1,0:T(8,128)(2,1)S(1)} async-done(((bf16[32,16,384]{2,1,0:T(8,128)(2,1)}), bf16[32,16,384]{2,1,0:T(8,128)(2,1)S(1)}, u32[]{:S(2)}, u32[]{:S(2)}) %all-to-all-start.4) | async-done | bytes 393248 | tf_op jit(solution)/shard_map/all_to_all | solution.py:411
  126.6 23.1 %all_to_all.36.b_ref = bf16[8,4,32,128]{3,2,1,0:T(8,128)(2,1)S(1)} all-to-all(bf16[8,4,32,128]{3,2,1,0:T(8,128)(2,1)S(1)} %get-tuple-element.63), channel_id=1, replica_groups={{32,40,48,56,64,72,80,88},{96,104,112,120,128,136,144,152},{160,168,176..., dimensions={0} | all-to-all | bytes 524288 | tf_op jit(solution)/shard_map/all_to_all | solution.py:299
  149.7 6.3 %all-to-all-start.6 = ((bf16[8,4,32,128]{3,2,1,0:T(8,128)(2,1)}), bf16[8,4,32,128]{3,2,1,0:T(8,128)(2,1)S(1)}, u32[]{:S(2)}, u32[]{:S(2)}) async-start(bf16[8,4,32,128]{3,2,1,0:T(8,128)(2,1)} %get-tuple-element.64), calls=%async_computation.6 | async-start | bytes 524288 | tf_op jit(solution)/shard_map/all_to_all | solution.py:299
  156.1 3.0 %collective-permute-start.8 = (f32[8,384]{1,0:T(8,128)S(1)}, f32[8,384]{1,0:T(8,128)S(1)}, u32[]{:S(2)}, u32[]{:S(2)}) collective-permute-start(f32[8,384]{1,0:T(8,128)S(1)} %get-tuple-element.73), channel_id=1, source_target_pairs={{0,1},{1,0},{2,3},{3,2},{4,5},{5,4},{6,7},{7,6},{8,9},{9,8},{10,11... | collective-permute-start | bytes 36872 | tf_op jit(solution)/shard_map/ppermute | solution.py:307
  159.1 11.3 %collective-permute-done.8 = f32[8,384]{1,0:T(8,128)S(1)} collective-permute-done((f32[8,384]{1,0:T(8,128)S(1)}, f32[8,384]{1,0:T(8,128)S(1)}, u32[]{:S(2)}, u32[]{:S(2)}) %collective-permute-start.8) | collective-permute-done | bytes 12320 | tf_op jit(solution)/shard_map/ppermute | solution.py:307
  170.4 3.9 %collective-permute-start.9 = (f32[8,384]{1,0:T(8,128)S(1)}, f32[8,384]{1,0:T(8,128)S(1)}, u32[]{:S(2)}, u32[]{:S(2)}) collective-permute-start(f32[8,384]{1,0:T(8,128)S(1)} %add.15), channel_id=1, source_target_pairs={{0,16},{8,24},{16,0},{24,8},{32,48},{40,56},{48,32},{56,40},{64,80... | collective-permute-start | bytes 36872 | tf_op jit(solution)/shard_map/ppermute | solution.py:321
  176.0 4.8 %collective-permute-start.10 = (f32[8,384]{1,0:T(8,128)S(1)}, f32[8,384]{1,0:T(8,128)S(1)}, u32[]{:S(2)}, u32[]{:S(2)}) collective-permute-start(f32[8,384]{1,0:T(8,128)S(1)} %add.16), channel_id=1, source_target_pairs={{0,32},{8,40},{16,48},{24,56},{32,0},{40,8},{48,16},{56,24},{64,96... | collective-permute-start | bytes 36872 | tf_op jit(solution)/shard_map/ppermute | solution.py:321
  182.4 5.0 %collective-permute-start.11 = (f32[8,384]{1,0:T(8,128)S(1)}, f32[8,384]{1,0:T(8,128)S(1)}, u32[]{:S(2)}, u32[]{:S(2)}) collective-permute-start(f32[8,384]{1,0:T(8,128)S(1)} %add.17), channel_id=1, source_target_pairs={{0,64},{8,72},{16,80},{24,88},{32,96},{40,104},{48,112},{56,120},{... | collective-permute-start | bytes 36872 | tf_op jit(solution)/shard_map/ppermute | solution.py:321
  187.5 4.4 %collective-permute-start.4 = (bf16[4,2,32,128]{3,2,1,0:T(8,128)(2,1)S(1)}, bf16[4,2,32,128]{3,2,1,0:T(8,128)(2,1)S(1)}, u32[]{:S(2)}, u32[]{:S(2)}) collective-permute-start(bf16[4,2,32,128]{3,2,1,0:T(8,128)(2,1)S(1)} %copy-done.13), channel_id=1, source_target_pairs={{0,1},{1,0},{2,3},{3,2},{4,5},{5,4},{6,7},{7,6},{8,9},{9,8},{10,11... | collective-permute-start | bytes 196616 | tf_op jit(solution)/shard_map/ppermute | solution.py:307
  191.9 2.5 %collective-permute-start.12 = (f32[1,8,256]{2,1,0:T(8,128)S(1)}, f32[1,8,256]{2,1,0:T(8,128)S(1)}, u32[]{:S(2)}, u32[]{:S(2)}) collective-permute-start(f32[1,8,256]{2,1,0:T(8,128)S(1)} %slice_bitcast_fusion), channel_id=1, source_target_pairs={{0,128},{8,136},{16,144},{24,152},{32,160},{40,168},{48,176},{56,1... | collective-permute-start | bytes 24584 | tf_op jit(solution)/shard_map/ppermute | solution.py:321
  195.3 8.0 %collective-permute-done.4.got_ref = bf16[4,2,32,128]{3,2,1,0:T(8,128)(2,1)S(1)} collective-permute-done((bf16[4,2,32,128]{3,2,1,0:T(8,128)(2,1)S(1)}, bf16[4,2,32,128]{3,2,1,0:T(8,128)(2,1)S(1)}, u32[]{:S(2)}, u32[]{:S(2)}) %collective-permute-start.4) | collective-permute-done | bytes 65568 | tf_op jit(solution)/shard_map/ppermute | solution.py:307
  203.3 3.7 %collective-permute-start.5 = (bf16[2,2,32,128]{3,2,1,0:T(8,128)(2,1)S(1)}, bf16[2,2,32,128]{3,2,1,0:T(8,128)(2,1)S(1)}, u32[]{:S(2)}, u32[]{:S(2)}) collective-permute-start(bf16[2,2,32,128]{3,2,1,0:T(8,128)(2,1)S(1)} %get-tuple-element.68), channel_id=1, source_target_pairs={{0,2},{1,3},{2,4},{3,5},{4,6},{5,7},{6,0},{7,1},{8,10},{9,11},{10,... | collective-permute-start | bytes 98312 | tf_op jit(solution)/shard_map/ppermute | solution.py:315
  207.0 2.4 %collective-permute-start.6 = (bf16[2,2,32,128]{3,2,1,0:T(8,128)(2,1)S(1)}, bf16[2,2,32,128]{3,2,1,0:T(8,128)(2,1)S(1)}, u32[]{:S(2)}, u32[]{:S(2)}) collective-permute-start(bf16[2,2,32,128]{3,2,1,0:T(8,128)(2,1)S(1)} %get-tuple-element.69), channel_id=1, source_target_pairs={{0,4},{1,5},{2,6},{3,7},{4,0},{5,1},{6,2},{7,3},{8,12},{9,13},{10,... | collective-permute-start | bytes 98312 | tf_op jit(solution)/shard_map/ppermute | solution.py:315
  209.4 2.6 %collective-permute-start.7 = (bf16[2,2,32,128]{3,2,1,0:T(8,128)(2,1)S(1)}, bf16[2,2,32,128]{3,2,1,0:T(8,128)(2,1)S(1)}, u32[]{:S(2)}, u32[]{:S(2)}) collective-permute-start(bf16[2,2,32,128]{3,2,1,0:T(8,128)(2,1)S(1)} %get-tuple-element.70), channel_id=1, source_target_pairs={{0,6},{1,7},{2,0},{3,1},{4,2},{5,3},{6,4},{7,5},{8,14},{9,15},{10,... | collective-permute-start | bytes 98312 | tf_op jit(solution)/shard_map/ppermute | solution.py:315
  212.1 3.6 %collective-permute-start.13 = (f32[2,8,256]{2,1,0:T(8,128)S(1)}, f32[2,8,256]{2,1,0:T(8,128)S(1)}, u32[]{:S(2)}, u32[]{:S(2)}) collective-permute-start(f32[2,8,256]{2,1,0:T(8,128)S(1)} %pad_maximum_fusion.2), channel_id=1, source_target_pairs={{0,256},{8,264},{16,272},{24,280},{32,288},{40,296},{48,304},{56,3... | collective-permute-start | bytes 49160 | tf_op jit(solution)/shard_map/ppermute | solution.py:321
  215.6 3.6 %collective-permute-done.13 = f32[2,8,256]{2,1,0:T(8,128)S(1)} collective-permute-done((f32[2,8,256]{2,1,0:T(8,128)S(1)}, f32[2,8,256]{2,1,0:T(8,128)S(1)}, u32[]{:S(2)}, u32[]{:S(2)}) %collective-permute-start.13) | collective-permute-done | bytes 16416 | tf_op jit(solution)/shard_map/ppermute | solution.py:321
  219.2 1.9 collective-permute-start.14
  (68 shorter events, 20.0 us)
Async XLA Ops:
  0.6 48.4 %copy-start.9 = (s32[56]{0:T(128)S(1)}, s32[56]{0:T(128)}, u32[]{:S(2)}) copy-start(s32[56]{0:T(128)} %dst_ref.7) | copy-start | bytes 676
  0.6 48.4 %copy-start.11 = (s32[56]{0:T(128)S(1)}, s32[56]{0:T(128)}, u32[]{:S(2)}) copy-start(s32[56]{0:T(128)} %src_ref.7) | copy-start | bytes 676
  1.4 0.9 copy-start.1
  26.5 38.3 %copy-start.4 = (bf16[256,256]{1,0:T(8,128)(2,1)S(1)}, bf16[256,256]{1,0:T(8,128)(2,1)}, u32[]{:S(2)}) copy-start(bf16[256,256]{1,0:T(8,128)(2,1)} %own_w_ref.1) | copy-start | bytes 393220
  26.5 22.6 %all-to-all-start.1 = ((bf16[8,4,32,128]{3,2,1,0:T(8,128)(2,1)}), bf16[8,4,32,128]{3,2,1,0:T(8,128)(2,1)S(1)}, u32[]{:S(2)}, u32[]{:S(2)}) async-start(bf16[8,4,32,128]{3,2,1,0:T(8,128)(2,1)} %get-tuple-element.44), calls=%async_computation.1 | async-start | bytes 524288 | tf_op jit(solution)/shard_map/all_to_all | solution.py:299
  31.5 0.9 copy-start.2
  32.4 0.9 copy-start.5
  33.3 31.6 %copy-start.3 = (bf16[256,256]{1,0:T(8,128)(2,1)S(1)}, bf16[256,256]{1,0:T(8,128)(2,1)}, u32[]{:S(2)}) copy-start(bf16[256,256]{1,0:T(8,128)(2,1)} %neigh_ref.1) | copy-start | bytes 393220
  33.3 31.6 %copy-start.14 = (f32[256]{0:T(256)S(1)}, f32[256]{0:T(256)}, u32[]{:S(2)}) copy-start(f32[256]{0:T(256)} %param.16) | copy-start | bytes 3076
  33.3 17.7 %collective-permute-start = (bf16[4,2,2,32,128]{4,3,2,1,0:T(8,128)(2,1)S(1)}, bf16[4,2,2,32,128]{4,3,2,1,0:T(8,128)(2,1)S(1)}, u32[]{:S(2)}, u32[]{:S(2)}) collective-permute-start(bf16[4,2,2,32,128]{4,3,2,1,0:T(8,128)(2,1)S(1)} %get-tuple-element.41), channel_id=1, source_target_pairs={{0,1},{1,0},{2,3},{3,2},{4,5},{5,4},{6,7},{7,6},{8,9},{9,8},{10,11... | collective-permute-start | bytes 393224 | tf_op jit(solution)/shard_map/ppermute | solution.py:307
  43.9 2.0 copy-start
  46.6 0.7 copy-start.10
  51.0 28.9 %all-to-all-start.2 = ((bf16[8,2,32,128]{3,2,1,0:T(8,128)(2,1)}), bf16[8,2,32,128]{3,2,1,0:T(8,128)(2,1)S(1)}, u32[]{:S(2)}, u32[]{:S(2)}) async-start(bf16[8,2,32,128]{3,2,1,0:T(8,128)(2,1)} %get-tuple-element.53), calls=%async_computation.2 | async-start | bytes 262144 | tf_op jit(solution)/shard_map/all_to_all | solution.py:303
  65.1 8.7 %collective-permute-start.1 = (bf16[2,2,2,32,128]{4,3,2,1,0:T(8,128)(2,1)S(1)}, bf16[2,2,2,32,128]{4,3,2,1,0:T(8,128)(2,1)S(1)}, u32[]{:S(2)}, u32[]{:S(2)}) collective-permute-start(bf16[2,2,2,32,128]{4,3,2,1,0:T(8,128)(2,1)S(1)} %get-tuple-element.50), channel_id=1, source_target_pairs={{0,2},{1,3},{2,4},{3,5},{4,6},{5,7},{6,0},{7,1},{8,10},{9,11},{10,... | collective-permute-start | bytes 196616 | tf_op jit(solution)/shard_map/ppermute | solution.py:315
  67.1 7.7 %collective-permute-start.2 = (bf16[2,2,2,32,128]{4,3,2,1,0:T(8,128)(2,1)S(1)}, bf16[2,2,2,32,128]{4,3,2,1,0:T(8,128)(2,1)S(1)}, u32[]{:S(2)}, u32[]{:S(2)}) collective-permute-start(bf16[2,2,2,32,128]{4,3,2,1,0:T(8,128)(2,1)S(1)} %get-tuple-element.51), channel_id=1, source_target_pairs={{0,4},{1,5},{2,6},{3,7},{4,0},{5,1},{6,2},{7,3},{8,12},{9,13},{10,... | collective-permute-start | bytes 196616 | tf_op jit(solution)/shard_map/ppermute | solution.py:315
  71.9 7.4 %collective-permute-start.3 = (bf16[2,2,2,32,128]{4,3,2,1,0:T(8,128)(2,1)S(1)}, bf16[2,2,2,32,128]{4,3,2,1,0:T(8,128)(2,1)S(1)}, u32[]{:S(2)}, u32[]{:S(2)}) collective-permute-start(bf16[2,2,2,32,128]{4,3,2,1,0:T(8,128)(2,1)S(1)} %get-tuple-element.52), channel_id=1, source_target_pairs={{0,6},{1,7},{2,0},{3,1},{4,2},{5,3},{6,4},{7,5},{8,14},{9,15},{10,... | collective-permute-start | bytes 196616 | tf_op jit(solution)/shard_map/ppermute | solution.py:315
  79.9 0.8 copy-start.7
  82.9 104.5 %copy-start.13 = (bf16[4,2,32,128]{3,2,1,0:T(8,128)(2,1)S(1)}, bf16[4,2,32,128]{3,2,1,0:T(8,128)(2,1)}, u32[]{:S(2)}) copy-start(bf16[4,2,32,128]{3,2,1,0:T(8,128)(2,1)} %copy-done.12) | copy-start | bytes 196612
  82.9 27.6 %all-to-all-start.3 = ((bf16[8,2,32,128]{3,2,1,0:T(8,128)(2,1)}), bf16[8,2,32,128]{3,2,1,0:T(8,128)(2,1)S(1)}, u32[]{:S(2)}, u32[]{:S(2)}) async-start(bf16[8,2,32,128]{3,2,1,0:T(8,128)(2,1)} %get-tuple-element.57), calls=%async_computation.3 | async-start | bytes 262144 | tf_op jit(solution)/shard_map/all_to_all | solution.py:303
  110.5 16.1 %all-to-all-start.4 = ((bf16[32,16,384]{2,1,0:T(8,128)(2,1)}), bf16[32,16,384]{2,1,0:T(8,128)(2,1)S(1)}, u32[]{:S(2)}, u32[]{:S(2)}) async-start(bf16[32,16,384]{2,1,0:T(8,128)(2,1)} %shard_map.126), calls=%async_computation.4 | async-start | bytes 786432 | tf_op jit(solution)/shard_map/all_to_all | solution.py:411
  149.7 73.3 %all-to-all-start.6 = ((bf16[8,4,32,128]{3,2,1,0:T(8,128)(2,1)}), bf16[8,4,32,128]{3,2,1,0:T(8,128)(2,1)S(1)}, u32[]{:S(2)}, u32[]{:S(2)}) async-start(bf16[8,4,32,128]{3,2,1,0:T(8,128)(2,1)} %get-tuple-element.64), calls=%async_computation.6 | async-start | bytes 524288 | tf_op jit(solution)/shard_map/all_to_all | solution.py:299
  156.1 14.3 %collective-permute-start.8 = (f32[8,384]{1,0:T(8,128)S(1)}, f32[8,384]{1,0:T(8,128)S(1)}, u32[]{:S(2)}, u32[]{:S(2)}) collective-permute-start(f32[8,384]{1,0:T(8,128)S(1)} %get-tuple-element.73), channel_id=1, source_target_pairs={{0,1},{1,0},{2,3},{3,2},{4,5},{5,4},{6,7},{7,6},{8,9},{9,8},{10,11... | collective-permute-start | bytes 36872 | tf_op jit(solution)/shard_map/ppermute | solution.py:307
  170.4 5.6 %collective-permute-start.9 = (f32[8,384]{1,0:T(8,128)S(1)}, f32[8,384]{1,0:T(8,128)S(1)}, u32[]{:S(2)}, u32[]{:S(2)}) collective-permute-start(f32[8,384]{1,0:T(8,128)S(1)} %add.15), channel_id=1, source_target_pairs={{0,16},{8,24},{16,0},{24,8},{32,48},{40,56},{48,32},{56,40},{64,80... | collective-permute-start | bytes 36872 | tf_op jit(solution)/shard_map/ppermute | solution.py:321
  176.0 6.5 %collective-permute-start.10 = (f32[8,384]{1,0:T(8,128)S(1)}, f32[8,384]{1,0:T(8,128)S(1)}, u32[]{:S(2)}, u32[]{:S(2)}) collective-permute-start(f32[8,384]{1,0:T(8,128)S(1)} %add.16), channel_id=1, source_target_pairs={{0,32},{8,40},{16,48},{24,56},{32,0},{40,8},{48,16},{56,24},{64,96... | collective-permute-start | bytes 36872 | tf_op jit(solution)/shard_map/ppermute | solution.py:321
  182.4 9.5 %collective-permute-start.11 = (f32[8,384]{1,0:T(8,128)S(1)}, f32[8,384]{1,0:T(8,128)S(1)}, u32[]{:S(2)}, u32[]{:S(2)}) collective-permute-start(f32[8,384]{1,0:T(8,128)S(1)} %add.17), channel_id=1, source_target_pairs={{0,64},{8,72},{16,80},{24,88},{32,96},{40,104},{48,112},{56,120},{... | collective-permute-start | bytes 36872 | tf_op jit(solution)/shard_map/ppermute | solution.py:321
  187.5 15.8 %collective-permute-start.4 = (bf16[4,2,32,128]{3,2,1,0:T(8,128)(2,1)S(1)}, bf16[4,2,32,128]{3,2,1,0:T(8,128)(2,1)S(1)}, u32[]{:S(2)}, u32[]{:S(2)}) collective-permute-start(bf16[4,2,32,128]{3,2,1,0:T(8,128)(2,1)S(1)} %copy-done.13), channel_id=1, source_target_pairs={{0,1},{1,0},{2,3},{3,2},{4,5},{5,4},{6,7},{7,6},{8,9},{9,8},{10,11... | collective-permute-start | bytes 196616 | tf_op jit(solution)/shard_map/ppermute | solution.py:307
  191.9 20.1 %collective-permute-start.12 = (f32[1,8,256]{2,1,0:T(8,128)S(1)}, f32[1,8,256]{2,1,0:T(8,128)S(1)}, u32[]{:S(2)}, u32[]{:S(2)}) collective-permute-start(f32[1,8,256]{2,1,0:T(8,128)S(1)} %slice_bitcast_fusion), channel_id=1, source_target_pairs={{0,128},{8,136},{16,144},{24,152},{32,160},{40,168},{48,176},{56,1... | collective-permute-start | bytes 24584 | tf_op jit(solution)/shard_map/ppermute | solution.py:321
  203.3 19.6 %collective-permute-start.5 = (bf16[2,2,32,128]{3,2,1,0:T(8,128)(2,1)S(1)}, bf16[2,2,32,128]{3,2,1,0:T(8,128)(2,1)S(1)}, u32[]{:S(2)}, u32[]{:S(2)}) collective-permute-start(bf16[2,2,32,128]{3,2,1,0:T(8,128)(2,1)S(1)} %get-tuple-element.68), channel_id=1, source_target_pairs={{0,2},{1,3},{2,4},{3,5},{4,6},{5,7},{6,0},{7,1},{8,10},{9,11},{10,... | collective-permute-start | bytes 98312 | tf_op jit(solution)/shard_map/ppermute | solution.py:315
  207.0 15.9 %collective-permute-start.6 = (bf16[2,2,32,128]{3,2,1,0:T(8,128)(2,1)S(1)}, bf16[2,2,32,128]{3,2,1,0:T(8,128)(2,1)S(1)}, u32[]{:S(2)}, u32[]{:S(2)}) collective-permute-start(bf16[2,2,32,128]{3,2,1,0:T(8,128)(2,1)S(1)} %get-tuple-element.69), channel_id=1, source_target_pairs={{0,4},{1,5},{2,6},{3,7},{4,0},{5,1},{6,2},{7,3},{8,12},{9,13},{10,... | collective-permute-start | bytes 98312 | tf_op jit(solution)/shard_map/ppermute | solution.py:315
  209.4 13.6 %collective-permute-start.7 = (bf16[2,2,32,128]{3,2,1,0:T(8,128)(2,1)S(1)}, bf16[2,2,32,128]{3,2,1,0:T(8,128)(2,1)S(1)}, u32[]{:S(2)}, u32[]{:S(2)}) collective-permute-start(bf16[2,2,32,128]{3,2,1,0:T(8,128)(2,1)S(1)} %get-tuple-element.70), channel_id=1, source_target_pairs={{0,6},{1,7},{2,0},{3,1},{4,2},{5,3},{6,4},{7,5},{8,14},{9,15},{10,... | collective-permute-start | bytes 98312 | tf_op jit(solution)/shard_map/ppermute | solution.py:315
  212.1 7.1 %collective-permute-start.13 = (f32[2,8,256]{2,1,0:T(8,128)S(1)}, f32[2,8,256]{2,1,0:T(8,128)S(1)}, u32[]{:S(2)}, u32[]{:S(2)}) collective-permute-start(f32[2,8,256]{2,1,0:T(8,128)S(1)} %pad_maximum_fusion.2), channel_id=1, source_target_pairs={{0,256},{8,264},{16,272},{24,280},{32,288},{40,296},{48,304},{56,3... | collective-permute-start | bytes 49160 | tf_op jit(solution)/shard_map/ppermute | solution.py:321
  219.2 3.1 %collective-permute-start.14 = (f32[4,8,256]{2,1,0:T(8,128)S(1)}, f32[4,8,256]{2,1,0:T(8,128)S(1)}, u32[]{:S(2)}, u32[]{:S(2)}) collective-permute-start(f32[4,8,256]{2,1,0:T(8,128)S(1)} %pad_maximum_fusion.1.near_ref), channel_id=1, source_target_pairs={{0,8},{8,0},{16,24},{24,16},{32,40},{40,32},{48,56},{56,48},{64,72... | collective-permute-start | bytes 98312 | tf_op jit(solution)/shard_map/ppermute | solution.py:321
  (3 other events, 1.9 us)

commit v4 on v2

--- a/solution.py
+++ b/solution.py
@@ -66,7 +66,7 @@
     return jnp.clip(place, 0, GROUP - 1)
 
 
-def pack_kernel(width, x_ref, cot_ref, send_ref, a_ref, b_ref, xc_ref):
+def pack_kernel(width, x_ref, send_ref, a_ref, b_ref):
     place_a, place_b = places()
     cap = send_ref.shape[1]
     for ref, place in ((b_ref, place_b), (a_ref, place_a)):
@@ -75,10 +75,40 @@
             for m in range(cap):
                 start = pl.multiple_of(send_ref[kind, m] * width, width)
                 ref[peer, m] = x_ref[:, pl.ds(start, width)]
-    for block in range(x_ref.shape[1] // width):
-        cols = slice(block * width, (block + 1) * width)
-        xc_ref[block // 2, 0, block % 2] = x_ref[:, cols]
-        xc_ref[block // 2, 1, block % 2] = cot_ref[:, cols]
+
+
+def column():
+    col = lax.axis_index("col")
+    return col // Z_HI, lax.rem(col, Z_HI)
+
+
+def range_half():
+    z = column()[1] * Z_LO + lax.rem(lax.axis_index("blk") // CORE, Z_LO)
+    middle = jnp.logical_and(z >= Z_LO // 2, z < Z_LO // 2 * 3)
+    return jnp.where(middle, 0, 1)
+
+
+def split_kernel(width, x_ref, cot_ref, plus_ref, minus_ref):
+    z_hi = column()[1]
+    per = plus_ref.shape[2]
+    for x in range(X):
+        for out, h in ((plus_ref, z_hi), (minus_ref, 1 - z_hi)):
+            for p in range(per):
+                start = pl.multiple_of(((x * Z_HI + h) * per + p) * width, width)
+                out[x, 0, p] = x_ref[:, pl.ds(start, width)]
+                out[x, 1, p] = cot_ref[:, pl.ds(start, width)]
+
+
+def join_kernel(xc_plus_ref, xc_minus_ref, agg_plus_ref, agg_minus_ref, out_ref):
+    for side, (xc, agg) in enumerate(((xc_plus_ref, agg_plus_ref), (xc_minus_ref, agg_minus_ref))):
+        for which in range(2):
+            out_ref[:, which, side] = xc[:, which]
+        out_ref[:, 2, side] = agg[...]
+
+
+def join_back_kernel(plus_ref, minus_ref, out_ref):
+    out_ref[:, 0] = plus_ref[...]
+    out_ref[:, 1] = minus_ref[...]
 
 
 def local_kernel(slots, chunk, x_ref, dst_ref, src_ref, cnt_ref, half_ref, acc_ref):
@@ -102,10 +132,14 @@
             acc_ref[dst] += dot(rows, half_ref[i], LAST)[: dim + 8]
 
 
-def aggregate_kernel(slots, a_ref, b_ref, dst_ref, src_ref, half_ref, acc_in, agg_ref, deg_ref, acc_ref):
+def aggregate_kernel(
+    slots, a_ref, b_ref, dst_ref, src_ref, half_ref, acc_in, plus_ref, minus_ref, deg_ref, acc_ref
+):
     place_a, place_b = places()
+    z_hi = column()[1]
     cap, dim, width = a_ref.shape[1:]
     blocks = acc_in.shape[0]
+    per = plus_ref.shape[1]
     ones = jnp.ones((16, width), BF16)
     acc_ref[...] = acc_in[...]
     for tile in range(slots):
@@ -119,31 +153,43 @@
         dst = dst_ref[tile]
         acc_ref[dst] += dot(rows, half_ref[tile], LAST)[: dim + 8]
     for block in range(blocks):
-        degree = jnp.maximum(acc_ref[block, dim : dim + 8], 1.0)
-        deg_ref[block] = degree
-        agg_ref[block // 2, block % 2] = (acc_ref[block, :dim] / degree[:1]).astype(BF16)
+        deg_ref[block] = jnp.maximum(acc_ref[block, dim : dim + 8], 1.0)
+    for x in range(X):
+        for out, h in ((plus_ref, z_hi), (minus_ref, 1 - z_hi)):
+            for p in range(per):
+                block = (x * Z_HI + h) * per + p
+                out[x, p] = (acc_ref[block, :dim] / deg_ref[block, :1]).astype(BF16)
 
 
 def node_kernel(
-    xc_ref, agg_ref, deg_ref, wt_ref, neigh_ref, own_w_ref, bias_ref, home_ref, dz_ref, xa_ref
+    in_ref, wt_ref, neigh_ref, own_w_ref, bias_ref, plus_ref, minus_ref, dz_ref, xa_ref, cot_ref, home_ref
 ):
-    cols, _, per_col, dim, width = xc_ref.shape
-    full = cols * dim
-    col = lax.axis_index("col")
+    _, _, sides, per_col, dim, width = in_ref.shape
+    full = X * Z_HI * dim
+    half = range_half()
+    for x in range(X):
+        for side, z in ((0, half), (1, 1 - half)):
+            start = (x * Z_HI + z) * dim
+            rows = pl.ds(pl.multiple_of(start, dim), dim)
+            agg_rows = pl.ds(pl.multiple_of(full + start, dim), dim)
+            for p in range(per_col):
+                lanes = slice(p * width, (p + 1) * width)
+                xa_ref[rows, lanes] = in_ref[x, 0, side, p]
+                cot_ref[rows, lanes] = in_ref[x, 1, side, p]
+                xa_ref[agg_rows, lanes] = in_ref[x, 2, side, p]
     for p in range(per_col):
         lanes = slice(p * width, (p + 1) * width)
-        x = xc_ref[:, 0, p].reshape(full, width)
-        cot = xc_ref[:, 1, p].reshape(full, width)
-        xa = jnp.concatenate([x, agg_ref[:, p].reshape(full, width)], axis=0)
-        xa_ref[:, lanes] = xa
-        pre = dot(wt_ref[...], xa) + bias_ref[...]
-        dz = (cot.astype(F32) * gelu_slope(pre)).astype(BF16)
+        pre = dot(wt_ref[...], xa_ref[:, lanes]) + bias_ref[...]
+        dz = (cot_ref[:, lanes].astype(F32) * gelu_slope(pre)).astype(BF16)
         dz_ref[:, lanes] = dz
-        degree = deg_ref[col * per_col + p][:1]
-        scaled = (dot(neigh_ref[...], dz) / degree).astype(BF16)
-        home_ref[:, 0, p] = scaled.reshape(cols, dim, width)
-        own = dot(own_w_ref[...], dz).astype(BF16)
-        home_ref[:, 1, p] = own.reshape(cols, dim, width)
+        home_ref[0, :, lanes] = dot(neigh_ref[...], dz).astype(BF16)
+        home_ref[1, :, lanes] = dot(own_w_ref[...], dz).astype(BF16)
+    for x in range(X):
+        for out, z in ((minus_ref, half), (plus_ref, 1 - half)):
+            rows = pl.ds(pl.multiple_of((x * Z_HI + z) * dim, dim), dim)
+            for which in range(2):
+                for p in range(per_col):
+                    out[x, which, p] = home_ref[which, rows, p * width : (p + 1) * width]
 
 
 def weight_kernel(dim, xa_ref, dz_ref, part_ref):
@@ -164,13 +210,22 @@
                 part_ref[piece, :, full:] = tail
 
 
-def contribution_kernel(slots, home_ref, dst_ref, src_ref, half_ref, a_ref, b_ref, hold_ref):
+def contribution_kernel(
+    slots, home_ref, deg_ref, dst_ref, src_ref, half_ref, a_ref, b_ref, scaled_ref, hold_ref
+):
     place_a, place_b = places()
-    blocks = home_ref.shape[0] * home_ref.shape[2]
+    z_hi = column()[1]
+    blocks = scaled_ref.shape[0]
     cap = a_ref.shape[1]
+    per = home_ref.shape[3]
+    for x in range(X):
+        for side, h in ((0, 1 - z_hi), (1, z_hi)):
+            for p in range(per):
+                block = (x * Z_HI + h) * per + p
+                value = home_ref[x, side, 0, p].astype(F32) / deg_ref[block, :1]
+                scaled_ref[block] = value.astype(BF16)
     for tile in range(slots):
-        dst = dst_ref[tile]
-        value = dot(home_ref[dst // 2, 0, lax.rem(dst, 2)], half_ref[tile])
+        value = dot(scaled_ref[dst_ref[tile]], half_ref[tile])
         hold_ref[src_ref[tile] - blocks] = value.astype(BF16)
     for ref, place in ((b_ref, place_b), (a_ref, place_a)):
         for peer in range(GROUP):
@@ -179,14 +234,15 @@
                 ref[peer, m] = hold_ref[kind * cap + m]
 
 
-def local_back_kernel(slots, home_ref, dst_ref, src_ref, half_ref, acc_ref):
-    per = home_ref.shape[2]
-    for block in range(acc_ref.shape[0]):
-        acc_ref[block] = home_ref[block // per, 1, block % per].astype(F32)
+def local_back_kernel(slots, scaled_ref, home_ref, dst_ref, src_ref, half_ref, acc_ref):
+    z_hi = column()[1]
+    per = home_ref.shape[3]
+    for x in range(X):
+        for side, h in ((0, 1 - z_hi), (1, z_hi)):
+            for p in range(per):
+                acc_ref[(x * Z_HI + h) * per + p] = home_ref[x, side, 1, p].astype(F32)
     for tile in range(slots, half_ref.shape[0]):
-        dst = dst_ref[tile]
-        src = src_ref[tile]
-        acc_ref[src] += dot(home_ref[dst // 2, 0, lax.rem(dst, 2)], half_ref[tile])
+        acc_ref[src_ref[tile]] += dot(scaled_ref[dst_ref[tile]], half_ref[tile])
 
 
 def finish_kernel(acc_in, a_ref, b_ref, send_ref, out_ref, acc_ref):
@@ -217,8 +273,26 @@
     return lax.all_to_all(rows, "blk", 0, 0, axis_index_groups=groups, tiled=False)
 
 
-def over_col(rows):
-    return lax.all_to_all(rows, "col", 0, 0, tiled=False)
+def over_x(rows):
+    groups = [[x * Z_HI + h for x in range(X)] for h in range(Z_HI)]
+    return lax.all_to_all(rows, "col", 0, 0, axis_index_groups=groups, tiled=False)
+
+
+def along_z(rows, step):
+    chips = Z_LO * Z_HI
+    route = []
+    for y in range(Y):
+        for core in range(CORE):
+            for x in range(X):
+                for z in range(chips):
+                    to = (z + step) % chips
+                    route.append(
+                        (
+                            rank(y, z % Z_LO, core, x, z // Z_LO),
+                            rank(y, to % Z_LO, core, x, to // Z_LO),
+                        )
+                    )
+    return lax.ppermute(rows, ("blk", "col"), sorted(route))
 
 
 def per_device(
@@ -234,19 +308,21 @@
     per_col = blocks // cols
     full = cols * dim
     chunk = 8
-    halo = jax.ShapeDtypeStruct((GROUP, cap, dim, width), BF16)
-    pairs = jax.ShapeDtypeStruct((cols, 2, per_col, dim, width), BF16)
-    ranged = jax.ShapeDtypeStruct((cols, per_col, dim, width), BF16)
-
-    send_a, send_b, xc = call(
-        functools.partial(pack_kernel, width),
-        (halo, halo, pairs),
-        [VMEM, VMEM, SMEM],
-    )(node_feats, cotangent, table)
+    shape = lambda *dims: jax.ShapeDtypeStruct(dims + (dim, width), BF16)
+    halo = shape(GROUP, cap)
+    step = Z_LO // 2
+
+    send_a, send_b = call(
+        functools.partial(pack_kernel, width), (halo, halo), [VMEM, SMEM]
+    )(node_feats, table)
     got_b = swap(send_b, GROUP // 2)
+    xc_plus, xc_minus = call(
+        functools.partial(split_kernel, width), (shape(X, 2, per_col),) * 2, [VMEM] * 2
+    )(node_feats, cotangent)
+    send_a, got_b, xc_plus, xc_minus = lax.optimization_barrier((send_a, got_b, xc_plus, xc_minus))
+    xc_plus = along_z(xc_plus, step)
+    xc_minus = along_z(xc_minus, -step)
     got_a = swap(send_a, 0)
-    xc, got_a = lax.optimization_barrier((xc, got_a))
-    xc = over_col(xc)
     whole = lambda shape: pl.BlockSpec(shape, lambda i: (0,) * len(shape))
     half, acc = pl.pallas_call(
         functools.partial(local_kernel, slots, chunk),
@@ -272,30 +348,39 @@
     )(node_feats, tile_dst, tile_src, tile_cnt)
     weight_t = jnp.concatenate([self_weight.T, neigh_weight.T], axis=1)
     bias_col = bias[:, None]
-    agg, degree = call(
+    agg_plus, agg_minus, degree = call(
         functools.partial(aggregate_kernel, slots),
-        (ranged, jax.ShapeDtypeStruct((blocks, 8, width), F32)),
+        (shape(X, per_col), shape(X, per_col), jax.ShapeDtypeStruct((blocks, 8, width), F32)),
         [VMEM, VMEM, SMEM, SMEM, VMEM, VMEM],
         [pltpu.VMEM((blocks, dim + 8, width), F32)],
     )(got_a, got_b, tile_dst, tile_src, half, acc)
-    agg, xc = lax.optimization_barrier((agg, xc))
-    agg = over_col(agg)
-    home, dz, xa = call(
+    agg_plus = along_z(agg_plus, step)
+    agg_minus = along_z(agg_minus, -step)
+    ranged = call(join_kernel, shape(X, 3, 2, per_col), [VMEM] * 4)(
+        xc_plus, xc_minus, agg_plus, agg_minus
+    )
+    ranged = over_x(ranged)
+    plus, minus, dz, xa = call(
         node_kernel,
         (
-            pairs,
+            shape(X, 2, per_col),
+            shape(X, 2, per_col),
             jax.ShapeDtypeStruct((full, per_col * width), BF16),
             jax.ShapeDtypeStruct((2 * full, per_col * width), BF16),
         ),
-        [VMEM] * 7,
-    )(xc, agg, degree, weight_t, neigh_weight, self_weight, bias_col)
-    home = over_col(home)
+        [VMEM] * 5,
+        [
+            pltpu.VMEM((full, per_col * width), BF16),
+            pltpu.VMEM((2, full, per_col * width), BF16),
+        ],
+    )(ranged, weight_t, neigh_weight, self_weight, bias_col)
+    plus = along_z(plus, step)
+    minus = along_z(minus, -step)
     part = call(
         functools.partial(weight_kernel, dim),
         jax.ShapeDtypeStruct((Y * CORE * X, 16, full + 128), BF16),
         [VMEM] * 2,
     )(xa, dz)
-    part, home = lax.optimization_barrier((part, home))
 
     both = ("blk", "col")
     flat = [
@@ -311,13 +396,15 @@
     ]
     plane = [[(y * Z_LO + l) * CORE + c for y in range(Y) for c in range(CORE)] for l in range(Z_LO)]
     part = lax.all_to_all(part, both, 0, 0, axis_index_groups=flat, tiled=False)
-    away_a, away_b = call(
+    home = call(join_back_kernel, shape(X, 2, 2, per_col), [VMEM] * 2)(plus, minus)
+    home, part = lax.optimization_barrier((home, part))
+    home = over_x(home)
+    away_a, away_b, scaled = call(
         functools.partial(contribution_kernel, slots),
-        (halo, halo),
-        [VMEM, SMEM, SMEM, VMEM],
+        (halo, halo, shape(blocks)),
+        [VMEM, VMEM, SMEM, SMEM, VMEM],
         [pltpu.VMEM((slots, dim, width), BF16)],
-    )(home, tile_dst, tile_src, half)
-    away_b, part = lax.optimization_barrier((away_b, part))
+    )(home, degree, tile_dst, tile_src, half)
     back_b = swap(away_b, GROUP // 2)
     away_a, back_b = lax.optimization_barrier((away_a, back_b))
     back_a = swap(away_a, 0)
@@ -334,12 +421,11 @@
     part = lax.all_to_all(part, "blk", 0, 0, axis_index_groups=plane, tiled=False)
     part = part.reshape(2, dim, full)
     grad_self, grad_neigh = part[0], part[1]
-
     acc = call(
         functools.partial(local_back_kernel, slots),
         jax.ShapeDtypeStruct((blocks, dim, width), F32),
-        [VMEM, SMEM, SMEM, VMEM],
-    )(home, tile_dst, tile_src, half)
+        [VMEM, VMEM, SMEM, SMEM, VMEM],
+    )(scaled, home, tile_dst, tile_src, half)
     grad_feats = call(
         finish_kernel,
         jax.ShapeDtypeStruct((dim, nodes), BF16),

time: 202 us -> 196 us (0.970)
  waiting for transfers between devices: 80.5 us -> 62.1 us
  starting transfers between devices: 61 us -> 79 us
  blocking collectives: 34.4 us -> 28.4 us
    all_to_all x3 -> x1, waiting for transfers between devices: 37.5 us -> 4.91 us  [over_x(): lax.all_to_all(rows, 'col', 0, 0, axis_index_groups=groups, tiled=False)]
    ppermute x0 -> x6, starting transfers between devices: none -> 31.2 us  [along_z(): return lax.ppermute(rows, ('blk', 'col'), sorted(route))]
    ppermute x0 -> x6, waiting for transfers between devices: none -> 23.2 us  [along_z(): return lax.ppermute(rows, ('blk', 'col'), sorted(route))]
    all_to_all x3 -> x1, starting transfers between devices: 27.4 us -> 4.78 us  [over_x(): lax.all_to_all(rows, 'col', 0, 0, axis_index_groups=groups, tiled=False)]
    all_to_all x2 -> x1, blocking collectives: 34.4 us -> 19.2 us  [swap(): lax.all_to_all(rows, 'blk', 0, 0, axis_index_groups=groups, tiled=False)]
    all_to_all x2 -> x3, starting transfers between devices: 16.8 us -> 26.6 us  [swap(): lax.all_to_all(rows, 'blk', 0, 0, axis_index_groups=groups, tiled=False)]
    all_to_all x0 -> x1, blocking collectives: none -> 9.21 us  [over_x(): lax.all_to_all(rows, 'col', 0, 0, axis_index_groups=groups, tiled=False)]
    all_to_all x1, waiting for transfers between devices: 7.1 us -> 0.01 us  [per_device(): part = lax.all_to_all(part, both, 0, 0, axis_index_groups=flat, tiled=False)]
  transfers between devices with their start and end apart: 8 -> 13, of which waited for: 8 -> 9; matrix products, arithmetic and copies ran while one was open for 1% -> 1% of each run, Pallas kernels for 4% -> 3%
where the time goes in v4:
time: 196 us; the launch traced here: 193 us
  starting transfers between devices  79 us (40%)
  waiting for transfers between devices  62.1 us (32%)
  blocking collectives  28.4 us (14%)
  Pallas kernels  11.5 us (6%)
  local copies, waits for them, and re-layouts  10.6 us (5%)
    ppermute x6, starting transfers between devices, along_z(): return lax.ppermute(rows, ('blk', 'col'), sorted(route))  31.2 us
    all_to_all x3, starting transfers between devices, swap(): lax.all_to_all(rows, 'blk', 0, 0, axis_index_groups=groups, tiled=False)  26.6 us
    ppermute x6, waiting for transfers between devices, along_z(): return lax.ppermute(rows, ('blk', 'col'), sorted(route))  23.2 us
    all_to_all x1, blocking collectives, swap(): lax.all_to_all(rows, 'blk', 0, 0, axis_index_groups=groups, tiled=False)  19.2 us
    all_to_all x3, waiting for transfers between devices, swap(): lax.all_to_all(rows, 'blk', 0, 0, axis_index_groups=groups, tiled=False)  15.1 us
    all_to_all x1, waiting for transfers between devices, per_device(): lax.all_to_all(part, both, 0, 0, axis_index_groups=line, tiled=False)  13.8 us
    all_to_all x1, blocking collectives, over_x(): lax.all_to_all(rows, 'col', 0, 0, axis_index_groups=groups, tiled=False)  9.21 us
    all_to_all x1, starting transfers between devices, per_device(): part = lax.all_to_all(part, both, 0, 0, axis_index_groups=flat, tiled=False)  7.34 us
  transfers between devices with their start and end apart: 13, of which 9 were waited for; matrix products, arithmetic and copies ran while one was open for 1% of the time, Pallas kernels for 3%

profile of v4, /device:TPU:6, one launch (start us, length us, event | category | flops | bytes accessed | tf_op | source)
XLA Modules:
  0.0 192.6 jit_solution(17584084082366340951)
XLA Ops:
  1.4 0.9 copy-done.1
  2.3 1.6 shard_map.120
  3.9 15.7 %all-to-all-start = ((bf16[8,4,32,128]{3,2,1,0:T(8,128)(2,1)}), bf16[8,4,32,128]{3,2,1,0:T(8,128)(2,1)S(1)}, u32[]{:S(2)}, u32[]{:S(2)}) async-start(bf16[8,4,32,128]{3,2,1,0:T(8,128)(2,1)} %get-tuple-element.31), calls=%async_computation | async-start | bytes 524288 | tf_op jit(solution)/shard_map/all_to_all | solution.py:273
  21.5 5.5 %all-to-all-done.b_ref = bf16[8,4,32,128]{3,2,1,0:T(8,128)(2,1)S(1)} async-done(((bf16[8,4,32,128]{3,2,1,0:T(8,128)(2,1)}), bf16[8,4,32,128]{3,2,1,0:T(8,128)(2,1)S(1)}, u32[]{:S(2)}, u32[]{:S(2)}) %all-to-all-start) | async-done | bytes 262176 | tf_op jit(solution)/shard_map/all_to_all | solution.py:273
  26.9 5.0 %all-to-all-start.1 = ((bf16[8,4,32,128]{3,2,1,0:T(8,128)(2,1)}), bf16[8,4,32,128]{3,2,1,0:T(8,128)(2,1)S(1)}, u32[]{:S(2)}, u32[]{:S(2)}) async-start(bf16[8,4,32,128]{3,2,1,0:T(8,128)(2,1)} %get-tuple-element.36), calls=%async_computation.1 | async-start | bytes 524288 | tf_op jit(solution)/shard_map/all_to_all | solution.py:273
  31.9 4.7 %collective-permute-start = (bf16[4,2,2,32,128]{4,3,2,1,0:T(8,128)(2,1)S(1)}, bf16[4,2,2,32,128]{4,3,2,1,0:T(8,128)(2,1)S(1)}, u32[]{:S(2)}, u32[]{:S(2)}) collective-permute-start(bf16[4,2,2,32,128]{4,3,2,1,0:T(8,128)(2,1)S(1)} %get-tuple-element.34), channel_id=1, source_target_pairs={{0,64},{1,65},{2,66},{3,67},{4,68},{5,69},{6,70},{7,71},{8,72},{9,... | collective-permute-start | bytes 393224 | tf_op jit(solution)/shard_map/ppermute | solution.py:295
  36.6 7.0 %collective-permute-start.1 = (bf16[4,2,2,32,128]{4,3,2,1,0:T(8,128)(2,1)S(1)}, bf16[4,2,2,32,128]{4,3,2,1,0:T(8,128)(2,1)S(1)}, u32[]{:S(2)}, u32[]{:S(2)}) collective-permute-start(bf16[4,2,2,32,128]{4,3,2,1,0:T(8,128)(2,1)S(1)} %get-tuple-element.35), channel_id=1, source_target_pairs={{0,65},{1,64},{2,67},{3,66},{4,69},{5,68},{6,71},{7,70},{8,73},{9,... | collective-permute-start | bytes 393224 | tf_op jit(solution)/shard_map/ppermute | solution.py:295
  43.6 2.0 %copy-done = s32[56,128,128]{2,1,0:T(8,128)S(1)} copy-done((s32[56,128,128]{2,1,0:T(8,128)S(1)}, s32[56,128,128]{2,1,0:T(8,128)}, u32[]{:S(2)}) %copy-start) | copy-done | bytes 3670040
  47.9 1.8 shard_map.122
  49.7 1.3 shard_map.123
  51.1 3.2 %collective-permute-start.2 = (bf16[4,2,32,128]{3,2,1,0:T(8,128)(2,1)S(1)}, bf16[4,2,32,128]{3,2,1,0:T(8,128)(2,1)S(1)}, u32[]{:S(2)}, u32[]{:S(2)}) collective-permute-start(bf16[4,2,32,128]{3,2,1,0:T(8,128)(2,1)S(1)} %get-tuple-element.40), channel_id=1, source_target_pairs={{0,64},{1,65},{2,66},{3,67},{4,68},{5,69},{6,70},{7,71},{8,72},{9,... | collective-permute-start | bytes 196616 | tf_op jit(solution)/shard_map/ppermute | solution.py:295
  54.3 6.6 %collective-permute-start.3 = (bf16[4,2,32,128]{3,2,1,0:T(8,128)(2,1)S(1)}, bf16[4,2,32,128]{3,2,1,0:T(8,128)(2,1)S(1)}, u32[]{:S(2)}, u32[]{:S(2)}) collective-permute-start(bf16[4,2,32,128]{3,2,1,0:T(8,128)(2,1)S(1)} %get-tuple-element.41), channel_id=1, source_target_pairs={{0,65},{1,64},{2,67},{3,66},{4,69},{5,68},{6,71},{7,70},{8,73},{9,... | collective-permute-start | bytes 196616 | tf_op jit(solution)/shard_map/ppermute | solution.py:295
  61.4 6.7 %collective-permute-done.3.agg_minus_ref = bf16[4,2,32,128]{3,2,1,0:T(8,128)(2,1)S(1)} collective-permute-done((bf16[4,2,32,128]{3,2,1,0:T(8,128)(2,1)S(1)}, bf16[4,2,32,128]{3,2,1,0:T(8,128)(2,1)S(1)}, u32[]{:S(2)}, u32[]{:S(2)}) %collective-permute-start.3) | collective-permute-done | bytes 65568 | tf_op jit(solution)/shard_map/ppermute | solution.py:295
  68.9 4.8 %all-to-all-start.2 = ((bf16[4,3,2,2,32,128]{5,4,3,2,1,0:T(8,128)(2,1)}), bf16[4,3,2,2,32,128]{5,4,3,2,1,0:T(8,128)(2,1)S(1)}, u32[]{:S(2)}, u32[]{:S(2)}) async-start(bf16[4,3,2,2,32,128]{5,4,3,2,1,0:T(8,128)(2,1)} %shard_map.124), calls=%async_computation.2 | async-start | bytes 786432 | tf_op jit(solution)/shard_map/all_to_all | solution.py:278
  74.1 4.9 %all-to-all-done.2.in_ref = bf16[4,3,2,2,32,128]{5,4,3,2,1,0:T(8,128)(2,1)S(1)} async-done(((bf16[4,3,2,2,32,128]{5,4,3,2,1,0:T(8,128)(2,1)}), bf16[4,3,2,2,32,128]{5,4,3,2,1,0:T(8,128)(2,1)S(1)}, u32[]{:S(2)}, u32[]{:S(2)}) %all-to-all-start.2) | async-done | bytes 393248 | tf_op jit(solution)/shard_map/all_to_all | solution.py:278
  79.0 0.9 shard_map.125
  79.9 1.1 shard_map.127
  81.0 7.3 %all-to-all-start.3 = ((bf16[32,16,384]{2,1,0:T(8,128)(2,1)}), bf16[32,16,384]{2,1,0:T(8,128)(2,1)S(1)}, u32[]{:S(2)}, u32[]{:S(2)}) async-start(bf16[32,16,384]{2,1,0:T(8,128)(2,1)} %shard_map.127), calls=%async_computation.3 | async-start | bytes 786432 | tf_op jit(solution)/shard_map/all_to_all | solution.py:398
  88.3 6.4 %collective-permute-start.4 = (bf16[4,2,2,32,128]{4,3,2,1,0:T(8,128)(2,1)S(1)}, bf16[4,2,2,32,128]{4,3,2,1,0:T(8,128)(2,1)S(1)}, u32[]{:S(2)}, u32[]{:S(2)}) collective-permute-start(bf16[4,2,2,32,128]{4,3,2,1,0:T(8,128)(2,1)S(1)} %get-tuple-element.42), channel_id=1, source_target_pairs={{0,64},{1,65},{2,66},{3,67},{4,68},{5,69},{6,70},{7,71},{8,72},{9,... | collective-permute-start | bytes 393224 | tf_op jit(solution)/shard_map/ppermute | solution.py:295
  94.7 3.4 %collective-permute-start.5 = (bf16[4,2,2,32,128]{4,3,2,1,0:T(8,128)(2,1)S(1)}, bf16[4,2,2,32,128]{4,3,2,1,0:T(8,128)(2,1)S(1)}, u32[]{:S(2)}, u32[]{:S(2)}) collective-permute-start(bf16[4,2,2,32,128]{4,3,2,1,0:T(8,128)(2,1)S(1)} %get-tuple-element.43), channel_id=1, source_target_pairs={{0,65},{1,64},{2,67},{3,66},{4,69},{5,68},{6,71},{7,70},{8,73},{9,... | collective-permute-start | bytes 393224 | tf_op jit(solution)/shard_map/ppermute | solution.py:295
  98.1 1.9 collective-permute-done.4.plus_ref
  100.0 14.0 %collective-permute-done.5.minus_ref = bf16[4,2,2,32,128]{4,3,2,1,0:T(8,128)(2,1)S(1)} collective-permute-done((bf16[4,2,2,32,128]{4,3,2,1,0:T(8,128)(2,1)S(1)}, bf16[4,2,2,32,128]{4,3,2,1,0:T(8,128)(2,1)S(1)}, u32[]{:S(2)}, u32[]{:S(2)}) %collective-permute-start.5) | collective-permute-done | bytes 131104 | tf_op jit(solution)/shard_map/ppermute | solution.py:295
  114.0 9.2 %all_to_all.45.home_ref = bf16[4,2,2,2,32,128]{5,4,3,2,1,0:T(8,128)(2,1)S(1)} all-to-all(bf16[4,2,2,2,32,128]{5,4,3,2,1,0:T(8,128)(2,1)S(1)} %shard_map.126), channel_id=1, replica_groups={{0,2,4,6},{1,3,5,7},{8,10,12,14},{9,11,13,15},{16,18,20,22},{17,19,21,2..., dimensions={0} | all-to-all | bytes 524288 | tf_op jit(solution)/shard_map/all_to_all | solution.py:278
  123.2 1.7 shard_map.128
  124.9 19.2 %all_to_all.46.b_ref = bf16[8,4,32,128]{3,2,1,0:T(8,128)(2,1)S(1)} all-to-all(bf16[8,4,32,128]{3,2,1,0:T(8,128)(2,1)S(1)} %get-tuple-element.51), channel_id=1, replica_groups={{32,40,48,56,64,72,80,88},{96,104,112,120,128,136,144,152},{160,168,176..., dimensions={0} | all-to-all | bytes 524288 | tf_op jit(solution)/shard_map/all_to_all | solution.py:273
  144.1 6.0 %all-to-all-start.6 = ((bf16[8,4,32,128]{3,2,1,0:T(8,128)(2,1)}), bf16[8,4,32,128]{3,2,1,0:T(8,128)(2,1)S(1)}, u32[]{:S(2)}, u32[]{:S(2)}) async-start(bf16[8,4,32,128]{3,2,1,0:T(8,128)(2,1)} %get-tuple-element.52), calls=%async_computation.6 | async-start | bytes 524288 | tf_op jit(solution)/shard_map/all_to_all | solution.py:273
  150.2 9.6 %all-to-all-done.6.a_ref = bf16[8,4,32,128]{3,2,1,0:T(8,128)(2,1)S(1)} async-done(((bf16[8,4,32,128]{3,2,1,0:T(8,128)(2,1)}), bf16[8,4,32,128]{3,2,1,0:T(8,128)(2,1)S(1)}, u32[]{:S(2)}, u32[]{:S(2)}) %all-to-all-start.6) | async-done | bytes 262176 | tf_op jit(solution)/shard_map/all_to_all | solution.py:273
  160.5 4.9 %all-to-all-start.7 = ((f32[16,8,384]{2,1,0:T(8,128)}), f32[16,8,384]{2,1,0:T(8,128)S(1)}, u32[]{:S(2)}, u32[]{:S(2)}) async-start(f32[16,8,384]{2,1,0:T(8,128)} %bitcast.6), calls=%async_computation.7 | async-start | bytes 393216 | tf_op jit(solution)/shard_map/all_to_all | solution.py:417
  166.3 1.4 shard_map.130
  167.7 13.8 %all-to-all-done.7 = f32[16,8,384]{2,1,0:T(8,128)S(1)} async-done(((f32[16,8,384]{2,1,0:T(8,128)}), f32[16,8,384]{2,1,0:T(8,128)S(1)}, u32[]{:S(2)}, u32[]{:S(2)}) %all-to-all-start.7) | async-done | bytes 196640 | tf_op jit(solution)/shard_map/all_to_all | solution.py:417
  182.2 4.1 %all-to-all-start.8 = ((f32[8,8,256]{2,1,0:T(8,128)}), f32[8,8,256]{2,1,0:T(8,128)S(1)}, u32[]{:S(2)}, u32[]{:S(2)}) async-start(f32[8,8,256]{2,1,0:T(8,128)} %broadcast_in_dim.8), calls=%async_computation.8 | async-start | bytes 131072 | tf_op jit(solution)/shard_map/all_to_all | solution.py:421
  186.9 5.0 %all-to-all-done.8 = f32[8,8,256]{2,1,0:T(8,128)S(1)} async-done(((f32[8,8,256]{2,1,0:T(8,128)}), f32[8,8,256]{2,1,0:T(8,128)S(1)}, u32[]{:S(2)}, u32[]{:S(2)}) %all-to-all-start.8) | async-done | bytes 65568 | tf_op jit(solution)/shard_map/all_to_all | solution.py:421
  (49 shorter events, 10.1 us)
Async XLA Ops:
  0.6 49.1 %copy-start.8 = (s32[56]{0:T(128)S(1)}, s32[56]{0:T(128)}, u32[]{:S(2)}) copy-start(s32[56]{0:T(128)} %dst_ref.7) | copy-start | bytes 676
  0.6 49.1 %copy-start.10 = (s32[56]{0:T(128)S(1)}, s32[56]{0:T(128)}, u32[]{:S(2)}) copy-start(s32[56]{0:T(128)} %src_ref.7) | copy-start | bytes 676
  1.4 0.9 copy-start.1
  3.9 23.0 %all-to-all-start = ((bf16[8,4,32,128]{3,2,1,0:T(8,128)(2,1)}), bf16[8,4,32,128]{3,2,1,0:T(8,128)(2,1)S(1)}, u32[]{:S(2)}, u32[]{:S(2)}) async-start(bf16[8,4,32,128]{3,2,1,0:T(8,128)(2,1)} %get-tuple-element.31), calls=%async_computation | async-start | bytes 524288 | tf_op jit(solution)/shard_map/all_to_all | solution.py:273
  19.6 0.9 copy-start.2
  20.5 0.9 copy-start.6
  26.9 46.8 %copy-start.4 = (bf16[256,256]{1,0:T(8,128)(2,1)S(1)}, bf16[256,256]{1,0:T(8,128)(2,1)}, u32[]{:S(2)}) copy-start(bf16[256,256]{1,0:T(8,128)(2,1)} %neigh_ref.1) | copy-start | bytes 393220
  26.9 46.9 %copy-start.5 = (bf16[256,256]{1,0:T(8,128)(2,1)S(1)}, bf16[256,256]{1,0:T(8,128)(2,1)}, u32[]{:S(2)}) copy-start(bf16[256,256]{1,0:T(8,128)(2,1)} %own_w_ref.1) | copy-start | bytes 393220
  26.9 47.0 %copy-start.11 = (f32[256]{0:T(256)S(1)}, f32[256]{0:T(256)}, u32[]{:S(2)}) copy-start(f32[256]{0:T(256)} %param.16) | copy-start | bytes 3076
  26.9 22.8 %all-to-all-start.1 = ((bf16[8,4,32,128]{3,2,1,0:T(8,128)(2,1)}), bf16[8,4,32,128]{3,2,1,0:T(8,128)(2,1)S(1)}, u32[]{:S(2)}, u32[]{:S(2)}) async-start(bf16[8,4,32,128]{3,2,1,0:T(8,128)(2,1)} %get-tuple-element.36), calls=%async_computation.1 | async-start | bytes 524288 | tf_op jit(solution)/shard_map/all_to_all | solution.py:273
  31.9 29.0 %collective-permute-start = (bf16[4,2,2,32,128]{4,3,2,1,0:T(8,128)(2,1)S(1)}, bf16[4,2,2,32,128]{4,3,2,1,0:T(8,128)(2,1)S(1)}, u32[]{:S(2)}, u32[]{:S(2)}) collective-permute-start(bf16[4,2,2,32,128]{4,3,2,1,0:T(8,128)(2,1)S(1)} %get-tuple-element.34), channel_id=1, source_target_pairs={{0,64},{1,65},{2,66},{3,67},{4,68},{5,69},{6,70},{7,71},{8,72},{9,... | collective-permute-start | bytes 393224 | tf_op jit(solution)/shard_map/ppermute | solution.py:295
  36.6 24.2 %collective-permute-start.1 = (bf16[4,2,2,32,128]{4,3,2,1,0:T(8,128)(2,1)S(1)}, bf16[4,2,2,32,128]{4,3,2,1,0:T(8,128)(2,1)S(1)}, u32[]{:S(2)}, u32[]{:S(2)}) collective-permute-start(bf16[4,2,2,32,128]{4,3,2,1,0:T(8,128)(2,1)S(1)} %get-tuple-element.35), channel_id=1, source_target_pairs={{0,65},{1,64},{2,67},{3,66},{4,69},{5,68},{6,71},{7,70},{8,73},{9,... | collective-permute-start | bytes 393224 | tf_op jit(solution)/shard_map/ppermute | solution.py:295
  43.6 2.0 %copy-start = (s32[56,128,128]{2,1,0:T(8,128)S(1)}, s32[56,128,128]{2,1,0:T(8,128)}, u32[]{:S(2)}) copy-start(s32[56,128,128]{2,1,0:T(8,128)} %cnt_ref.1) | copy-start | bytes 11010052
  45.7 0.9 copy-start.3
  46.6 0.7 copy-start.7
  47.2 0.7 copy-start.9
  51.1 10.3 %collective-permute-start.2 = (bf16[4,2,32,128]{3,2,1,0:T(8,128)(2,1)S(1)}, bf16[4,2,32,128]{3,2,1,0:T(8,128)(2,1)S(1)}, u32[]{:S(2)}, u32[]{:S(2)}) collective-permute-start(bf16[4,2,32,128]{3,2,1,0:T(8,128)(2,1)S(1)} %get-tuple-element.40), channel_id=1, source_target_pairs={{0,64},{1,65},{2,66},{3,67},{4,68},{5,69},{6,70},{7,71},{8,72},{9,... | collective-permute-start | bytes 196616 | tf_op jit(solution)/shard_map/ppermute | solution.py:295
  54.3 13.8 %collective-permute-start.3 = (bf16[4,2,32,128]{3,2,1,0:T(8,128)(2,1)S(1)}, bf16[4,2,32,128]{3,2,1,0:T(8,128)(2,1)S(1)}, u32[]{:S(2)}, u32[]{:S(2)}) collective-permute-start(bf16[4,2,32,128]{3,2,1,0:T(8,128)(2,1)S(1)} %get-tuple-element.41), channel_id=1, source_target_pairs={{0,65},{1,64},{2,67},{3,66},{4,69},{5,68},{6,71},{7,70},{8,73},{9,... | collective-permute-start | bytes 196616 | tf_op jit(solution)/shard_map/ppermute | solution.py:295
  68.9 10.1 %all-to-all-start.2 = ((bf16[4,3,2,2,32,128]{5,4,3,2,1,0:T(8,128)(2,1)}), bf16[4,3,2,2,32,128]{5,4,3,2,1,0:T(8,128)(2,1)S(1)}, u32[]{:S(2)}, u32[]{:S(2)}) async-start(bf16[4,3,2,2,32,128]{5,4,3,2,1,0:T(8,128)(2,1)} %shard_map.124), calls=%async_computation.2 | async-start | bytes 786432 | tf_op jit(solution)/shard_map/all_to_all | solution.py:278
  81.0 33.1 %all-to-all-start.3 = ((bf16[32,16,384]{2,1,0:T(8,128)(2,1)}), bf16[32,16,384]{2,1,0:T(8,128)(2,1)S(1)}, u32[]{:S(2)}, u32[]{:S(2)}) async-start(bf16[32,16,384]{2,1,0:T(8,128)(2,1)} %shard_map.127), calls=%async_computation.3 | async-start | bytes 786432 | tf_op jit(solution)/shard_map/all_to_all | solution.py:398
  88.3 11.7 %collective-permute-start.4 = (bf16[4,2,2,32,128]{4,3,2,1,0:T(8,128)(2,1)S(1)}, bf16[4,2,2,32,128]{4,3,2,1,0:T(8,128)(2,1)S(1)}, u32[]{:S(2)}, u32[]{:S(2)}) collective-permute-start(bf16[4,2,2,32,128]{4,3,2,1,0:T(8,128)(2,1)S(1)} %get-tuple-element.42), channel_id=1, source_target_pairs={{0,64},{1,65},{2,66},{3,67},{4,68},{5,69},{6,70},{7,71},{8,72},{9,... | collective-permute-start | bytes 393224 | tf_op jit(solution)/shard_map/ppermute | solution.py:295
  94.7 19.3 %collective-permute-start.5 = (bf16[4,2,2,32,128]{4,3,2,1,0:T(8,128)(2,1)S(1)}, bf16[4,2,2,32,128]{4,3,2,1,0:T(8,128)(2,1)S(1)}, u32[]{:S(2)}, u32[]{:S(2)}) collective-permute-start(bf16[4,2,2,32,128]{4,3,2,1,0:T(8,128)(2,1)S(1)} %get-tuple-element.43), channel_id=1, source_target_pairs={{0,65},{1,64},{2,67},{3,66},{4,69},{5,68},{6,71},{7,70},{8,73},{9,... | collective-permute-start | bytes 393224 | tf_op jit(solution)/shard_map/ppermute | solution.py:295
  144.1 15.7 %all-to-all-start.6 = ((bf16[8,4,32,128]{3,2,1,0:T(8,128)(2,1)}), bf16[8,4,32,128]{3,2,1,0:T(8,128)(2,1)S(1)}, u32[]{:S(2)}, u32[]{:S(2)}) async-start(bf16[8,4,32,128]{3,2,1,0:T(8,128)(2,1)} %get-tuple-element.52), calls=%async_computation.6 | async-start | bytes 524288 | tf_op jit(solution)/shard_map/all_to_all | solution.py:273
  160.5 21.0 %all-to-all-start.7 = ((f32[16,8,384]{2,1,0:T(8,128)}), f32[16,8,384]{2,1,0:T(8,128)S(1)}, u32[]{:S(2)}, u32[]{:S(2)}) async-start(f32[16,8,384]{2,1,0:T(8,128)} %bitcast.6), calls=%async_computation.7 | async-start | bytes 393216 | tf_op jit(solution)/shard_map/all_to_all | solution.py:417
  182.2 9.7 %all-to-all-start.8 = ((f32[8,8,256]{2,1,0:T(8,128)}), f32[8,8,256]{2,1,0:T(8,128)S(1)}, u32[]{:S(2)}, u32[]{:S(2)}) async-start(f32[8,8,256]{2,1,0:T(8,128)} %broadcast_in_dim.8), calls=%async_computation.8 | async-start | bytes 131072 | tf_op jit(solution)/shard_map/all_to_all | solution.py:421

commit v5 on v4

--- a/solution.py
+++ b/solution.py
@@ -319,10 +319,6 @@
     xc_plus, xc_minus = call(
         functools.partial(split_kernel, width), (shape(X, 2, per_col),) * 2, [VMEM] * 2
     )(node_feats, cotangent)
-    send_a, got_b, xc_plus, xc_minus = lax.optimization_barrier((send_a, got_b, xc_plus, xc_minus))
-    xc_plus = along_z(xc_plus, step)
-    xc_minus = along_z(xc_minus, -step)
-    got_a = swap(send_a, 0)
     whole = lambda shape: pl.BlockSpec(shape, lambda i: (0,) * len(shape))
     half, acc = pl.pallas_call(
         functools.partial(local_kernel, slots, chunk),
@@ -346,6 +342,12 @@
             flops=60000000, bytes_accessed=6000000, transcendentals=0
         ),
     )(node_feats, tile_dst, tile_src, tile_cnt)
+    send_a, got_b, xc_plus, xc_minus, half, acc = lax.optimization_barrier(
+        (send_a, got_b, xc_plus, xc_minus, half, acc)
+    )
+    xc_plus = along_z(xc_plus, step)
+    xc_minus = along_z(xc_minus, -step)
+    got_a = swap(send_a, 0)
     weight_t = jnp.concatenate([self_weight.T, neigh_weight.T], axis=1)
     bias_col = bias[:, None]
     agg_plus, agg_minus, degree = call(
@@ -412,14 +414,15 @@
     tail = jnp.concatenate([part[0:4, full:], part[8:12, full:]], axis=0)
     ends = [jnp.concatenate([part[8 * h : 8 * h + 8, :full], tail], axis=1) for h in range(Z_HI)]
     part = jnp.broadcast_to(jnp.stack(ends)[:, None], (Z_HI, Z_LO, 8, full + 128))
-    part = part.reshape(Z_HI * Z_LO, 8, full + 128)
+    part = part.reshape(Z_HI * Z_LO, 8, full + 128).astype(BF16)
     part, back_a = lax.optimization_barrier((part, back_a))
-    part = jnp.sum(lax.all_to_all(part, both, 0, 0, axis_index_groups=line, tiled=False), axis=0)
+    part = lax.all_to_all(part, both, 0, 0, axis_index_groups=line, tiled=False)
+    part = jnp.sum(part.astype(F32), axis=0)
     grad_bias = jnp.concatenate([part[0, full:], part[4, full:]])
     grad_bias = lax.dynamic_slice_in_dim(grad_bias, lax.axis_index("col") * dim, dim, 0)
-    part = jnp.broadcast_to(part[None, :, :full], (Y * CORE, 8, full))
+    part = jnp.broadcast_to(part[None, :, :full].astype(BF16), (Y * CORE, 8, full))
     part = lax.all_to_all(part, "blk", 0, 0, axis_index_groups=plane, tiled=False)
-    part = part.reshape(2, dim, full)
+    part = part.astype(F32).reshape(2, dim, full)
     grad_self, grad_neigh = part[0], part[1]
     acc = call(
         functools.partial(local_back_kernel, slots),

time: 196 us -> 187 us (0.954)
  waiting for transfers between devices: 62.1 us -> 51.4 us
    all_to_all x3, waiting for transfers between devices: 15.1 us -> 9.89 us  [swap(): lax.all_to_all(rows, 'blk', 0, 0, axis_index_groups=groups, tiled=False)]
    all_to_all x1, waiting for transfers between devices: 13.8 us -> 10.9 us  [per_device(): part = lax.all_to_all(part, both, 0, 0, axis_index_groups=line, tiled=False)]
    ppermute x6, waiting for transfers between devices: 23.2 us -> 20.9 us  [along_z(): return lax.ppermute(rows, ('blk', 'col'), sorted(route))]
    unnamed x26 -> x24, local copies, waits for them, and re-layouts: 7.18 us -> 6.27 us
  transfers between devices with their start and end apart: 13 -> 13, of which waited for: 9 -> 10; matrix products, arithmetic and copies ran while one was open for 1% -> 1% of each run, Pallas kernels for 3% -> 3%
where the time goes in v5:
time: 187 us; the launch traced here: 183 us
  starting transfers between devices  80.9 us (43%)
  waiting for transfers between devices  51.4 us (27%)
  blocking collectives  29 us (16%)
  Pallas kernels  11.5 us (6%)
  local copies, waits for them, and re-layouts  9.68 us (5%)
    ppermute x6, starting transfers between devices, along_z(): return lax.ppermute(rows, ('blk', 'col'), sorted(route))  31.2 us
    all_to_all x3, starting transfers between devices, swap(): lax.all_to_all(rows, 'blk', 0, 0, axis_index_groups=groups, tiled=False)  25.6 us
    ppermute x6, waiting for transfers between devices, along_z(): return lax.ppermute(rows, ('blk', 'col'), sorted(route))  20.9 us
    all_to_all x1, blocking collectives, swap(): lax.all_to_all(rows, 'blk', 0, 0, axis_index_groups=groups, tiled=False)  19.6 us
    all_to_all x1, waiting for transfers between devices, per_device(): part = lax.all_to_all(part, both, 0, 0, axis_index_groups=line, tiled=False)  10.9 us
    all_to_all x3, waiting for transfers between devices, swap(): lax.all_to_all(rows, 'blk', 0, 0, axis_index_groups=groups, tiled=False)  9.89 us
    all_to_all x1, blocking collectives, over_x(): lax.all_to_all(rows, 'col', 0, 0, axis_index_groups=groups, tiled=False)  9.38 us
    all_to_all x1, starting transfers between devices, per_device(): part = lax.all_to_all(part, both, 0, 0, axis_index_groups=flat, tiled=False)  8.66 us
  transfers between devices with their start and end apart: 13, of which 10 were waited for; matrix products, arithmetic and copies ran while one was open for 1% of the time, Pallas kernels for 3%

profile of v5, /device:TPU:6, one launch (start us, length us, event | category | flops | bytes accessed | tf_op | source)
XLA Modules:
  0.0 183.5 jit_solution(13773080579412362760)
XLA Ops:
  2.3 1.6 shard_map.120
  3.9 15.7 %all-to-all-start = ((bf16[8,4,32,128]{3,2,1,0:T(8,128)(2,1)}), bf16[8,4,32,128]{3,2,1,0:T(8,128)(2,1)S(1)}, u32[]{:S(2)}, u32[]{:S(2)}) async-start(bf16[8,4,32,128]{3,2,1,0:T(8,128)(2,1)} %get-tuple-element.33), calls=%async_computation | async-start | bytes 524288 | tf_op jit(solution)/shard_map/all_to_all | solution.py:273
  21.5 2.0 %copy-done = s32[56,128,128]{2,1,0:T(8,128)S(1)} copy-done((s32[56,128,128]{2,1,0:T(8,128)S(1)}, s32[56,128,128]{2,1,0:T(8,128)}, u32[]{:S(2)}) %copy-start) | copy-done | bytes 3670040
  24.8 1.8 shard_map.122
  26.9 4.8 %all-to-all-start.1 = ((bf16[8,4,32,128]{3,2,1,0:T(8,128)(2,1)}), bf16[8,4,32,128]{3,2,1,0:T(8,128)(2,1)S(1)}, u32[]{:S(2)}, u32[]{:S(2)}) async-start(bf16[8,4,32,128]{3,2,1,0:T(8,128)(2,1)} %get-tuple-element.40), calls=%async_computation.1 | async-start | bytes 524288 | tf_op jit(solution)/shard_map/all_to_all | solution.py:273
  31.8 4.7 %collective-permute-start = (bf16[4,2,2,32,128]{4,3,2,1,0:T(8,128)(2,1)S(1)}, bf16[4,2,2,32,128]{4,3,2,1,0:T(8,128)(2,1)S(1)}, u32[]{:S(2)}, u32[]{:S(2)}) collective-permute-start(bf16[4,2,2,32,128]{4,3,2,1,0:T(8,128)(2,1)S(1)} %get-tuple-element.38), channel_id=1, source_target_pairs={{0,64},{1,65},{2,66},{3,67},{4,68},{5,69},{6,70},{7,71},{8,72},{9,... | collective-permute-start | bytes 393224 | tf_op jit(solution)/shard_map/ppermute | solution.py:295
  36.5 7.0 %collective-permute-start.1 = (bf16[4,2,2,32,128]{4,3,2,1,0:T(8,128)(2,1)S(1)}, bf16[4,2,2,32,128]{4,3,2,1,0:T(8,128)(2,1)S(1)}, u32[]{:S(2)}, u32[]{:S(2)}) collective-permute-start(bf16[4,2,2,32,128]{4,3,2,1,0:T(8,128)(2,1)S(1)} %get-tuple-element.39), channel_id=1, source_target_pairs={{0,65},{1,64},{2,67},{3,66},{4,69},{5,68},{6,71},{7,70},{8,73},{9,... | collective-permute-start | bytes 393224 | tf_op jit(solution)/shard_map/ppermute | solution.py:295
  43.5 1.3 shard_map.123
  44.9 3.2 %collective-permute-start.2 = (bf16[4,2,32,128]{3,2,1,0:T(8,128)(2,1)S(1)}, bf16[4,2,32,128]{3,2,1,0:T(8,128)(2,1)S(1)}, u32[]{:S(2)}, u32[]{:S(2)}) collective-permute-start(bf16[4,2,32,128]{3,2,1,0:T(8,128)(2,1)S(1)} %get-tuple-element.44), channel_id=1, source_target_pairs={{0,64},{1,65},{2,66},{3,67},{4,68},{5,69},{6,70},{7,71},{8,72},{9,... | collective-permute-start | bytes 196616 | tf_op jit(solution)/shard_map/ppermute | solution.py:295
  48.1 6.6 %collective-permute-start.3 = (bf16[4,2,32,128]{3,2,1,0:T(8,128)(2,1)S(1)}, bf16[4,2,32,128]{3,2,1,0:T(8,128)(2,1)S(1)}, u32[]{:S(2)}, u32[]{:S(2)}) collective-permute-start(bf16[4,2,32,128]{3,2,1,0:T(8,128)(2,1)S(1)} %get-tuple-element.45), channel_id=1, source_target_pairs={{0,65},{1,64},{2,67},{3,66},{4,69},{5,68},{6,71},{7,70},{8,73},{9,... | collective-permute-start | bytes 196616 | tf_op jit(solution)/shard_map/ppermute | solution.py:295
  54.6 1.2 collective-permute-done.1.xc_minus_ref
  55.8 6.2 %collective-permute-done.2.agg_plus_ref = bf16[4,2,32,128]{3,2,1,0:T(8,128)(2,1)S(1)} collective-permute-done((bf16[4,2,32,128]{3,2,1,0:T(8,128)(2,1)S(1)}, bf16[4,2,32,128]{3,2,1,0:T(8,128)(2,1)S(1)}, u32[]{:S(2)}, u32[]{:S(2)}) %collective-permute-start.2) | collective-permute-done | bytes 65568 | tf_op jit(solution)/shard_map/ppermute | solution.py:295
  62.0 0.9 collective-permute-done.3.agg_minus_ref
  63.7 4.8 %all-to-all-start.2 = ((bf16[4,3,2,2,32,128]{5,4,3,2,1,0:T(8,128)(2,1)}), bf16[4,3,2,2,32,128]{5,4,3,2,1,0:T(8,128)(2,1)S(1)}, u32[]{:S(2)}, u32[]{:S(2)}) async-start(bf16[4,3,2,2,32,128]{5,4,3,2,1,0:T(8,128)(2,1)} %shard_map.124), calls=%async_computation.2 | async-start | bytes 786432 | tf_op jit(solution)/shard_map/all_to_all | solution.py:278
  68.9 4.9 %all-to-all-done.2.in_ref = bf16[4,3,2,2,32,128]{5,4,3,2,1,0:T(8,128)(2,1)S(1)} async-done(((bf16[4,3,2,2,32,128]{5,4,3,2,1,0:T(8,128)(2,1)}), bf16[4,3,2,2,32,128]{5,4,3,2,1,0:T(8,128)(2,1)S(1)}, u32[]{:S(2)}, u32[]{:S(2)}) %all-to-all-start.2) | async-done | bytes 393248 | tf_op jit(solution)/shard_map/all_to_all | solution.py:278
  73.8 0.9 shard_map.125
  74.7 1.1 shard_map.127
  75.8 8.7 %all-to-all-start.3 = ((bf16[32,16,384]{2,1,0:T(8,128)(2,1)}), bf16[32,16,384]{2,1,0:T(8,128)(2,1)S(1)}, u32[]{:S(2)}, u32[]{:S(2)}) async-start(bf16[32,16,384]{2,1,0:T(8,128)(2,1)} %shard_map.127), calls=%async_computation.3 | async-start | bytes 786432 | tf_op jit(solution)/shard_map/all_to_all | solution.py:400
  84.4 5.8 %collective-permute-start.4 = (bf16[4,2,2,32,128]{4,3,2,1,0:T(8,128)(2,1)S(1)}, bf16[4,2,2,32,128]{4,3,2,1,0:T(8,128)(2,1)S(1)}, u32[]{:S(2)}, u32[]{:S(2)}) collective-permute-start(bf16[4,2,2,32,128]{4,3,2,1,0:T(8,128)(2,1)S(1)} %get-tuple-element.46), channel_id=1, source_target_pairs={{0,64},{1,65},{2,66},{3,67},{4,68},{5,69},{6,70},{7,71},{8,72},{9,... | collective-permute-start | bytes 393224 | tf_op jit(solution)/shard_map/ppermute | solution.py:295
  90.2 4.0 %collective-permute-start.5 = (bf16[4,2,2,32,128]{4,3,2,1,0:T(8,128)(2,1)S(1)}, bf16[4,2,2,32,128]{4,3,2,1,0:T(8,128)(2,1)S(1)}, u32[]{:S(2)}, u32[]{:S(2)}) collective-permute-start(bf16[4,2,2,32,128]{4,3,2,1,0:T(8,128)(2,1)S(1)} %get-tuple-element.47), channel_id=1, source_target_pairs={{0,65},{1,64},{2,67},{3,66},{4,69},{5,68},{6,71},{7,70},{8,73},{9,... | collective-permute-start | bytes 393224 | tf_op jit(solution)/shard_map/ppermute | solution.py:295
  94.2 4.0 %collective-permute-done.4.plus_ref = bf16[4,2,2,32,128]{4,3,2,1,0:T(8,128)(2,1)S(1)} collective-permute-done((bf16[4,2,2,32,128]{4,3,2,1,0:T(8,128)(2,1)S(1)}, bf16[4,2,2,32,128]{4,3,2,1,0:T(8,128)(2,1)S(1)}, u32[]{:S(2)}, u32[]{:S(2)}) %collective-permute-start.4) | collective-permute-done | bytes 131104 | tf_op jit(solution)/shard_map/ppermute | solution.py:295
  98.2 8.6 %collective-permute-done.5.minus_ref = bf16[4,2,2,32,128]{4,3,2,1,0:T(8,128)(2,1)S(1)} collective-permute-done((bf16[4,2,2,32,128]{4,3,2,1,0:T(8,128)(2,1)S(1)}, bf16[4,2,2,32,128]{4,3,2,1,0:T(8,128)(2,1)S(1)}, u32[]{:S(2)}, u32[]{:S(2)}) %collective-permute-start.5) | collective-permute-done | bytes 131104 | tf_op jit(solution)/shard_map/ppermute | solution.py:295
  106.8 9.4 %all_to_all.45.home_ref = bf16[4,2,2,2,32,128]{5,4,3,2,1,0:T(8,128)(2,1)S(1)} all-to-all(bf16[4,2,2,2,32,128]{5,4,3,2,1,0:T(8,128)(2,1)S(1)} %shard_map.126), channel_id=1, replica_groups={{0,2,4,6},{1,3,5,7},{8,10,12,14},{9,11,13,15},{16,18,20,22},{17,19,21,2..., dimensions={0} | all-to-all | bytes 524288 | tf_op jit(solution)/shard_map/all_to_all | solution.py:278
  116.2 1.7 shard_map.128
  117.9 19.6 %all_to_all.46.b_ref = bf16[8,4,32,128]{3,2,1,0:T(8,128)(2,1)S(1)} all-to-all(bf16[8,4,32,128]{3,2,1,0:T(8,128)(2,1)S(1)} %get-tuple-element.55), channel_id=1, replica_groups={{32,40,48,56,64,72,80,88},{96,104,112,120,128,136,144,152},{160,168,176..., dimensions={0} | all-to-all | bytes 524288 | tf_op jit(solution)/shard_map/all_to_all | solution.py:273
  137.5 5.0 %all-to-all-start.6 = ((bf16[8,4,32,128]{3,2,1,0:T(8,128)(2,1)}), bf16[8,4,32,128]{3,2,1,0:T(8,128)(2,1)S(1)}, u32[]{:S(2)}, u32[]{:S(2)}) async-start(bf16[8,4,32,128]{3,2,1,0:T(8,128)(2,1)} %get-tuple-element.56), calls=%async_computation.6 | async-start | bytes 524288 | tf_op jit(solution)/shard_map/all_to_all | solution.py:273
  142.6 9.6 %all-to-all-done.6.a_ref = bf16[8,4,32,128]{3,2,1,0:T(8,128)(2,1)S(1)} async-done(((bf16[8,4,32,128]{3,2,1,0:T(8,128)(2,1)}), bf16[8,4,32,128]{3,2,1,0:T(8,128)(2,1)S(1)}, u32[]{:S(2)}, u32[]{:S(2)}) %all-to-all-start.6) | async-done | bytes 262176 | tf_op jit(solution)/shard_map/all_to_all | solution.py:273
  152.9 5.6 %all-to-all-start.7 = ((bf16[16,8,384]{2,1,0:T(8,128)(2,1)}), bf16[16,8,384]{2,1,0:T(8,128)(2,1)S(1)}, u32[]{:S(2)}, u32[]{:S(2)}) async-start(bf16[16,8,384]{2,1,0:T(8,128)(2,1)} %bitcast.6), calls=%async_computation.7 | async-start | bytes 196608 | tf_op jit(solution)/shard_map/all_to_all | solution.py:419
  159.4 1.4 shard_map.130
  160.8 10.9 %all-to-all-done.7 = bf16[16,8,384]{2,1,0:T(8,128)(2,1)S(1)} async-done(((bf16[16,8,384]{2,1,0:T(8,128)(2,1)}), bf16[16,8,384]{2,1,0:T(8,128)(2,1)S(1)}, u32[]{:S(2)}, u32[]{:S(2)}) %all-to-all-start.7) | async-done | bytes 98336 | tf_op jit(solution)/shard_map/all_to_all | solution.py:419
  172.3 5.1 %all-to-all-start.8 = ((bf16[8,8,256]{2,1,0:T(8,128)(2,1)}), bf16[8,8,256]{2,1,0:T(8,128)(2,1)S(1)}, u32[]{:S(2)}, u32[]{:S(2)}) async-start(bf16[8,8,256]{2,1,0:T(8,128)(2,1)} %broadcast_in_dim.8), calls=%async_computation.8 | async-start | bytes 65536 | tf_op jit(solution)/shard_map/all_to_all | solution.py:424
  178.0 4.8 %all-to-all-done.8 = bf16[8,8,256]{2,1,0:T(8,128)(2,1)S(1)} async-done(((bf16[8,8,256]{2,1,0:T(8,128)(2,1)}), bf16[8,8,256]{2,1,0:T(8,128)(2,1)S(1)}, u32[]{:S(2)}, u32[]{:S(2)}) %all-to-all-start.8) | async-done | bytes 32800 | tf_op jit(solution)/shard_map/all_to_all | solution.py:424
  (49 shorter events, 9.8 us)
Async XLA Ops:
  0.6 42.9 %copy-start.7 = (s32[56]{0:T(128)S(1)}, s32[56]{0:T(128)}, u32[]{:S(2)}) copy-start(s32[56]{0:T(128)} %dst_ref.7) | copy-start | bytes 676
  0.6 42.9 %copy-start.9 = (s32[56]{0:T(128)S(1)}, s32[56]{0:T(128)}, u32[]{:S(2)}) copy-start(s32[56]{0:T(128)} %src_ref.7) | copy-start | bytes 676
  1.4 0.9 copy-start.1
  3.9 23.0 %all-to-all-start = ((bf16[8,4,32,128]{3,2,1,0:T(8,128)(2,1)}), bf16[8,4,32,128]{3,2,1,0:T(8,128)(2,1)S(1)}, u32[]{:S(2)}, u32[]{:S(2)}) async-start(bf16[8,4,32,128]{3,2,1,0:T(8,128)(2,1)} %get-tuple-element.33), calls=%async_computation | async-start | bytes 524288 | tf_op jit(solution)/shard_map/all_to_all | solution.py:273
  19.6 0.9 copy-start.2
  20.5 0.9 copy-start.5
  21.5 2.0 %copy-start = (s32[56,128,128]{2,1,0:T(8,128)S(1)}, s32[56,128,128]{2,1,0:T(8,128)}, u32[]{:S(2)}) copy-start(s32[56,128,128]{2,1,0:T(8,128)} %cnt_ref.1) | copy-start | bytes 11010052
  23.5 0.7 copy-start.6
  24.2 0.7 copy-start.8
  24.8 43.7 %copy-start.3 = (bf16[256,256]{1,0:T(8,128)(2,1)S(1)}, bf16[256,256]{1,0:T(8,128)(2,1)}, u32[]{:S(2)}) copy-start(bf16[256,256]{1,0:T(8,128)(2,1)} %neigh_ref.1) | copy-start | bytes 393220
  24.8 43.8 %copy-start.4 = (bf16[256,256]{1,0:T(8,128)(2,1)S(1)}, bf16[256,256]{1,0:T(8,128)(2,1)}, u32[]{:S(2)}) copy-start(bf16[256,256]{1,0:T(8,128)(2,1)} %own_w_ref.1) | copy-start | bytes 393220
  24.8 43.9 %copy-start.10 = (f32[256]{0:T(256)S(1)}, f32[256]{0:T(256)}, u32[]{:S(2)}) copy-start(f32[256]{0:T(256)} %param.16) | copy-start | bytes 3076
  26.9 16.6 %all-to-all-start.1 = ((bf16[8,4,32,128]{3,2,1,0:T(8,128)(2,1)}), bf16[8,4,32,128]{3,2,1,0:T(8,128)(2,1)S(1)}, u32[]{:S(2)}, u32[]{:S(2)}) async-start(bf16[8,4,32,128]{3,2,1,0:T(8,128)(2,1)} %get-tuple-element.40), calls=%async_computation.1 | async-start | bytes 524288 | tf_op jit(solution)/shard_map/all_to_all | solution.py:273
  31.8 22.9 %collective-permute-start = (bf16[4,2,2,32,128]{4,3,2,1,0:T(8,128)(2,1)S(1)}, bf16[4,2,2,32,128]{4,3,2,1,0:T(8,128)(2,1)S(1)}, u32[]{:S(2)}, u32[]{:S(2)}) collective-permute-start(bf16[4,2,2,32,128]{4,3,2,1,0:T(8,128)(2,1)S(1)} %get-tuple-element.38), channel_id=1, source_target_pairs={{0,64},{1,65},{2,66},{3,67},{4,68},{5,69},{6,70},{7,71},{8,72},{9,... | collective-permute-start | bytes 393224 | tf_op jit(solution)/shard_map/ppermute | solution.py:295
  36.5 19.4 %collective-permute-start.1 = (bf16[4,2,2,32,128]{4,3,2,1,0:T(8,128)(2,1)S(1)}, bf16[4,2,2,32,128]{4,3,2,1,0:T(8,128)(2,1)S(1)}, u32[]{:S(2)}, u32[]{:S(2)}) collective-permute-start(bf16[4,2,2,32,128]{4,3,2,1,0:T(8,128)(2,1)S(1)} %get-tuple-element.39), channel_id=1, source_target_pairs={{0,65},{1,64},{2,67},{3,66},{4,69},{5,68},{6,71},{7,70},{8,73},{9,... | collective-permute-start | bytes 393224 | tf_op jit(solution)/shard_map/ppermute | solution.py:295
  44.9 17.1 %collective-permute-start.2 = (bf16[4,2,32,128]{3,2,1,0:T(8,128)(2,1)S(1)}, bf16[4,2,32,128]{3,2,1,0:T(8,128)(2,1)S(1)}, u32[]{:S(2)}, u32[]{:S(2)}) collective-permute-start(bf16[4,2,32,128]{3,2,1,0:T(8,128)(2,1)S(1)} %get-tuple-element.44), channel_id=1, source_target_pairs={{0,64},{1,65},{2,66},{3,67},{4,68},{5,69},{6,70},{7,71},{8,72},{9,... | collective-permute-start | bytes 196616 | tf_op jit(solution)/shard_map/ppermute | solution.py:295
  48.1 14.9 %collective-permute-start.3 = (bf16[4,2,32,128]{3,2,1,0:T(8,128)(2,1)S(1)}, bf16[4,2,32,128]{3,2,1,0:T(8,128)(2,1)S(1)}, u32[]{:S(2)}, u32[]{:S(2)}) collective-permute-start(bf16[4,2,32,128]{3,2,1,0:T(8,128)(2,1)S(1)} %get-tuple-element.45), channel_id=1, source_target_pairs={{0,65},{1,64},{2,67},{3,66},{4,69},{5,68},{6,71},{7,70},{8,73},{9,... | collective-permute-start | bytes 196616 | tf_op jit(solution)/shard_map/ppermute | solution.py:295
  63.7 10.1 %all-to-all-start.2 = ((bf16[4,3,2,2,32,128]{5,4,3,2,1,0:T(8,128)(2,1)}), bf16[4,3,2,2,32,128]{5,4,3,2,1,0:T(8,128)(2,1)S(1)}, u32[]{:S(2)}, u32[]{:S(2)}) async-start(bf16[4,3,2,2,32,128]{5,4,3,2,1,0:T(8,128)(2,1)} %shard_map.124), calls=%async_computation.2 | async-start | bytes 786432 | tf_op jit(solution)/shard_map/all_to_all | solution.py:278
  75.8 31.0 %all-to-all-start.3 = ((bf16[32,16,384]{2,1,0:T(8,128)(2,1)}), bf16[32,16,384]{2,1,0:T(8,128)(2,1)S(1)}, u32[]{:S(2)}, u32[]{:S(2)}) async-start(bf16[32,16,384]{2,1,0:T(8,128)(2,1)} %shard_map.127), calls=%async_computation.3 | async-start | bytes 786432 | tf_op jit(solution)/shard_map/all_to_all | solution.py:400
  84.4 13.8 %collective-permute-start.4 = (bf16[4,2,2,32,128]{4,3,2,1,0:T(8,128)(2,1)S(1)}, bf16[4,2,2,32,128]{4,3,2,1,0:T(8,128)(2,1)S(1)}, u32[]{:S(2)}, u32[]{:S(2)}) collective-permute-start(bf16[4,2,2,32,128]{4,3,2,1,0:T(8,128)(2,1)S(1)} %get-tuple-element.46), channel_id=1, source_target_pairs={{0,64},{1,65},{2,66},{3,67},{4,68},{5,69},{6,70},{7,71},{8,72},{9,... | collective-permute-start | bytes 393224 | tf_op jit(solution)/shard_map/ppermute | solution.py:295
  90.2 16.5 %collective-permute-start.5 = (bf16[4,2,2,32,128]{4,3,2,1,0:T(8,128)(2,1)S(1)}, bf16[4,2,2,32,128]{4,3,2,1,0:T(8,128)(2,1)S(1)}, u32[]{:S(2)}, u32[]{:S(2)}) collective-permute-start(bf16[4,2,2,32,128]{4,3,2,1,0:T(8,128)(2,1)S(1)} %get-tuple-element.47), channel_id=1, source_target_pairs={{0,65},{1,64},{2,67},{3,66},{4,69},{5,68},{6,71},{7,70},{8,73},{9,... | collective-permute-start | bytes 393224 | tf_op jit(solution)/shard_map/ppermute | solution.py:295
  137.5 14.8 %all-to-all-start.6 = ((bf16[8,4,32,128]{3,2,1,0:T(8,128)(2,1)}), bf16[8,4,32,128]{3,2,1,0:T(8,128)(2,1)S(1)}, u32[]{:S(2)}, u32[]{:S(2)}) async-start(bf16[8,4,32,128]{3,2,1,0:T(8,128)(2,1)} %get-tuple-element.56), calls=%async_computation.6 | async-start | bytes 524288 | tf_op jit(solution)/shard_map/all_to_all | solution.py:273
  152.9 18.8 %all-to-all-start.7 = ((bf16[16,8,384]{2,1,0:T(8,128)(2,1)}), bf16[16,8,384]{2,1,0:T(8,128)(2,1)S(1)}, u32[]{:S(2)}, u32[]{:S(2)}) async-start(bf16[16,8,384]{2,1,0:T(8,128)(2,1)} %bitcast.6), calls=%async_computation.7 | async-start | bytes 196608 | tf_op jit(solution)/shard_map/all_to_all | solution.py:419
  172.3 10.5 %all-to-all-start.8 = ((bf16[8,8,256]{2,1,0:T(8,128)(2,1)}), bf16[8,8,256]{2,1,0:T(8,128)(2,1)S(1)}, u32[]{:S(2)}, u32[]{:S(2)}) async-start(bf16[8,8,256]{2,1,0:T(8,128)(2,1)} %broadcast_in_dim.8), calls=%async_computation.8 | async-start | bytes 65536 | tf_op jit(solution)/shard_map/all_to_all | solution.py:424

commit v6 on v5

--- a/solution.py
+++ b/solution.py
@@ -211,12 +211,13 @@
 
 
 def contribution_kernel(
-    slots, home_ref, deg_ref, dst_ref, src_ref, half_ref, a_ref, b_ref, scaled_ref, hold_ref
+    slots, home_ref, deg_ref, dst_ref, src_ref, half_ref, b_ref, scaled_ref, *rest
 ):
+    near_refs, hold_ref = rest[:-1], rest[-1]
     place_a, place_b = places()
     z_hi = column()[1]
     blocks = scaled_ref.shape[0]
-    cap = a_ref.shape[1]
+    cap = b_ref.shape[1]
     per = home_ref.shape[3]
     for x in range(X):
         for side, h in ((0, 1 - z_hi), (1, z_hi)):
@@ -227,11 +228,14 @@
     for tile in range(slots):
         value = dot(scaled_ref[dst_ref[tile]], half_ref[tile])
         hold_ref[src_ref[tile] - blocks] = value.astype(BF16)
-    for ref, place in ((b_ref, place_b), (a_ref, place_a)):
-        for peer in range(GROUP):
-            kind = kind_of(place - peer)
-            for m in range(cap):
-                ref[peer, m] = hold_ref[kind * cap + m]
+    for peer in range(GROUP):
+        kind = kind_of(place_b - peer)
+        for m in range(cap):
+            b_ref[peer, m] = hold_ref[kind * cap + m]
+    for flip, ref in enumerate(near_refs, start=1):
+        kind = kind_of(place_a - jnp.bitwise_xor(place_a, flip))
+        for m in range(cap):
+            ref[m] = hold_ref[kind * cap + m]
 
 
 def local_back_kernel(slots, scaled_ref, home_ref, dst_ref, src_ref, half_ref, acc_ref):
@@ -245,18 +249,25 @@
         acc_ref[src_ref[tile]] += dot(scaled_ref[dst_ref[tile]], half_ref[tile])
 
 
-def finish_kernel(acc_in, a_ref, b_ref, send_ref, out_ref, acc_ref):
+def finish_kernel(acc_in, b_ref, send_ref, *rest):
+    near_refs, (out_ref, acc_ref) = rest[:-2], rest[-2:]
     place_a, place_b = places()
     kinds, cap = send_ref.shape
     width = acc_in.shape[2]
     acc_ref[...] = acc_in[...]
     for kind in range(kinds):
         offset = (kind // 2 + 1) * (1 - 2 * (kind % 2))
-        row_a = place_a + offset
-        row_b = place_b + offset
+        away = jnp.logical_not(inside(place_a + offset))
+        row_b = bounded(place_b + offset)
         for m in range(cap):
-            got = jnp.where(inside(row_a), a_ref[bounded(row_a), m], b_ref[bounded(row_b), m])
-            acc_ref[send_ref[kind, m]] += got.astype(F32)
+            got = jnp.where(away, b_ref[row_b, m].astype(F32), 0.0)
+            acc_ref[send_ref[kind, m]] += got
+    for flip, ref in enumerate(near_refs, start=1):
+        offset = jnp.bitwise_xor(place_a, flip) - place_a
+        used = jnp.abs(offset) <= kinds // 2
+        kind = kind_of(offset)
+        for m in range(cap):
+            acc_ref[send_ref[kind, m]] += jnp.where(used, ref[m].astype(F32), 0.0)
     for block in range(acc_ref.shape[0]):
         out_ref[:, block * width : (block + 1) * width] = acc_ref[block].astype(BF16)
 
@@ -271,6 +282,15 @@
         [(first + shift + i) % devices for i in range(GROUP)] for first in range(0, devices, GROUP)
     ]
     return lax.all_to_all(rows, "blk", 0, 0, axis_index_groups=groups, tiled=False)
+
+
+def flipped(rows, flip):
+    route = [
+        (e, e ^ flip)
+        for e in range(lax.axis_size("blk"))
+        if abs((e ^ flip) - e) <= GROUP // 2
+    ]
+    return lax.ppermute(rows, "blk", route)
 
 
 def over_x(rows):
@@ -401,21 +421,20 @@
     home = call(join_back_kernel, shape(X, 2, 2, per_col), [VMEM] * 2)(plus, minus)
     home, part = lax.optimization_barrier((home, part))
     home = over_x(home)
-    away_a, away_b, scaled = call(
+    away_b, scaled, *near = call(
         functools.partial(contribution_kernel, slots),
-        (halo, halo, shape(blocks)),
+        (halo, shape(blocks)) + (shape(cap),) * (GROUP - 1),
         [VMEM, VMEM, SMEM, SMEM, VMEM],
         [pltpu.VMEM((slots, dim, width), BF16)],
     )(home, degree, tile_dst, tile_src, half)
     back_b = swap(away_b, GROUP // 2)
-    away_a, back_b = lax.optimization_barrier((away_a, back_b))
-    back_a = swap(away_a, 0)
+    near = [flipped(rows, flip) for flip, rows in enumerate(near, start=1)]
     part = jnp.sum(part.astype(F32), axis=0)
     tail = jnp.concatenate([part[0:4, full:], part[8:12, full:]], axis=0)
     ends = [jnp.concatenate([part[8 * h : 8 * h + 8, :full], tail], axis=1) for h in range(Z_HI)]
     part = jnp.broadcast_to(jnp.stack(ends)[:, None], (Z_HI, Z_LO, 8, full + 128))
     part = part.reshape(Z_HI * Z_LO, 8, full + 128).astype(BF16)
-    part, back_a = lax.optimization_barrier((part, back_a))
+    part, back_b = lax.optimization_barrier((part, back_b))
     part = lax.all_to_all(part, both, 0, 0, axis_index_groups=line, tiled=False)
     part = jnp.sum(part.astype(F32), axis=0)
     grad_bias = jnp.concatenate([part[0, full:], part[4, full:]])
@@ -432,9 +451,9 @@
     grad_feats = call(
         finish_kernel,
         jax.ShapeDtypeStruct((dim, nodes), BF16),
-        [VMEM, VMEM, VMEM, SMEM],
+        [VMEM, VMEM, SMEM] + [VMEM] * (GROUP - 1),
         [pltpu.VMEM((blocks, dim, width), F32)],
-    )(acc, back_a, back_b, table)
+    )(acc, back_b, table, *near)
     return grad_feats, grad_self, grad_neigh, grad_bias
 
 

time: 187 us -> 188 us (level)
  starting transfers between devices: 80.9 us -> 112 us
  blocking collectives: 29 us -> 9.38 us
  waiting for transfers between devices: 51.4 us -> 39.5 us
    ppermute x0 -> x7, starting transfers between devices: none -> 20.7 us  [flipped(): return lax.ppermute(rows, 'blk', route)]
    all_to_all x1 -> x0, blocking collectives: 19.6 us -> none  [swap(): lax.all_to_all(rows, 'blk', 0, 0, axis_index_groups=groups, tiled=False)]
    all_to_all x1, waiting for transfers between devices: 10.9 us -> 0.01 us  [per_device(): part = lax.all_to_all(part, both, 0, 0, axis_index_groups=line, tiled=False)]
    all_to_all x3, starting transfers between devices: 25.6 us -> 33.6 us  [swap(): lax.all_to_all(rows, 'blk', 0, 0, axis_index_groups=groups, tiled=False)]
    all_to_all x3, waiting for transfers between devices: 9.89 us -> 6.49 us  [swap(): lax.all_to_all(rows, 'blk', 0, 0, axis_index_groups=groups, tiled=False)]
    ppermute x0 -> x7, waiting for transfers between devices: none -> 2.43 us  [flipped(): return lax.ppermute(rows, 'blk', route)]
    all_to_all x1, starting transfers between devices: 5.61 us -> 7.5 us  [per_device(): part = lax.all_to_all(part, both, 0, 0, axis_index_groups=line, tiled=False)]
    unnamed x24 -> x26, local copies, waits for them, and re-layouts: 6.27 us -> 6.28 us
  transfers between devices with their start and end apart: 13 -> 20, of which waited for: 10 -> 10; matrix products, arithmetic and copies ran while one was open for 1% -> 1% of each run, Pallas kernels for 3% -> 3%
where the time goes in v6:
time: 188 us; the launch traced here: 184 us
  starting transfers between devices  112 us (60%)
  waiting for transfers between devices  39.5 us (21%)
  Pallas kernels  11.7 us (6%)
  local copies, waits for them, and re-layouts  9.67 us (5%)
  blocking collectives  9.38 us (5%)
    all_to_all x3, starting transfers between devices, swap(): lax.all_to_all(rows, 'blk', 0, 0, axis_index_groups=groups, tiled=False)  33.6 us
    ppermute x6, starting transfers between devices, along_z(): return lax.ppermute(rows, ('blk', 'col'), sorted(route))  31.2 us
    ppermute x6, waiting for transfers between devices, along_z(): return lax.ppermute(rows, ('blk', 'col'), sorted(route))  20.9 us
    ppermute x7, starting transfers between devices, flipped(): return lax.ppermute(rows, 'blk', route)  20.7 us
    all_to_all x1, blocking collectives, over_x(): lax.all_to_all(rows, 'col', 0, 0, axis_index_groups=groups, tiled=False)  9.38 us
    all_to_all x1, starting transfers between devices, per_device(): part = lax.all_to_all(part, both, 0, 0, axis_index_groups=flat, tiled=False)  8.66 us
    all_to_all x1, starting transfers between devices, per_device(): part = lax.all_to_all(part, both, 0, 0, axis_index_groups=line, tiled=False)  7.5 us
    all_to_all x3, waiting for transfers between devices, swap(): lax.all_to_all(rows, 'blk', 0, 0, axis_index_groups=groups, tiled=False)  6.49 us
  transfers between devices with their start and end apart: 20, of which 10 were waited for; matrix products, arithmetic and copies ran while one was open for 1% of the time, Pallas kernels for 3%

profile of v6, /device:TPU:6, one launch (start us, length us, event | category | flops | bytes accessed | tf_op | source)
XLA Modules:
  0.0 184.0 jit_solution(6835951768281328936)
XLA Ops:
  2.3 1.6 shard_map.120
  3.9 15.7 %all-to-all-start = ((bf16[8,4,32,128]{3,2,1,0:T(8,128)(2,1)}), bf16[8,4,32,128]{3,2,1,0:T(8,128)(2,1)S(1)}, u32[]{:S(2)}, u32[]{:S(2)}) async-start(bf16[8,4,32,128]{3,2,1,0:T(8,128)(2,1)} %get-tuple-element.37), calls=%async_computation | async-start | bytes 524288 | tf_op jit(solution)/shard_map/all_to_all | solution.py:284
  21.5 2.0 %copy-done = s32[56,128,128]{2,1,0:T(8,128)S(1)} copy-done((s32[56,128,128]{2,1,0:T(8,128)S(1)}, s32[56,128,128]{2,1,0:T(8,128)}, u32[]{:S(2)}) %copy-start) | copy-done | bytes 3670040
  24.8 1.8 shard_map.122
  26.9 4.8 %all-to-all-start.1 = ((bf16[8,4,32,128]{3,2,1,0:T(8,128)(2,1)}), bf16[8,4,32,128]{3,2,1,0:T(8,128)(2,1)S(1)}, u32[]{:S(2)}, u32[]{:S(2)}) async-start(bf16[8,4,32,128]{3,2,1,0:T(8,128)(2,1)} %get-tuple-element.44), calls=%async_computation.1 | async-start | bytes 524288 | tf_op jit(solution)/shard_map/all_to_all | solution.py:284
  31.8 4.7 %collective-permute-start = (bf16[4,2,2,32,128]{4,3,2,1,0:T(8,128)(2,1)S(1)}, bf16[4,2,2,32,128]{4,3,2,1,0:T(8,128)(2,1)S(1)}, u32[]{:S(2)}, u32[]{:S(2)}) collective-permute-start(bf16[4,2,2,32,128]{4,3,2,1,0:T(8,128)(2,1)S(1)} %get-tuple-element.42), channel_id=1, source_target_pairs={{0,64},{1,65},{2,66},{3,67},{4,68},{5,69},{6,70},{7,71},{8,72},{9,... | collective-permute-start | bytes 393224 | tf_op jit(solution)/shard_map/ppermute | solution.py:315
  36.5 7.0 %collective-permute-start.1 = (bf16[4,2,2,32,128]{4,3,2,1,0:T(8,128)(2,1)S(1)}, bf16[4,2,2,32,128]{4,3,2,1,0:T(8,128)(2,1)S(1)}, u32[]{:S(2)}, u32[]{:S(2)}) collective-permute-start(bf16[4,2,2,32,128]{4,3,2,1,0:T(8,128)(2,1)S(1)} %get-tuple-element.43), channel_id=1, source_target_pairs={{0,65},{1,64},{2,67},{3,66},{4,69},{5,68},{6,71},{7,70},{8,73},{9,... | collective-permute-start | bytes 393224 | tf_op jit(solution)/shard_map/ppermute | solution.py:315
  43.5 1.3 shard_map.123
  44.9 3.2 %collective-permute-start.2 = (bf16[4,2,32,128]{3,2,1,0:T(8,128)(2,1)S(1)}, bf16[4,2,32,128]{3,2,1,0:T(8,128)(2,1)S(1)}, u32[]{:S(2)}, u32[]{:S(2)}) collective-permute-start(bf16[4,2,32,128]{3,2,1,0:T(8,128)(2,1)S(1)} %get-tuple-element.48), channel_id=1, source_target_pairs={{0,64},{1,65},{2,66},{3,67},{4,68},{5,69},{6,70},{7,71},{8,72},{9,... | collective-permute-start | bytes 196616 | tf_op jit(solution)/shard_map/ppermute | solution.py:315
  48.1 6.6 %collective-permute-start.3 = (bf16[4,2,32,128]{3,2,1,0:T(8,128)(2,1)S(1)}, bf16[4,2,32,128]{3,2,1,0:T(8,128)(2,1)S(1)}, u32[]{:S(2)}, u32[]{:S(2)}) collective-permute-start(bf16[4,2,32,128]{3,2,1,0:T(8,128)(2,1)S(1)} %get-tuple-element.49), channel_id=1, source_target_pairs={{0,65},{1,64},{2,67},{3,66},{4,69},{5,68},{6,71},{7,70},{8,73},{9,... | collective-permute-start | bytes 196616 | tf_op jit(solution)/shard_map/ppermute | solution.py:315
  54.7 1.2 collective-permute-done.1.xc_minus_ref
  55.9 6.2 %collective-permute-done.2.agg_plus_ref = bf16[4,2,32,128]{3,2,1,0:T(8,128)(2,1)S(1)} collective-permute-done((bf16[4,2,32,128]{3,2,1,0:T(8,128)(2,1)S(1)}, bf16[4,2,32,128]{3,2,1,0:T(8,128)(2,1)S(1)}, u32[]{:S(2)}, u32[]{:S(2)}) %collective-permute-start.2) | collective-permute-done | bytes 65568 | tf_op jit(solution)/shard_map/ppermute | solution.py:315
  63.7 4.8 %all-to-all-start.2 = ((bf16[4,3,2,2,32,128]{5,4,3,2,1,0:T(8,128)(2,1)}), bf16[4,3,2,2,32,128]{5,4,3,2,1,0:T(8,128)(2,1)S(1)}, u32[]{:S(2)}, u32[]{:S(2)}) async-start(bf16[4,3,2,2,32,128]{5,4,3,2,1,0:T(8,128)(2,1)} %shard_map.124), calls=%async_computation.2 | async-start | bytes 786432 | tf_op jit(solution)/shard_map/all_to_all | solution.py:298
  68.9 4.9 %all-to-all-done.2.in_ref = bf16[4,3,2,2,32,128]{5,4,3,2,1,0:T(8,128)(2,1)S(1)} async-done(((bf16[4,3,2,2,32,128]{5,4,3,2,1,0:T(8,128)(2,1)}), bf16[4,3,2,2,32,128]{5,4,3,2,1,0:T(8,128)(2,1)S(1)}, u32[]{:S(2)}, u32[]{:S(2)}) %all-to-all-start.2) | async-done | bytes 393248 | tf_op jit(solution)/shard_map/all_to_all | solution.py:298
  75.8 8.7 %all-to-all-start.3 = ((bf16[32,16,384]{2,1,0:T(8,128)(2,1)}), bf16[32,16,384]{2,1,0:T(8,128)(2,1)S(1)}, u32[]{:S(2)}, u32[]{:S(2)}) async-start(bf16[32,16,384]{2,1,0:T(8,128)(2,1)} %shard_map.127), calls=%async_computation.3 | async-start | bytes 786432 | tf_op jit(solution)/shard_map/all_to_all | solution.py:420
  84.5 5.8 %collective-permute-start.4 = (bf16[4,2,2,32,128]{4,3,2,1,0:T(8,128)(2,1)S(1)}, bf16[4,2,2,32,128]{4,3,2,1,0:T(8,128)(2,1)S(1)}, u32[]{:S(2)}, u32[]{:S(2)}) collective-permute-start(bf16[4,2,2,32,128]{4,3,2,1,0:T(8,128)(2,1)S(1)} %get-tuple-element.50), channel_id=1, source_target_pairs={{0,64},{1,65},{2,66},{3,67},{4,68},{5,69},{6,70},{7,71},{8,72},{9,... | collective-permute-start | bytes 393224 | tf_op jit(solution)/shard_map/ppermute | solution.py:315
  90.3 4.0 %collective-permute-start.5 = (bf16[4,2,2,32,128]{4,3,2,1,0:T(8,128)(2,1)S(1)}, bf16[4,2,2,32,128]{4,3,2,1,0:T(8,128)(2,1)S(1)}, u32[]{:S(2)}, u32[]{:S(2)}) collective-permute-start(bf16[4,2,2,32,128]{4,3,2,1,0:T(8,128)(2,1)S(1)} %get-tuple-element.51), channel_id=1, source_target_pairs={{0,65},{1,64},{2,67},{3,66},{4,69},{5,68},{6,71},{7,70},{8,73},{9,... | collective-permute-start | bytes 393224 | tf_op jit(solution)/shard_map/ppermute | solution.py:315
  94.2 4.1 %collective-permute-done.4.plus_ref = bf16[4,2,2,32,128]{4,3,2,1,0:T(8,128)(2,1)S(1)} collective-permute-done((bf16[4,2,2,32,128]{4,3,2,1,0:T(8,128)(2,1)S(1)}, bf16[4,2,2,32,128]{4,3,2,1,0:T(8,128)(2,1)S(1)}, u32[]{:S(2)}, u32[]{:S(2)}) %collective-permute-start.4) | collective-permute-done | bytes 131104 | tf_op jit(solution)/shard_map/ppermute | solution.py:315
  98.3 8.5 %collective-permute-done.5.minus_ref = bf16[4,2,2,32,128]{4,3,2,1,0:T(8,128)(2,1)S(1)} collective-permute-done((bf16[4,2,2,32,128]{4,3,2,1,0:T(8,128)(2,1)S(1)}, bf16[4,2,2,32,128]{4,3,2,1,0:T(8,128)(2,1)S(1)}, u32[]{:S(2)}, u32[]{:S(2)}) %collective-permute-start.5) | collective-permute-done | bytes 131104 | tf_op jit(solution)/shard_map/ppermute | solution.py:315
  106.8 9.4 %all_to_all.40.home_ref = bf16[4,2,2,2,32,128]{5,4,3,2,1,0:T(8,128)(2,1)S(1)} all-to-all(bf16[4,2,2,2,32,128]{5,4,3,2,1,0:T(8,128)(2,1)S(1)} %shard_map.126), channel_id=1, replica_groups={{0,2,4,6},{1,3,5,7},{8,10,12,14},{9,11,13,15},{16,18,20,22},{17,19,21,2..., dimensions={0} | all-to-all | bytes 524288 | tf_op jit(solution)/shard_map/all_to_all | solution.py:298
  116.2 1.7 shard_map.128
  117.9 13.1 %all-to-all-start.5 = ((bf16[8,4,32,128]{3,2,1,0:T(8,128)(2,1)}), bf16[8,4,32,128]{3,2,1,0:T(8,128)(2,1)S(1)}, u32[]{:S(2)}, u32[]{:S(2)}) async-start(bf16[8,4,32,128]{3,2,1,0:T(8,128)(2,1)} %get-tuple-element.58), calls=%async_computation.5 | async-start | bytes 524288 | tf_op jit(solution)/shard_map/all_to_all | solution.py:284
  132.1 6.2 %all-to-all-done.5.b_ref = bf16[8,4,32,128]{3,2,1,0:T(8,128)(2,1)S(1)} async-done(((bf16[8,4,32,128]{3,2,1,0:T(8,128)(2,1)}), bf16[8,4,32,128]{3,2,1,0:T(8,128)(2,1)S(1)}, u32[]{:S(2)}, u32[]{:S(2)}) %all-to-all-start.5) | async-done | bytes 262176 | tf_op jit(solution)/shard_map/all_to_all | solution.py:284
  139.0 7.5 %all-to-all-start.6 = ((bf16[16,8,384]{2,1,0:T(8,128)(2,1)}), bf16[16,8,384]{2,1,0:T(8,128)(2,1)S(1)}, u32[]{:S(2)}, u32[]{:S(2)}) async-start(bf16[16,8,384]{2,1,0:T(8,128)(2,1)} %bitcast.6), calls=%async_computation.6 | async-start | bytes 196608 | tf_op jit(solution)/shard_map/all_to_all | solution.py:438
  148.5 6.1 %collective-permute-start.6 = (bf16[4,32,128]{2,1,0:T(8,128)(2,1)S(1)}, bf16[4,32,128]{2,1,0:T(8,128)(2,1)S(1)}, u32[]{:S(2)}, u32[]{:S(2)}) collective-permute-start(bf16[4,32,128]{2,1,0:T(8,128)(2,1)S(1)} %get-tuple-element.60), channel_id=1, source_target_pairs={{0,8},{8,0},{16,24},{24,16},{32,40},{40,32},{48,56},{56,48},{64,72... | collective-permute-start | bytes 98312 | tf_op jit(solution)/shard_map/ppermute | solution.py:293
  154.6 7.2 %collective-permute-start.7 = (bf16[4,32,128]{2,1,0:T(8,128)(2,1)S(1)}, bf16[4,32,128]{2,1,0:T(8,128)(2,1)S(1)}, u32[]{:S(2)}, u32[]{:S(2)}) collective-permute-start(bf16[4,32,128]{2,1,0:T(8,128)(2,1)S(1)} %get-tuple-element.61), channel_id=1, source_target_pairs={{0,16},{8,24},{16,0},{24,8},{32,48},{40,56},{48,32},{56,40},{64,80... | collective-permute-start | bytes 98312 | tf_op jit(solution)/shard_map/ppermute | solution.py:293
  161.8 2.0 %collective-permute-start.8 = (bf16[4,32,128]{2,1,0:T(8,128)(2,1)S(1)}, bf16[4,32,128]{2,1,0:T(8,128)(2,1)S(1)}, u32[]{:S(2)}, u32[]{:S(2)}) collective-permute-start(bf16[4,32,128]{2,1,0:T(8,128)(2,1)S(1)} %get-tuple-element.62), channel_id=1, source_target_pairs={{0,24},{8,16},{16,8},{24,0},{32,56},{40,48},{48,40},{56,32},{64,88... | collective-permute-start | bytes 98312 | tf_op jit(solution)/shard_map/ppermute | solution.py:293
  163.9 3.4 %collective-permute-start.9 = (bf16[4,32,128]{2,1,0:T(8,128)(2,1)S(1)}, bf16[4,32,128]{2,1,0:T(8,128)(2,1)S(1)}, u32[]{:S(2)}, u32[]{:S(2)}) collective-permute-start(bf16[4,32,128]{2,1,0:T(8,128)(2,1)S(1)} %get-tuple-element.63), channel_id=1, source_target_pairs={{0,32},{8,40},{16,48},{24,56},{32,0},{40,8},{48,16},{56,24},{64,96... | collective-permute-start | bytes 98312 | tf_op jit(solution)/shard_map/ppermute | solution.py:293
  168.2 2.4 %collective-permute-done.9.rest_3_ = bf16[4,32,128]{2,1,0:T(8,128)(2,1)S(1)} collective-permute-done((bf16[4,32,128]{2,1,0:T(8,128)(2,1)S(1)}, bf16[4,32,128]{2,1,0:T(8,128)(2,1)S(1)}, u32[]{:S(2)}, u32[]{:S(2)}) %collective-permute-start.9) | collective-permute-done | bytes 32800 | tf_op jit(solution)/shard_map/ppermute | solution.py:293
  170.6 1.6 shard_map.130
  172.8 5.1 %all-to-all-start.7 = ((bf16[8,8,256]{2,1,0:T(8,128)(2,1)}), bf16[8,8,256]{2,1,0:T(8,128)(2,1)S(1)}, u32[]{:S(2)}, u32[]{:S(2)}) async-start(bf16[8,8,256]{2,1,0:T(8,128)(2,1)} %broadcast_in_dim.8), calls=%async_computation.7 | async-start | bytes 65536 | tf_op jit(solution)/shard_map/all_to_all | solution.py:443
  178.5 4.8 %all-to-all-done.7 = bf16[8,8,256]{2,1,0:T(8,128)(2,1)S(1)} async-done(((bf16[8,8,256]{2,1,0:T(8,128)(2,1)}), bf16[8,8,256]{2,1,0:T(8,128)(2,1)S(1)}, u32[]{:S(2)}, u32[]{:S(2)}) %all-to-all-start.7) | async-done | bytes 32800 | tf_op jit(solution)/shard_map/all_to_all | solution.py:443
  (64 shorter events, 15.7 us)
Async XLA Ops:
  0.6 42.9 %copy-start.7 = (s32[56]{0:T(128)S(1)}, s32[56]{0:T(128)}, u32[]{:S(2)}) copy-start(s32[56]{0:T(128)} %dst_ref.7) | copy-start | bytes 676
  0.6 42.9 %copy-start.9 = (s32[56]{0:T(128)S(1)}, s32[56]{0:T(128)}, u32[]{:S(2)}) copy-start(s32[56]{0:T(128)} %src_ref.7) | copy-start | bytes 676
  1.4 0.9 copy-start.1
  3.9 23.0 %all-to-all-start = ((bf16[8,4,32,128]{3,2,1,0:T(8,128)(2,1)}), bf16[8,4,32,128]{3,2,1,0:T(8,128)(2,1)S(1)}, u32[]{:S(2)}, u32[]{:S(2)}) async-start(bf16[8,4,32,128]{3,2,1,0:T(8,128)(2,1)} %get-tuple-element.37), calls=%async_computation | async-start | bytes 524288 | tf_op jit(solution)/shard_map/all_to_all | solution.py:284
  19.6 0.9 copy-start.2
  20.5 0.9 copy-start.5
  21.5 2.0 %copy-start = (s32[56,128,128]{2,1,0:T(8,128)S(1)}, s32[56,128,128]{2,1,0:T(8,128)}, u32[]{:S(2)}) copy-start(s32[56,128,128]{2,1,0:T(8,128)} %cnt_ref.1) | copy-start | bytes 11010052
  23.5 0.7 copy-start.6
  24.2 0.7 copy-start.8
  24.8 43.7 %copy-start.4 = (bf16[256,256]{1,0:T(8,128)(2,1)S(1)}, bf16[256,256]{1,0:T(8,128)(2,1)}, u32[]{:S(2)}) copy-start(bf16[256,256]{1,0:T(8,128)(2,1)} %own_w_ref.1) | copy-start | bytes 393220
  24.8 43.8 %copy-start.3 = (bf16[256,256]{1,0:T(8,128)(2,1)S(1)}, bf16[256,256]{1,0:T(8,128)(2,1)}, u32[]{:S(2)}) copy-start(bf16[256,256]{1,0:T(8,128)(2,1)} %neigh_ref.1) | copy-start | bytes 393220
  24.8 43.9 %copy-start.11 = (f32[256]{0:T(256)S(1)}, f32[256]{0:T(256)}, u32[]{:S(2)}) copy-start(f32[256]{0:T(256)} %param.16) | copy-start | bytes 3076
  26.9 16.6 %all-to-all-start.1 = ((bf16[8,4,32,128]{3,2,1,0:T(8,128)(2,1)}), bf16[8,4,32,128]{3,2,1,0:T(8,128)(2,1)S(1)}, u32[]{:S(2)}, u32[]{:S(2)}) async-start(bf16[8,4,32,128]{3,2,1,0:T(8,128)(2,1)} %get-tuple-element.44), calls=%async_computation.1 | async-start | bytes 524288 | tf_op jit(solution)/shard_map/all_to_all | solution.py:284
  31.8 22.9 %collective-permute-start = (bf16[4,2,2,32,128]{4,3,2,1,0:T(8,128)(2,1)S(1)}, bf16[4,2,2,32,128]{4,3,2,1,0:T(8,128)(2,1)S(1)}, u32[]{:S(2)}, u32[]{:S(2)}) collective-permute-start(bf16[4,2,2,32,128]{4,3,2,1,0:T(8,128)(2,1)S(1)} %get-tuple-element.42), channel_id=1, source_target_pairs={{0,64},{1,65},{2,66},{3,67},{4,68},{5,69},{6,70},{7,71},{8,72},{9,... | collective-permute-start | bytes 393224 | tf_op jit(solution)/shard_map/ppermute | solution.py:315
  36.5 19.4 %collective-permute-start.1 = (bf16[4,2,2,32,128]{4,3,2,1,0:T(8,128)(2,1)S(1)}, bf16[4,2,2,32,128]{4,3,2,1,0:T(8,128)(2,1)S(1)}, u32[]{:S(2)}, u32[]{:S(2)}) collective-permute-start(bf16[4,2,2,32,128]{4,3,2,1,0:T(8,128)(2,1)S(1)} %get-tuple-element.43), channel_id=1, source_target_pairs={{0,65},{1,64},{2,67},{3,66},{4,69},{5,68},{6,71},{7,70},{8,73},{9,... | collective-permute-start | bytes 393224 | tf_op jit(solution)/shard_map/ppermute | solution.py:315
  44.9 17.1 %collective-permute-start.2 = (bf16[4,2,32,128]{3,2,1,0:T(8,128)(2,1)S(1)}, bf16[4,2,32,128]{3,2,1,0:T(8,128)(2,1)S(1)}, u32[]{:S(2)}, u32[]{:S(2)}) collective-permute-start(bf16[4,2,32,128]{3,2,1,0:T(8,128)(2,1)S(1)} %get-tuple-element.48), channel_id=1, source_target_pairs={{0,64},{1,65},{2,66},{3,67},{4,68},{5,69},{6,70},{7,71},{8,72},{9,... | collective-permute-start | bytes 196616 | tf_op jit(solution)/shard_map/ppermute | solution.py:315
  48.1 14.9 %collective-permute-start.3 = (bf16[4,2,32,128]{3,2,1,0:T(8,128)(2,1)S(1)}, bf16[4,2,32,128]{3,2,1,0:T(8,128)(2,1)S(1)}, u32[]{:S(2)}, u32[]{:S(2)}) collective-permute-start(bf16[4,2,32,128]{3,2,1,0:T(8,128)(2,1)S(1)} %get-tuple-element.49), channel_id=1, source_target_pairs={{0,65},{1,64},{2,67},{3,66},{4,69},{5,68},{6,71},{7,70},{8,73},{9,... | collective-permute-start | bytes 196616 | tf_op jit(solution)/shard_map/ppermute | solution.py:315
  63.7 10.1 %all-to-all-start.2 = ((bf16[4,3,2,2,32,128]{5,4,3,2,1,0:T(8,128)(2,1)}), bf16[4,3,2,2,32,128]{5,4,3,2,1,0:T(8,128)(2,1)S(1)}, u32[]{:S(2)}, u32[]{:S(2)}) async-start(bf16[4,3,2,2,32,128]{5,4,3,2,1,0:T(8,128)(2,1)} %shard_map.124), calls=%async_computation.2 | async-start | bytes 786432 | tf_op jit(solution)/shard_map/all_to_all | solution.py:298
  75.8 31.0 %all-to-all-start.3 = ((bf16[32,16,384]{2,1,0:T(8,128)(2,1)}), bf16[32,16,384]{2,1,0:T(8,128)(2,1)S(1)}, u32[]{:S(2)}, u32[]{:S(2)}) async-start(bf16[32,16,384]{2,1,0:T(8,128)(2,1)} %shard_map.127), calls=%async_computation.3 | async-start | bytes 786432 | tf_op jit(solution)/shard_map/all_to_all | solution.py:420
  84.5 13.8 %collective-permute-start.4 = (bf16[4,2,2,32,128]{4,3,2,1,0:T(8,128)(2,1)S(1)}, bf16[4,2,2,32,128]{4,3,2,1,0:T(8,128)(2,1)S(1)}, u32[]{:S(2)}, u32[]{:S(2)}) collective-permute-start(bf16[4,2,2,32,128]{4,3,2,1,0:T(8,128)(2,1)S(1)} %get-tuple-element.50), channel_id=1, source_target_pairs={{0,64},{1,65},{2,66},{3,67},{4,68},{5,69},{6,70},{7,71},{8,72},{9,... | collective-permute-start | bytes 393224 | tf_op jit(solution)/shard_map/ppermute | solution.py:315
  90.3 16.5 %collective-permute-start.5 = (bf16[4,2,2,32,128]{4,3,2,1,0:T(8,128)(2,1)S(1)}, bf16[4,2,2,32,128]{4,3,2,1,0:T(8,128)(2,1)S(1)}, u32[]{:S(2)}, u32[]{:S(2)}) collective-permute-start(bf16[4,2,2,32,128]{4,3,2,1,0:T(8,128)(2,1)S(1)} %get-tuple-element.51), channel_id=1, source_target_pairs={{0,65},{1,64},{2,67},{3,66},{4,69},{5,68},{6,71},{7,70},{8,73},{9,... | collective-permute-start | bytes 393224 | tf_op jit(solution)/shard_map/ppermute | solution.py:315
  106.8 9.4 %copy-start.10 = (bf16[32,16,384]{2,1,0:T(8,128)(2,1)}, bf16[32,16,384]{2,1,0:T(8,128)(2,1)S(1)}, u32[]{:S(2)}) copy-start(bf16[32,16,384]{2,1,0:T(8,128)(2,1)S(1)} %all-to-all-done.3) | copy-start | bytes 1179652
  117.9 20.4 %all-to-all-start.5 = ((bf16[8,4,32,128]{3,2,1,0:T(8,128)(2,1)}), bf16[8,4,32,128]{3,2,1,0:T(8,128)(2,1)S(1)}, u32[]{:S(2)}, u32[]{:S(2)}) async-start(bf16[8,4,32,128]{3,2,1,0:T(8,128)(2,1)} %get-tuple-element.58), calls=%async_computation.5 | async-start | bytes 524288 | tf_op jit(solution)/shard_map/all_to_all | solution.py:284
  139.0 33.2 %all-to-all-start.6 = ((bf16[16,8,384]{2,1,0:T(8,128)(2,1)}), bf16[16,8,384]{2,1,0:T(8,128)(2,1)S(1)}, u32[]{:S(2)}, u32[]{:S(2)}) async-start(bf16[16,8,384]{2,1,0:T(8,128)(2,1)} %bitcast.6), calls=%async_computation.6 | async-start | bytes 196608 | tf_op jit(solution)/shard_map/all_to_all | solution.py:438
  146.5 15.3 %collective-permute-start.10 = (bf16[4,32,128]{2,1,0:T(8,128)(2,1)S(1)}, bf16[4,32,128]{2,1,0:T(8,128)(2,1)S(1)}, u32[]{:S(2)}, u32[]{:S(2)}) collective-permute-start(bf16[4,32,128]{2,1,0:T(8,128)(2,1)S(1)} %get-tuple-element.64), channel_id=1, source_target_pairs={{8,32},{24,48},{32,8},{48,24},{72,96},{88,112},{96,72},{112,88},{1... | collective-permute-start | bytes 98312 | tf_op jit(solution)/shard_map/ppermute | solution.py:293
  147.1 16.7 %collective-permute-start.11 = (bf16[4,32,128]{2,1,0:T(8,128)(2,1)S(1)}, bf16[4,32,128]{2,1,0:T(8,128)(2,1)S(1)}, u32[]{:S(2)}, u32[]{:S(2)}) collective-permute-start(bf16[4,32,128]{2,1,0:T(8,128)(2,1)S(1)} %get-tuple-element.65), channel_id=1, source_target_pairs={{16,32},{24,40},{32,16},{40,24},{80,96},{88,104},{96,80},{104,88},... | collective-permute-start | bytes 98312 | tf_op jit(solution)/shard_map/ppermute | solution.py:293
  147.8 20.3 %collective-permute-start.12 = (bf16[4,32,128]{2,1,0:T(8,128)(2,1)S(1)}, bf16[4,32,128]{2,1,0:T(8,128)(2,1)S(1)}, u32[]{:S(2)}, u32[]{:S(2)}) collective-permute-start(bf16[4,32,128]{2,1,0:T(8,128)(2,1)S(1)} %get-tuple-element.66), channel_id=1, source_target_pairs={{16,40},{24,32},{32,24},{40,16},{80,104},{88,96},{96,88},{104,80},... | collective-permute-start | bytes 98312 | tf_op jit(solution)/shard_map/ppermute | solution.py:293
  148.5 19.6 %collective-permute-start.6 = (bf16[4,32,128]{2,1,0:T(8,128)(2,1)S(1)}, bf16[4,32,128]{2,1,0:T(8,128)(2,1)S(1)}, u32[]{:S(2)}, u32[]{:S(2)}) collective-permute-start(bf16[4,32,128]{2,1,0:T(8,128)(2,1)S(1)} %get-tuple-element.60), channel_id=1, source_target_pairs={{0,8},{8,0},{16,24},{24,16},{32,40},{40,32},{48,56},{56,48},{64,72... | collective-permute-start | bytes 98312 | tf_op jit(solution)/shard_map/ppermute | solution.py:293
  154.6 13.6 %collective-permute-start.7 = (bf16[4,32,128]{2,1,0:T(8,128)(2,1)S(1)}, bf16[4,32,128]{2,1,0:T(8,128)(2,1)S(1)}, u32[]{:S(2)}, u32[]{:S(2)}) collective-permute-start(bf16[4,32,128]{2,1,0:T(8,128)(2,1)S(1)} %get-tuple-element.61), channel_id=1, source_target_pairs={{0,16},{8,24},{16,0},{24,8},{32,48},{40,56},{48,32},{56,40},{64,80... | collective-permute-start | bytes 98312 | tf_op jit(solution)/shard_map/ppermute | solution.py:293
  161.8 6.3 %collective-permute-start.8 = (bf16[4,32,128]{2,1,0:T(8,128)(2,1)S(1)}, bf16[4,32,128]{2,1,0:T(8,128)(2,1)S(1)}, u32[]{:S(2)}, u32[]{:S(2)}) collective-permute-start(bf16[4,32,128]{2,1,0:T(8,128)(2,1)S(1)} %get-tuple-element.62), channel_id=1, source_target_pairs={{0,24},{8,16},{16,8},{24,0},{32,56},{40,48},{48,40},{56,32},{64,88... | collective-permute-start | bytes 98312 | tf_op jit(solution)/shard_map/ppermute | solution.py:293
  163.9 6.7 %collective-permute-start.9 = (bf16[4,32,128]{2,1,0:T(8,128)(2,1)S(1)}, bf16[4,32,128]{2,1,0:T(8,128)(2,1)S(1)}, u32[]{:S(2)}, u32[]{:S(2)}) collective-permute-start(bf16[4,32,128]{2,1,0:T(8,128)(2,1)S(1)} %get-tuple-element.63), channel_id=1, source_target_pairs={{0,32},{8,40},{16,48},{24,56},{32,0},{40,8},{48,16},{56,24},{64,96... | collective-permute-start | bytes 98312 | tf_op jit(solution)/shard_map/ppermute | solution.py:293
  172.8 10.5 %all-to-all-start.7 = ((bf16[8,8,256]{2,1,0:T(8,128)(2,1)}), bf16[8,8,256]{2,1,0:T(8,128)(2,1)S(1)}, u32[]{:S(2)}, u32[]{:S(2)}) async-start(bf16[8,8,256]{2,1,0:T(8,128)(2,1)} %broadcast_in_dim.8), calls=%async_computation.7 | async-start | bytes 65536 | tf_op jit(solution)/shard_map/all_to_all | solution.py:443

commit v7 on v5

--- a/solution.py
+++ b/solution.py
@@ -106,9 +106,35 @@
         out_ref[:, 2, side] = agg[...]
 
 
-def join_back_kernel(plus_ref, minus_ref, out_ref):
-    out_ref[:, 0] = plus_ref[...]
-    out_ref[:, 1] = minus_ref[...]
+def turn_kernel(plus_ref, minus_ref, *outs):
+    x = column()[0]
+    for step, out in enumerate(outs):
+        to = lax.rem(x + step, X)
+        out[0] = plus_ref[to]
+        out[1] = minus_ref[to]
+
+
+def fold_kernel(part_ref, out_ref):
+    full = part_ref.shape[2] - 128
+    total = part_ref[0].astype(F32)
+    for i in range(1, part_ref.shape[0]):
+        total += part_ref[i].astype(F32)
+    total = total.astype(BF16)
+    tail = jnp.concatenate([total[0:4, full:], total[8:12, full:]], axis=0)
+    for z in range(Z_HI * Z_LO):
+        first = z // Z_LO * 8
+        out_ref[z, :, :full] = total[first : first + 8, :full]
+        out_ref[z, :, full:] = tail
+
+
+def gather_kernel(part_ref, out_ref, tail_ref):
+    full = part_ref.shape[2] - 128
+    total = part_ref[0].astype(F32)
+    for i in range(1, part_ref.shape[0]):
+        total += part_ref[i].astype(F32)
+    tail_ref[...] = total[:, full:]
+    for i in range(out_ref.shape[0]):
+        out_ref[i] = total[:, :full].astype(BF16)
 
 
 def local_kernel(slots, chunk, x_ref, dst_ref, src_ref, cnt_ref, half_ref, acc_ref):
@@ -210,20 +236,25 @@
                 part_ref[piece, :, full:] = tail
 
 
+def home_pieces(refs, which):
+    x, z_hi = column()
+    per = refs[0].shape[2]
+    for step, ref in enumerate(refs):
+        source = lax.rem(x + X - step, X)
+        for side, h in ((0, 1 - z_hi), (1, z_hi)):
+            for p in range(per):
+                yield (source * Z_HI + h) * per + p, ref[side, which, p]
+
+
 def contribution_kernel(
-    slots, home_ref, deg_ref, dst_ref, src_ref, half_ref, a_ref, b_ref, scaled_ref, hold_ref
+    slots, zero_ref, one_ref, two_ref, three_ref, deg_ref, dst_ref, src_ref, half_ref, *outs
 ):
+    a_ref, b_ref, scaled_ref, hold_ref = outs
     place_a, place_b = places()
-    z_hi = column()[1]
     blocks = scaled_ref.shape[0]
     cap = a_ref.shape[1]
-    per = home_ref.shape[3]
-    for x in range(X):
-        for side, h in ((0, 1 - z_hi), (1, z_hi)):
-            for p in range(per):
-                block = (x * Z_HI + h) * per + p
-                value = home_ref[x, side, 0, p].astype(F32) / deg_ref[block, :1]
-                scaled_ref[block] = value.astype(BF16)
+    for block, piece in home_pieces((zero_ref, one_ref, two_ref, three_ref), 0):
+        scaled_ref[block] = (piece.astype(F32) / deg_ref[block][:1]).astype(BF16)
     for tile in range(slots):
         value = dot(scaled_ref[dst_ref[tile]], half_ref[tile])
         hold_ref[src_ref[tile] - blocks] = value.astype(BF16)
@@ -234,13 +265,11 @@
                 ref[peer, m] = hold_ref[kind * cap + m]
 
 
-def local_back_kernel(slots, scaled_ref, home_ref, dst_ref, src_ref, half_ref, acc_ref):
-    z_hi = column()[1]
-    per = home_ref.shape[3]
-    for x in range(X):
-        for side, h in ((0, 1 - z_hi), (1, z_hi)):
-            for p in range(per):
-                acc_ref[(x * Z_HI + h) * per + p] = home_ref[x, side, 1, p].astype(F32)
+def local_back_kernel(
+    slots, zero_ref, one_ref, two_ref, three_ref, scaled_ref, dst_ref, src_ref, half_ref, acc_ref
+):
+    for block, piece in home_pieces((zero_ref, one_ref, two_ref, three_ref), 1):
+        acc_ref[block] = piece.astype(F32)
     for tile in range(slots, half_ref.shape[0]):
         acc_ref[src_ref[tile]] += dot(scaled_ref[dst_ref[tile]], half_ref[tile])
 
@@ -398,37 +427,43 @@
     ]
     plane = [[(y * Z_LO + l) * CORE + c for y in range(Y) for c in range(CORE)] for l in range(Z_LO)]
     part = lax.all_to_all(part, both, 0, 0, axis_index_groups=flat, tiled=False)
-    home = call(join_back_kernel, shape(X, 2, 2, per_col), [VMEM] * 2)(plus, minus)
-    home, part = lax.optimization_barrier((home, part))
-    home = over_x(home)
+    (part,) = call(
+        fold_kernel, (jax.ShapeDtypeStruct((Z_HI * Z_LO, 8, full + 128), BF16),), [VMEM]
+    )(part)
+    part, plus, minus = lax.optimization_barrier((part, plus, minus))
+    part = lax.all_to_all(part, both, 0, 0, axis_index_groups=line, tiled=False)
+    home = call(turn_kernel, (shape(2, 2, per_col),) * X, [VMEM] * 2)(plus, minus)
+    route = lambda turn: [(c, (c + Z_HI * turn) % cols) for c in range(cols)]
+    home = [home[0]] + [lax.ppermute(home[turn], "col", route(turn)) for turn in range(1, X)]
     away_a, away_b, scaled = call(
         functools.partial(contribution_kernel, slots),
         (halo, halo, shape(blocks)),
-        [VMEM, VMEM, SMEM, SMEM, VMEM],
+        [VMEM] * 5 + [SMEM, SMEM, VMEM],
         [pltpu.VMEM((slots, dim, width), BF16)],
-    )(home, degree, tile_dst, tile_src, half)
+    )(*home, degree, tile_dst, tile_src, half)
+    away_b, part = lax.optimization_barrier((away_b, part))
     back_b = swap(away_b, GROUP // 2)
     away_a, back_b = lax.optimization_barrier((away_a, back_b))
     back_a = swap(away_a, 0)
-    part = jnp.sum(part.astype(F32), axis=0)
-    tail = jnp.concatenate([part[0:4, full:], part[8:12, full:]], axis=0)
-    ends = [jnp.concatenate([part[8 * h : 8 * h + 8, :full], tail], axis=1) for h in range(Z_HI)]
-    part = jnp.broadcast_to(jnp.stack(ends)[:, None], (Z_HI, Z_LO, 8, full + 128))
-    part = part.reshape(Z_HI * Z_LO, 8, full + 128).astype(BF16)
+    part, tail = call(
+        gather_kernel,
+        (
+            jax.ShapeDtypeStruct((Y * CORE, 8, full), BF16),
+            jax.ShapeDtypeStruct((8, 128), F32),
+        ),
+        [VMEM],
+    )(part)
+    grad_bias = jnp.concatenate([tail[0], tail[4]])
+    grad_bias = lax.dynamic_slice_in_dim(grad_bias, lax.axis_index("col") * dim, dim, 0)
     part, back_a = lax.optimization_barrier((part, back_a))
-    part = lax.all_to_all(part, both, 0, 0, axis_index_groups=line, tiled=False)
-    part = jnp.sum(part.astype(F32), axis=0)
-    grad_bias = jnp.concatenate([part[0, full:], part[4, full:]])
-    grad_bias = lax.dynamic_slice_in_dim(grad_bias, lax.axis_index("col") * dim, dim, 0)
-    part = jnp.broadcast_to(part[None, :, :full].astype(BF16), (Y * CORE, 8, full))
     part = lax.all_to_all(part, "blk", 0, 0, axis_index_groups=plane, tiled=False)
     part = part.astype(F32).reshape(2, dim, full)
     grad_self, grad_neigh = part[0], part[1]
     acc = call(
         functools.partial(local_back_kernel, slots),
         jax.ShapeDtypeStruct((blocks, dim, width), F32),
-        [VMEM, VMEM, SMEM, SMEM, VMEM],
-    )(scaled, home, tile_dst, tile_src, half)
+        [VMEM] * 5 + [SMEM, SMEM, VMEM],
+    )(*home, scaled, tile_dst, tile_src, half)
     grad_feats = call(
         finish_kernel,
         jax.ShapeDtypeStruct((dim, nodes), BF16),

time: 187 us -> 179 us (0.957)
  starting transfers between devices: 80.9 us -> 92.3 us
  blocking collectives: 29 us -> 19.7 us
  waiting for transfers between devices: 51.4 us -> 42.4 us
    all_to_all x1, waiting for transfers between devices: 10.9 us -> 0.01 us  [per_device(): part = lax.all_to_all(part, both, 0, 0, axis_index_groups=line, tiled=False)]
    all_to_all x1 -> x0, blocking collectives: 9.38 us -> none  [over_x(): lax.all_to_all(rows, 'col', 0, 0, axis_index_groups=groups, tiled=False)]
    ppermute x0 -> x3, starting transfers between devices: none -> 8.66 us  [per_device(): lax.ppermute(home[turn], 'col', route(turn))]
    ppermute x0 -> x3, waiting for transfers between devices: none -> 5.43 us  [per_device(): lax.ppermute(home[turn], 'col', route(turn))]
    all_to_all x1, starting transfers between devices: 5.61 us -> 9.16 us  [per_device(): part = lax.all_to_all(part, both, 0, 0, axis_index_groups=line, tiled=False)]
  transfers between devices with their start and end apart: 13 -> 16, of which waited for: 10 -> 11; matrix products, arithmetic and copies ran while one was open for 1% -> 1% of each run, Pallas kernels for 3% -> 5%
where the time goes in v7:
time: 179 us; the launch traced here: 177 us
  starting transfers between devices  92.3 us (52%)
  waiting for transfers between devices  42.4 us (24%)
  blocking collectives  19.7 us (11%)
  Pallas kernels  12.9 us (7%)
  local copies, waits for them, and re-layouts  8.4 us (5%)
    ppermute x6, starting transfers between devices, along_z(): return lax.ppermute(rows, ('blk', 'col'), sorted(route))  31.2 us
    all_to_all x3, starting transfers between devices, swap(): lax.all_to_all(rows, 'blk', 0, 0, axis_index_groups=groups, tiled=False)  25.6 us
    ppermute x6, waiting for transfers between devices, along_z(): return lax.ppermute(rows, ('blk', 'col'), sorted(route))  20.1 us
    all_to_all x1, blocking collectives, swap(): lax.all_to_all(rows, 'blk', 0, 0, axis_index_groups=groups, tiled=False)  19.7 us
    all_to_all x1, starting transfers between devices, per_device(): part = lax.all_to_all(part, both, 0, 0, axis_index_groups=line, tiled=False)  9.16 us
    ppermute x3, starting transfers between devices, per_device(): lax.ppermute(home[turn], 'col', route(turn))  8.66 us
    all_to_all x1, starting transfers between devices, per_device(): part = lax.all_to_all(part, both, 0, 0, axis_index_groups=flat, tiled=False)  8.66 us
    all_to_all x3, waiting for transfers between devices, swap(): lax.all_to_all(rows, 'blk', 0, 0, axis_index_groups=groups, tiled=False)  8.52 us
  transfers between devices with their start and end apart: 16, of which 11 were waited for; matrix products, arithmetic and copies ran while one was open for 1% of the time, Pallas kernels for 5%

profile of v7, /device:TPU:6, one launch (start us, length us, event | category | flops | bytes accessed | tf_op | source)
XLA Modules:
  0.0 176.7 jit_solution(9154608405146393489)
XLA Ops:
  2.3 1.6 shard_map.120
  3.9 15.7 %all-to-all-start = ((bf16[8,4,32,128]{3,2,1,0:T(8,128)(2,1)}), bf16[8,4,32,128]{3,2,1,0:T(8,128)(2,1)S(1)}, u32[]{:S(2)}, u32[]{:S(2)}) async-start(bf16[8,4,32,128]{3,2,1,0:T(8,128)(2,1)} %get-tuple-element.42), calls=%async_computation | async-start | bytes 524288 | tf_op jit(solution)/shard_map/all_to_all | solution.py:302
  21.5 2.0 %copy-done = s32[56,128,128]{2,1,0:T(8,128)S(1)} copy-done((s32[56,128,128]{2,1,0:T(8,128)S(1)}, s32[56,128,128]{2,1,0:T(8,128)}, u32[]{:S(2)}) %copy-start) | copy-done | bytes 3670040
  24.8 1.8 %shard_map.122 = (bf16[56,128,128]{2,1,0:T(8,128)(2,1)S(1)}, f32[16,40,128]{2,1,0:T(8,128)S(1)}) custom-call(bf16[32,2048]{1,0:T(8,128)(2,1)S(1)} %copy-done.2, s32[56]{0:T(128)S(1)} %copy-done.6, s32[56]{0:T(128)S(1)} %copy-done.8, s32[56,128,128]{2,1,0:T(8,128)S(1)} %copy-done), custom_call_target="tpu_custom_call" | custom-call | flops 60000000 | bytes 6000000 | tf_op jit(solution)/shard_map/pallas_call | solution.py:352
  26.9 4.8 %all-to-all-start.1 = ((bf16[8,4,32,128]{3,2,1,0:T(8,128)(2,1)}), bf16[8,4,32,128]{3,2,1,0:T(8,128)(2,1)S(1)}, u32[]{:S(2)}, u32[]{:S(2)}) async-start(bf16[8,4,32,128]{3,2,1,0:T(8,128)(2,1)} %get-tuple-element.49), calls=%async_computation.1 | async-start | bytes 524288 | tf_op jit(solution)/shard_map/all_to_all | solution.py:302
  31.7 4.7 %collective-permute-start = (bf16[4,2,2,32,128]{4,3,2,1,0:T(8,128)(2,1)S(1)}, bf16[4,2,2,32,128]{4,3,2,1,0:T(8,128)(2,1)S(1)}, u32[]{:S(2)}, u32[]{:S(2)}) collective-permute-start(bf16[4,2,2,32,128]{4,3,2,1,0:T(8,128)(2,1)S(1)} %get-tuple-element.47), channel_id=1, source_target_pairs={{0,64},{1,65},{2,66},{3,67},{4,68},{5,69},{6,70},{7,71},{8,72},{9,... | collective-permute-start | bytes 393224 | tf_op jit(solution)/shard_map/ppermute | solution.py:324
  36.5 7.0 %collective-permute-start.1 = (bf16[4,2,2,32,128]{4,3,2,1,0:T(8,128)(2,1)S(1)}, bf16[4,2,2,32,128]{4,3,2,1,0:T(8,128)(2,1)S(1)}, u32[]{:S(2)}, u32[]{:S(2)}) collective-permute-start(bf16[4,2,2,32,128]{4,3,2,1,0:T(8,128)(2,1)S(1)} %get-tuple-element.48), channel_id=1, source_target_pairs={{0,65},{1,64},{2,67},{3,66},{4,69},{5,68},{6,71},{7,70},{8,73},{9,... | collective-permute-start | bytes 393224 | tf_op jit(solution)/shard_map/ppermute | solution.py:324
  43.5 1.3 shard_map.123
  44.9 3.2 %collective-permute-start.2 = (bf16[4,2,32,128]{3,2,1,0:T(8,128)(2,1)S(1)}, bf16[4,2,32,128]{3,2,1,0:T(8,128)(2,1)S(1)}, u32[]{:S(2)}, u32[]{:S(2)}) collective-permute-start(bf16[4,2,32,128]{3,2,1,0:T(8,128)(2,1)S(1)} %get-tuple-element.53), channel_id=1, source_target_pairs={{0,64},{1,65},{2,66},{3,67},{4,68},{5,69},{6,70},{7,71},{8,72},{9,... | collective-permute-start | bytes 196616 | tf_op jit(solution)/shard_map/ppermute | solution.py:324
  48.1 6.6 %collective-permute-start.3 = (bf16[4,2,32,128]{3,2,1,0:T(8,128)(2,1)S(1)}, bf16[4,2,32,128]{3,2,1,0:T(8,128)(2,1)S(1)}, u32[]{:S(2)}, u32[]{:S(2)}) collective-permute-start(bf16[4,2,32,128]{3,2,1,0:T(8,128)(2,1)S(1)} %get-tuple-element.54), channel_id=1, source_target_pairs={{0,65},{1,64},{2,67},{3,66},{4,69},{5,68},{6,71},{7,70},{8,73},{9,... | collective-permute-start | bytes 196616 | tf_op jit(solution)/shard_map/ppermute | solution.py:324
  54.6 1.2 collective-permute-done.1.xc_minus_ref
  55.8 6.2 %collective-permute-done.2.agg_plus_ref = bf16[4,2,32,128]{3,2,1,0:T(8,128)(2,1)S(1)} collective-permute-done((bf16[4,2,32,128]{3,2,1,0:T(8,128)(2,1)S(1)}, bf16[4,2,32,128]{3,2,1,0:T(8,128)(2,1)S(1)}, u32[]{:S(2)}, u32[]{:S(2)}) %collective-permute-start.2) | collective-permute-done | bytes 65568 | tf_op jit(solution)/shard_map/ppermute | solution.py:324
  63.7 4.8 %all-to-all-start.2 = ((bf16[4,3,2,2,32,128]{5,4,3,2,1,0:T(8,128)(2,1)}), bf16[4,3,2,2,32,128]{5,4,3,2,1,0:T(8,128)(2,1)S(1)}, u32[]{:S(2)}, u32[]{:S(2)}) async-start(bf16[4,3,2,2,32,128]{5,4,3,2,1,0:T(8,128)(2,1)} %shard_map.124), calls=%async_computation.2 | async-start | bytes 786432 | tf_op jit(solution)/shard_map/all_to_all | solution.py:307
  68.9 4.9 %all-to-all-done.2.in_ref = bf16[4,3,2,2,32,128]{5,4,3,2,1,0:T(8,128)(2,1)S(1)} async-done(((bf16[4,3,2,2,32,128]{5,4,3,2,1,0:T(8,128)(2,1)}), bf16[4,3,2,2,32,128]{5,4,3,2,1,0:T(8,128)(2,1)S(1)}, u32[]{:S(2)}, u32[]{:S(2)}) %all-to-all-start.2) | async-done | bytes 393248 | tf_op jit(solution)/shard_map/all_to_all | solution.py:307
  75.8 8.7 %all-to-all-start.3 = ((bf16[32,16,384]{2,1,0:T(8,128)(2,1)}), bf16[32,16,384]{2,1,0:T(8,128)(2,1)S(1)}, u32[]{:S(2)}, u32[]{:S(2)}) async-start(bf16[32,16,384]{2,1,0:T(8,128)(2,1)} %shard_map.126), calls=%async_computation.3 | async-start | bytes 786432 | tf_op jit(solution)/shard_map/all_to_all | solution.py:429
  84.4 5.8 %collective-permute-start.4 = (bf16[4,2,2,32,128]{4,3,2,1,0:T(8,128)(2,1)S(1)}, bf16[4,2,2,32,128]{4,3,2,1,0:T(8,128)(2,1)S(1)}, u32[]{:S(2)}, u32[]{:S(2)}) collective-permute-start(bf16[4,2,2,32,128]{4,3,2,1,0:T(8,128)(2,1)S(1)} %get-tuple-element.57), channel_id=1, source_target_pairs={{0,64},{1,65},{2,66},{3,67},{4,68},{5,69},{6,70},{7,71},{8,72},{9,... | collective-permute-start | bytes 393224 | tf_op jit(solution)/shard_map/ppermute | solution.py:324
  90.2 4.0 %collective-permute-start.5 = (bf16[4,2,2,32,128]{4,3,2,1,0:T(8,128)(2,1)S(1)}, bf16[4,2,2,32,128]{4,3,2,1,0:T(8,128)(2,1)S(1)}, u32[]{:S(2)}, u32[]{:S(2)}) collective-permute-start(bf16[4,2,2,32,128]{4,3,2,1,0:T(8,128)(2,1)S(1)} %get-tuple-element.58), channel_id=1, source_target_pairs={{0,65},{1,64},{2,67},{3,66},{4,69},{5,68},{6,71},{7,70},{8,73},{9,... | collective-permute-start | bytes 393224 | tf_op jit(solution)/shard_map/ppermute | solution.py:324
  94.9 3.3 %collective-permute-done.4.plus_ref = bf16[4,2,2,32,128]{4,3,2,1,0:T(8,128)(2,1)S(1)} collective-permute-done((bf16[4,2,2,32,128]{4,3,2,1,0:T(8,128)(2,1)S(1)}, bf16[4,2,2,32,128]{4,3,2,1,0:T(8,128)(2,1)S(1)}, u32[]{:S(2)}, u32[]{:S(2)}) %collective-permute-start.4) | collective-permute-done | bytes 131104 | tf_op jit(solution)/shard_map/ppermute | solution.py:324
  98.3 8.5 %collective-permute-done.5.minus_ref = bf16[4,2,2,32,128]{4,3,2,1,0:T(8,128)(2,1)S(1)} collective-permute-done((bf16[4,2,2,32,128]{4,3,2,1,0:T(8,128)(2,1)S(1)}, bf16[4,2,2,32,128]{4,3,2,1,0:T(8,128)(2,1)S(1)}, u32[]{:S(2)}, u32[]{:S(2)}) %collective-permute-start.5) | collective-permute-done | bytes 131104 | tf_op jit(solution)/shard_map/ppermute | solution.py:324
  106.7 9.2 %all-to-all-start.4 = ((bf16[16,8,384]{2,1,0:T(8,128)(2,1)}), bf16[16,8,384]{2,1,0:T(8,128)(2,1)S(1)}, u32[]{:S(2)}, u32[]{:S(2)}) async-start(bf16[16,8,384]{2,1,0:T(8,128)(2,1)} %shard_map.127), calls=%async_computation.4 | async-start | bytes 196608 | tf_op jit(solution)/shard_map/all_to_all | solution.py:434
  115.9 2.3 %collective-permute-start.6 = (bf16[2,2,2,32,128]{4,3,2,1,0:T(8,128)(2,1)S(1)}, bf16[2,2,2,32,128]{4,3,2,1,0:T(8,128)(2,1)S(1)}, u32[]{:S(2)}, u32[]{:S(2)}) collective-permute-start(bf16[2,2,2,32,128]{4,3,2,1,0:T(8,128)(2,1)S(1)} %get-tuple-element.62), channel_id=1, source_target_pairs={{0,2},{1,3},{2,4},{3,5},{4,6},{5,7},{6,0},{7,1},{8,10},{9,11},{10,... | collective-permute-start | bytes 196616 | tf_op jit(solution)/shard_map/ppermute | solution.py:437
  118.2 4.5 %collective-permute-start.7 = (bf16[2,2,2,32,128]{4,3,2,1,0:T(8,128)(2,1)S(1)}, bf16[2,2,2,32,128]{4,3,2,1,0:T(8,128)(2,1)S(1)}, u32[]{:S(2)}, u32[]{:S(2)}) collective-permute-start(bf16[2,2,2,32,128]{4,3,2,1,0:T(8,128)(2,1)S(1)} %get-tuple-element.63), channel_id=1, source_target_pairs={{0,4},{1,5},{2,6},{3,7},{4,0},{5,1},{6,2},{7,3},{8,12},{9,13},{10,... | collective-permute-start | bytes 196616 | tf_op jit(solution)/shard_map/ppermute | solution.py:437
  122.7 1.9 %collective-permute-start.8 = (bf16[2,2,2,32,128]{4,3,2,1,0:T(8,128)(2,1)S(1)}, bf16[2,2,2,32,128]{4,3,2,1,0:T(8,128)(2,1)S(1)}, u32[]{:S(2)}, u32[]{:S(2)}) collective-permute-start(bf16[2,2,2,32,128]{4,3,2,1,0:T(8,128)(2,1)S(1)} %get-tuple-element.64), channel_id=1, source_target_pairs={{0,6},{1,7},{2,0},{3,1},{4,2},{5,3},{6,4},{7,5},{8,14},{9,15},{10,... | collective-permute-start | bytes 196616 | tf_op jit(solution)/shard_map/ppermute | solution.py:437
  124.6 1.2 collective-permute-done.7.two_ref
  125.9 4.2 %collective-permute-done.8.three_ref = bf16[2,2,2,32,128]{4,3,2,1,0:T(8,128)(2,1)S(1)} collective-permute-done((bf16[2,2,2,32,128]{4,3,2,1,0:T(8,128)(2,1)S(1)}, bf16[2,2,2,32,128]{4,3,2,1,0:T(8,128)(2,1)S(1)}, u32[]{:S(2)}, u32[]{:S(2)}) %collective-permute-start.8) | collective-permute-done | bytes 65568 | tf_op jit(solution)/shard_map/ppermute | solution.py:437
  130.1 1.7 shard_map.129
  131.8 19.7 %all_to_all.40.b_ref = bf16[8,4,32,128]{3,2,1,0:T(8,128)(2,1)S(1)} all-to-all(bf16[8,4,32,128]{3,2,1,0:T(8,128)(2,1)S(1)} %get-tuple-element.72), channel_id=1, replica_groups={{32,40,48,56,64,72,80,88},{96,104,112,120,128,136,144,152},{160,168,176..., dimensions={0} | all-to-all | bytes 524288 | tf_op jit(solution)/shard_map/all_to_all | solution.py:302
  151.5 5.1 %all-to-all-start.6 = ((bf16[8,4,32,128]{3,2,1,0:T(8,128)(2,1)}), bf16[8,4,32,128]{3,2,1,0:T(8,128)(2,1)S(1)}, u32[]{:S(2)}, u32[]{:S(2)}) async-start(bf16[8,4,32,128]{3,2,1,0:T(8,128)(2,1)} %get-tuple-element.73), calls=%async_computation.6 | async-start | bytes 524288 | tf_op jit(solution)/shard_map/all_to_all | solution.py:302
  158.1 8.2 %all-to-all-done.6.a_ref = bf16[8,4,32,128]{3,2,1,0:T(8,128)(2,1)S(1)} async-done(((bf16[8,4,32,128]{3,2,1,0:T(8,128)(2,1)}), bf16[8,4,32,128]{3,2,1,0:T(8,128)(2,1)S(1)}, u32[]{:S(2)}, u32[]{:S(2)}) %all-to-all-start.6) | async-done | bytes 262176 | tf_op jit(solution)/shard_map/all_to_all | solution.py:302
  166.3 4.3 %all-to-all-start.7 = ((bf16[8,8,256]{2,1,0:T(8,128)(2,1)}), bf16[8,8,256]{2,1,0:T(8,128)(2,1)S(1)}, u32[]{:S(2)}, u32[]{:S(2)}) async-start(bf16[8,8,256]{2,1,0:T(8,128)(2,1)} %get-tuple-element.76), calls=%async_computation.7 | async-start | bytes 65536 | tf_op jit(solution)/shard_map/all_to_all | solution.py:459
  171.2 1.4 shard_map.132
  172.6 3.4 %all-to-all-done.7 = bf16[8,8,256]{2,1,0:T(8,128)(2,1)S(1)} async-done(((bf16[8,8,256]{2,1,0:T(8,128)(2,1)}), bf16[8,8,256]{2,1,0:T(8,128)(2,1)S(1)}, u32[]{:S(2)}, u32[]{:S(2)}) %all-to-all-start.7) | async-done | bytes 32800 | tf_op jit(solution)/shard_map/all_to_all | solution.py:459
  (46 shorter events, 12.7 us)
Async XLA Ops:
  0.6 42.9 %copy-start.7 = (s32[56]{0:T(128)S(1)}, s32[56]{0:T(128)}, u32[]{:S(2)}) copy-start(s32[56]{0:T(128)} %dst_ref.7) | copy-start | bytes 676
  0.6 42.9 %copy-start.9 = (s32[56]{0:T(128)S(1)}, s32[56]{0:T(128)}, u32[]{:S(2)}) copy-start(s32[56]{0:T(128)} %src_ref.7) | copy-start | bytes 676
  1.4 0.9 copy-start.1
  3.9 23.0 %all-to-all-start = ((bf16[8,4,32,128]{3,2,1,0:T(8,128)(2,1)}), bf16[8,4,32,128]{3,2,1,0:T(8,128)(2,1)S(1)}, u32[]{:S(2)}, u32[]{:S(2)}) async-start(bf16[8,4,32,128]{3,2,1,0:T(8,128)(2,1)} %get-tuple-element.42), calls=%async_computation | async-start | bytes 524288 | tf_op jit(solution)/shard_map/all_to_all | solution.py:302
  19.6 0.9 copy-start.2
  20.5 0.9 copy-start.5
  21.5 2.0 %copy-start = (s32[56,128,128]{2,1,0:T(8,128)S(1)}, s32[56,128,128]{2,1,0:T(8,128)}, u32[]{:S(2)}) copy-start(s32[56,128,128]{2,1,0:T(8,128)} %cnt_ref.1) | copy-start | bytes 11010052
  23.5 0.7 copy-start.6
  24.2 0.7 copy-start.8
  24.8 43.7 %copy-start.4 = (bf16[256,256]{1,0:T(8,128)(2,1)S(1)}, bf16[256,256]{1,0:T(8,128)(2,1)}, u32[]{:S(2)}) copy-start(bf16[256,256]{1,0:T(8,128)(2,1)} %own_w_ref.1) | copy-start | bytes 393220
  24.8 43.8 %copy-start.3 = (bf16[256,256]{1,0:T(8,128)(2,1)S(1)}, bf16[256,256]{1,0:T(8,128)(2,1)}, u32[]{:S(2)}) copy-start(bf16[256,256]{1,0:T(8,128)(2,1)} %neigh_ref.1) | copy-start | bytes 393220
  24.8 43.9 %copy-start.10 = (f32[256]{0:T(256)S(1)}, f32[256]{0:T(256)}, u32[]{:S(2)}) copy-start(f32[256]{0:T(256)} %param.16) | copy-start | bytes 3076
  26.9 16.6 %all-to-all-start.1 = ((bf16[8,4,32,128]{3,2,1,0:T(8,128)(2,1)}), bf16[8,4,32,128]{3,2,1,0:T(8,128)(2,1)S(1)}, u32[]{:S(2)}, u32[]{:S(2)}) async-start(bf16[8,4,32,128]{3,2,1,0:T(8,128)(2,1)} %get-tuple-element.49), calls=%async_computation.1 | async-start | bytes 524288 | tf_op jit(solution)/shard_map/all_to_all | solution.py:302
  31.7 22.9 %collective-permute-start = (bf16[4,2,2,32,128]{4,3,2,1,0:T(8,128)(2,1)S(1)}, bf16[4,2,2,32,128]{4,3,2,1,0:T(8,128)(2,1)S(1)}, u32[]{:S(2)}, u32[]{:S(2)}) collective-permute-start(bf16[4,2,2,32,128]{4,3,2,1,0:T(8,128)(2,1)S(1)} %get-tuple-element.47), channel_id=1, source_target_pairs={{0,64},{1,65},{2,66},{3,67},{4,68},{5,69},{6,70},{7,71},{8,72},{9,... | collective-permute-start | bytes 393224 | tf_op jit(solution)/shard_map/ppermute | solution.py:324
  36.5 19.4 %collective-permute-start.1 = (bf16[4,2,2,32,128]{4,3,2,1,0:T(8,128)(2,1)S(1)}, bf16[4,2,2,32,128]{4,3,2,1,0:T(8,128)(2,1)S(1)}, u32[]{:S(2)}, u32[]{:S(2)}) collective-permute-start(bf16[4,2,2,32,128]{4,3,2,1,0:T(8,128)(2,1)S(1)} %get-tuple-element.48), channel_id=1, source_target_pairs={{0,65},{1,64},{2,67},{3,66},{4,69},{5,68},{6,71},{7,70},{8,73},{9,... | collective-permute-start | bytes 393224 | tf_op jit(solution)/shard_map/ppermute | solution.py:324
  44.9 17.1 %collective-permute-start.2 = (bf16[4,2,32,128]{3,2,1,0:T(8,128)(2,1)S(1)}, bf16[4,2,32,128]{3,2,1,0:T(8,128)(2,1)S(1)}, u32[]{:S(2)}, u32[]{:S(2)}) collective-permute-start(bf16[4,2,32,128]{3,2,1,0:T(8,128)(2,1)S(1)} %get-tuple-element.53), channel_id=1, source_target_pairs={{0,64},{1,65},{2,66},{3,67},{4,68},{5,69},{6,70},{7,71},{8,72},{9,... | collective-permute-start | bytes 196616 | tf_op jit(solution)/shard_map/ppermute | solution.py:324
  48.1 14.9 %collective-permute-start.3 = (bf16[4,2,32,128]{3,2,1,0:T(8,128)(2,1)S(1)}, bf16[4,2,32,128]{3,2,1,0:T(8,128)(2,1)S(1)}, u32[]{:S(2)}, u32[]{:S(2)}) collective-permute-start(bf16[4,2,32,128]{3,2,1,0:T(8,128)(2,1)S(1)} %get-tuple-element.54), channel_id=1, source_target_pairs={{0,65},{1,64},{2,67},{3,66},{4,69},{5,68},{6,71},{7,70},{8,73},{9,... | collective-permute-start | bytes 196616 | tf_op jit(solution)/shard_map/ppermute | solution.py:324
  63.7 10.1 %all-to-all-start.2 = ((bf16[4,3,2,2,32,128]{5,4,3,2,1,0:T(8,128)(2,1)}), bf16[4,3,2,2,32,128]{5,4,3,2,1,0:T(8,128)(2,1)S(1)}, u32[]{:S(2)}, u32[]{:S(2)}) async-start(bf16[4,3,2,2,32,128]{5,4,3,2,1,0:T(8,128)(2,1)} %shard_map.124), calls=%async_computation.2 | async-start | bytes 786432 | tf_op jit(solution)/shard_map/all_to_all | solution.py:307
  75.8 18.4 %all-to-all-start.3 = ((bf16[32,16,384]{2,1,0:T(8,128)(2,1)}), bf16[32,16,384]{2,1,0:T(8,128)(2,1)S(1)}, u32[]{:S(2)}, u32[]{:S(2)}) async-start(bf16[32,16,384]{2,1,0:T(8,128)(2,1)} %shard_map.126), calls=%async_computation.3 | async-start | bytes 786432 | tf_op jit(solution)/shard_map/all_to_all | solution.py:429
  84.4 13.8 %collective-permute-start.4 = (bf16[4,2,2,32,128]{4,3,2,1,0:T(8,128)(2,1)S(1)}, bf16[4,2,2,32,128]{4,3,2,1,0:T(8,128)(2,1)S(1)}, u32[]{:S(2)}, u32[]{:S(2)}) collective-permute-start(bf16[4,2,2,32,128]{4,3,2,1,0:T(8,128)(2,1)S(1)} %get-tuple-element.57), channel_id=1, source_target_pairs={{0,64},{1,65},{2,66},{3,67},{4,68},{5,69},{6,70},{7,71},{8,72},{9,... | collective-permute-start | bytes 393224 | tf_op jit(solution)/shard_map/ppermute | solution.py:324
  90.2 16.5 %collective-permute-start.5 = (bf16[4,2,2,32,128]{4,3,2,1,0:T(8,128)(2,1)S(1)}, bf16[4,2,2,32,128]{4,3,2,1,0:T(8,128)(2,1)S(1)}, u32[]{:S(2)}, u32[]{:S(2)}) collective-permute-start(bf16[4,2,2,32,128]{4,3,2,1,0:T(8,128)(2,1)S(1)} %get-tuple-element.58), channel_id=1, source_target_pairs={{0,65},{1,64},{2,67},{3,66},{4,69},{5,68},{6,71},{7,70},{8,73},{9,... | collective-permute-start | bytes 393224 | tf_op jit(solution)/shard_map/ppermute | solution.py:324
  106.7 25.0 %all-to-all-start.4 = ((bf16[16,8,384]{2,1,0:T(8,128)(2,1)}), bf16[16,8,384]{2,1,0:T(8,128)(2,1)S(1)}, u32[]{:S(2)}, u32[]{:S(2)}) async-start(bf16[16,8,384]{2,1,0:T(8,128)(2,1)} %shard_map.127), calls=%async_computation.4 | async-start | bytes 196608 | tf_op jit(solution)/shard_map/all_to_all | solution.py:434
  115.9 8.7 %collective-permute-start.6 = (bf16[2,2,2,32,128]{4,3,2,1,0:T(8,128)(2,1)S(1)}, bf16[2,2,2,32,128]{4,3,2,1,0:T(8,128)(2,1)S(1)}, u32[]{:S(2)}, u32[]{:S(2)}) collective-permute-start(bf16[2,2,2,32,128]{4,3,2,1,0:T(8,128)(2,1)S(1)} %get-tuple-element.62), channel_id=1, source_target_pairs={{0,2},{1,3},{2,4},{3,5},{4,6},{5,7},{6,0},{7,1},{8,10},{9,11},{10,... | collective-permute-start | bytes 196616 | tf_op jit(solution)/shard_map/ppermute | solution.py:437
  118.2 7.7 %collective-permute-start.7 = (bf16[2,2,2,32,128]{4,3,2,1,0:T(8,128)(2,1)S(1)}, bf16[2,2,2,32,128]{4,3,2,1,0:T(8,128)(2,1)S(1)}, u32[]{:S(2)}, u32[]{:S(2)}) collective-permute-start(bf16[2,2,2,32,128]{4,3,2,1,0:T(8,128)(2,1)S(1)} %get-tuple-element.63), channel_id=1, source_target_pairs={{0,4},{1,5},{2,6},{3,7},{4,0},{5,1},{6,2},{7,3},{8,12},{9,13},{10,... | collective-permute-start | bytes 196616 | tf_op jit(solution)/shard_map/ppermute | solution.py:437
  122.7 7.4 %collective-permute-start.8 = (bf16[2,2,2,32,128]{4,3,2,1,0:T(8,128)(2,1)S(1)}, bf16[2,2,2,32,128]{4,3,2,1,0:T(8,128)(2,1)S(1)}, u32[]{:S(2)}, u32[]{:S(2)}) collective-permute-start(bf16[2,2,2,32,128]{4,3,2,1,0:T(8,128)(2,1)S(1)} %get-tuple-element.64), channel_id=1, source_target_pairs={{0,6},{1,7},{2,0},{3,1},{4,2},{5,3},{6,4},{7,5},{8,14},{9,15},{10,... | collective-permute-start | bytes 196616 | tf_op jit(solution)/shard_map/ppermute | solution.py:437
  151.5 14.8 %all-to-all-start.6 = ((bf16[8,4,32,128]{3,2,1,0:T(8,128)(2,1)}), bf16[8,4,32,128]{3,2,1,0:T(8,128)(2,1)S(1)}, u32[]{:S(2)}, u32[]{:S(2)}) async-start(bf16[8,4,32,128]{3,2,1,0:T(8,128)(2,1)} %get-tuple-element.73), calls=%async_computation.6 | async-start | bytes 524288 | tf_op jit(solution)/shard_map/all_to_all | solution.py:302
  166.3 9.7 %all-to-all-start.7 = ((bf16[8,8,256]{2,1,0:T(8,128)(2,1)}), bf16[8,8,256]{2,1,0:T(8,128)(2,1)S(1)}, u32[]{:S(2)}, u32[]{:S(2)}) async-start(bf16[8,8,256]{2,1,0:T(8,128)(2,1)} %get-tuple-element.76), calls=%async_computation.7 | async-start | bytes 65536 | tf_op jit(solution)/shard_map/all_to_all | solution.py:459

commit v8 on v7

--- a/solution.py
+++ b/solution.py
@@ -127,14 +127,29 @@
         out_ref[z, :, full:] = tail
 
 
-def gather_kernel(part_ref, out_ref, tail_ref):
+def total_kernel(part_ref, out_ref, tail_ref):
     full = part_ref.shape[2] - 128
     total = part_ref[0].astype(F32)
     for i in range(1, part_ref.shape[0]):
         total += part_ref[i].astype(F32)
+    out_ref[...] = total[:, :full]
     tail_ref[...] = total[:, full:]
-    for i in range(out_ref.shape[0]):
-        out_ref[i] = total[:, :full].astype(BF16)
+
+
+def pair_kernel(one_ref, two_ref, out_ref):
+    half = one_ref.shape[0]
+    out_ref[:half] = one_ref[...]
+    out_ref[half:] = two_ref[...]
+
+
+def order_kernel(near_ref, far_ref, self_ref, neigh_ref):
+    blk = lax.axis_index("blk")
+    mine = blk // (Z_LO * CORE) * CORE + lax.rem(blk, CORE)
+    for piece in range(Y * CORE):
+        offset = jnp.bitwise_xor(mine, piece)
+        rows = jnp.where(lax.rem(offset, 2) == 0, near_ref[offset // 2], far_ref[offset // 2])
+        out = self_ref if piece < 4 else neigh_ref
+        out[piece % 4 * 8 : piece % 4 * 8 + 8] = rows
 
 
 def local_kernel(slots, chunk, x_ref, dst_ref, src_ref, cnt_ref, half_ref, acc_ref):
@@ -300,6 +315,10 @@
         [(first + shift + i) % devices for i in range(GROUP)] for first in range(0, devices, GROUP)
     ]
     return lax.all_to_all(rows, "blk", 0, 0, axis_index_groups=groups, tiled=False)
+
+
+def across(rows, bit):
+    return lax.ppermute(rows, "blk", [(e, e ^ bit) for e in range(lax.axis_size("blk"))])
 
 
 def over_x(rows):
@@ -425,7 +444,6 @@
         for c in range(CORE)
         for x in range(X)
     ]
-    plane = [[(y * Z_LO + l) * CORE + c for y in range(Y) for c in range(CORE)] for l in range(Z_LO)]
     part = lax.all_to_all(part, both, 0, 0, axis_index_groups=flat, tiled=False)
     (part,) = call(
         fold_kernel, (jax.ShapeDtypeStruct((Z_HI * Z_LO, 8, full + 128), BF16),), [VMEM]
@@ -441,24 +459,26 @@
         [VMEM] * 5 + [SMEM, SMEM, VMEM],
         [pltpu.VMEM((slots, dim, width), BF16)],
     )(*home, degree, tile_dst, tile_src, half)
-    away_b, part = lax.optimization_barrier((away_b, part))
-    back_b = swap(away_b, GROUP // 2)
-    away_a, back_b = lax.optimization_barrier((away_a, back_b))
-    back_a = swap(away_a, 0)
-    part, tail = call(
-        gather_kernel,
-        (
-            jax.ShapeDtypeStruct((Y * CORE, 8, full), BF16),
-            jax.ShapeDtypeStruct((8, 128), F32),
-        ),
+    row = jax.ShapeDtypeStruct((1, 8, full), F32)
+    rows, tail = call(
+        lambda part_ref, out_ref, tail_ref: total_kernel(part_ref, out_ref.at[0], tail_ref),
+        (row, jax.ShapeDtypeStruct((8, 128), F32)),
         [VMEM],
     )(part)
     grad_bias = jnp.concatenate([tail[0], tail[4]])
     grad_bias = lax.dynamic_slice_in_dim(grad_bias, lax.axis_index("col") * dim, dim, 0)
-    part, back_a = lax.optimization_barrier((part, back_a))
-    part = lax.all_to_all(part, "blk", 0, 0, axis_index_groups=plane, tiled=False)
-    part = part.astype(F32).reshape(2, dim, full)
-    grad_self, grad_neigh = part[0], part[1]
+    away_b, rows = lax.optimization_barrier((away_b, rows))
+    back_b = swap(away_b, GROUP // 2)
+    pair = call(pair_kernel, jax.ShapeDtypeStruct((2, 8, full), F32), [VMEM] * 2)(
+        rows, across(rows, Z_LO * CORE)
+    )
+    away_a, back_b, pair = lax.optimization_barrier((away_a, back_b, pair))
+    back_a = swap(away_a, 0)
+    rows = call(pair_kernel, jax.ShapeDtypeStruct((4, 8, full), F32), [VMEM] * 2)(
+        pair, across(pair, 2 * Z_LO * CORE)
+    )
+    grad = jax.ShapeDtypeStruct((dim, full), F32)
+    grad_self, grad_neigh = call(order_kernel, (grad, grad), [VMEM] * 2)(rows, across(rows, 1))
     acc = call(
         functools.partial(local_back_kernel, slots),
         jax.ShapeDtypeStruct((blocks, dim, width), F32),

time: 179 us -> 173 us (0.966)
  blocking collectives: 19.7 us -> 0 us
  starting transfers between devices: 92.3 us -> 110 us
  waiting for transfers between devices: 42.4 us -> 39 us
    all_to_all x1 -> x0, blocking collectives: 19.7 us -> none  [swap(): lax.all_to_all(rows, 'blk', 0, 0, axis_index_groups=groups, tiled=False)]
    all_to_all x3 -> x4, starting transfers between devices: 25.6 us -> 38.7 us  [swap(): lax.all_to_all(rows, 'blk', 0, 0, axis_index_groups=groups, tiled=False)]
    ppermute x0 -> x3, starting transfers between devices: none -> 8.7 us  [across(): lax.ppermute(rows, 'blk', [(e, e ^ bit) for e in range(lax.axis_size('blk...]
    ppermute x0 -> x3, waiting for transfers between devices: none -> 6.42 us  [across(): lax.ppermute(rows, 'blk', [(e, e ^ bit) for e in range(lax.axis_size('blk...]
    all_to_all x3 -> x4, waiting for transfers between devices: 8.52 us -> 2.12 us  [swap(): lax.all_to_all(rows, 'blk', 0, 0, axis_index_groups=groups, tiled=False)]
    all_to_all x1 -> x0, starting transfers between devices: 4.26 us -> none  [per_device(): lax.all_to_all(part, 'blk', 0, 0, axis_index_groups=plane, tiled=False)]
    all_to_all x1 -> x0, waiting for transfers between devices: 3.41 us -> none  [per_device(): lax.all_to_all(part, 'blk', 0, 0, axis_index_groups=plane, tiled=False)]
  transfers between devices with their start and end apart: 16 -> 19, of which waited for: 11 -> 13; matrix products, arithmetic and copies ran while one was open for 1% -> 1% of each run, Pallas kernels for 5% -> 4%
where the time goes in v8:
time: 173 us; the launch traced here: 171 us
  starting transfers between devices  110 us (64%)
  waiting for transfers between devices  39 us (23%)
  Pallas kernels  13.1 us (8%)
  local copies, waits for them, and re-layouts  7.77 us (4%)
    all_to_all x4, starting transfers between devices, swap(): lax.all_to_all(rows, 'blk', 0, 0, axis_index_groups=groups, tiled=False)  38.7 us
    ppermute x6, starting transfers between devices, along_z(): return lax.ppermute(rows, ('blk', 'col'), sorted(route))  31.2 us
    ppermute x6, waiting for transfers between devices, along_z(): return lax.ppermute(rows, ('blk', 'col'), sorted(route))  20.1 us
    all_to_all x1, starting transfers between devices, per_device(): part = lax.all_to_all(part, both, 0, 0, axis_index_groups=line, tiled=False)  9.17 us
    ppermute x3, starting transfers between devices, across(): lax.ppermute(rows, 'blk', [(e, e ^ bit) for e in range(lax.axis_size('blk...  8.7 us
    ppermute x3, starting transfers between devices, per_device(): lax.ppermute(home[turn], 'col', route(turn))  8.66 us
    all_to_all x1, starting transfers between devices, per_device(): part = lax.all_to_all(part, both, 0, 0, axis_index_groups=flat, tiled=False)  8.65 us
    ppermute x3, waiting for transfers between devices, across(): lax.ppermute(rows, 'blk', [(e, e ^ bit) for e in range(lax.axis_size('blk...  6.42 us
  transfers between devices with their start and end apart: 19, of which 13 were waited for; matrix products, arithmetic and copies ran while one was open for 1% of the time, Pallas kernels for 4%

profile of v8, /device:TPU:6, one launch (start us, length us, event | category | flops | bytes accessed | tf_op | source)
XLA Modules:
  0.0 170.7 jit_solution(8503266633840800860)
XLA Ops:
  2.3 1.6 shard_map.120
  3.9 15.7 %all-to-all-start = ((bf16[8,4,32,128]{3,2,1,0:T(8,128)(2,1)}), bf16[8,4,32,128]{3,2,1,0:T(8,128)(2,1)S(1)}, u32[]{:S(2)}, u32[]{:S(2)}) async-start(bf16[8,4,32,128]{3,2,1,0:T(8,128)(2,1)} %get-tuple-element.43), calls=%async_computation | async-start | bytes 524288 | tf_op jit(solution)/shard_map/all_to_all | solution.py:317
  21.5 2.0 %copy-done = s32[56,128,128]{2,1,0:T(8,128)S(1)} copy-done((s32[56,128,128]{2,1,0:T(8,128)S(1)}, s32[56,128,128]{2,1,0:T(8,128)}, u32[]{:S(2)}) %copy-start) | copy-done | bytes 3670040
  24.8 1.8 %shard_map.122 = (bf16[56,128,128]{2,1,0:T(8,128)(2,1)S(1)}, f32[16,40,128]{2,1,0:T(8,128)S(1)}) custom-call(bf16[32,2048]{1,0:T(8,128)(2,1)S(1)} %copy-done.2, s32[56]{0:T(128)S(1)} %copy-done.6, s32[56]{0:T(128)S(1)} %copy-done.8, s32[56,128,128]{2,1,0:T(8,128)S(1)} %copy-done), custom_call_target="tpu_custom_call" | custom-call | flops 60000000 | bytes 6000000 | tf_op jit(solution)/shard_map/pallas_call | solution.py:371
  26.9 4.8 %all-to-all-start.1 = ((bf16[8,4,32,128]{3,2,1,0:T(8,128)(2,1)}), bf16[8,4,32,128]{3,2,1,0:T(8,128)(2,1)S(1)}, u32[]{:S(2)}, u32[]{:S(2)}) async-start(bf16[8,4,32,128]{3,2,1,0:T(8,128)(2,1)} %get-tuple-element.50), calls=%async_computation.1 | async-start | bytes 524288 | tf_op jit(solution)/shard_map/all_to_all | solution.py:317
  31.8 4.7 %collective-permute-start = (bf16[4,2,2,32,128]{4,3,2,1,0:T(8,128)(2,1)S(1)}, bf16[4,2,2,32,128]{4,3,2,1,0:T(8,128)(2,1)S(1)}, u32[]{:S(2)}, u32[]{:S(2)}) collective-permute-start(bf16[4,2,2,32,128]{4,3,2,1,0:T(8,128)(2,1)S(1)} %get-tuple-element.48), channel_id=1, source_target_pairs={{0,64},{1,65},{2,66},{3,67},{4,68},{5,69},{6,70},{7,71},{8,72},{9,... | collective-permute-start | bytes 393224 | tf_op jit(solution)/shard_map/ppermute | solution.py:343
  36.5 7.0 %collective-permute-start.1 = (bf16[4,2,2,32,128]{4,3,2,1,0:T(8,128)(2,1)S(1)}, bf16[4,2,2,32,128]{4,3,2,1,0:T(8,128)(2,1)S(1)}, u32[]{:S(2)}, u32[]{:S(2)}) collective-permute-start(bf16[4,2,2,32,128]{4,3,2,1,0:T(8,128)(2,1)S(1)} %get-tuple-element.49), channel_id=1, source_target_pairs={{0,65},{1,64},{2,67},{3,66},{4,69},{5,68},{6,71},{7,70},{8,73},{9,... | collective-permute-start | bytes 393224 | tf_op jit(solution)/shard_map/ppermute | solution.py:343
  44.9 3.2 %collective-permute-start.2 = (bf16[4,2,32,128]{3,2,1,0:T(8,128)(2,1)S(1)}, bf16[4,2,32,128]{3,2,1,0:T(8,128)(2,1)S(1)}, u32[]{:S(2)}, u32[]{:S(2)}) collective-permute-start(bf16[4,2,32,128]{3,2,1,0:T(8,128)(2,1)S(1)} %get-tuple-element.54), channel_id=1, source_target_pairs={{0,64},{1,65},{2,66},{3,67},{4,68},{5,69},{6,70},{7,71},{8,72},{9,... | collective-permute-start | bytes 196616 | tf_op jit(solution)/shard_map/ppermute | solution.py:343
  48.1 6.6 %collective-permute-start.3 = (bf16[4,2,32,128]{3,2,1,0:T(8,128)(2,1)S(1)}, bf16[4,2,32,128]{3,2,1,0:T(8,128)(2,1)S(1)}, u32[]{:S(2)}, u32[]{:S(2)}) collective-permute-start(bf16[4,2,32,128]{3,2,1,0:T(8,128)(2,1)S(1)} %get-tuple-element.55), channel_id=1, source_target_pairs={{0,65},{1,64},{2,67},{3,66},{4,69},{5,68},{6,71},{7,70},{8,73},{9,... | collective-permute-start | bytes 196616 | tf_op jit(solution)/shard_map/ppermute | solution.py:343
  55.9 6.2 %collective-permute-done.2.agg_plus_ref = bf16[4,2,32,128]{3,2,1,0:T(8,128)(2,1)S(1)} collective-permute-done((bf16[4,2,32,128]{3,2,1,0:T(8,128)(2,1)S(1)}, bf16[4,2,32,128]{3,2,1,0:T(8,128)(2,1)S(1)}, u32[]{:S(2)}, u32[]{:S(2)}) %collective-permute-start.2) | collective-permute-done | bytes 65568 | tf_op jit(solution)/shard_map/ppermute | solution.py:343
  63.7 4.8 %all-to-all-start.2 = ((bf16[4,3,2,2,32,128]{5,4,3,2,1,0:T(8,128)(2,1)}), bf16[4,3,2,2,32,128]{5,4,3,2,1,0:T(8,128)(2,1)S(1)}, u32[]{:S(2)}, u32[]{:S(2)}) async-start(bf16[4,3,2,2,32,128]{5,4,3,2,1,0:T(8,128)(2,1)} %shard_map.124), calls=%async_computation.2 | async-start | bytes 786432 | tf_op jit(solution)/shard_map/all_to_all | solution.py:326
  68.9 4.9 %all-to-all-done.2.in_ref = bf16[4,3,2,2,32,128]{5,4,3,2,1,0:T(8,128)(2,1)S(1)} async-done(((bf16[4,3,2,2,32,128]{5,4,3,2,1,0:T(8,128)(2,1)}), bf16[4,3,2,2,32,128]{5,4,3,2,1,0:T(8,128)(2,1)S(1)}, u32[]{:S(2)}, u32[]{:S(2)}) %all-to-all-start.2) | async-done | bytes 393248 | tf_op jit(solution)/shard_map/all_to_all | solution.py:326
  75.8 8.7 %all-to-all-start.3 = ((bf16[32,16,384]{2,1,0:T(8,128)(2,1)}), bf16[32,16,384]{2,1,0:T(8,128)(2,1)S(1)}, u32[]{:S(2)}, u32[]{:S(2)}) async-start(bf16[32,16,384]{2,1,0:T(8,128)(2,1)} %shard_map.126), calls=%async_computation.3 | async-start | bytes 786432 | tf_op jit(solution)/shard_map/all_to_all | solution.py:447
  84.5 5.8 %collective-permute-start.4 = (bf16[4,2,2,32,128]{4,3,2,1,0:T(8,128)(2,1)S(1)}, bf16[4,2,2,32,128]{4,3,2,1,0:T(8,128)(2,1)S(1)}, u32[]{:S(2)}, u32[]{:S(2)}) collective-permute-start(bf16[4,2,2,32,128]{4,3,2,1,0:T(8,128)(2,1)S(1)} %get-tuple-element.58), channel_id=1, source_target_pairs={{0,64},{1,65},{2,66},{3,67},{4,68},{5,69},{6,70},{7,71},{8,72},{9,... | collective-permute-start | bytes 393224 | tf_op jit(solution)/shard_map/ppermute | solution.py:343
  90.3 4.0 %collective-permute-start.5 = (bf16[4,2,2,32,128]{4,3,2,1,0:T(8,128)(2,1)S(1)}, bf16[4,2,2,32,128]{4,3,2,1,0:T(8,128)(2,1)S(1)}, u32[]{:S(2)}, u32[]{:S(2)}) collective-permute-start(bf16[4,2,2,32,128]{4,3,2,1,0:T(8,128)(2,1)S(1)} %get-tuple-element.59), channel_id=1, source_target_pairs={{0,65},{1,64},{2,67},{3,66},{4,69},{5,68},{6,71},{7,70},{8,73},{9,... | collective-permute-start | bytes 393224 | tf_op jit(solution)/shard_map/ppermute | solution.py:343
  95.0 3.4 %collective-permute-done.4.plus_ref = bf16[4,2,2,32,128]{4,3,2,1,0:T(8,128)(2,1)S(1)} collective-permute-done((bf16[4,2,2,32,128]{4,3,2,1,0:T(8,128)(2,1)S(1)}, bf16[4,2,2,32,128]{4,3,2,1,0:T(8,128)(2,1)S(1)}, u32[]{:S(2)}, u32[]{:S(2)}) %collective-permute-start.4) | collective-permute-done | bytes 131104 | tf_op jit(solution)/shard_map/ppermute | solution.py:343
  98.3 8.5 %collective-permute-done.5.minus_ref = bf16[4,2,2,32,128]{4,3,2,1,0:T(8,128)(2,1)S(1)} collective-permute-done((bf16[4,2,2,32,128]{4,3,2,1,0:T(8,128)(2,1)S(1)}, bf16[4,2,2,32,128]{4,3,2,1,0:T(8,128)(2,1)S(1)}, u32[]{:S(2)}, u32[]{:S(2)}) %collective-permute-start.5) | collective-permute-done | bytes 131104 | tf_op jit(solution)/shard_map/ppermute | solution.py:343
  106.8 9.2 %all-to-all-start.4 = ((bf16[16,8,384]{2,1,0:T(8,128)(2,1)}), bf16[16,8,384]{2,1,0:T(8,128)(2,1)S(1)}, u32[]{:S(2)}, u32[]{:S(2)}) async-start(bf16[16,8,384]{2,1,0:T(8,128)(2,1)} %shard_map.127), calls=%async_computation.4 | async-start | bytes 196608 | tf_op jit(solution)/shard_map/all_to_all | solution.py:452
  116.0 2.3 %collective-permute-start.6 = (bf16[2,2,2,32,128]{4,3,2,1,0:T(8,128)(2,1)S(1)}, bf16[2,2,2,32,128]{4,3,2,1,0:T(8,128)(2,1)S(1)}, u32[]{:S(2)}, u32[]{:S(2)}) collective-permute-start(bf16[2,2,2,32,128]{4,3,2,1,0:T(8,128)(2,1)S(1)} %get-tuple-element.63), channel_id=1, source_target_pairs={{0,2},{1,3},{2,4},{3,5},{4,6},{5,7},{6,0},{7,1},{8,10},{9,11},{10,... | collective-permute-start | bytes 196616 | tf_op jit(solution)/shard_map/ppermute | solution.py:455
  118.3 4.5 %collective-permute-start.7 = (bf16[2,2,2,32,128]{4,3,2,1,0:T(8,128)(2,1)S(1)}, bf16[2,2,2,32,128]{4,3,2,1,0:T(8,128)(2,1)S(1)}, u32[]{:S(2)}, u32[]{:S(2)}) collective-permute-start(bf16[2,2,2,32,128]{4,3,2,1,0:T(8,128)(2,1)S(1)} %get-tuple-element.64), channel_id=1, source_target_pairs={{0,4},{1,5},{2,6},{3,7},{4,0},{5,1},{6,2},{7,3},{8,12},{9,13},{10,... | collective-permute-start | bytes 196616 | tf_op jit(solution)/shard_map/ppermute | solution.py:455
  122.7 1.9 %collective-permute-start.8 = (bf16[2,2,2,32,128]{4,3,2,1,0:T(8,128)(2,1)S(1)}, bf16[2,2,2,32,128]{4,3,2,1,0:T(8,128)(2,1)S(1)}, u32[]{:S(2)}, u32[]{:S(2)}) collective-permute-start(bf16[2,2,2,32,128]{4,3,2,1,0:T(8,128)(2,1)S(1)} %get-tuple-element.65), channel_id=1, source_target_pairs={{0,6},{1,7},{2,0},{3,1},{4,2},{5,3},{6,4},{7,5},{8,14},{9,15},{10,... | collective-permute-start | bytes 196616 | tf_op jit(solution)/shard_map/ppermute | solution.py:455
  125.9 4.2 %collective-permute-done.8.three_ref = bf16[2,2,2,32,128]{4,3,2,1,0:T(8,128)(2,1)S(1)} collective-permute-done((bf16[2,2,2,32,128]{4,3,2,1,0:T(8,128)(2,1)S(1)}, bf16[2,2,2,32,128]{4,3,2,1,0:T(8,128)(2,1)S(1)}, u32[]{:S(2)}, u32[]{:S(2)}) %collective-permute-start.8) | collective-permute-done | bytes 65568 | tf_op jit(solution)/shard_map/ppermute | solution.py:455
  130.1 1.8 %shard_map.129 = (bf16[8,4,32,128]{3,2,1,0:T(8,128)(2,1)}, bf16[8,4,32,128]{3,2,1,0:T(8,128)(2,1)}, bf16[16,32,128]{2,1,0:T(8,128)(2,1)S(1)}) custom-call(bf16[2,2,2,32,128]{4,3,2,1,0:T(8,128)(2,1)S(1)} %get-tuple-element.62.zero_ref, bf16[2,2,2,32,128]{4,3,2,1,0:T(8,128)(2,1)S(1)} %collective-permute-done.6.one_ref, ...), custom_call_target="tpu_custom_call" | custom-call | flops 10000000 | bytes 1000000 | tf_op jit(solution)/shard_map/pallas_call | solution.py:456
  132.0 13.1 %all-to-all-start.5 = ((bf16[8,4,32,128]{3,2,1,0:T(8,128)(2,1)}), bf16[8,4,32,128]{3,2,1,0:T(8,128)(2,1)S(1)}, u32[]{:S(2)}, u32[]{:S(2)}) async-start(bf16[8,4,32,128]{3,2,1,0:T(8,128)(2,1)} %get-tuple-element.72), calls=%async_computation.5 | async-start | bytes 524288 | tf_op jit(solution)/shard_map/all_to_all | solution.py:317
  145.1 1.9 %collective-permute-start.9 = (f32[1,8,256]{2,1,0:T(8,128)S(1)}, f32[1,8,256]{2,1,0:T(8,128)S(1)}, u32[]{:S(2)}, u32[]{:S(2)}) collective-permute-start(f32[1,8,256]{2,1,0:T(8,128)S(1)} %get-tuple-element.73.one_ref), channel_id=1, source_target_pairs={{0,128},{8,136},{16,144},{24,152},{32,160},{40,168},{48,176},{56,1... | collective-permute-start | bytes 24584 | tf_op jit(solution)/shard_map/ppermute | solution.py:321
  147.0 3.6 %collective-permute-done.9.two_ref = f32[1,8,256]{2,1,0:T(8,128)S(1)} collective-permute-done((f32[1,8,256]{2,1,0:T(8,128)S(1)}, f32[1,8,256]{2,1,0:T(8,128)S(1)}, u32[]{:S(2)}, u32[]{:S(2)}) %collective-permute-start.9) | collective-permute-done | bytes 8224 | tf_op jit(solution)/shard_map/ppermute | solution.py:321
  150.6 1.8 %all-to-all-done.5.b_ref = bf16[8,4,32,128]{3,2,1,0:T(8,128)(2,1)S(1)} async-done(((bf16[8,4,32,128]{3,2,1,0:T(8,128)(2,1)}), bf16[8,4,32,128]{3,2,1,0:T(8,128)(2,1)S(1)}, u32[]{:S(2)}, u32[]{:S(2)}) %all-to-all-start.5) | async-done | bytes 262176 | tf_op jit(solution)/shard_map/all_to_all | solution.py:317
  152.5 5.1 %all-to-all-start.6 = ((bf16[8,4,32,128]{3,2,1,0:T(8,128)(2,1)}), bf16[8,4,32,128]{3,2,1,0:T(8,128)(2,1)S(1)}, u32[]{:S(2)}, u32[]{:S(2)}) async-start(bf16[8,4,32,128]{3,2,1,0:T(8,128)(2,1)} %get-tuple-element.74), calls=%async_computation.6 | async-start | bytes 524288 | tf_op jit(solution)/shard_map/all_to_all | solution.py:317
  158.4 4.9 %collective-permute-start.10 = (f32[2,8,256]{2,1,0:T(8,128)S(1)}, f32[2,8,256]{2,1,0:T(8,128)S(1)}, u32[]{:S(2)}, u32[]{:S(2)}) collective-permute-start(f32[2,8,256]{2,1,0:T(8,128)S(1)} %shard_map.132.one_ref), channel_id=1, source_target_pairs={{0,256},{8,264},{16,272},{24,280},{32,288},{40,296},{48,304},{56,3... | collective-permute-start | bytes 49160 | tf_op jit(solution)/shard_map/ppermute | solution.py:321
  163.3 2.2 %collective-permute-done.10.two_ref = f32[2,8,256]{2,1,0:T(8,128)S(1)} collective-permute-done((f32[2,8,256]{2,1,0:T(8,128)S(1)}, f32[2,8,256]{2,1,0:T(8,128)S(1)}, u32[]{:S(2)}, u32[]{:S(2)}) %collective-permute-start.10) | collective-permute-done | bytes 16416 | tf_op jit(solution)/shard_map/ppermute | solution.py:321
  165.5 1.9 %collective-permute-start.11 = (f32[4,8,256]{2,1,0:T(8,128)S(1)}, f32[4,8,256]{2,1,0:T(8,128)S(1)}, u32[]{:S(2)}, u32[]{:S(2)}) collective-permute-start(f32[4,8,256]{2,1,0:T(8,128)S(1)} %shard_map.134.near_ref), channel_id=1, source_target_pairs={{0,8},{8,0},{16,24},{24,16},{32,40},{40,32},{48,56},{56,48},{64,72... | collective-permute-start | bytes 98312 | tf_op jit(solution)/shard_map/ppermute | solution.py:321
  169.3 1.4 shard_map.133
  (52 shorter events, 16.5 us)
Async XLA Ops:
  0.6 42.9 %copy-start.7 = (s32[56]{0:T(128)S(1)}, s32[56]{0:T(128)}, u32[]{:S(2)}) copy-start(s32[56]{0:T(128)} %dst_ref.7) | copy-start | bytes 676
  0.6 42.9 %copy-start.9 = (s32[56]{0:T(128)S(1)}, s32[56]{0:T(128)}, u32[]{:S(2)}) copy-start(s32[56]{0:T(128)} %src_ref.7) | copy-start | bytes 676
  1.4 0.9 copy-start.1
  3.9 23.0 %all-to-all-start = ((bf16[8,4,32,128]{3,2,1,0:T(8,128)(2,1)}), bf16[8,4,32,128]{3,2,1,0:T(8,128)(2,1)S(1)}, u32[]{:S(2)}, u32[]{:S(2)}) async-start(bf16[8,4,32,128]{3,2,1,0:T(8,128)(2,1)} %get-tuple-element.43), calls=%async_computation | async-start | bytes 524288 | tf_op jit(solution)/shard_map/all_to_all | solution.py:317
  19.6 0.9 copy-start.2
  20.5 0.9 copy-start.5
  21.5 2.0 %copy-start = (s32[56,128,128]{2,1,0:T(8,128)S(1)}, s32[56,128,128]{2,1,0:T(8,128)}, u32[]{:S(2)}) copy-start(s32[56,128,128]{2,1,0:T(8,128)} %cnt_ref.1) | copy-start | bytes 11010052
  23.5 0.7 copy-start.6
  24.2 0.7 copy-start.8
  24.8 43.7 %copy-start.4 = (bf16[256,256]{1,0:T(8,128)(2,1)S(1)}, bf16[256,256]{1,0:T(8,128)(2,1)}, u32[]{:S(2)}) copy-start(bf16[256,256]{1,0:T(8,128)(2,1)} %own_w_ref.1) | copy-start | bytes 393220
  24.8 43.8 %copy-start.3 = (bf16[256,256]{1,0:T(8,128)(2,1)S(1)}, bf16[256,256]{1,0:T(8,128)(2,1)}, u32[]{:S(2)}) copy-start(bf16[256,256]{1,0:T(8,128)(2,1)} %neigh_ref.1) | copy-start | bytes 393220
  24.8 43.9 %copy-start.10 = (f32[256]{0:T(256)S(1)}, f32[256]{0:T(256)}, u32[]{:S(2)}) copy-start(f32[256]{0:T(256)} %param.16) | copy-start | bytes 3076
  26.9 16.6 %all-to-all-start.1 = ((bf16[8,4,32,128]{3,2,1,0:T(8,128)(2,1)}), bf16[8,4,32,128]{3,2,1,0:T(8,128)(2,1)S(1)}, u32[]{:S(2)}, u32[]{:S(2)}) async-start(bf16[8,4,32,128]{3,2,1,0:T(8,128)(2,1)} %get-tuple-element.50), calls=%async_computation.1 | async-start | bytes 524288 | tf_op jit(solution)/shard_map/all_to_all | solution.py:317
  31.8 22.9 %collective-permute-start = (bf16[4,2,2,32,128]{4,3,2,1,0:T(8,128)(2,1)S(1)}, bf16[4,2,2,32,128]{4,3,2,1,0:T(8,128)(2,1)S(1)}, u32[]{:S(2)}, u32[]{:S(2)}) collective-permute-start(bf16[4,2,2,32,128]{4,3,2,1,0:T(8,128)(2,1)S(1)} %get-tuple-element.48), channel_id=1, source_target_pairs={{0,64},{1,65},{2,66},{3,67},{4,68},{5,69},{6,70},{7,71},{8,72},{9,... | collective-permute-start | bytes 393224 | tf_op jit(solution)/shard_map/ppermute | solution.py:343
  36.5 19.4 %collective-permute-start.1 = (bf16[4,2,2,32,128]{4,3,2,1,0:T(8,128)(2,1)S(1)}, bf16[4,2,2,32,128]{4,3,2,1,0:T(8,128)(2,1)S(1)}, u32[]{:S(2)}, u32[]{:S(2)}) collective-permute-start(bf16[4,2,2,32,128]{4,3,2,1,0:T(8,128)(2,1)S(1)} %get-tuple-element.49), channel_id=1, source_target_pairs={{0,65},{1,64},{2,67},{3,66},{4,69},{5,68},{6,71},{7,70},{8,73},{9,... | collective-permute-start | bytes 393224 | tf_op jit(solution)/shard_map/ppermute | solution.py:343
  44.9 17.1 %collective-permute-start.2 = (bf16[4,2,32,128]{3,2,1,0:T(8,128)(2,1)S(1)}, bf16[4,2,32,128]{3,2,1,0:T(8,128)(2,1)S(1)}, u32[]{:S(2)}, u32[]{:S(2)}) collective-permute-start(bf16[4,2,32,128]{3,2,1,0:T(8,128)(2,1)S(1)} %get-tuple-element.54), channel_id=1, source_target_pairs={{0,64},{1,65},{2,66},{3,67},{4,68},{5,69},{6,70},{7,71},{8,72},{9,... | collective-permute-start | bytes 196616 | tf_op jit(solution)/shard_map/ppermute | solution.py:343
  48.1 14.9 %collective-permute-start.3 = (bf16[4,2,32,128]{3,2,1,0:T(8,128)(2,1)S(1)}, bf16[4,2,32,128]{3,2,1,0:T(8,128)(2,1)S(1)}, u32[]{:S(2)}, u32[]{:S(2)}) collective-permute-start(bf16[4,2,32,128]{3,2,1,0:T(8,128)(2,1)S(1)} %get-tuple-element.55), channel_id=1, source_target_pairs={{0,65},{1,64},{2,67},{3,66},{4,69},{5,68},{6,71},{7,70},{8,73},{9,... | collective-permute-start | bytes 196616 | tf_op jit(solution)/shard_map/ppermute | solution.py:343
  63.7 10.1 %all-to-all-start.2 = ((bf16[4,3,2,2,32,128]{5,4,3,2,1,0:T(8,128)(2,1)}), bf16[4,3,2,2,32,128]{5,4,3,2,1,0:T(8,128)(2,1)S(1)}, u32[]{:S(2)}, u32[]{:S(2)}) async-start(bf16[4,3,2,2,32,128]{5,4,3,2,1,0:T(8,128)(2,1)} %shard_map.124), calls=%async_computation.2 | async-start | bytes 786432 | tf_op jit(solution)/shard_map/all_to_all | solution.py:326
  75.8 18.4 %all-to-all-start.3 = ((bf16[32,16,384]{2,1,0:T(8,128)(2,1)}), bf16[32,16,384]{2,1,0:T(8,128)(2,1)S(1)}, u32[]{:S(2)}, u32[]{:S(2)}) async-start(bf16[32,16,384]{2,1,0:T(8,128)(2,1)} %shard_map.126), calls=%async_computation.3 | async-start | bytes 786432 | tf_op jit(solution)/shard_map/all_to_all | solution.py:447
  84.5 13.8 %collective-permute-start.4 = (bf16[4,2,2,32,128]{4,3,2,1,0:T(8,128)(2,1)S(1)}, bf16[4,2,2,32,128]{4,3,2,1,0:T(8,128)(2,1)S(1)}, u32[]{:S(2)}, u32[]{:S(2)}) collective-permute-start(bf16[4,2,2,32,128]{4,3,2,1,0:T(8,128)(2,1)S(1)} %get-tuple-element.58), channel_id=1, source_target_pairs={{0,64},{1,65},{2,66},{3,67},{4,68},{5,69},{6,70},{7,71},{8,72},{9,... | collective-permute-start | bytes 393224 | tf_op jit(solution)/shard_map/ppermute | solution.py:343
  90.3 16.5 %collective-permute-start.5 = (bf16[4,2,2,32,128]{4,3,2,1,0:T(8,128)(2,1)S(1)}, bf16[4,2,2,32,128]{4,3,2,1,0:T(8,128)(2,1)S(1)}, u32[]{:S(2)}, u32[]{:S(2)}) collective-permute-start(bf16[4,2,2,32,128]{4,3,2,1,0:T(8,128)(2,1)S(1)} %get-tuple-element.59), channel_id=1, source_target_pairs={{0,65},{1,64},{2,67},{3,66},{4,69},{5,68},{6,71},{7,70},{8,73},{9,... | collective-permute-start | bytes 393224 | tf_op jit(solution)/shard_map/ppermute | solution.py:343
  106.8 25.2 %all-to-all-start.4 = ((bf16[16,8,384]{2,1,0:T(8,128)(2,1)}), bf16[16,8,384]{2,1,0:T(8,128)(2,1)S(1)}, u32[]{:S(2)}, u32[]{:S(2)}) async-start(bf16[16,8,384]{2,1,0:T(8,128)(2,1)} %shard_map.127), calls=%async_computation.4 | async-start | bytes 196608 | tf_op jit(solution)/shard_map/all_to_all | solution.py:452
  116.0 8.7 %collective-permute-start.6 = (bf16[2,2,2,32,128]{4,3,2,1,0:T(8,128)(2,1)S(1)}, bf16[2,2,2,32,128]{4,3,2,1,0:T(8,128)(2,1)S(1)}, u32[]{:S(2)}, u32[]{:S(2)}) collective-permute-start(bf16[2,2,2,32,128]{4,3,2,1,0:T(8,128)(2,1)S(1)} %get-tuple-element.63), channel_id=1, source_target_pairs={{0,2},{1,3},{2,4},{3,5},{4,6},{5,7},{6,0},{7,1},{8,10},{9,11},{10,... | collective-permute-start | bytes 196616 | tf_op jit(solution)/shard_map/ppermute | solution.py:455
  118.3 7.7 %collective-permute-start.7 = (bf16[2,2,2,32,128]{4,3,2,1,0:T(8,128)(2,1)S(1)}, bf16[2,2,2,32,128]{4,3,2,1,0:T(8,128)(2,1)S(1)}, u32[]{:S(2)}, u32[]{:S(2)}) collective-permute-start(bf16[2,2,2,32,128]{4,3,2,1,0:T(8,128)(2,1)S(1)} %get-tuple-element.64), channel_id=1, source_target_pairs={{0,4},{1,5},{2,6},{3,7},{4,0},{5,1},{6,2},{7,3},{8,12},{9,13},{10,... | collective-permute-start | bytes 196616 | tf_op jit(solution)/shard_map/ppermute | solution.py:455
  122.7 7.4 %collective-permute-start.8 = (bf16[2,2,2,32,128]{4,3,2,1,0:T(8,128)(2,1)S(1)}, bf16[2,2,2,32,128]{4,3,2,1,0:T(8,128)(2,1)S(1)}, u32[]{:S(2)}, u32[]{:S(2)}) collective-permute-start(bf16[2,2,2,32,128]{4,3,2,1,0:T(8,128)(2,1)S(1)} %get-tuple-element.65), channel_id=1, source_target_pairs={{0,6},{1,7},{2,0},{3,1},{4,2},{5,3},{6,4},{7,5},{8,14},{9,15},{10,... | collective-permute-start | bytes 196616 | tf_op jit(solution)/shard_map/ppermute | solution.py:455
  132.0 20.5 %all-to-all-start.5 = ((bf16[8,4,32,128]{3,2,1,0:T(8,128)(2,1)}), bf16[8,4,32,128]{3,2,1,0:T(8,128)(2,1)S(1)}, u32[]{:S(2)}, u32[]{:S(2)}) async-start(bf16[8,4,32,128]{3,2,1,0:T(8,128)(2,1)} %get-tuple-element.72), calls=%async_computation.5 | async-start | bytes 524288 | tf_op jit(solution)/shard_map/all_to_all | solution.py:317
  145.1 5.5 %collective-permute-start.9 = (f32[1,8,256]{2,1,0:T(8,128)S(1)}, f32[1,8,256]{2,1,0:T(8,128)S(1)}, u32[]{:S(2)}, u32[]{:S(2)}) collective-permute-start(f32[1,8,256]{2,1,0:T(8,128)S(1)} %get-tuple-element.73.one_ref), channel_id=1, source_target_pairs={{0,128},{8,136},{16,144},{24,152},{32,160},{40,168},{48,176},{56,1... | collective-permute-start | bytes 24584 | tf_op jit(solution)/shard_map/ppermute | solution.py:321
  152.5 16.8 %all-to-all-start.6 = ((bf16[8,4,32,128]{3,2,1,0:T(8,128)(2,1)}), bf16[8,4,32,128]{3,2,1,0:T(8,128)(2,1)S(1)}, u32[]{:S(2)}, u32[]{:S(2)}) async-start(bf16[8,4,32,128]{3,2,1,0:T(8,128)(2,1)} %get-tuple-element.74), calls=%async_computation.6 | async-start | bytes 524288 | tf_op jit(solution)/shard_map/all_to_all | solution.py:317
  158.4 7.1 %collective-permute-start.10 = (f32[2,8,256]{2,1,0:T(8,128)S(1)}, f32[2,8,256]{2,1,0:T(8,128)S(1)}, u32[]{:S(2)}, u32[]{:S(2)}) collective-permute-start(f32[2,8,256]{2,1,0:T(8,128)S(1)} %shard_map.132.one_ref), channel_id=1, source_target_pairs={{0,256},{8,264},{16,272},{24,280},{32,288},{40,296},{48,304},{56,3... | collective-permute-start | bytes 49160 | tf_op jit(solution)/shard_map/ppermute | solution.py:321
  165.5 3.1 %collective-permute-start.11 = (f32[4,8,256]{2,1,0:T(8,128)S(1)}, f32[4,8,256]{2,1,0:T(8,128)S(1)}, u32[]{:S(2)}, u32[]{:S(2)}) collective-permute-start(f32[4,8,256]{2,1,0:T(8,128)S(1)} %shard_map.134.near_ref), channel_id=1, source_target_pairs={{0,8},{8,0},{16,24},{24,16},{32,40},{40,32},{48,56},{56,48},{64,72... | collective-permute-start | bytes 98312 | tf_op jit(solution)/shard_map/ppermute | solution.py:321

commit v9 on v8

--- a/solution.py
+++ b/solution.py
@@ -66,8 +66,10 @@
     return jnp.clip(place, 0, GROUP - 1)
 
 
-def pack_kernel(width, x_ref, send_ref, a_ref, b_ref):
+def pack_kernel(width, x_ref, send_ref, a_ref, b_ref, block_ref):
     place_a, place_b = places()
+    for block in range(block_ref.shape[0]):
+        block_ref[block] = x_ref[:, block * width : (block + 1) * width]
     cap = send_ref.shape[1]
     for ref, place in ((b_ref, place_b), (a_ref, place_a)):
         for peer in range(GROUP):
@@ -94,8 +96,9 @@
     for x in range(X):
         for out, h in ((plus_ref, z_hi), (minus_ref, 1 - z_hi)):
             for p in range(per):
-                start = pl.multiple_of(((x * Z_HI + h) * per + p) * width, width)
-                out[x, 0, p] = x_ref[:, pl.ds(start, width)]
+                block = (x * Z_HI + h) * per + p
+                start = pl.multiple_of(block * width, width)
+                out[x, 0, p] = x_ref[block]
                 out[x, 1, p] = cot_ref[:, pl.ds(start, width)]
 
 
@@ -155,7 +158,7 @@
 def local_kernel(slots, chunk, x_ref, dst_ref, src_ref, cnt_ref, half_ref, acc_ref):
     step = pl.program_id(0)
     width = cnt_ref.shape[1]
-    dim = x_ref.shape[0]
+    dim = x_ref.shape[1]
     half_ref[...] = cnt_ref[...].astype(F32).astype(BF16)
 
     @pl.when(step == 0)
@@ -167,8 +170,7 @@
         ones = jnp.ones((16, width), BF16)
         for i in range(chunk):
             tile = step * chunk + i
-            start = pl.multiple_of(src_ref[tile] * width, width)
-            rows = jnp.concatenate([x_ref[:, pl.ds(start, width)], ones], axis=0)
+            rows = jnp.concatenate([x_ref[src_ref[tile]], ones], axis=0)
             dst = dst_ref[tile]
             acc_ref[dst] += dot(rows, half_ref[i], LAST)[: dim + 8]
 
@@ -360,13 +362,13 @@
     halo = shape(GROUP, cap)
     step = Z_LO // 2
 
-    send_a, send_b = call(
-        functools.partial(pack_kernel, width), (halo, halo), [VMEM, SMEM]
+    send_a, send_b, feats = call(
+        functools.partial(pack_kernel, width), (halo, halo, shape(blocks)), [VMEM, SMEM]
     )(node_feats, table)
     got_b = swap(send_b, GROUP // 2)
     xc_plus, xc_minus = call(
         functools.partial(split_kernel, width), (shape(X, 2, per_col),) * 2, [VMEM] * 2
-    )(node_feats, cotangent)
+    )(feats, cotangent)
     whole = lambda shape: pl.BlockSpec(shape, lambda i: (0,) * len(shape))
     half, acc = pl.pallas_call(
         functools.partial(local_kernel, slots, chunk),
@@ -376,7 +378,7 @@
             jax.ShapeDtypeStruct((blocks, dim + 8, width), F32),
         ),
         in_specs=[
-            whole((dim, nodes)),
+            whole((blocks, dim, width)),
             SMEM,
             SMEM,
             pl.BlockSpec((chunk, width, width), lambda i: (i, 0, 0)),
@@ -389,7 +391,7 @@
         cost_estimate=pl.CostEstimate(
             flops=60000000, bytes_accessed=6000000, transcendentals=0
         ),
-    )(node_feats, tile_dst, tile_src, tile_cnt)
+    )(feats, tile_dst, tile_src, tile_cnt)
     send_a, got_b, xc_plus, xc_minus, half, acc = lax.optimization_barrier(
         (send_a, got_b, xc_plus, xc_minus, half, acc)
     )
@@ -445,12 +447,12 @@
         for x in range(X)
     ]
     part = lax.all_to_all(part, both, 0, 0, axis_index_groups=flat, tiled=False)
+    home = call(turn_kernel, (shape(2, 2, per_col),) * X, [VMEM] * 2, cost=(1e10, 1e6))(plus, minus)
+    part, *home = lax.optimization_barrier((part, *home))
     (part,) = call(
         fold_kernel, (jax.ShapeDtypeStruct((Z_HI * Z_LO, 8, full + 128), BF16),), [VMEM]
     )(part)
-    part, plus, minus = lax.optimization_barrier((part, plus, minus))
     part = lax.all_to_all(part, both, 0, 0, axis_index_groups=line, tiled=False)
-    home = call(turn_kernel, (shape(2, 2, per_col),) * X, [VMEM] * 2)(plus, minus)
     route = lambda turn: [(c, (c + Z_HI * turn) % cols) for c in range(cols)]
     home = [home[0]] + [lax.ppermute(home[turn], "col", route(turn)) for turn in range(1, X)]
     away_a, away_b, scaled = call(

time: 173 us -> 171 us (0.988)
    ppermute x6, waiting for transfers between devices: 20.1 us -> 8.32 us  [along_z(): return lax.ppermute(rows, ('blk', 'col'), sorted(route))]
    all_to_all x1, waiting for transfers between devices: 0.01 us -> 8.72 us  [per_device(): part = lax.all_to_all(part, both, 0, 0, axis_index_groups=flat, tiled=False)]
    unnamed x24 -> x22, local copies, waits for them, and re-layouts: 6.27 us -> 5.37 us
  transfers between devices with their start and end apart: 19 -> 19, of which waited for: 13 -> 12; matrix products, arithmetic and copies ran while one was open for 1% -> 1% of each run, Pallas kernels for 4% -> 5%
where the time goes in v9:
time: 171 us; the launch traced here: 168 us
  starting transfers between devices  110 us (64%)
  waiting for transfers between devices  37.3 us (22%)
  Pallas kernels  13 us (8%)
  local copies, waits for them, and re-layouts  6.86 us (4%)
    all_to_all x4, starting transfers between devices, swap(): lax.all_to_all(rows, 'blk', 0, 0, axis_index_groups=groups, tiled=False)  38.8 us
    ppermute x6, starting transfers between devices, along_z(): return lax.ppermute(rows, ('blk', 'col'), sorted(route))  31.2 us
    all_to_all x1, starting transfers between devices, per_device(): part = lax.all_to_all(part, both, 0, 0, axis_index_groups=line, tiled=False)  9.89 us
    all_to_all x1, waiting for transfers between devices, per_device(): part = lax.all_to_all(part, both, 0, 0, axis_index_groups=flat, tiled=False)  8.72 us
    all_to_all x1, starting transfers between devices, per_device(): part = lax.all_to_all(part, both, 0, 0, axis_index_groups=flat, tiled=False)  8.65 us
    ppermute x3, starting transfers between devices, per_device(): lax.ppermute(home[turn], 'col', route(turn))  8.38 us
    ppermute x6, waiting for transfers between devices, along_z(): return lax.ppermute(rows, ('blk', 'col'), sorted(route))  8.32 us
    ppermute x3, starting transfers between devices, across(): lax.ppermute(rows, 'blk', [(e, e ^ bit) for e in range(lax.axis_size('blk...  7.99 us
  transfers between devices with their start and end apart: 19, of which 12 were waited for; matrix products, arithmetic and copies ran while one was open for 1% of the time, Pallas kernels for 5%

profile of v9, /device:TPU:6, one launch (start us, length us, event | category | flops | bytes accessed | tf_op | source)
XLA Modules:
  0.0 167.8 jit_solution(6674449275349651390)
XLA Ops:
  2.3 1.6 shard_map.120
  3.9 15.7 %all-to-all-start = ((bf16[8,4,32,128]{3,2,1,0:T(8,128)(2,1)}), bf16[8,4,32,128]{3,2,1,0:T(8,128)(2,1)S(1)}, u32[]{:S(2)}, u32[]{:S(2)}) async-start(bf16[8,4,32,128]{3,2,1,0:T(8,128)(2,1)} %get-tuple-element.46), calls=%async_computation | async-start | bytes 524288 | tf_op jit(solution)/shard_map/all_to_all | solution.py:319
  20.6 2.0 %copy-done = s32[56,128,128]{2,1,0:T(8,128)S(1)} copy-done((s32[56,128,128]{2,1,0:T(8,128)S(1)}, s32[56,128,128]{2,1,0:T(8,128)}, u32[]{:S(2)}) %copy-start) | copy-done | bytes 3670040
  23.9 1.8 %shard_map.122 = (bf16[56,128,128]{2,1,0:T(8,128)(2,1)S(1)}, f32[16,40,128]{2,1,0:T(8,128)S(1)}) custom-call(bf16[16,32,128]{2,1,0:T(8,128)(2,1)S(1)} %get-tuple-element.47.x_ref, s32[56]{0:T(128)S(1)} %copy-done.5, s32[56]{0:T(128)S(1)} %copy-done.7, s32[56,128,128]{2,1,0:T(8,128)S(1)} %copy-done), custom_call_target="tpu_custom_call" | custom-call | flops 60000000 | bytes 6000000 | tf_op jit(solution)/shard_map/pallas_call | solution.py:373
  26.9 4.8 %all-to-all-start.1 = ((bf16[8,4,32,128]{3,2,1,0:T(8,128)(2,1)}), bf16[8,4,32,128]{3,2,1,0:T(8,128)(2,1)S(1)}, u32[]{:S(2)}, u32[]{:S(2)}) async-start(bf16[8,4,32,128]{3,2,1,0:T(8,128)(2,1)} %get-tuple-element.54), calls=%async_computation.1 | async-start | bytes 524288 | tf_op jit(solution)/shard_map/all_to_all | solution.py:319
  31.8 4.7 %collective-permute-start = (bf16[4,2,2,32,128]{4,3,2,1,0:T(8,128)(2,1)S(1)}, bf16[4,2,2,32,128]{4,3,2,1,0:T(8,128)(2,1)S(1)}, u32[]{:S(2)}, u32[]{:S(2)}) collective-permute-start(bf16[4,2,2,32,128]{4,3,2,1,0:T(8,128)(2,1)S(1)} %get-tuple-element.52), channel_id=1, source_target_pairs={{0,64},{1,65},{2,66},{3,67},{4,68},{5,69},{6,70},{7,71},{8,72},{9,... | collective-permute-start | bytes 393224 | tf_op jit(solution)/shard_map/ppermute | solution.py:345
  36.5 7.0 %collective-permute-start.1 = (bf16[4,2,2,32,128]{4,3,2,1,0:T(8,128)(2,1)S(1)}, bf16[4,2,2,32,128]{4,3,2,1,0:T(8,128)(2,1)S(1)}, u32[]{:S(2)}, u32[]{:S(2)}) collective-permute-start(bf16[4,2,2,32,128]{4,3,2,1,0:T(8,128)(2,1)S(1)} %get-tuple-element.53), channel_id=1, source_target_pairs={{0,65},{1,64},{2,67},{3,66},{4,69},{5,68},{6,71},{7,70},{8,73},{9,... | collective-permute-start | bytes 393224 | tf_op jit(solution)/shard_map/ppermute | solution.py:345
  44.9 3.2 %collective-permute-start.2 = (bf16[4,2,32,128]{3,2,1,0:T(8,128)(2,1)S(1)}, bf16[4,2,32,128]{3,2,1,0:T(8,128)(2,1)S(1)}, u32[]{:S(2)}, u32[]{:S(2)}) collective-permute-start(bf16[4,2,32,128]{3,2,1,0:T(8,128)(2,1)S(1)} %get-tuple-element.58), channel_id=1, source_target_pairs={{0,64},{1,65},{2,66},{3,67},{4,68},{5,69},{6,70},{7,71},{8,72},{9,... | collective-permute-start | bytes 196616 | tf_op jit(solution)/shard_map/ppermute | solution.py:345
  48.1 6.6 %collective-permute-start.3 = (bf16[4,2,32,128]{3,2,1,0:T(8,128)(2,1)S(1)}, bf16[4,2,32,128]{3,2,1,0:T(8,128)(2,1)S(1)}, u32[]{:S(2)}, u32[]{:S(2)}) collective-permute-start(bf16[4,2,32,128]{3,2,1,0:T(8,128)(2,1)S(1)} %get-tuple-element.59), channel_id=1, source_target_pairs={{0,65},{1,64},{2,67},{3,66},{4,69},{5,68},{6,71},{7,70},{8,73},{9,... | collective-permute-start | bytes 196616 | tf_op jit(solution)/shard_map/ppermute | solution.py:345
  55.9 6.2 %collective-permute-done.2.agg_plus_ref = bf16[4,2,32,128]{3,2,1,0:T(8,128)(2,1)S(1)} collective-permute-done((bf16[4,2,32,128]{3,2,1,0:T(8,128)(2,1)S(1)}, bf16[4,2,32,128]{3,2,1,0:T(8,128)(2,1)S(1)}, u32[]{:S(2)}, u32[]{:S(2)}) %collective-permute-start.2) | collective-permute-done | bytes 65568 | tf_op jit(solution)/shard_map/ppermute | solution.py:345
  63.7 4.8 %all-to-all-start.2 = ((bf16[4,3,2,2,32,128]{5,4,3,2,1,0:T(8,128)(2,1)}), bf16[4,3,2,2,32,128]{5,4,3,2,1,0:T(8,128)(2,1)S(1)}, u32[]{:S(2)}, u32[]{:S(2)}) async-start(bf16[4,3,2,2,32,128]{5,4,3,2,1,0:T(8,128)(2,1)} %shard_map.124), calls=%async_computation.2 | async-start | bytes 786432 | tf_op jit(solution)/shard_map/all_to_all | solution.py:328
  68.9 4.9 %all-to-all-done.2.in_ref = bf16[4,3,2,2,32,128]{5,4,3,2,1,0:T(8,128)(2,1)S(1)} async-done(((bf16[4,3,2,2,32,128]{5,4,3,2,1,0:T(8,128)(2,1)}), bf16[4,3,2,2,32,128]{5,4,3,2,1,0:T(8,128)(2,1)S(1)}, u32[]{:S(2)}, u32[]{:S(2)}) %all-to-all-start.2) | async-done | bytes 393248 | tf_op jit(solution)/shard_map/all_to_all | solution.py:328
  74.7 6.7 %collective-permute-start.4 = (bf16[4,2,2,32,128]{4,3,2,1,0:T(8,128)(2,1)S(1)}, bf16[4,2,2,32,128]{4,3,2,1,0:T(8,128)(2,1)S(1)}, u32[]{:S(2)}, u32[]{:S(2)}) collective-permute-start(bf16[4,2,2,32,128]{4,3,2,1,0:T(8,128)(2,1)S(1)} %get-tuple-element.62), channel_id=1, source_target_pairs={{0,64},{1,65},{2,66},{3,67},{4,68},{5,69},{6,70},{7,71},{8,72},{9,... | collective-permute-start | bytes 393224 | tf_op jit(solution)/shard_map/ppermute | solution.py:345
  81.4 3.1 %collective-permute-start.5 = (bf16[4,2,2,32,128]{4,3,2,1,0:T(8,128)(2,1)S(1)}, bf16[4,2,2,32,128]{4,3,2,1,0:T(8,128)(2,1)S(1)}, u32[]{:S(2)}, u32[]{:S(2)}) collective-permute-start(bf16[4,2,2,32,128]{4,3,2,1,0:T(8,128)(2,1)S(1)} %get-tuple-element.63), channel_id=1, source_target_pairs={{0,65},{1,64},{2,67},{3,66},{4,69},{5,68},{6,71},{7,70},{8,73},{9,... | collective-permute-start | bytes 393224 | tf_op jit(solution)/shard_map/ppermute | solution.py:345
  85.6 8.7 %all-to-all-start.3 = ((bf16[32,16,384]{2,1,0:T(8,128)(2,1)}), bf16[32,16,384]{2,1,0:T(8,128)(2,1)S(1)}, u32[]{:S(2)}, u32[]{:S(2)}) async-start(bf16[32,16,384]{2,1,0:T(8,128)(2,1)} %shard_map.126), calls=%async_computation.3 | async-start | bytes 786432 | tf_op jit(solution)/shard_map/all_to_all | solution.py:449
  94.3 8.7 %all-to-all-done.3.part_ref = bf16[32,16,384]{2,1,0:T(8,128)(2,1)S(1)} async-done(((bf16[32,16,384]{2,1,0:T(8,128)(2,1)}), bf16[32,16,384]{2,1,0:T(8,128)(2,1)S(1)}, u32[]{:S(2)}, u32[]{:S(2)}) %all-to-all-start.3) | async-done | bytes 393248 | tf_op jit(solution)/shard_map/all_to_all | solution.py:449
  103.7 9.9 %all-to-all-start.4 = ((bf16[16,8,384]{2,1,0:T(8,128)(2,1)}), bf16[16,8,384]{2,1,0:T(8,128)(2,1)S(1)}, u32[]{:S(2)}, u32[]{:S(2)}) async-start(bf16[16,8,384]{2,1,0:T(8,128)(2,1)} %shard_map.130), calls=%async_computation.4 | async-start | bytes 196608 | tf_op jit(solution)/shard_map/all_to_all | solution.py:455
  113.6 3.7 %collective-permute-start.6 = (bf16[2,2,2,32,128]{4,3,2,1,0:T(8,128)(2,1)S(1)}, bf16[2,2,2,32,128]{4,3,2,1,0:T(8,128)(2,1)S(1)}, u32[]{:S(2)}, u32[]{:S(2)}) collective-permute-start(bf16[2,2,2,32,128]{4,3,2,1,0:T(8,128)(2,1)S(1)} %get-tuple-element.69), channel_id=1, source_target_pairs={{0,2},{1,3},{2,4},{3,5},{4,6},{5,7},{6,0},{7,1},{8,10},{9,11},{10,... | collective-permute-start | bytes 196616 | tf_op jit(solution)/shard_map/ppermute | solution.py:457
  117.3 2.5 %collective-permute-start.7 = (bf16[2,2,2,32,128]{4,3,2,1,0:T(8,128)(2,1)S(1)}, bf16[2,2,2,32,128]{4,3,2,1,0:T(8,128)(2,1)S(1)}, u32[]{:S(2)}, u32[]{:S(2)}) collective-permute-start(bf16[2,2,2,32,128]{4,3,2,1,0:T(8,128)(2,1)S(1)} %get-tuple-element.70), channel_id=1, source_target_pairs={{0,4},{1,5},{2,6},{3,7},{4,0},{5,1},{6,2},{7,3},{8,12},{9,13},{10,... | collective-permute-start | bytes 196616 | tf_op jit(solution)/shard_map/ppermute | solution.py:457
  119.8 2.2 %collective-permute-start.8 = (bf16[2,2,2,32,128]{4,3,2,1,0:T(8,128)(2,1)S(1)}, bf16[2,2,2,32,128]{4,3,2,1,0:T(8,128)(2,1)S(1)}, u32[]{:S(2)}, u32[]{:S(2)}) collective-permute-start(bf16[2,2,2,32,128]{4,3,2,1,0:T(8,128)(2,1)S(1)} %get-tuple-element.71), channel_id=1, source_target_pairs={{0,6},{1,7},{2,0},{3,1},{4,2},{5,3},{6,4},{7,5},{8,14},{9,15},{10,... | collective-permute-start | bytes 196616 | tf_op jit(solution)/shard_map/ppermute | solution.py:457
  122.0 3.0 %collective-permute-done.7.two_ref = bf16[2,2,2,32,128]{4,3,2,1,0:T(8,128)(2,1)S(1)} collective-permute-done((bf16[2,2,2,32,128]{4,3,2,1,0:T(8,128)(2,1)S(1)}, bf16[2,2,2,32,128]{4,3,2,1,0:T(8,128)(2,1)S(1)}, u32[]{:S(2)}, u32[]{:S(2)}) %collective-permute-start.7) | collective-permute-done | bytes 65568 | tf_op jit(solution)/shard_map/ppermute | solution.py:457
  125.0 2.1 %collective-permute-done.8.three_ref = bf16[2,2,2,32,128]{4,3,2,1,0:T(8,128)(2,1)S(1)} collective-permute-done((bf16[2,2,2,32,128]{4,3,2,1,0:T(8,128)(2,1)S(1)}, bf16[2,2,2,32,128]{4,3,2,1,0:T(8,128)(2,1)S(1)}, u32[]{:S(2)}, u32[]{:S(2)}) %collective-permute-start.8) | collective-permute-done | bytes 65568 | tf_op jit(solution)/shard_map/ppermute | solution.py:457
  127.2 1.8 %shard_map.128 = (bf16[8,4,32,128]{3,2,1,0:T(8,128)(2,1)}, bf16[8,4,32,128]{3,2,1,0:T(8,128)(2,1)}, bf16[16,32,128]{2,1,0:T(8,128)(2,1)S(1)}) custom-call(bf16[2,2,2,32,128]{4,3,2,1,0:T(8,128)(2,1)S(1)} %get-tuple-element.68.zero_ref, bf16[2,2,2,32,128]{4,3,2,1,0:T(8,128)(2,1)S(1)} %collective-permute-done.6.one_ref, ...), custom_call_target="tpu_custom_call" | custom-call | flops 10000000 | bytes 1000000 | tf_op jit(solution)/shard_map/pallas_call | solution.py:458
  129.0 11.6 %all-to-all-start.5 = ((bf16[8,4,32,128]{3,2,1,0:T(8,128)(2,1)}), bf16[8,4,32,128]{3,2,1,0:T(8,128)(2,1)S(1)}, u32[]{:S(2)}, u32[]{:S(2)}) async-start(bf16[8,4,32,128]{3,2,1,0:T(8,128)(2,1)} %get-tuple-element.78), calls=%async_computation.5 | async-start | bytes 524288 | tf_op jit(solution)/shard_map/all_to_all | solution.py:319
  140.6 2.8 %collective-permute-start.9 = (f32[1,8,256]{2,1,0:T(8,128)S(1)}, f32[1,8,256]{2,1,0:T(8,128)S(1)}, u32[]{:S(2)}, u32[]{:S(2)}) collective-permute-start(f32[1,8,256]{2,1,0:T(8,128)S(1)} %get-tuple-element.79.one_ref), channel_id=1, source_target_pairs={{0,128},{8,136},{16,144},{24,152},{32,160},{40,168},{48,176},{56,1... | collective-permute-start | bytes 24584 | tf_op jit(solution)/shard_map/ppermute | solution.py:323
  143.3 2.8 %collective-permute-done.9.two_ref = f32[1,8,256]{2,1,0:T(8,128)S(1)} collective-permute-done((f32[1,8,256]{2,1,0:T(8,128)S(1)}, f32[1,8,256]{2,1,0:T(8,128)S(1)}, u32[]{:S(2)}, u32[]{:S(2)}) %collective-permute-start.9) | collective-permute-done | bytes 8224 | tf_op jit(solution)/shard_map/ppermute | solution.py:323
  146.1 1.8 %all-to-all-done.5.b_ref = bf16[8,4,32,128]{3,2,1,0:T(8,128)(2,1)S(1)} async-done(((bf16[8,4,32,128]{3,2,1,0:T(8,128)(2,1)}), bf16[8,4,32,128]{3,2,1,0:T(8,128)(2,1)S(1)}, u32[]{:S(2)}, u32[]{:S(2)}) %all-to-all-start.5) | async-done | bytes 262176 | tf_op jit(solution)/shard_map/all_to_all | solution.py:319
  147.9 6.7 %all-to-all-start.6 = ((bf16[8,4,32,128]{3,2,1,0:T(8,128)(2,1)}), bf16[8,4,32,128]{3,2,1,0:T(8,128)(2,1)S(1)}, u32[]{:S(2)}, u32[]{:S(2)}) async-start(bf16[8,4,32,128]{3,2,1,0:T(8,128)(2,1)} %get-tuple-element.80), calls=%async_computation.6 | async-start | bytes 524288 | tf_op jit(solution)/shard_map/all_to_all | solution.py:319
  155.4 3.3 %collective-permute-start.10 = (f32[2,8,256]{2,1,0:T(8,128)S(1)}, f32[2,8,256]{2,1,0:T(8,128)S(1)}, u32[]{:S(2)}, u32[]{:S(2)}) collective-permute-start(f32[2,8,256]{2,1,0:T(8,128)S(1)} %shard_map.132.one_ref), channel_id=1, source_target_pairs={{0,256},{8,264},{16,272},{24,280},{32,288},{40,296},{48,304},{56,3... | collective-permute-start | bytes 49160 | tf_op jit(solution)/shard_map/ppermute | solution.py:323
  158.8 3.8 %collective-permute-done.10.two_ref = f32[2,8,256]{2,1,0:T(8,128)S(1)} collective-permute-done((f32[2,8,256]{2,1,0:T(8,128)S(1)}, f32[2,8,256]{2,1,0:T(8,128)S(1)}, u32[]{:S(2)}, u32[]{:S(2)}) %collective-permute-start.10) | collective-permute-done | bytes 16416 | tf_op jit(solution)/shard_map/ppermute | solution.py:323
  162.6 1.9 %collective-permute-start.11 = (f32[4,8,256]{2,1,0:T(8,128)S(1)}, f32[4,8,256]{2,1,0:T(8,128)S(1)}, u32[]{:S(2)}, u32[]{:S(2)}) collective-permute-start(f32[4,8,256]{2,1,0:T(8,128)S(1)} %shard_map.134.near_ref), channel_id=1, source_target_pairs={{0,8},{8,0},{16,24},{24,16},{32,40},{40,32},{48,56},{56,48},{64,72... | collective-permute-start | bytes 98312 | tf_op jit(solution)/shard_map/ppermute | solution.py:323
  166.3 1.4 shard_map.133
  (50 shorter events, 15.2 us)
Async XLA Ops:
  0.6 42.9 %copy-start.6 = (s32[56]{0:T(128)S(1)}, s32[56]{0:T(128)}, u32[]{:S(2)}) copy-start(s32[56]{0:T(128)} %dst_ref.7) | copy-start | bytes 676
  0.6 42.9 %copy-start.8 = (s32[56]{0:T(128)S(1)}, s32[56]{0:T(128)}, u32[]{:S(2)}) copy-start(s32[56]{0:T(128)} %src_ref.7) | copy-start | bytes 676
  1.4 0.9 copy-start.3
  3.9 23.0 %all-to-all-start = ((bf16[8,4,32,128]{3,2,1,0:T(8,128)(2,1)}), bf16[8,4,32,128]{3,2,1,0:T(8,128)(2,1)S(1)}, u32[]{:S(2)}, u32[]{:S(2)}) async-start(bf16[8,4,32,128]{3,2,1,0:T(8,128)(2,1)} %get-tuple-element.46), calls=%async_computation | async-start | bytes 524288 | tf_op jit(solution)/shard_map/all_to_all | solution.py:319
  19.6 0.9 copy-start.4
  20.5 2.0 %copy-start = (s32[56,128,128]{2,1,0:T(8,128)S(1)}, s32[56,128,128]{2,1,0:T(8,128)}, u32[]{:S(2)}) copy-start(s32[56,128,128]{2,1,0:T(8,128)} %cnt_ref.1) | copy-start | bytes 11010052
  22.6 0.7 copy-start.5
  23.2 0.7 copy-start.7
  23.9 44.6 %copy-start.2 = (bf16[256,256]{1,0:T(8,128)(2,1)S(1)}, bf16[256,256]{1,0:T(8,128)(2,1)}, u32[]{:S(2)}) copy-start(bf16[256,256]{1,0:T(8,128)(2,1)} %own_w_ref.1) | copy-start | bytes 393220
  23.9 44.7 %copy-start.1 = (bf16[256,256]{1,0:T(8,128)(2,1)S(1)}, bf16[256,256]{1,0:T(8,128)(2,1)}, u32[]{:S(2)}) copy-start(bf16[256,256]{1,0:T(8,128)(2,1)} %neigh_ref.1) | copy-start | bytes 393220
  23.9 44.8 %copy-start.9 = (f32[256]{0:T(256)S(1)}, f32[256]{0:T(256)}, u32[]{:S(2)}) copy-start(f32[256]{0:T(256)} %param.16) | copy-start | bytes 3076
  26.9 16.6 %all-to-all-start.1 = ((bf16[8,4,32,128]{3,2,1,0:T(8,128)(2,1)}), bf16[8,4,32,128]{3,2,1,0:T(8,128)(2,1)S(1)}, u32[]{:S(2)}, u32[]{:S(2)}) async-start(bf16[8,4,32,128]{3,2,1,0:T(8,128)(2,1)} %get-tuple-element.54), calls=%async_computation.1 | async-start | bytes 524288 | tf_op jit(solution)/shard_map/all_to_all | solution.py:319
  31.8 22.9 %collective-permute-start = (bf16[4,2,2,32,128]{4,3,2,1,0:T(8,128)(2,1)S(1)}, bf16[4,2,2,32,128]{4,3,2,1,0:T(8,128)(2,1)S(1)}, u32[]{:S(2)}, u32[]{:S(2)}) collective-permute-start(bf16[4,2,2,32,128]{4,3,2,1,0:T(8,128)(2,1)S(1)} %get-tuple-element.52), channel_id=1, source_target_pairs={{0,64},{1,65},{2,66},{3,67},{4,68},{5,69},{6,70},{7,71},{8,72},{9,... | collective-permute-start | bytes 393224 | tf_op jit(solution)/shard_map/ppermute | solution.py:345
  36.5 19.4 %collective-permute-start.1 = (bf16[4,2,2,32,128]{4,3,2,1,0:T(8,128)(2,1)S(1)}, bf16[4,2,2,32,128]{4,3,2,1,0:T(8,128)(2,1)S(1)}, u32[]{:S(2)}, u32[]{:S(2)}) collective-permute-start(bf16[4,2,2,32,128]{4,3,2,1,0:T(8,128)(2,1)S(1)} %get-tuple-element.53), channel_id=1, source_target_pairs={{0,65},{1,64},{2,67},{3,66},{4,69},{5,68},{6,71},{7,70},{8,73},{9,... | collective-permute-start | bytes 393224 | tf_op jit(solution)/shard_map/ppermute | solution.py:345
  44.9 17.1 %collective-permute-start.2 = (bf16[4,2,32,128]{3,2,1,0:T(8,128)(2,1)S(1)}, bf16[4,2,32,128]{3,2,1,0:T(8,128)(2,1)S(1)}, u32[]{:S(2)}, u32[]{:S(2)}) collective-permute-start(bf16[4,2,32,128]{3,2,1,0:T(8,128)(2,1)S(1)} %get-tuple-element.58), channel_id=1, source_target_pairs={{0,64},{1,65},{2,66},{3,67},{4,68},{5,69},{6,70},{7,71},{8,72},{9,... | collective-permute-start | bytes 196616 | tf_op jit(solution)/shard_map/ppermute | solution.py:345
  48.1 14.9 %collective-permute-start.3 = (bf16[4,2,32,128]{3,2,1,0:T(8,128)(2,1)S(1)}, bf16[4,2,32,128]{3,2,1,0:T(8,128)(2,1)S(1)}, u32[]{:S(2)}, u32[]{:S(2)}) collective-permute-start(bf16[4,2,32,128]{3,2,1,0:T(8,128)(2,1)S(1)} %get-tuple-element.59), channel_id=1, source_target_pairs={{0,65},{1,64},{2,67},{3,66},{4,69},{5,68},{6,71},{7,70},{8,73},{9,... | collective-permute-start | bytes 196616 | tf_op jit(solution)/shard_map/ppermute | solution.py:345
  63.7 10.1 %all-to-all-start.2 = ((bf16[4,3,2,2,32,128]{5,4,3,2,1,0:T(8,128)(2,1)}), bf16[4,3,2,2,32,128]{5,4,3,2,1,0:T(8,128)(2,1)S(1)}, u32[]{:S(2)}, u32[]{:S(2)}) async-start(bf16[4,3,2,2,32,128]{5,4,3,2,1,0:T(8,128)(2,1)} %shard_map.124), calls=%async_computation.2 | async-start | bytes 786432 | tf_op jit(solution)/shard_map/all_to_all | solution.py:328
  74.7 19.5 %collective-permute-start.4 = (bf16[4,2,2,32,128]{4,3,2,1,0:T(8,128)(2,1)S(1)}, bf16[4,2,2,32,128]{4,3,2,1,0:T(8,128)(2,1)S(1)}, u32[]{:S(2)}, u32[]{:S(2)}) collective-permute-start(bf16[4,2,2,32,128]{4,3,2,1,0:T(8,128)(2,1)S(1)} %get-tuple-element.62), channel_id=1, source_target_pairs={{0,64},{1,65},{2,66},{3,67},{4,68},{5,69},{6,70},{7,71},{8,72},{9,... | collective-permute-start | bytes 393224 | tf_op jit(solution)/shard_map/ppermute | solution.py:345
  81.4 12.8 %collective-permute-start.5 = (bf16[4,2,2,32,128]{4,3,2,1,0:T(8,128)(2,1)S(1)}, bf16[4,2,2,32,128]{4,3,2,1,0:T(8,128)(2,1)S(1)}, u32[]{:S(2)}, u32[]{:S(2)}) collective-permute-start(bf16[4,2,2,32,128]{4,3,2,1,0:T(8,128)(2,1)S(1)} %get-tuple-element.63), channel_id=1, source_target_pairs={{0,65},{1,64},{2,67},{3,66},{4,69},{5,68},{6,71},{7,70},{8,73},{9,... | collective-permute-start | bytes 393224 | tf_op jit(solution)/shard_map/ppermute | solution.py:345
  85.6 17.4 %all-to-all-start.3 = ((bf16[32,16,384]{2,1,0:T(8,128)(2,1)}), bf16[32,16,384]{2,1,0:T(8,128)(2,1)S(1)}, u32[]{:S(2)}, u32[]{:S(2)}) async-start(bf16[32,16,384]{2,1,0:T(8,128)(2,1)} %shard_map.126), calls=%async_computation.3 | async-start | bytes 786432 | tf_op jit(solution)/shard_map/all_to_all | solution.py:449
  103.7 25.2 %all-to-all-start.4 = ((bf16[16,8,384]{2,1,0:T(8,128)(2,1)}), bf16[16,8,384]{2,1,0:T(8,128)(2,1)S(1)}, u32[]{:S(2)}, u32[]{:S(2)}) async-start(bf16[16,8,384]{2,1,0:T(8,128)(2,1)} %shard_map.130), calls=%async_computation.4 | async-start | bytes 196608 | tf_op jit(solution)/shard_map/all_to_all | solution.py:455
  113.6 8.4 %collective-permute-start.6 = (bf16[2,2,2,32,128]{4,3,2,1,0:T(8,128)(2,1)S(1)}, bf16[2,2,2,32,128]{4,3,2,1,0:T(8,128)(2,1)S(1)}, u32[]{:S(2)}, u32[]{:S(2)}) collective-permute-start(bf16[2,2,2,32,128]{4,3,2,1,0:T(8,128)(2,1)S(1)} %get-tuple-element.69), channel_id=1, source_target_pairs={{0,2},{1,3},{2,4},{3,5},{4,6},{5,7},{6,0},{7,1},{8,10},{9,11},{10,... | collective-permute-start | bytes 196616 | tf_op jit(solution)/shard_map/ppermute | solution.py:457
  117.3 7.7 %collective-permute-start.7 = (bf16[2,2,2,32,128]{4,3,2,1,0:T(8,128)(2,1)S(1)}, bf16[2,2,2,32,128]{4,3,2,1,0:T(8,128)(2,1)S(1)}, u32[]{:S(2)}, u32[]{:S(2)}) collective-permute-start(bf16[2,2,2,32,128]{4,3,2,1,0:T(8,128)(2,1)S(1)} %get-tuple-element.70), channel_id=1, source_target_pairs={{0,4},{1,5},{2,6},{3,7},{4,0},{5,1},{6,2},{7,3},{8,12},{9,13},{10,... | collective-permute-start | bytes 196616 | tf_op jit(solution)/shard_map/ppermute | solution.py:457
  119.8 7.4 %collective-permute-start.8 = (bf16[2,2,2,32,128]{4,3,2,1,0:T(8,128)(2,1)S(1)}, bf16[2,2,2,32,128]{4,3,2,1,0:T(8,128)(2,1)S(1)}, u32[]{:S(2)}, u32[]{:S(2)}) collective-permute-start(bf16[2,2,2,32,128]{4,3,2,1,0:T(8,128)(2,1)S(1)} %get-tuple-element.71), channel_id=1, source_target_pairs={{0,6},{1,7},{2,0},{3,1},{4,2},{5,3},{6,4},{7,5},{8,14},{9,15},{10,... | collective-permute-start | bytes 196616 | tf_op jit(solution)/shard_map/ppermute | solution.py:457
  129.0 18.9 %all-to-all-start.5 = ((bf16[8,4,32,128]{3,2,1,0:T(8,128)(2,1)}), bf16[8,4,32,128]{3,2,1,0:T(8,128)(2,1)S(1)}, u32[]{:S(2)}, u32[]{:S(2)}) async-start(bf16[8,4,32,128]{3,2,1,0:T(8,128)(2,1)} %get-tuple-element.78), calls=%async_computation.5 | async-start | bytes 524288 | tf_op jit(solution)/shard_map/all_to_all | solution.py:319
  140.6 5.5 %collective-permute-start.9 = (f32[1,8,256]{2,1,0:T(8,128)S(1)}, f32[1,8,256]{2,1,0:T(8,128)S(1)}, u32[]{:S(2)}, u32[]{:S(2)}) collective-permute-start(f32[1,8,256]{2,1,0:T(8,128)S(1)} %get-tuple-element.79.one_ref), channel_id=1, source_target_pairs={{0,128},{8,136},{16,144},{24,152},{32,160},{40,168},{48,176},{56,1... | collective-permute-start | bytes 24584 | tf_op jit(solution)/shard_map/ppermute | solution.py:323
  147.9 18.4 %all-to-all-start.6 = ((bf16[8,4,32,128]{3,2,1,0:T(8,128)(2,1)}), bf16[8,4,32,128]{3,2,1,0:T(8,128)(2,1)S(1)}, u32[]{:S(2)}, u32[]{:S(2)}) async-start(bf16[8,4,32,128]{3,2,1,0:T(8,128)(2,1)} %get-tuple-element.80), calls=%async_computation.6 | async-start | bytes 524288 | tf_op jit(solution)/shard_map/all_to_all | solution.py:319
  155.4 7.1 %collective-permute-start.10 = (f32[2,8,256]{2,1,0:T(8,128)S(1)}, f32[2,8,256]{2,1,0:T(8,128)S(1)}, u32[]{:S(2)}, u32[]{:S(2)}) collective-permute-start(f32[2,8,256]{2,1,0:T(8,128)S(1)} %shard_map.132.one_ref), channel_id=1, source_target_pairs={{0,256},{8,264},{16,272},{24,280},{32,288},{40,296},{48,304},{56,3... | collective-permute-start | bytes 49160 | tf_op jit(solution)/shard_map/ppermute | solution.py:323
  162.6 3.1 %collective-permute-start.11 = (f32[4,8,256]{2,1,0:T(8,128)S(1)}, f32[4,8,256]{2,1,0:T(8,128)S(1)}, u32[]{:S(2)}, u32[]{:S(2)}) collective-permute-start(f32[4,8,256]{2,1,0:T(8,128)S(1)} %shard_map.134.near_ref), channel_id=1, source_target_pairs={{0,8},{8,0},{16,24},{24,16},{32,40},{40,32},{48,56},{56,48},{64,72... | collective-permute-start | bytes 98312 | tf_op jit(solution)/shard_map/ppermute | solution.py:323

commit v10 on v9

--- a/solution.py
+++ b/solution.py
@@ -150,7 +150,8 @@
     mine = blk // (Z_LO * CORE) * CORE + lax.rem(blk, CORE)
     for piece in range(Y * CORE):
         offset = jnp.bitwise_xor(mine, piece)
-        rows = jnp.where(lax.rem(offset, 2) == 0, near_ref[offset // 2], far_ref[offset // 2])
+        place = lax.rem(offset, 4)
+        rows = jnp.where(offset < 4, near_ref[place], far_ref[place])
         out = self_ref if piece < 4 else neigh_ref
         out[piece % 4 * 8 : piece % 4 * 8 + 8] = rows
 
@@ -471,21 +472,20 @@
     grad_bias = lax.dynamic_slice_in_dim(grad_bias, lax.axis_index("col") * dim, dim, 0)
     away_b, rows = lax.optimization_barrier((away_b, rows))
     back_b = swap(away_b, GROUP // 2)
-    pair = call(pair_kernel, jax.ShapeDtypeStruct((2, 8, full), F32), [VMEM] * 2)(
-        rows, across(rows, Z_LO * CORE)
-    )
-    away_a, back_b, pair = lax.optimization_barrier((away_a, back_b, pair))
-    back_a = swap(away_a, 0)
-    rows = call(pair_kernel, jax.ShapeDtypeStruct((4, 8, full), F32), [VMEM] * 2)(
-        pair, across(pair, 2 * Z_LO * CORE)
-    )
-    grad = jax.ShapeDtypeStruct((dim, full), F32)
-    grad_self, grad_neigh = call(order_kernel, (grad, grad), [VMEM] * 2)(rows, across(rows, 1))
+    for bit in (1, Z_LO * CORE):
+        double = jax.ShapeDtypeStruct((2 * rows.shape[0], 8, full), F32)
+        rows = call(pair_kernel, double, [VMEM] * 2)(rows, across(rows, bit))
     acc = call(
         functools.partial(local_back_kernel, slots),
         jax.ShapeDtypeStruct((blocks, dim, width), F32),
         [VMEM] * 5 + [SMEM, SMEM, VMEM],
     )(*home, scaled, tile_dst, tile_src, half)
+    away_a, back_b, rows, acc = lax.optimization_barrier((away_a, back_b, rows, acc))
+    back_a = swap(away_a, 0)
+    grad = jax.ShapeDtypeStruct((dim, full), F32)
+    grad_self, grad_neigh = call(order_kernel, (grad, grad), [VMEM] * 2)(
+        rows, across(rows, 2 * Z_LO * CORE)
+    )
     grad_feats = call(
         finish_kernel,
         jax.ShapeDtypeStruct((dim, nodes), BF16),

time: 171 us -> 168 us (0.982)
  starting transfers between devices: 110 us -> 108 us
where the time goes in v10:
time: 168 us; the launch traced here: 166 us
  starting transfers between devices  108 us (64%)
  waiting for transfers between devices  36.5 us (22%)
  Pallas kernels  13 us (8%)
  local copies, waits for them, and re-layouts  6.86 us (4%)
    all_to_all x4, starting transfers between devices, swap(): lax.all_to_all(rows, 'blk', 0, 0, axis_index_groups=groups, tiled=False)  37.4 us
    ppermute x6, starting transfers between devices, along_z(): return lax.ppermute(rows, ('blk', 'col'), sorted(route))  31.2 us
    all_to_all x1, starting transfers between devices, per_device(): part = lax.all_to_all(part, both, 0, 0, axis_index_groups=line, tiled=False)  9.89 us
    all_to_all x1, waiting for transfers between devices, per_device(): part = lax.all_to_all(part, both, 0, 0, axis_index_groups=flat, tiled=False)  8.72 us
    all_to_all x1, starting transfers between devices, per_device(): part = lax.all_to_all(part, both, 0, 0, axis_index_groups=flat, tiled=False)  8.65 us
    ppermute x3, starting transfers between devices, per_device(): lax.ppermute(home[turn], 'col', route(turn))  8.38 us
    ppermute x6, waiting for transfers between devices, along_z(): return lax.ppermute(rows, ('blk', 'col'), sorted(route))  8.33 us
    ppermute x3, starting transfers between devices, across(): lax.ppermute(rows, 'blk', [(e, e ^ bit) for e in range(lax.axis_size('blk...  8.12 us
  transfers between devices with their start and end apart: 19, of which 12 were waited for; matrix products, arithmetic and copies ran while one was open for 1% of the time, Pallas kernels for 5%

profile of v10, /device:TPU:6, one launch (start us, length us, event | category | flops | bytes accessed | tf_op | source)
XLA Modules:
  0.0 165.8 jit_solution(15317359792963676706)
XLA Ops:
  2.3 1.6 shard_map.120
  3.9 15.7 %all-to-all-start = ((bf16[8,4,32,128]{3,2,1,0:T(8,128)(2,1)}), bf16[8,4,32,128]{3,2,1,0:T(8,128)(2,1)S(1)}, u32[]{:S(2)}, u32[]{:S(2)}) async-start(bf16[8,4,32,128]{3,2,1,0:T(8,128)(2,1)} %get-tuple-element.47), calls=%async_computation | async-start | bytes 524288 | tf_op jit(solution)/shard_map/all_to_all | solution.py:320
  20.6 2.0 %copy-done = s32[56,128,128]{2,1,0:T(8,128)S(1)} copy-done((s32[56,128,128]{2,1,0:T(8,128)S(1)}, s32[56,128,128]{2,1,0:T(8,128)}, u32[]{:S(2)}) %copy-start) | copy-done | bytes 3670040
  23.9 1.8 %shard_map.122 = (bf16[56,128,128]{2,1,0:T(8,128)(2,1)S(1)}, f32[16,40,128]{2,1,0:T(8,128)S(1)}) custom-call(bf16[16,32,128]{2,1,0:T(8,128)(2,1)S(1)} %get-tuple-element.48.x_ref, s32[56]{0:T(128)S(1)} %copy-done.5, s32[56]{0:T(128)S(1)} %copy-done.7, s32[56,128,128]{2,1,0:T(8,128)S(1)} %copy-done), custom_call_target="tpu_custom_call" | custom-call | flops 60000000 | bytes 6000000 | tf_op jit(solution)/shard_map/pallas_call | solution.py:374
  26.9 4.8 %all-to-all-start.1 = ((bf16[8,4,32,128]{3,2,1,0:T(8,128)(2,1)}), bf16[8,4,32,128]{3,2,1,0:T(8,128)(2,1)S(1)}, u32[]{:S(2)}, u32[]{:S(2)}) async-start(bf16[8,4,32,128]{3,2,1,0:T(8,128)(2,1)} %get-tuple-element.55), calls=%async_computation.1 | async-start | bytes 524288 | tf_op jit(solution)/shard_map/all_to_all | solution.py:320
  31.8 4.7 %collective-permute-start = (bf16[4,2,2,32,128]{4,3,2,1,0:T(8,128)(2,1)S(1)}, bf16[4,2,2,32,128]{4,3,2,1,0:T(8,128)(2,1)S(1)}, u32[]{:S(2)}, u32[]{:S(2)}) collective-permute-start(bf16[4,2,2,32,128]{4,3,2,1,0:T(8,128)(2,1)S(1)} %get-tuple-element.53), channel_id=1, source_target_pairs={{0,64},{1,65},{2,66},{3,67},{4,68},{5,69},{6,70},{7,71},{8,72},{9,... | collective-permute-start | bytes 393224 | tf_op jit(solution)/shard_map/ppermute | solution.py:346
  36.5 7.0 %collective-permute-start.1 = (bf16[4,2,2,32,128]{4,3,2,1,0:T(8,128)(2,1)S(1)}, bf16[4,2,2,32,128]{4,3,2,1,0:T(8,128)(2,1)S(1)}, u32[]{:S(2)}, u32[]{:S(2)}) collective-permute-start(bf16[4,2,2,32,128]{4,3,2,1,0:T(8,128)(2,1)S(1)} %get-tuple-element.54), channel_id=1, source_target_pairs={{0,65},{1,64},{2,67},{3,66},{4,69},{5,68},{6,71},{7,70},{8,73},{9,... | collective-permute-start | bytes 393224 | tf_op jit(solution)/shard_map/ppermute | solution.py:346
  44.9 3.2 %collective-permute-start.2 = (bf16[4,2,32,128]{3,2,1,0:T(8,128)(2,1)S(1)}, bf16[4,2,32,128]{3,2,1,0:T(8,128)(2,1)S(1)}, u32[]{:S(2)}, u32[]{:S(2)}) collective-permute-start(bf16[4,2,32,128]{3,2,1,0:T(8,128)(2,1)S(1)} %get-tuple-element.59), channel_id=1, source_target_pairs={{0,64},{1,65},{2,66},{3,67},{4,68},{5,69},{6,70},{7,71},{8,72},{9,... | collective-permute-start | bytes 196616 | tf_op jit(solution)/shard_map/ppermute | solution.py:346
  48.1 6.6 %collective-permute-start.3 = (bf16[4,2,32,128]{3,2,1,0:T(8,128)(2,1)S(1)}, bf16[4,2,32,128]{3,2,1,0:T(8,128)(2,1)S(1)}, u32[]{:S(2)}, u32[]{:S(2)}) collective-permute-start(bf16[4,2,32,128]{3,2,1,0:T(8,128)(2,1)S(1)} %get-tuple-element.60), channel_id=1, source_target_pairs={{0,65},{1,64},{2,67},{3,66},{4,69},{5,68},{6,71},{7,70},{8,73},{9,... | collective-permute-start | bytes 196616 | tf_op jit(solution)/shard_map/ppermute | solution.py:346
  55.9 6.2 %collective-permute-done.2.agg_plus_ref = bf16[4,2,32,128]{3,2,1,0:T(8,128)(2,1)S(1)} collective-permute-done((bf16[4,2,32,128]{3,2,1,0:T(8,128)(2,1)S(1)}, bf16[4,2,32,128]{3,2,1,0:T(8,128)(2,1)S(1)}, u32[]{:S(2)}, u32[]{:S(2)}) %collective-permute-start.2) | collective-permute-done | bytes 65568 | tf_op jit(solution)/shard_map/ppermute | solution.py:346
  63.7 4.8 %all-to-all-start.2 = ((bf16[4,3,2,2,32,128]{5,4,3,2,1,0:T(8,128)(2,1)}), bf16[4,3,2,2,32,128]{5,4,3,2,1,0:T(8,128)(2,1)S(1)}, u32[]{:S(2)}, u32[]{:S(2)}) async-start(bf16[4,3,2,2,32,128]{5,4,3,2,1,0:T(8,128)(2,1)} %shard_map.124), calls=%async_computation.2 | async-start | bytes 786432 | tf_op jit(solution)/shard_map/all_to_all | solution.py:329
  68.9 4.9 %all-to-all-done.2.in_ref = bf16[4,3,2,2,32,128]{5,4,3,2,1,0:T(8,128)(2,1)S(1)} async-done(((bf16[4,3,2,2,32,128]{5,4,3,2,1,0:T(8,128)(2,1)}), bf16[4,3,2,2,32,128]{5,4,3,2,1,0:T(8,128)(2,1)S(1)}, u32[]{:S(2)}, u32[]{:S(2)}) %all-to-all-start.2) | async-done | bytes 393248 | tf_op jit(solution)/shard_map/all_to_all | solution.py:329
  74.7 6.7 %collective-permute-start.4 = (bf16[4,2,2,32,128]{4,3,2,1,0:T(8,128)(2,1)S(1)}, bf16[4,2,2,32,128]{4,3,2,1,0:T(8,128)(2,1)S(1)}, u32[]{:S(2)}, u32[]{:S(2)}) collective-permute-start(bf16[4,2,2,32,128]{4,3,2,1,0:T(8,128)(2,1)S(1)} %get-tuple-element.63), channel_id=1, source_target_pairs={{0,64},{1,65},{2,66},{3,67},{4,68},{5,69},{6,70},{7,71},{8,72},{9,... | collective-permute-start | bytes 393224 | tf_op jit(solution)/shard_map/ppermute | solution.py:346
  81.4 3.1 %collective-permute-start.5 = (bf16[4,2,2,32,128]{4,3,2,1,0:T(8,128)(2,1)S(1)}, bf16[4,2,2,32,128]{4,3,2,1,0:T(8,128)(2,1)S(1)}, u32[]{:S(2)}, u32[]{:S(2)}) collective-permute-start(bf16[4,2,2,32,128]{4,3,2,1,0:T(8,128)(2,1)S(1)} %get-tuple-element.64), channel_id=1, source_target_pairs={{0,65},{1,64},{2,67},{3,66},{4,69},{5,68},{6,71},{7,70},{8,73},{9,... | collective-permute-start | bytes 393224 | tf_op jit(solution)/shard_map/ppermute | solution.py:346
  85.6 8.7 %all-to-all-start.3 = ((bf16[32,16,384]{2,1,0:T(8,128)(2,1)}), bf16[32,16,384]{2,1,0:T(8,128)(2,1)S(1)}, u32[]{:S(2)}, u32[]{:S(2)}) async-start(bf16[32,16,384]{2,1,0:T(8,128)(2,1)} %shard_map.126), calls=%async_computation.3 | async-start | bytes 786432 | tf_op jit(solution)/shard_map/all_to_all | solution.py:450
  94.3 8.7 %all-to-all-done.3.part_ref = bf16[32,16,384]{2,1,0:T(8,128)(2,1)S(1)} async-done(((bf16[32,16,384]{2,1,0:T(8,128)(2,1)}), bf16[32,16,384]{2,1,0:T(8,128)(2,1)S(1)}, u32[]{:S(2)}, u32[]{:S(2)}) %all-to-all-start.3) | async-done | bytes 393248 | tf_op jit(solution)/shard_map/all_to_all | solution.py:450
  103.7 9.9 %all-to-all-start.4 = ((bf16[16,8,384]{2,1,0:T(8,128)(2,1)}), bf16[16,8,384]{2,1,0:T(8,128)(2,1)S(1)}, u32[]{:S(2)}, u32[]{:S(2)}) async-start(bf16[16,8,384]{2,1,0:T(8,128)(2,1)} %shard_map.129), calls=%async_computation.4 | async-start | bytes 196608 | tf_op jit(solution)/shard_map/all_to_all | solution.py:456
  113.6 3.7 %collective-permute-start.6 = (bf16[2,2,2,32,128]{4,3,2,1,0:T(8,128)(2,1)S(1)}, bf16[2,2,2,32,128]{4,3,2,1,0:T(8,128)(2,1)S(1)}, u32[]{:S(2)}, u32[]{:S(2)}) collective-permute-start(bf16[2,2,2,32,128]{4,3,2,1,0:T(8,128)(2,1)S(1)} %get-tuple-element.70), channel_id=1, source_target_pairs={{0,2},{1,3},{2,4},{3,5},{4,6},{5,7},{6,0},{7,1},{8,10},{9,11},{10,... | collective-permute-start | bytes 196616 | tf_op jit(solution)/shard_map/ppermute | solution.py:458
  117.3 2.5 %collective-permute-start.7 = (bf16[2,2,2,32,128]{4,3,2,1,0:T(8,128)(2,1)S(1)}, bf16[2,2,2,32,128]{4,3,2,1,0:T(8,128)(2,1)S(1)}, u32[]{:S(2)}, u32[]{:S(2)}) collective-permute-start(bf16[2,2,2,32,128]{4,3,2,1,0:T(8,128)(2,1)S(1)} %get-tuple-element.71), channel_id=1, source_target_pairs={{0,4},{1,5},{2,6},{3,7},{4,0},{5,1},{6,2},{7,3},{8,12},{9,13},{10,... | collective-permute-start | bytes 196616 | tf_op jit(solution)/shard_map/ppermute | solution.py:458
  119.8 2.2 %collective-permute-start.8 = (bf16[2,2,2,32,128]{4,3,2,1,0:T(8,128)(2,1)S(1)}, bf16[2,2,2,32,128]{4,3,2,1,0:T(8,128)(2,1)S(1)}, u32[]{:S(2)}, u32[]{:S(2)}) collective-permute-start(bf16[2,2,2,32,128]{4,3,2,1,0:T(8,128)(2,1)S(1)} %get-tuple-element.72), channel_id=1, source_target_pairs={{0,6},{1,7},{2,0},{3,1},{4,2},{5,3},{6,4},{7,5},{8,14},{9,15},{10,... | collective-permute-start | bytes 196616 | tf_op jit(solution)/shard_map/ppermute | solution.py:458
  122.0 3.0 %collective-permute-done.7.two_ref = bf16[2,2,2,32,128]{4,3,2,1,0:T(8,128)(2,1)S(1)} collective-permute-done((bf16[2,2,2,32,128]{4,3,2,1,0:T(8,128)(2,1)S(1)}, bf16[2,2,2,32,128]{4,3,2,1,0:T(8,128)(2,1)S(1)}, u32[]{:S(2)}, u32[]{:S(2)}) %collective-permute-start.7) | collective-permute-done | bytes 65568 | tf_op jit(solution)/shard_map/ppermute | solution.py:458
  125.0 2.1 %collective-permute-done.8.three_ref = bf16[2,2,2,32,128]{4,3,2,1,0:T(8,128)(2,1)S(1)} collective-permute-done((bf16[2,2,2,32,128]{4,3,2,1,0:T(8,128)(2,1)S(1)}, bf16[2,2,2,32,128]{4,3,2,1,0:T(8,128)(2,1)S(1)}, u32[]{:S(2)}, u32[]{:S(2)}) %collective-permute-start.8) | collective-permute-done | bytes 65568 | tf_op jit(solution)/shard_map/ppermute | solution.py:458
  127.2 1.8 %shard_map.128 = (bf16[8,4,32,128]{3,2,1,0:T(8,128)(2,1)}, bf16[8,4,32,128]{3,2,1,0:T(8,128)(2,1)}, bf16[16,32,128]{2,1,0:T(8,128)(2,1)S(1)}) custom-call(bf16[2,2,2,32,128]{4,3,2,1,0:T(8,128)(2,1)S(1)} %get-tuple-element.69.zero_ref, bf16[2,2,2,32,128]{4,3,2,1,0:T(8,128)(2,1)S(1)} %collective-permute-done.6.one_ref, ...), custom_call_target="tpu_custom_call" | custom-call | flops 10000000 | bytes 1000000 | tf_op jit(solution)/shard_map/pallas_call | solution.py:459
  129.0 11.6 %all-to-all-start.5 = ((bf16[8,4,32,128]{3,2,1,0:T(8,128)(2,1)}), bf16[8,4,32,128]{3,2,1,0:T(8,128)(2,1)S(1)}, u32[]{:S(2)}, u32[]{:S(2)}) async-start(bf16[8,4,32,128]{3,2,1,0:T(8,128)(2,1)} %get-tuple-element.78), calls=%async_computation.5 | async-start | bytes 524288 | tf_op jit(solution)/shard_map/all_to_all | solution.py:320
  140.6 2.0 %collective-permute-start.9 = (f32[1,8,256]{2,1,0:T(8,128)S(1)}, f32[1,8,256]{2,1,0:T(8,128)S(1)}, u32[]{:S(2)}, u32[]{:S(2)}) collective-permute-start(f32[1,8,256]{2,1,0:T(8,128)S(1)} %get-tuple-element.79.one_ref), channel_id=1, source_target_pairs={{0,8},{8,0},{16,24},{24,16},{32,40},{40,32},{48,56},{56,48},{64,72... | collective-permute-start | bytes 24584 | tf_op jit(solution)/shard_map/ppermute | solution.py:324
  143.6 2.7 %collective-permute-start.10 = (f32[2,8,256]{2,1,0:T(8,128)S(1)}, f32[2,8,256]{2,1,0:T(8,128)S(1)}, u32[]{:S(2)}, u32[]{:S(2)}) collective-permute-start(f32[2,8,256]{2,1,0:T(8,128)S(1)} %shard_map.131.one_ref), channel_id=1, source_target_pairs={{0,128},{8,136},{16,144},{24,152},{32,160},{40,168},{48,176},{56,1... | collective-permute-start | bytes 49160 | tf_op jit(solution)/shard_map/ppermute | solution.py:324
  147.2 2.0 %collective-permute-done.10.two_ref = f32[2,8,256]{2,1,0:T(8,128)S(1)} collective-permute-done((f32[2,8,256]{2,1,0:T(8,128)S(1)}, f32[2,8,256]{2,1,0:T(8,128)S(1)}, u32[]{:S(2)}, u32[]{:S(2)}) %collective-permute-start.10) | collective-permute-done | bytes 16416 | tf_op jit(solution)/shard_map/ppermute | solution.py:324
  149.2 5.3 %all-to-all-start.6 = ((bf16[8,4,32,128]{3,2,1,0:T(8,128)(2,1)}), bf16[8,4,32,128]{3,2,1,0:T(8,128)(2,1)S(1)}, u32[]{:S(2)}, u32[]{:S(2)}) async-start(bf16[8,4,32,128]{3,2,1,0:T(8,128)(2,1)} %get-tuple-element.82), calls=%async_computation.6 | async-start | bytes 524288 | tf_op jit(solution)/shard_map/all_to_all | solution.py:320
  154.6 3.3 %collective-permute-start.11 = (f32[4,8,256]{2,1,0:T(8,128)S(1)}, f32[4,8,256]{2,1,0:T(8,128)S(1)}, u32[]{:S(2)}, u32[]{:S(2)}) collective-permute-start(f32[4,8,256]{2,1,0:T(8,128)S(1)} %shard_map.132.near_ref), channel_id=1, source_target_pairs={{0,256},{8,264},{16,272},{24,280},{32,288},{40,296},{48,304},{56,3... | collective-permute-start | bytes 98312 | tf_op jit(solution)/shard_map/ppermute | solution.py:324
  158.5 3.4 %collective-permute-done.11.far_ref = f32[4,8,256]{2,1,0:T(8,128)S(1)} collective-permute-done((f32[4,8,256]{2,1,0:T(8,128)S(1)}, f32[4,8,256]{2,1,0:T(8,128)S(1)}, u32[]{:S(2)}, u32[]{:S(2)}) %collective-permute-start.11) | collective-permute-done | bytes 32800 | tf_op jit(solution)/shard_map/ppermute | solution.py:324
  162.5 1.8 %all-to-all-done.6.a_ref = bf16[8,4,32,128]{3,2,1,0:T(8,128)(2,1)S(1)} async-done(((bf16[8,4,32,128]{3,2,1,0:T(8,128)(2,1)}), bf16[8,4,32,128]{3,2,1,0:T(8,128)(2,1)S(1)}, u32[]{:S(2)}, u32[]{:S(2)}) %all-to-all-start.6) | async-done | bytes 262176 | tf_op jit(solution)/shard_map/all_to_all | solution.py:320
  164.3 1.4 shard_map.134
  (50 shorter events, 15.6 us)
Async XLA Ops:
  0.6 42.9 %copy-start.6 = (s32[56]{0:T(128)S(1)}, s32[56]{0:T(128)}, u32[]{:S(2)}) copy-start(s32[56]{0:T(128)} %dst_ref.7) | copy-start | bytes 676
  0.6 42.9 %copy-start.8 = (s32[56]{0:T(128)S(1)}, s32[56]{0:T(128)}, u32[]{:S(2)}) copy-start(s32[56]{0:T(128)} %src_ref.7) | copy-start | bytes 676
  1.4 0.9 copy-start.3
  3.9 23.0 %all-to-all-start = ((bf16[8,4,32,128]{3,2,1,0:T(8,128)(2,1)}), bf16[8,4,32,128]{3,2,1,0:T(8,128)(2,1)S(1)}, u32[]{:S(2)}, u32[]{:S(2)}) async-start(bf16[8,4,32,128]{3,2,1,0:T(8,128)(2,1)} %get-tuple-element.47), calls=%async_computation | async-start | bytes 524288 | tf_op jit(solution)/shard_map/all_to_all | solution.py:320
  19.6 0.9 copy-start.4
  20.5 2.0 %copy-start = (s32[56,128,128]{2,1,0:T(8,128)S(1)}, s32[56,128,128]{2,1,0:T(8,128)}, u32[]{:S(2)}) copy-start(s32[56,128,128]{2,1,0:T(8,128)} %cnt_ref.1) | copy-start | bytes 11010052
  22.6 0.7 copy-start.5
  23.2 0.7 copy-start.7
  23.9 44.6 %copy-start.2 = (bf16[256,256]{1,0:T(8,128)(2,1)S(1)}, bf16[256,256]{1,0:T(8,128)(2,1)}, u32[]{:S(2)}) copy-start(bf16[256,256]{1,0:T(8,128)(2,1)} %own_w_ref.1) | copy-start | bytes 393220
  23.9 44.7 %copy-start.1 = (bf16[256,256]{1,0:T(8,128)(2,1)S(1)}, bf16[256,256]{1,0:T(8,128)(2,1)}, u32[]{:S(2)}) copy-start(bf16[256,256]{1,0:T(8,128)(2,1)} %neigh_ref.1) | copy-start | bytes 393220
  23.9 44.8 %copy-start.9 = (f32[256]{0:T(256)S(1)}, f32[256]{0:T(256)}, u32[]{:S(2)}) copy-start(f32[256]{0:T(256)} %param.16) | copy-start | bytes 3076
  26.9 16.6 %all-to-all-start.1 = ((bf16[8,4,32,128]{3,2,1,0:T(8,128)(2,1)}), bf16[8,4,32,128]{3,2,1,0:T(8,128)(2,1)S(1)}, u32[]{:S(2)}, u32[]{:S(2)}) async-start(bf16[8,4,32,128]{3,2,1,0:T(8,128)(2,1)} %get-tuple-element.55), calls=%async_computation.1 | async-start | bytes 524288 | tf_op jit(solution)/shard_map/all_to_all | solution.py:320
  31.8 22.9 %collective-permute-start = (bf16[4,2,2,32,128]{4,3,2,1,0:T(8,128)(2,1)S(1)}, bf16[4,2,2,32,128]{4,3,2,1,0:T(8,128)(2,1)S(1)}, u32[]{:S(2)}, u32[]{:S(2)}) collective-permute-start(bf16[4,2,2,32,128]{4,3,2,1,0:T(8,128)(2,1)S(1)} %get-tuple-element.53), channel_id=1, source_target_pairs={{0,64},{1,65},{2,66},{3,67},{4,68},{5,69},{6,70},{7,71},{8,72},{9,... | collective-permute-start | bytes 393224 | tf_op jit(solution)/shard_map/ppermute | solution.py:346
  36.5 19.4 %collective-permute-start.1 = (bf16[4,2,2,32,128]{4,3,2,1,0:T(8,128)(2,1)S(1)}, bf16[4,2,2,32,128]{4,3,2,1,0:T(8,128)(2,1)S(1)}, u32[]{:S(2)}, u32[]{:S(2)}) collective-permute-start(bf16[4,2,2,32,128]{4,3,2,1,0:T(8,128)(2,1)S(1)} %get-tuple-element.54), channel_id=1, source_target_pairs={{0,65},{1,64},{2,67},{3,66},{4,69},{5,68},{6,71},{7,70},{8,73},{9,... | collective-permute-start | bytes 393224 | tf_op jit(solution)/shard_map/ppermute | solution.py:346
  44.9 17.1 %collective-permute-start.2 = (bf16[4,2,32,128]{3,2,1,0:T(8,128)(2,1)S(1)}, bf16[4,2,32,128]{3,2,1,0:T(8,128)(2,1)S(1)}, u32[]{:S(2)}, u32[]{:S(2)}) collective-permute-start(bf16[4,2,32,128]{3,2,1,0:T(8,128)(2,1)S(1)} %get-tuple-element.59), channel_id=1, source_target_pairs={{0,64},{1,65},{2,66},{3,67},{4,68},{5,69},{6,70},{7,71},{8,72},{9,... | collective-permute-start | bytes 196616 | tf_op jit(solution)/shard_map/ppermute | solution.py:346
  48.1 14.9 %collective-permute-start.3 = (bf16[4,2,32,128]{3,2,1,0:T(8,128)(2,1)S(1)}, bf16[4,2,32,128]{3,2,1,0:T(8,128)(2,1)S(1)}, u32[]{:S(2)}, u32[]{:S(2)}) collective-permute-start(bf16[4,2,32,128]{3,2,1,0:T(8,128)(2,1)S(1)} %get-tuple-element.60), channel_id=1, source_target_pairs={{0,65},{1,64},{2,67},{3,66},{4,69},{5,68},{6,71},{7,70},{8,73},{9,... | collective-permute-start | bytes 196616 | tf_op jit(solution)/shard_map/ppermute | solution.py:346
  63.7 10.1 %all-to-all-start.2 = ((bf16[4,3,2,2,32,128]{5,4,3,2,1,0:T(8,128)(2,1)}), bf16[4,3,2,2,32,128]{5,4,3,2,1,0:T(8,128)(2,1)S(1)}, u32[]{:S(2)}, u32[]{:S(2)}) async-start(bf16[4,3,2,2,32,128]{5,4,3,2,1,0:T(8,128)(2,1)} %shard_map.124), calls=%async_computation.2 | async-start | bytes 786432 | tf_op jit(solution)/shard_map/all_to_all | solution.py:329
  74.7 19.5 %collective-permute-start.4 = (bf16[4,2,2,32,128]{4,3,2,1,0:T(8,128)(2,1)S(1)}, bf16[4,2,2,32,128]{4,3,2,1,0:T(8,128)(2,1)S(1)}, u32[]{:S(2)}, u32[]{:S(2)}) collective-permute-start(bf16[4,2,2,32,128]{4,3,2,1,0:T(8,128)(2,1)S(1)} %get-tuple-element.63), channel_id=1, source_target_pairs={{0,64},{1,65},{2,66},{3,67},{4,68},{5,69},{6,70},{7,71},{8,72},{9,... | collective-permute-start | bytes 393224 | tf_op jit(solution)/shard_map/ppermute | solution.py:346
  81.4 12.8 %collective-permute-start.5 = (bf16[4,2,2,32,128]{4,3,2,1,0:T(8,128)(2,1)S(1)}, bf16[4,2,2,32,128]{4,3,2,1,0:T(8,128)(2,1)S(1)}, u32[]{:S(2)}, u32[]{:S(2)}) collective-permute-start(bf16[4,2,2,32,128]{4,3,2,1,0:T(8,128)(2,1)S(1)} %get-tuple-element.64), channel_id=1, source_target_pairs={{0,65},{1,64},{2,67},{3,66},{4,69},{5,68},{6,71},{7,70},{8,73},{9,... | collective-permute-start | bytes 393224 | tf_op jit(solution)/shard_map/ppermute | solution.py:346
  85.6 17.4 %all-to-all-start.3 = ((bf16[32,16,384]{2,1,0:T(8,128)(2,1)}), bf16[32,16,384]{2,1,0:T(8,128)(2,1)S(1)}, u32[]{:S(2)}, u32[]{:S(2)}) async-start(bf16[32,16,384]{2,1,0:T(8,128)(2,1)} %shard_map.126), calls=%async_computation.3 | async-start | bytes 786432 | tf_op jit(solution)/shard_map/all_to_all | solution.py:450
  103.7 25.2 %all-to-all-start.4 = ((bf16[16,8,384]{2,1,0:T(8,128)(2,1)}), bf16[16,8,384]{2,1,0:T(8,128)(2,1)S(1)}, u32[]{:S(2)}, u32[]{:S(2)}) async-start(bf16[16,8,384]{2,1,0:T(8,128)(2,1)} %shard_map.129), calls=%async_computation.4 | async-start | bytes 196608 | tf_op jit(solution)/shard_map/all_to_all | solution.py:456
  113.6 8.4 %collective-permute-start.6 = (bf16[2,2,2,32,128]{4,3,2,1,0:T(8,128)(2,1)S(1)}, bf16[2,2,2,32,128]{4,3,2,1,0:T(8,128)(2,1)S(1)}, u32[]{:S(2)}, u32[]{:S(2)}) collective-permute-start(bf16[2,2,2,32,128]{4,3,2,1,0:T(8,128)(2,1)S(1)} %get-tuple-element.70), channel_id=1, source_target_pairs={{0,2},{1,3},{2,4},{3,5},{4,6},{5,7},{6,0},{7,1},{8,10},{9,11},{10,... | collective-permute-start | bytes 196616 | tf_op jit(solution)/shard_map/ppermute | solution.py:458
  117.3 7.7 %collective-permute-start.7 = (bf16[2,2,2,32,128]{4,3,2,1,0:T(8,128)(2,1)S(1)}, bf16[2,2,2,32,128]{4,3,2,1,0:T(8,128)(2,1)S(1)}, u32[]{:S(2)}, u32[]{:S(2)}) collective-permute-start(bf16[2,2,2,32,128]{4,3,2,1,0:T(8,128)(2,1)S(1)} %get-tuple-element.71), channel_id=1, source_target_pairs={{0,4},{1,5},{2,6},{3,7},{4,0},{5,1},{6,2},{7,3},{8,12},{9,13},{10,... | collective-permute-start | bytes 196616 | tf_op jit(solution)/shard_map/ppermute | solution.py:458
  119.8 7.4 %collective-permute-start.8 = (bf16[2,2,2,32,128]{4,3,2,1,0:T(8,128)(2,1)S(1)}, bf16[2,2,2,32,128]{4,3,2,1,0:T(8,128)(2,1)S(1)}, u32[]{:S(2)}, u32[]{:S(2)}) collective-permute-start(bf16[2,2,2,32,128]{4,3,2,1,0:T(8,128)(2,1)S(1)} %get-tuple-element.72), channel_id=1, source_target_pairs={{0,6},{1,7},{2,0},{3,1},{4,2},{5,3},{6,4},{7,5},{8,14},{9,15},{10,... | collective-permute-start | bytes 196616 | tf_op jit(solution)/shard_map/ppermute | solution.py:458
  129.0 20.3 %all-to-all-start.5 = ((bf16[8,4,32,128]{3,2,1,0:T(8,128)(2,1)}), bf16[8,4,32,128]{3,2,1,0:T(8,128)(2,1)S(1)}, u32[]{:S(2)}, u32[]{:S(2)}) async-start(bf16[8,4,32,128]{3,2,1,0:T(8,128)(2,1)} %get-tuple-element.78), calls=%async_computation.5 | async-start | bytes 524288 | tf_op jit(solution)/shard_map/all_to_all | solution.py:320
  140.6 3.1 %collective-permute-start.9 = (f32[1,8,256]{2,1,0:T(8,128)S(1)}, f32[1,8,256]{2,1,0:T(8,128)S(1)}, u32[]{:S(2)}, u32[]{:S(2)}) collective-permute-start(f32[1,8,256]{2,1,0:T(8,128)S(1)} %get-tuple-element.79.one_ref), channel_id=1, source_target_pairs={{0,8},{8,0},{16,24},{24,16},{32,40},{40,32},{48,56},{56,48},{64,72... | collective-permute-start | bytes 24584 | tf_op jit(solution)/shard_map/ppermute | solution.py:324
  143.6 5.6 %collective-permute-start.10 = (f32[2,8,256]{2,1,0:T(8,128)S(1)}, f32[2,8,256]{2,1,0:T(8,128)S(1)}, u32[]{:S(2)}, u32[]{:S(2)}) collective-permute-start(f32[2,8,256]{2,1,0:T(8,128)S(1)} %shard_map.131.one_ref), channel_id=1, source_target_pairs={{0,128},{8,136},{16,144},{24,152},{32,160},{40,168},{48,176},{56,1... | collective-permute-start | bytes 49160 | tf_op jit(solution)/shard_map/ppermute | solution.py:324
  149.2 15.1 %all-to-all-start.6 = ((bf16[8,4,32,128]{3,2,1,0:T(8,128)(2,1)}), bf16[8,4,32,128]{3,2,1,0:T(8,128)(2,1)S(1)}, u32[]{:S(2)}, u32[]{:S(2)}) async-start(bf16[8,4,32,128]{3,2,1,0:T(8,128)(2,1)} %get-tuple-element.82), calls=%async_computation.6 | async-start | bytes 524288 | tf_op jit(solution)/shard_map/all_to_all | solution.py:320
  154.6 7.3 %collective-permute-start.11 = (f32[4,8,256]{2,1,0:T(8,128)S(1)}, f32[4,8,256]{2,1,0:T(8,128)S(1)}, u32[]{:S(2)}, u32[]{:S(2)}) collective-permute-start(f32[4,8,256]{2,1,0:T(8,128)S(1)} %shard_map.132.near_ref), channel_id=1, source_target_pairs={{0,256},{8,264},{16,272},{24,280},{32,288},{40,296},{48,304},{56,3... | collective-permute-start | bytes 98312 | tf_op jit(solution)/shard_map/ppermute | solution.py:324

commit v11 on v10

--- a/solution.py
+++ b/solution.py
@@ -66,17 +66,23 @@
     return jnp.clip(place, 0, GROUP - 1)
 
 
-def pack_kernel(width, x_ref, send_ref, a_ref, b_ref, block_ref):
-    place_a, place_b = places()
+def pack_kernel(width, x_ref, send_ref, b_ref, block_ref):
+    place = places()[1]
+    for peer in range(GROUP):
+        kind = kind_of(peer - place)
+        for m in range(send_ref.shape[0]):
+            start = pl.multiple_of(send_ref[m, kind] * width, width)
+            b_ref[peer, m] = x_ref[:, pl.ds(start, width)]
     for block in range(block_ref.shape[0]):
         block_ref[block] = x_ref[:, block * width : (block + 1) * width]
-    cap = send_ref.shape[1]
-    for ref, place in ((b_ref, place_b), (a_ref, place_a)):
-        for peer in range(GROUP):
-            kind = kind_of(peer - place)
-            for m in range(cap):
-                start = pl.multiple_of(send_ref[kind, m] * width, width)
-                ref[peer, m] = x_ref[:, pl.ds(start, width)]
+
+
+def near_kernel(x_ref, send_ref, a_ref):
+    place = places()[0]
+    for peer in range(GROUP):
+        kind = kind_of(peer - place)
+        for m in range(send_ref.shape[0]):
+            a_ref[peer, m] = x_ref[send_ref[m, kind]]
 
 
 def column():
@@ -117,26 +123,29 @@
         out[1] = minus_ref[to]
 
 
-def fold_kernel(part_ref, out_ref):
-    full = part_ref.shape[2] - 128
+def summed(part_ref):
     total = part_ref[0].astype(F32)
     for i in range(1, part_ref.shape[0]):
         total += part_ref[i].astype(F32)
-    total = total.astype(BF16)
-    tail = jnp.concatenate([total[0:4, full:], total[8:12, full:]], axis=0)
+    return total
+
+
+def fold_kernel(part_ref, out_ref):
+    total = summed(part_ref).astype(BF16)
+    halves = out_ref.shape[1] - 1
     for z in range(Z_HI * Z_LO):
-        first = z // Z_LO * 8
-        out_ref[z, :, :full] = total[first : first + 8, :full]
-        out_ref[z, :, full:] = tail
+        first = z // Z_LO * halves
+        for half in range(halves):
+            out_ref[z, half] = total[first + half]
+        out_ref[z, halves] = total[Z_HI * halves]
 
 
 def total_kernel(part_ref, out_ref, tail_ref):
-    full = part_ref.shape[2] - 128
-    total = part_ref[0].astype(F32)
-    for i in range(1, part_ref.shape[0]):
-        total += part_ref[i].astype(F32)
-    out_ref[...] = total[:, :full]
-    tail_ref[...] = total[:, full:]
+    total = summed(part_ref)
+    halves = part_ref.shape[1] - 1
+    for half in range(halves):
+        out_ref[0, :, half * 128 : (half + 1) * 128] = total[half]
+    tail_ref[...] = total[halves]
 
 
 def pair_kernel(one_ref, two_ref, out_ref):
@@ -240,18 +249,18 @@
     full = dz_ref.shape[0]
     grads = dot(xa_ref[...], dz_ref[...], LAST)
     total = dot(jnp.ones((16, dz_ref.shape[1]), BF16), dz_ref[...], LAST)
-    tail = jnp.concatenate([total[:8, :128], total[8:, 128:]], axis=0).astype(BF16)
+    tail = jnp.concatenate([total[:4, :128], total[4:8, 128:]], axis=0).astype(BF16)
+    halves = full // 128
     for which in range(2):
         for quarter in range(4):
             for x in range(X):
-                rows = [
-                    grads[start : start + 8]
-                    for z in range(Z_HI)
-                    for start in [which * full + (x * Z_HI + z) * dim + quarter * 8]
-                ]
                 piece = (which * 4 + quarter) * X + x
-                part_ref[piece, :, :full] = jnp.concatenate(rows, axis=0).astype(BF16)
-                part_ref[piece, :, full:] = tail
+                for z in range(Z_HI):
+                    start = which * full + (x * Z_HI + z) * dim + quarter * 8
+                    for half in range(halves):
+                        tile = grads[start : start + 8, half * 128 : (half + 1) * 128]
+                        part_ref[piece, z * halves + half] = tile.astype(BF16)
+                part_ref[piece, Z_HI * halves] = tail
 
 
 def home_pieces(refs, which):
@@ -294,7 +303,7 @@
 
 def finish_kernel(acc_in, a_ref, b_ref, send_ref, out_ref, acc_ref):
     place_a, place_b = places()
-    kinds, cap = send_ref.shape
+    cap, kinds = send_ref.shape
     width = acc_in.shape[2]
     acc_ref[...] = acc_in[...]
     for kind in range(kinds):
@@ -303,7 +312,7 @@
         row_b = place_b + offset
         for m in range(cap):
             got = jnp.where(inside(row_a), a_ref[bounded(row_a), m], b_ref[bounded(row_b), m])
-            acc_ref[send_ref[kind, m]] += got.astype(F32)
+            acc_ref[send_ref[m, kind]] += got.astype(F32)
     for block in range(acc_ref.shape[0]):
         out_ref[:, block * width : (block + 1) * width] = acc_ref[block].astype(BF16)
 
@@ -352,8 +361,8 @@
     dim, nodes = node_feats.shape
     tiles, width = tile_cnt.shape[:2]
     blocks = nodes // width
-    table = send_blk[0]
-    kinds, cap = table.shape
+    table = send_blk[0].T
+    cap, kinds = table.shape
     slots = kinds * cap
     cols = X * Z_HI
     per_col = blocks // cols
@@ -363,10 +372,11 @@
     halo = shape(GROUP, cap)
     step = Z_LO // 2
 
-    send_a, send_b, feats = call(
-        functools.partial(pack_kernel, width), (halo, halo, shape(blocks)), [VMEM, SMEM]
+    send_b, feats = call(
+        functools.partial(pack_kernel, width), (halo, shape(blocks)), [VMEM, SMEM]
     )(node_feats, table)
     got_b = swap(send_b, GROUP // 2)
+    send_a = call(near_kernel, halo, [VMEM, SMEM])(feats, table)
     xc_plus, xc_minus = call(
         functools.partial(split_kernel, width), (shape(X, 2, per_col),) * 2, [VMEM] * 2
     )(feats, cotangent)
@@ -431,7 +441,7 @@
     minus = along_z(minus, -step)
     part = call(
         functools.partial(weight_kernel, dim),
-        jax.ShapeDtypeStruct((Y * CORE * X, 16, full + 128), BF16),
+        jax.ShapeDtypeStruct((Y * CORE * X, Z_HI * full // 128 + 1, 8, 128), BF16),
         [VMEM] * 2,
     )(xa, dz)
 
@@ -451,7 +461,7 @@
     home = call(turn_kernel, (shape(2, 2, per_col),) * X, [VMEM] * 2, cost=(1e10, 1e6))(plus, minus)
     part, *home = lax.optimization_barrier((part, *home))
     (part,) = call(
-        fold_kernel, (jax.ShapeDtypeStruct((Z_HI * Z_LO, 8, full + 128), BF16),), [VMEM]
+        fold_kernel, (jax.ShapeDtypeStruct((Z_HI * Z_LO, full // 128 + 1, 8, 128), BF16),), [VMEM]
     )(part)
     part = lax.all_to_all(part, both, 0, 0, axis_index_groups=line, tiled=False)
     route = lambda turn: [(c, (c + Z_HI * turn) % cols) for c in range(cols)]
@@ -464,7 +474,7 @@
     )(*home, degree, tile_dst, tile_src, half)
     row = jax.ShapeDtypeStruct((1, 8, full), F32)
     rows, tail = call(
-        lambda part_ref, out_ref, tail_ref: total_kernel(part_ref, out_ref.at[0], tail_ref),
+        total_kernel,
         (row, jax.ShapeDtypeStruct((8, 128), F32)),
         [VMEM],
     )(part)
@@ -480,7 +490,7 @@
         jax.ShapeDtypeStruct((blocks, dim, width), F32),
         [VMEM] * 5 + [SMEM, SMEM, VMEM],
     )(*home, scaled, tile_dst, tile_src, half)
-    away_a, back_b, rows, acc = lax.optimization_barrier((away_a, back_b, rows, acc))
+    away_a, back_b, rows = lax.optimization_barrier((away_a, back_b, rows))
     back_a = swap(away_a, 0)
     grad = jax.ShapeDtypeStruct((dim, full), F32)
     grad_self, grad_neigh = call(order_kernel, (grad, grad), [VMEM] * 2)(

time: 168 us -> 167 us (level)
  waiting for transfers between devices: 36.5 us -> 34.4 us
    all_to_all x4, waiting for transfers between devices: 3 us -> 0.92 us  [swap(): lax.all_to_all(rows, 'blk', 0, 0, axis_index_groups=groups, tiled=False)]
    unnamed x22 -> x28, local copies, waits for them, and re-layouts: 5.37 us -> 6.74 us
    pallas_call x3 -> x4, Pallas kernels: 2.31 us -> 3.46 us  [the longest x1 1.39 us: per_device(): call(functools.partial(pack_kernel, width), (halo, shape(blocks)), [VMEM,...]
  transfers between devices with their start and end apart: 19 -> 19, of which waited for: 12 -> 11; matrix products, arithmetic and copies ran while one was open for 1% -> 1% of each run, Pallas kernels for 5% -> 5%
where the time goes in v11:
time: 167 us; the launch traced here: 165 us
  starting transfers between devices  108 us (65%)
  waiting for transfers between devices  34.4 us (21%)
  Pallas kernels  14.1 us (8%)
  local copies, waits for them, and re-layouts  7.47 us (4%)
    all_to_all x4, starting transfers between devices, swap(): lax.all_to_all(rows, 'blk', 0, 0, axis_index_groups=groups, tiled=False)  36.6 us
    ppermute x6, starting transfers between devices, along_z(): return lax.ppermute(rows, ('blk', 'col'), sorted(route))  31.2 us
    all_to_all x1, starting transfers between devices, per_device(): part = lax.all_to_all(part, both, 0, 0, axis_index_groups=line, tiled=False)  9.88 us
    all_to_all x1, starting transfers between devices, per_device(): part = lax.all_to_all(part, both, 0, 0, axis_index_groups=flat, tiled=False)  8.66 us
    ppermute x3, starting transfers between devices, per_device(): lax.ppermute(home[turn], 'col', route(turn))  8.38 us
    ppermute x6, waiting for transfers between devices, along_z(): return lax.ppermute(rows, ('blk', 'col'), sorted(route))  8.32 us
    ppermute x3, starting transfers between devices, across(): lax.ppermute(rows, 'blk', [(e, e ^ bit) for e in range(lax.axis_size('blk...  8.19 us
    all_to_all x1, waiting for transfers between devices, per_device(): part = lax.all_to_all(part, both, 0, 0, axis_index_groups=flat, tiled=False)  8.07 us
  transfers between devices with their start and end apart: 19, of which 11 were waited for; matrix products, arithmetic and copies ran while one was open for 1% of the time, Pallas kernels for 5%

profile of v11, /device:TPU:6, one launch (start us, length us, event | category | flops | bytes accessed | tf_op | source)
XLA Modules:
  0.0 164.7 jit_solution(985823585193963566)
XLA Ops:
  2.3 1.4 shard_map.120
  3.6 15.7 %all-to-all-start = ((bf16[8,4,32,128]{3,2,1,0:T(8,128)(2,1)}), bf16[8,4,32,128]{3,2,1,0:T(8,128)(2,1)S(1)}, u32[]{:S(2)}, u32[]{:S(2)}) async-start(bf16[8,4,32,128]{3,2,1,0:T(8,128)(2,1)} %get-tuple-element.45), calls=%async_computation | async-start | bytes 524288 | tf_op jit(solution)/shard_map/all_to_all | solution.py:329
  20.0 1.4 shard_map.121
  22.3 2.0 %copy-done = s32[56,128,128]{2,1,0:T(8,128)S(1)} copy-done((s32[56,128,128]{2,1,0:T(8,128)S(1)}, s32[56,128,128]{2,1,0:T(8,128)}, u32[]{:S(2)}) %copy-start) | copy-done | bytes 3670040
  25.7 1.8 %shard_map.123 = (bf16[56,128,128]{2,1,0:T(8,128)(2,1)S(1)}, f32[16,40,128]{2,1,0:T(8,128)S(1)}) custom-call(bf16[16,32,128]{2,1,0:T(8,128)(2,1)S(1)} %get-tuple-element.44.x_ref, s32[56]{0:T(128)S(1)} %copy-done.8, s32[56]{0:T(128)S(1)} %copy-done.10, s32[56,128,128]{2,1,0:T(8,128)S(1)} %copy-done), custom_call_target="tpu_custom_call" | custom-call | flops 60000000 | bytes 6000000 | tf_op jit(solution)/shard_map/pallas_call | solution.py:384
  27.5 4.0 %all-to-all-start.1 = ((bf16[8,4,32,128]{3,2,1,0:T(8,128)(2,1)}), bf16[8,4,32,128]{3,2,1,0:T(8,128)(2,1)S(1)}, u32[]{:S(2)}, u32[]{:S(2)}) async-start(bf16[8,4,32,128]{3,2,1,0:T(8,128)(2,1)} %shard_map.121), calls=%async_computation.1 | async-start | bytes 524288 | tf_op jit(solution)/shard_map/all_to_all | solution.py:329
  31.5 4.7 %collective-permute-start = (bf16[4,2,2,32,128]{4,3,2,1,0:T(8,128)(2,1)S(1)}, bf16[4,2,2,32,128]{4,3,2,1,0:T(8,128)(2,1)S(1)}, u32[]{:S(2)}, u32[]{:S(2)}) collective-permute-start(bf16[4,2,2,32,128]{4,3,2,1,0:T(8,128)(2,1)S(1)} %get-tuple-element.50), channel_id=1, source_target_pairs={{0,64},{1,65},{2,66},{3,67},{4,68},{5,69},{6,70},{7,71},{8,72},{9,... | collective-permute-start | bytes 393224 | tf_op jit(solution)/shard_map/ppermute | solution.py:355
  36.2 7.0 %collective-permute-start.1 = (bf16[4,2,2,32,128]{4,3,2,1,0:T(8,128)(2,1)S(1)}, bf16[4,2,2,32,128]{4,3,2,1,0:T(8,128)(2,1)S(1)}, u32[]{:S(2)}, u32[]{:S(2)}) collective-permute-start(bf16[4,2,2,32,128]{4,3,2,1,0:T(8,128)(2,1)S(1)} %get-tuple-element.51), channel_id=1, source_target_pairs={{0,65},{1,64},{2,67},{3,66},{4,69},{5,68},{6,71},{7,70},{8,73},{9,... | collective-permute-start | bytes 393224 | tf_op jit(solution)/shard_map/ppermute | solution.py:355
  44.6 3.3 %collective-permute-start.2 = (bf16[4,2,32,128]{3,2,1,0:T(8,128)(2,1)S(1)}, bf16[4,2,32,128]{3,2,1,0:T(8,128)(2,1)S(1)}, u32[]{:S(2)}, u32[]{:S(2)}) collective-permute-start(bf16[4,2,32,128]{3,2,1,0:T(8,128)(2,1)S(1)} %get-tuple-element.56), channel_id=1, source_target_pairs={{0,64},{1,65},{2,66},{3,67},{4,68},{5,69},{6,70},{7,71},{8,72},{9,... | collective-permute-start | bytes 196616 | tf_op jit(solution)/shard_map/ppermute | solution.py:355
  47.9 6.5 %collective-permute-start.3 = (bf16[4,2,32,128]{3,2,1,0:T(8,128)(2,1)S(1)}, bf16[4,2,32,128]{3,2,1,0:T(8,128)(2,1)S(1)}, u32[]{:S(2)}, u32[]{:S(2)}) collective-permute-start(bf16[4,2,32,128]{3,2,1,0:T(8,128)(2,1)S(1)} %get-tuple-element.57), channel_id=1, source_target_pairs={{0,65},{1,64},{2,67},{3,66},{4,69},{5,68},{6,71},{7,70},{8,73},{9,... | collective-permute-start | bytes 196616 | tf_op jit(solution)/shard_map/ppermute | solution.py:355
  55.6 6.2 %collective-permute-done.2.agg_plus_ref = bf16[4,2,32,128]{3,2,1,0:T(8,128)(2,1)S(1)} collective-permute-done((bf16[4,2,32,128]{3,2,1,0:T(8,128)(2,1)S(1)}, bf16[4,2,32,128]{3,2,1,0:T(8,128)(2,1)S(1)}, u32[]{:S(2)}, u32[]{:S(2)}) %collective-permute-start.2) | collective-permute-done | bytes 65568 | tf_op jit(solution)/shard_map/ppermute | solution.py:355
  63.5 4.8 %all-to-all-start.2 = ((bf16[4,3,2,2,32,128]{5,4,3,2,1,0:T(8,128)(2,1)}), bf16[4,3,2,2,32,128]{5,4,3,2,1,0:T(8,128)(2,1)S(1)}, u32[]{:S(2)}, u32[]{:S(2)}) async-start(bf16[4,3,2,2,32,128]{5,4,3,2,1,0:T(8,128)(2,1)} %shard_map.125), calls=%async_computation.2 | async-start | bytes 786432 | tf_op jit(solution)/shard_map/all_to_all | solution.py:338
  68.6 4.9 %all-to-all-done.2.in_ref = bf16[4,3,2,2,32,128]{5,4,3,2,1,0:T(8,128)(2,1)S(1)} async-done(((bf16[4,3,2,2,32,128]{5,4,3,2,1,0:T(8,128)(2,1)}), bf16[4,3,2,2,32,128]{5,4,3,2,1,0:T(8,128)(2,1)S(1)}, u32[]{:S(2)}, u32[]{:S(2)}) %all-to-all-start.2) | async-done | bytes 393248 | tf_op jit(solution)/shard_map/all_to_all | solution.py:338
  74.4 6.7 %collective-permute-start.4 = (bf16[4,2,2,32,128]{4,3,2,1,0:T(8,128)(2,1)S(1)}, bf16[4,2,2,32,128]{4,3,2,1,0:T(8,128)(2,1)S(1)}, u32[]{:S(2)}, u32[]{:S(2)}) collective-permute-start(bf16[4,2,2,32,128]{4,3,2,1,0:T(8,128)(2,1)S(1)} %get-tuple-element.60), channel_id=1, source_target_pairs={{0,64},{1,65},{2,66},{3,67},{4,68},{5,69},{6,70},{7,71},{8,72},{9,... | collective-permute-start | bytes 393224 | tf_op jit(solution)/shard_map/ppermute | solution.py:355
  81.1 3.1 %collective-permute-start.5 = (bf16[4,2,2,32,128]{4,3,2,1,0:T(8,128)(2,1)S(1)}, bf16[4,2,2,32,128]{4,3,2,1,0:T(8,128)(2,1)S(1)}, u32[]{:S(2)}, u32[]{:S(2)}) collective-permute-start(bf16[4,2,2,32,128]{4,3,2,1,0:T(8,128)(2,1)S(1)} %get-tuple-element.61), channel_id=1, source_target_pairs={{0,65},{1,64},{2,67},{3,66},{4,69},{5,68},{6,71},{7,70},{8,73},{9,... | collective-permute-start | bytes 393224 | tf_op jit(solution)/shard_map/ppermute | solution.py:355
  85.3 8.7 %all-to-all-start.3 = ((bf16[32,5,8,128]{3,2,1,0:T(8,128)(2,1)}), bf16[32,5,8,128]{3,2,1,0:T(8,128)(2,1)S(1)}, u32[]{:S(2)}, u32[]{:S(2)}) async-start(bf16[32,5,8,128]{3,2,1,0:T(8,128)(2,1)} %shard_map.127), calls=%async_computation.3 | async-start | bytes 655360 | tf_op jit(solution)/shard_map/all_to_all | solution.py:460
  94.0 8.1 %all-to-all-done.3.part_ref = bf16[32,5,8,128]{3,2,1,0:T(8,128)(2,1)S(1)} async-done(((bf16[32,5,8,128]{3,2,1,0:T(8,128)(2,1)}), bf16[32,5,8,128]{3,2,1,0:T(8,128)(2,1)S(1)}, u32[]{:S(2)}, u32[]{:S(2)}) %all-to-all-start.3) | async-done | bytes 327712 | tf_op jit(solution)/shard_map/all_to_all | solution.py:460
  102.8 9.9 %all-to-all-start.4 = ((bf16[16,3,8,128]{3,2,1,0:T(8,128)(2,1)}), bf16[16,3,8,128]{3,2,1,0:T(8,128)(2,1)S(1)}, u32[]{:S(2)}, u32[]{:S(2)}) async-start(bf16[16,3,8,128]{3,2,1,0:T(8,128)(2,1)} %shard_map.131), calls=%async_computation.4 | async-start | bytes 196608 | tf_op jit(solution)/shard_map/all_to_all | solution.py:466
  112.7 3.7 %collective-permute-start.6 = (bf16[2,2,2,32,128]{4,3,2,1,0:T(8,128)(2,1)S(1)}, bf16[2,2,2,32,128]{4,3,2,1,0:T(8,128)(2,1)S(1)}, u32[]{:S(2)}, u32[]{:S(2)}) collective-permute-start(bf16[2,2,2,32,128]{4,3,2,1,0:T(8,128)(2,1)S(1)} %get-tuple-element.67), channel_id=1, source_target_pairs={{0,2},{1,3},{2,4},{3,5},{4,6},{5,7},{6,0},{7,1},{8,10},{9,11},{10,... | collective-permute-start | bytes 196616 | tf_op jit(solution)/shard_map/ppermute | solution.py:468
  116.4 2.4 %collective-permute-start.7 = (bf16[2,2,2,32,128]{4,3,2,1,0:T(8,128)(2,1)S(1)}, bf16[2,2,2,32,128]{4,3,2,1,0:T(8,128)(2,1)S(1)}, u32[]{:S(2)}, u32[]{:S(2)}) collective-permute-start(bf16[2,2,2,32,128]{4,3,2,1,0:T(8,128)(2,1)S(1)} %get-tuple-element.68), channel_id=1, source_target_pairs={{0,4},{1,5},{2,6},{3,7},{4,0},{5,1},{6,2},{7,3},{8,12},{9,13},{10,... | collective-permute-start | bytes 196616 | tf_op jit(solution)/shard_map/ppermute | solution.py:468
  118.8 2.3 %collective-permute-start.8 = (bf16[2,2,2,32,128]{4,3,2,1,0:T(8,128)(2,1)S(1)}, bf16[2,2,2,32,128]{4,3,2,1,0:T(8,128)(2,1)S(1)}, u32[]{:S(2)}, u32[]{:S(2)}) collective-permute-start(bf16[2,2,2,32,128]{4,3,2,1,0:T(8,128)(2,1)S(1)} %get-tuple-element.69), channel_id=1, source_target_pairs={{0,6},{1,7},{2,0},{3,1},{4,2},{5,3},{6,4},{7,5},{8,14},{9,15},{10,... | collective-permute-start | bytes 196616 | tf_op jit(solution)/shard_map/ppermute | solution.py:468
  121.1 3.0 %collective-permute-done.7.two_ref = bf16[2,2,2,32,128]{4,3,2,1,0:T(8,128)(2,1)S(1)} collective-permute-done((bf16[2,2,2,32,128]{4,3,2,1,0:T(8,128)(2,1)S(1)}, bf16[2,2,2,32,128]{4,3,2,1,0:T(8,128)(2,1)S(1)}, u32[]{:S(2)}, u32[]{:S(2)}) %collective-permute-start.7) | collective-permute-done | bytes 65568 | tf_op jit(solution)/shard_map/ppermute | solution.py:468
  124.1 2.1 %collective-permute-done.8.three_ref = bf16[2,2,2,32,128]{4,3,2,1,0:T(8,128)(2,1)S(1)} collective-permute-done((bf16[2,2,2,32,128]{4,3,2,1,0:T(8,128)(2,1)S(1)}, bf16[2,2,2,32,128]{4,3,2,1,0:T(8,128)(2,1)S(1)}, u32[]{:S(2)}, u32[]{:S(2)}) %collective-permute-start.8) | collective-permute-done | bytes 65568 | tf_op jit(solution)/shard_map/ppermute | solution.py:468
  126.1 1.8 %shard_map.129 = (bf16[8,4,32,128]{3,2,1,0:T(8,128)(2,1)}, bf16[8,4,32,128]{3,2,1,0:T(8,128)(2,1)}, bf16[16,32,128]{2,1,0:T(8,128)(2,1)S(1)}) custom-call(bf16[2,2,2,32,128]{4,3,2,1,0:T(8,128)(2,1)S(1)} %get-tuple-element.66.zero_ref, bf16[2,2,2,32,128]{4,3,2,1,0:T(8,128)(2,1)S(1)} %collective-permute-done.6.one_ref, ...), custom_call_target="tpu_custom_call" | custom-call | flops 10000000 | bytes 1000000 | tf_op jit(solution)/shard_map/pallas_call | solution.py:469
  128.0 11.6 %all-to-all-start.5 = ((bf16[8,4,32,128]{3,2,1,0:T(8,128)(2,1)}), bf16[8,4,32,128]{3,2,1,0:T(8,128)(2,1)S(1)}, u32[]{:S(2)}, u32[]{:S(2)}) async-start(bf16[8,4,32,128]{3,2,1,0:T(8,128)(2,1)} %get-tuple-element.76), calls=%async_computation.5 | async-start | bytes 524288 | tf_op jit(solution)/shard_map/all_to_all | solution.py:329
  139.5 2.0 %collective-permute-start.9 = (f32[1,8,256]{2,1,0:T(8,128)S(1)}, f32[1,8,256]{2,1,0:T(8,128)S(1)}, u32[]{:S(2)}, u32[]{:S(2)}) collective-permute-start(f32[1,8,256]{2,1,0:T(8,128)S(1)} %get-tuple-element.77.one_ref), channel_id=1, source_target_pairs={{0,8},{8,0},{16,24},{24,16},{32,40},{40,32},{48,56},{56,48},{64,72... | collective-permute-start | bytes 24584 | tf_op jit(solution)/shard_map/ppermute | solution.py:333
  142.6 2.7 %collective-permute-start.10 = (f32[2,8,256]{2,1,0:T(8,128)S(1)}, f32[2,8,256]{2,1,0:T(8,128)S(1)}, u32[]{:S(2)}, u32[]{:S(2)}) collective-permute-start(f32[2,8,256]{2,1,0:T(8,128)S(1)} %shard_map.133.one_ref), channel_id=1, source_target_pairs={{0,128},{8,136},{16,144},{24,152},{32,160},{40,168},{48,176},{56,1... | collective-permute-start | bytes 49160 | tf_op jit(solution)/shard_map/ppermute | solution.py:333
  145.4 2.9 %collective-permute-done.10.two_ref = f32[2,8,256]{2,1,0:T(8,128)S(1)} collective-permute-done((f32[2,8,256]{2,1,0:T(8,128)S(1)}, f32[2,8,256]{2,1,0:T(8,128)S(1)}, u32[]{:S(2)}, u32[]{:S(2)}) %collective-permute-start.10) | collective-permute-done | bytes 16416 | tf_op jit(solution)/shard_map/ppermute | solution.py:333
  148.2 5.3 %all-to-all-start.6 = ((bf16[8,4,32,128]{3,2,1,0:T(8,128)(2,1)}), bf16[8,4,32,128]{3,2,1,0:T(8,128)(2,1)S(1)}, u32[]{:S(2)}, u32[]{:S(2)}) async-start(bf16[8,4,32,128]{3,2,1,0:T(8,128)(2,1)} %get-tuple-element.78), calls=%async_computation.6 | async-start | bytes 524288 | tf_op jit(solution)/shard_map/all_to_all | solution.py:329
  154.4 3.4 %collective-permute-start.11 = (f32[4,8,256]{2,1,0:T(8,128)S(1)}, f32[4,8,256]{2,1,0:T(8,128)S(1)}, u32[]{:S(2)}, u32[]{:S(2)}) collective-permute-start(f32[4,8,256]{2,1,0:T(8,128)S(1)} %shard_map.134.near_ref), channel_id=1, source_target_pairs={{0,256},{8,264},{16,272},{24,280},{32,288},{40,296},{48,304},{56,3... | collective-permute-start | bytes 98312 | tf_op jit(solution)/shard_map/ppermute | solution.py:333
  158.4 3.3 %collective-permute-done.11.far_ref = f32[4,8,256]{2,1,0:T(8,128)S(1)} collective-permute-done((f32[4,8,256]{2,1,0:T(8,128)S(1)}, f32[4,8,256]{2,1,0:T(8,128)S(1)}, u32[]{:S(2)}, u32[]{:S(2)}) %collective-permute-start.11) | collective-permute-done | bytes 32800 | tf_op jit(solution)/shard_map/ppermute | solution.py:333
  163.3 1.4 shard_map.135
  (56 shorter events, 15.9 us)
Async XLA Ops:
  0.6 42.6 %copy-start.9 = (s32[56]{0:T(128)S(1)}, s32[56]{0:T(128)}, u32[]{:S(2)}) copy-start(s32[56]{0:T(128)} %dst_ref.7) | copy-start | bytes 676
  0.6 42.6 %copy-start.11 = (s32[56]{0:T(128)S(1)}, s32[56]{0:T(128)}, u32[]{:S(2)}) copy-start(s32[56]{0:T(128)} %src_ref.7) | copy-start | bytes 676
  0.7 0.9 copy-start.3
  1.6 0.7 copy-start.5
  3.6 23.8 %all-to-all-start = ((bf16[8,4,32,128]{3,2,1,0:T(8,128)(2,1)}), bf16[8,4,32,128]{3,2,1,0:T(8,128)(2,1)S(1)}, u32[]{:S(2)}, u32[]{:S(2)}) async-start(bf16[8,4,32,128]{3,2,1,0:T(8,128)(2,1)} %get-tuple-element.45), calls=%async_computation | async-start | bytes 524288 | tf_op jit(solution)/shard_map/all_to_all | solution.py:329
  19.3 0.7 copy-start.6
  21.4 0.9 copy-start.4
  22.3 2.0 %copy-start = (s32[56,128,128]{2,1,0:T(8,128)S(1)}, s32[56,128,128]{2,1,0:T(8,128)}, u32[]{:S(2)}) copy-start(s32[56,128,128]{2,1,0:T(8,128)} %cnt_ref.1) | copy-start | bytes 11010052
  24.4 0.7 copy-start.8
  25.0 0.7 copy-start.10
  25.7 42.6 %copy-start.2 = (bf16[256,256]{1,0:T(8,128)(2,1)S(1)}, bf16[256,256]{1,0:T(8,128)(2,1)}, u32[]{:S(2)}) copy-start(bf16[256,256]{1,0:T(8,128)(2,1)} %own_w_ref.1) | copy-start | bytes 393220
  25.7 42.7 %copy-start.1 = (bf16[256,256]{1,0:T(8,128)(2,1)S(1)}, bf16[256,256]{1,0:T(8,128)(2,1)}, u32[]{:S(2)}) copy-start(bf16[256,256]{1,0:T(8,128)(2,1)} %neigh_ref.1) | copy-start | bytes 393220
  25.7 42.8 %copy-start.12 = (f32[256]{0:T(256)S(1)}, f32[256]{0:T(256)}, u32[]{:S(2)}) copy-start(f32[256]{0:T(256)} %param.16) | copy-start | bytes 3076
  27.5 15.7 %all-to-all-start.1 = ((bf16[8,4,32,128]{3,2,1,0:T(8,128)(2,1)}), bf16[8,4,32,128]{3,2,1,0:T(8,128)(2,1)S(1)}, u32[]{:S(2)}, u32[]{:S(2)}) async-start(bf16[8,4,32,128]{3,2,1,0:T(8,128)(2,1)} %shard_map.121), calls=%async_computation.1 | async-start | bytes 524288 | tf_op jit(solution)/shard_map/all_to_all | solution.py:329
  31.5 22.9 %collective-permute-start = (bf16[4,2,2,32,128]{4,3,2,1,0:T(8,128)(2,1)S(1)}, bf16[4,2,2,32,128]{4,3,2,1,0:T(8,128)(2,1)S(1)}, u32[]{:S(2)}, u32[]{:S(2)}) collective-permute-start(bf16[4,2,2,32,128]{4,3,2,1,0:T(8,128)(2,1)S(1)} %get-tuple-element.50), channel_id=1, source_target_pairs={{0,64},{1,65},{2,66},{3,67},{4,68},{5,69},{6,70},{7,71},{8,72},{9,... | collective-permute-start | bytes 393224 | tf_op jit(solution)/shard_map/ppermute | solution.py:355
  36.2 19.4 %collective-permute-start.1 = (bf16[4,2,2,32,128]{4,3,2,1,0:T(8,128)(2,1)S(1)}, bf16[4,2,2,32,128]{4,3,2,1,0:T(8,128)(2,1)S(1)}, u32[]{:S(2)}, u32[]{:S(2)}) collective-permute-start(bf16[4,2,2,32,128]{4,3,2,1,0:T(8,128)(2,1)S(1)} %get-tuple-element.51), channel_id=1, source_target_pairs={{0,65},{1,64},{2,67},{3,66},{4,69},{5,68},{6,71},{7,70},{8,73},{9,... | collective-permute-start | bytes 393224 | tf_op jit(solution)/shard_map/ppermute | solution.py:355
  44.6 17.1 %collective-permute-start.2 = (bf16[4,2,32,128]{3,2,1,0:T(8,128)(2,1)S(1)}, bf16[4,2,32,128]{3,2,1,0:T(8,128)(2,1)S(1)}, u32[]{:S(2)}, u32[]{:S(2)}) collective-permute-start(bf16[4,2,32,128]{3,2,1,0:T(8,128)(2,1)S(1)} %get-tuple-element.56), channel_id=1, source_target_pairs={{0,64},{1,65},{2,66},{3,67},{4,68},{5,69},{6,70},{7,71},{8,72},{9,... | collective-permute-start | bytes 196616 | tf_op jit(solution)/shard_map/ppermute | solution.py:355
  47.9 14.8 %collective-permute-start.3 = (bf16[4,2,32,128]{3,2,1,0:T(8,128)(2,1)S(1)}, bf16[4,2,32,128]{3,2,1,0:T(8,128)(2,1)S(1)}, u32[]{:S(2)}, u32[]{:S(2)}) collective-permute-start(bf16[4,2,32,128]{3,2,1,0:T(8,128)(2,1)S(1)} %get-tuple-element.57), channel_id=1, source_target_pairs={{0,65},{1,64},{2,67},{3,66},{4,69},{5,68},{6,71},{7,70},{8,73},{9,... | collective-permute-start | bytes 196616 | tf_op jit(solution)/shard_map/ppermute | solution.py:355
  63.5 10.1 %all-to-all-start.2 = ((bf16[4,3,2,2,32,128]{5,4,3,2,1,0:T(8,128)(2,1)}), bf16[4,3,2,2,32,128]{5,4,3,2,1,0:T(8,128)(2,1)S(1)}, u32[]{:S(2)}, u32[]{:S(2)}) async-start(bf16[4,3,2,2,32,128]{5,4,3,2,1,0:T(8,128)(2,1)} %shard_map.125), calls=%async_computation.2 | async-start | bytes 786432 | tf_op jit(solution)/shard_map/all_to_all | solution.py:338
  74.4 19.5 %collective-permute-start.4 = (bf16[4,2,2,32,128]{4,3,2,1,0:T(8,128)(2,1)S(1)}, bf16[4,2,2,32,128]{4,3,2,1,0:T(8,128)(2,1)S(1)}, u32[]{:S(2)}, u32[]{:S(2)}) collective-permute-start(bf16[4,2,2,32,128]{4,3,2,1,0:T(8,128)(2,1)S(1)} %get-tuple-element.60), channel_id=1, source_target_pairs={{0,64},{1,65},{2,66},{3,67},{4,68},{5,69},{6,70},{7,71},{8,72},{9,... | collective-permute-start | bytes 393224 | tf_op jit(solution)/shard_map/ppermute | solution.py:355
  81.1 12.8 %collective-permute-start.5 = (bf16[4,2,2,32,128]{4,3,2,1,0:T(8,128)(2,1)S(1)}, bf16[4,2,2,32,128]{4,3,2,1,0:T(8,128)(2,1)S(1)}, u32[]{:S(2)}, u32[]{:S(2)}) collective-permute-start(bf16[4,2,2,32,128]{4,3,2,1,0:T(8,128)(2,1)S(1)} %get-tuple-element.61), channel_id=1, source_target_pairs={{0,65},{1,64},{2,67},{3,66},{4,69},{5,68},{6,71},{7,70},{8,73},{9,... | collective-permute-start | bytes 393224 | tf_op jit(solution)/shard_map/ppermute | solution.py:355
  85.3 16.8 %all-to-all-start.3 = ((bf16[32,5,8,128]{3,2,1,0:T(8,128)(2,1)}), bf16[32,5,8,128]{3,2,1,0:T(8,128)(2,1)S(1)}, u32[]{:S(2)}, u32[]{:S(2)}) async-start(bf16[32,5,8,128]{3,2,1,0:T(8,128)(2,1)} %shard_map.127), calls=%async_computation.3 | async-start | bytes 655360 | tf_op jit(solution)/shard_map/all_to_all | solution.py:460
  94.0 69.3 %copy-start.7 = (s32[1,8,4]{1,2,0:T(4,128)S(1)}, s32[1,8,4]{1,2,0:T(4,128)}, u32[]{:S(2)}) copy-start(s32[1,8,4]{1,2,0:T(4,128)} %param.13) | copy-start | bytes 388
  102.8 25.2 %all-to-all-start.4 = ((bf16[16,3,8,128]{3,2,1,0:T(8,128)(2,1)}), bf16[16,3,8,128]{3,2,1,0:T(8,128)(2,1)S(1)}, u32[]{:S(2)}, u32[]{:S(2)}) async-start(bf16[16,3,8,128]{3,2,1,0:T(8,128)(2,1)} %shard_map.131), calls=%async_computation.4 | async-start | bytes 196608 | tf_op jit(solution)/shard_map/all_to_all | solution.py:466
  112.7 8.4 %collective-permute-start.6 = (bf16[2,2,2,32,128]{4,3,2,1,0:T(8,128)(2,1)S(1)}, bf16[2,2,2,32,128]{4,3,2,1,0:T(8,128)(2,1)S(1)}, u32[]{:S(2)}, u32[]{:S(2)}) collective-permute-start(bf16[2,2,2,32,128]{4,3,2,1,0:T(8,128)(2,1)S(1)} %get-tuple-element.67), channel_id=1, source_target_pairs={{0,2},{1,3},{2,4},{3,5},{4,6},{5,7},{6,0},{7,1},{8,10},{9,11},{10,... | collective-permute-start | bytes 196616 | tf_op jit(solution)/shard_map/ppermute | solution.py:468
  116.4 7.7 %collective-permute-start.7 = (bf16[2,2,2,32,128]{4,3,2,1,0:T(8,128)(2,1)S(1)}, bf16[2,2,2,32,128]{4,3,2,1,0:T(8,128)(2,1)S(1)}, u32[]{:S(2)}, u32[]{:S(2)}) collective-permute-start(bf16[2,2,2,32,128]{4,3,2,1,0:T(8,128)(2,1)S(1)} %get-tuple-element.68), channel_id=1, source_target_pairs={{0,4},{1,5},{2,6},{3,7},{4,0},{5,1},{6,2},{7,3},{8,12},{9,13},{10,... | collective-permute-start | bytes 196616 | tf_op jit(solution)/shard_map/ppermute | solution.py:468
  118.8 7.4 %collective-permute-start.8 = (bf16[2,2,2,32,128]{4,3,2,1,0:T(8,128)(2,1)S(1)}, bf16[2,2,2,32,128]{4,3,2,1,0:T(8,128)(2,1)S(1)}, u32[]{:S(2)}, u32[]{:S(2)}) collective-permute-start(bf16[2,2,2,32,128]{4,3,2,1,0:T(8,128)(2,1)S(1)} %get-tuple-element.69), channel_id=1, source_target_pairs={{0,6},{1,7},{2,0},{3,1},{4,2},{5,3},{6,4},{7,5},{8,14},{9,15},{10,... | collective-permute-start | bytes 196616 | tf_op jit(solution)/shard_map/ppermute | solution.py:468
  128.0 20.3 %all-to-all-start.5 = ((bf16[8,4,32,128]{3,2,1,0:T(8,128)(2,1)}), bf16[8,4,32,128]{3,2,1,0:T(8,128)(2,1)S(1)}, u32[]{:S(2)}, u32[]{:S(2)}) async-start(bf16[8,4,32,128]{3,2,1,0:T(8,128)(2,1)} %get-tuple-element.76), calls=%async_computation.5 | async-start | bytes 524288 | tf_op jit(solution)/shard_map/all_to_all | solution.py:329
  139.5 3.1 %collective-permute-start.9 = (f32[1,8,256]{2,1,0:T(8,128)S(1)}, f32[1,8,256]{2,1,0:T(8,128)S(1)}, u32[]{:S(2)}, u32[]{:S(2)}) collective-permute-start(f32[1,8,256]{2,1,0:T(8,128)S(1)} %get-tuple-element.77.one_ref), channel_id=1, source_target_pairs={{0,8},{8,0},{16,24},{24,16},{32,40},{40,32},{48,56},{56,48},{64,72... | collective-permute-start | bytes 24584 | tf_op jit(solution)/shard_map/ppermute | solution.py:333
  142.6 5.6 %collective-permute-start.10 = (f32[2,8,256]{2,1,0:T(8,128)S(1)}, f32[2,8,256]{2,1,0:T(8,128)S(1)}, u32[]{:S(2)}, u32[]{:S(2)}) collective-permute-start(f32[2,8,256]{2,1,0:T(8,128)S(1)} %shard_map.133.one_ref), channel_id=1, source_target_pairs={{0,128},{8,136},{16,144},{24,152},{32,160},{40,168},{48,176},{56,1... | collective-permute-start | bytes 49160 | tf_op jit(solution)/shard_map/ppermute | solution.py:333
  148.2 15.1 %all-to-all-start.6 = ((bf16[8,4,32,128]{3,2,1,0:T(8,128)(2,1)}), bf16[8,4,32,128]{3,2,1,0:T(8,128)(2,1)S(1)}, u32[]{:S(2)}, u32[]{:S(2)}) async-start(bf16[8,4,32,128]{3,2,1,0:T(8,128)(2,1)} %get-tuple-element.78), calls=%async_computation.6 | async-start | bytes 524288 | tf_op jit(solution)/shard_map/all_to_all | solution.py:329
  154.4 7.3 %collective-permute-start.11 = (f32[4,8,256]{2,1,0:T(8,128)S(1)}, f32[4,8,256]{2,1,0:T(8,128)S(1)}, u32[]{:S(2)}, u32[]{:S(2)}) collective-permute-start(f32[4,8,256]{2,1,0:T(8,128)S(1)} %shard_map.134.near_ref), channel_id=1, source_target_pairs={{0,256},{8,264},{16,272},{24,280},{32,288},{40,296},{48,304},{56,3... | collective-permute-start | bytes 98312 | tf_op jit(solution)/shard_map/ppermute | solution.py:333

commit v12 on v11

--- a/solution.py
+++ b/solution.py
@@ -66,23 +66,24 @@
     return jnp.clip(place, 0, GROUP - 1)
 
 
-def pack_kernel(width, x_ref, send_ref, b_ref, block_ref):
-    place = places()[1]
-    for peer in range(GROUP):
-        kind = kind_of(peer - place)
-        for m in range(send_ref.shape[0]):
-            start = pl.multiple_of(send_ref[m, kind] * width, width)
-            b_ref[peer, m] = x_ref[:, pl.ds(start, width)]
+def pack_kernel(width, x_hbm, send_hbm, a_ref, b_ref, block_ref, x_ref, send_ref, sems):
+    copies = (
+        pltpu.make_async_copy(x_hbm, x_ref, sems.at[0]),
+        pltpu.make_async_copy(send_hbm, send_ref, sems.at[1]),
+    )
+    for copy in copies:
+        copy.start()
+    for copy in copies:
+        copy.wait()
     for block in range(block_ref.shape[0]):
         block_ref[block] = x_ref[:, block * width : (block + 1) * width]
-
-
-def near_kernel(x_ref, send_ref, a_ref):
-    place = places()[0]
-    for peer in range(GROUP):
-        kind = kind_of(peer - place)
-        for m in range(send_ref.shape[0]):
-            a_ref[peer, m] = x_ref[send_ref[m, kind]]
+    place_a, place_b = places()
+    for ref, place in ((b_ref, place_b), (a_ref, place_a)):
+        for peer in range(GROUP):
+            kind = kind_of(peer - place)
+            for m in range(send_ref.shape[0]):
+                start = pl.multiple_of(send_ref[m, kind] * width, width)
+                ref[peer, m] = x_ref[:, pl.ds(start, width)]
 
 
 def column():
@@ -165,7 +166,8 @@
         out[piece % 4 * 8 : piece % 4 * 8 + 8] = rows
 
 
-def local_kernel(slots, chunk, x_ref, dst_ref, src_ref, cnt_ref, half_ref, acc_ref):
+def local_kernel(slots, chunk, x_ref, ends_ref, cnt_ref, half_ref, acc_ref):
+    dst_ref, src_ref = ends_ref.at[0], ends_ref.at[1]
     step = pl.program_id(0)
     width = cnt_ref.shape[1]
     dim = x_ref.shape[1]
@@ -186,8 +188,9 @@
 
 
 def aggregate_kernel(
-    slots, a_ref, b_ref, dst_ref, src_ref, half_ref, acc_in, plus_ref, minus_ref, deg_ref, acc_ref
+    slots, a_ref, b_ref, ends_ref, half_ref, acc_in, plus_ref, minus_ref, deg_ref, acc_ref
 ):
+    dst_ref, src_ref = ends_ref.at[0], ends_ref.at[1]
     place_a, place_b = places()
     z_hi = column()[1]
     cap, dim, width = a_ref.shape[1:]
@@ -274,8 +277,9 @@
 
 
 def contribution_kernel(
-    slots, zero_ref, one_ref, two_ref, three_ref, deg_ref, dst_ref, src_ref, half_ref, *outs
+    slots, zero_ref, one_ref, two_ref, three_ref, deg_ref, ends_ref, half_ref, *outs
 ):
+    dst_ref, src_ref = ends_ref.at[0], ends_ref.at[1]
     a_ref, b_ref, scaled_ref, hold_ref = outs
     place_a, place_b = places()
     blocks = scaled_ref.shape[0]
@@ -293,8 +297,9 @@
 
 
 def local_back_kernel(
-    slots, zero_ref, one_ref, two_ref, three_ref, scaled_ref, dst_ref, src_ref, half_ref, acc_ref
+    slots, zero_ref, one_ref, two_ref, three_ref, scaled_ref, ends_ref, half_ref, acc_ref
 ):
+    dst_ref, src_ref = ends_ref.at[0], ends_ref.at[1]
     for block, piece in home_pieces((zero_ref, one_ref, two_ref, three_ref), 1):
         acc_ref[block] = piece.astype(F32)
     for tile in range(slots, half_ref.shape[0]):
@@ -362,6 +367,7 @@
     tiles, width = tile_cnt.shape[:2]
     blocks = nodes // width
     table = send_blk[0].T
+    ends = jnp.stack([tile_dst, tile_src])
     cap, kinds = table.shape
     slots = kinds * cap
     cols = X * Z_HI
@@ -372,11 +378,18 @@
     halo = shape(GROUP, cap)
     step = Z_LO // 2
 
-    send_b, feats = call(
-        functools.partial(pack_kernel, width), (halo, shape(blocks)), [VMEM, SMEM]
+    hbm = pl.BlockSpec(memory_space=pltpu.HBM)
+    send_a, send_b, feats = call(
+        functools.partial(pack_kernel, width),
+        (halo, halo, shape(blocks)),
+        [hbm, hbm],
+        [
+            pltpu.VMEM((dim, nodes), BF16),
+            pltpu.SMEM((cap, kinds), jnp.int32),
+            pltpu.SemaphoreType.DMA((2,)),
+        ],
     )(node_feats, table)
     got_b = swap(send_b, GROUP // 2)
-    send_a = call(near_kernel, halo, [VMEM, SMEM])(feats, table)
     xc_plus, xc_minus = call(
         functools.partial(split_kernel, width), (shape(X, 2, per_col),) * 2, [VMEM] * 2
     )(feats, cotangent)
@@ -391,7 +404,6 @@
         in_specs=[
             whole((blocks, dim, width)),
             SMEM,
-            SMEM,
             pl.BlockSpec((chunk, width, width), lambda i: (i, 0, 0)),
         ],
         out_specs=(
@@ -402,7 +414,7 @@
         cost_estimate=pl.CostEstimate(
             flops=60000000, bytes_accessed=6000000, transcendentals=0
         ),
-    )(feats, tile_dst, tile_src, tile_cnt)
+    )(feats, ends, tile_cnt)
     send_a, got_b, xc_plus, xc_minus, half, acc = lax.optimization_barrier(
         (send_a, got_b, xc_plus, xc_minus, half, acc)
     )
@@ -414,9 +426,9 @@
     agg_plus, agg_minus, degree = call(
         functools.partial(aggregate_kernel, slots),
         (shape(X, per_col), shape(X, per_col), jax.ShapeDtypeStruct((blocks, 8, width), F32)),
-        [VMEM, VMEM, SMEM, SMEM, VMEM, VMEM],
+        [VMEM, VMEM, SMEM, VMEM, VMEM],
         [pltpu.VMEM((blocks, dim + 8, width), F32)],
-    )(got_a, got_b, tile_dst, tile_src, half, acc)
+    )(got_a, got_b, ends, half, acc)
     agg_plus = along_z(agg_plus, step)
     agg_minus = along_z(agg_minus, -step)
     ranged = call(join_kernel, shape(X, 3, 2, per_col), [VMEM] * 4)(
@@ -469,9 +481,9 @@
     away_a, away_b, scaled = call(
         functools.partial(contribution_kernel, slots),
         (halo, halo, shape(blocks)),
-        [VMEM] * 5 + [SMEM, SMEM, VMEM],
+        [VMEM] * 5 + [SMEM, VMEM],
         [pltpu.VMEM((slots, dim, width), BF16)],
-    )(*home, degree, tile_dst, tile_src, half)
+    )(*home, degree, ends, half)
     row = jax.ShapeDtypeStruct((1, 8, full), F32)
     rows, tail = call(
         total_kernel,
@@ -488,8 +500,8 @@
     acc = call(
         functools.partial(local_back_kernel, slots),
         jax.ShapeDtypeStruct((blocks, dim, width), F32),
-        [VMEM] * 5 + [SMEM, SMEM, VMEM],
-    )(*home, scaled, tile_dst, tile_src, half)
+        [VMEM] * 5 + [SMEM, VMEM],
+    )(*home, scaled, ends, half)
     away_a, back_b, rows = lax.optimization_barrier((away_a, back_b, rows))
     back_a = swap(away_a, 0)
     grad = jax.ShapeDtypeStruct((dim, full), F32)

time: 167 us -> 167 us (level)
  local copies, waits for them, and re-layouts: 7.47 us -> 5.46 us
  waiting for transfers between devices: 34.4 us -> 36.3 us
    unnamed x28 -> x18, local copies, waits for them, and re-layouts: 6.74 us -> 4.73 us
    all_to_all x4, waiting for transfers between devices: 0.92 us -> 2.76 us  [swap(): lax.all_to_all(rows, 'blk', 0, 0, axis_index_groups=groups, tiled=False)]
  transfers between devices with their start and end apart: 19 -> 19, of which waited for: 11 -> 12; matrix products, arithmetic and copies ran while one was open for 1% -> 1% of each run, Pallas kernels for 5% -> 5%
where the time goes in v12:
time: 167 us; the launch traced here: 165 us
  starting transfers between devices  109 us (65%)
  waiting for transfers between devices  36.3 us (22%)
  Pallas kernels  13.1 us (8%)
  local copies, waits for them, and re-layouts  5.46 us (3%)
    all_to_all x4, starting transfers between devices, swap(): lax.all_to_all(rows, 'blk', 0, 0, axis_index_groups=groups, tiled=False)  37.4 us
    ppermute x6, starting transfers between devices, along_z(): return lax.ppermute(rows, ('blk', 'col'), sorted(route))  31.2 us
    all_to_all x1, starting transfers between devices, per_device(): part = lax.all_to_all(part, both, 0, 0, axis_index_groups=line, tiled=False)  9.88 us
    all_to_all x1, starting transfers between devices, per_device(): part = lax.all_to_all(part, both, 0, 0, axis_index_groups=flat, tiled=False)  8.68 us
    ppermute x3, starting transfers between devices, per_device(): lax.ppermute(home[turn], 'col', route(turn))  8.38 us
    ppermute x6, waiting for transfers between devices, along_z(): return lax.ppermute(rows, ('blk', 'col'), sorted(route))  8.32 us
    ppermute x3, starting transfers between devices, across(): lax.ppermute(rows, 'blk', [(e, e ^ bit) for e in range(lax.axis_size('blk...  8.19 us
    all_to_all x1, waiting for transfers between devices, per_device(): part = lax.all_to_all(part, both, 0, 0, axis_index_groups=flat, tiled=False)  8.07 us
  transfers between devices with their start and end apart: 19, of which 12 were waited for; matrix products, arithmetic and copies ran while one was open for 1% of the time, Pallas kernels for 5%

profile of v12, /device:TPU:6, one launch (start us, length us, event | category | flops | bytes accessed | tf_op | source)
XLA Modules:
  0.0 165.0 jit_solution(13376451008205126143)
XLA Ops:
  2.2 1.7 %shard_map.120 = (bf16[8,4,32,128]{3,2,1,0:T(8,128)(2,1)}, bf16[8,4,32,128]{3,2,1,0:T(8,128)(2,1)}, bf16[16,32,128]{2,1,0:T(8,128)(2,1)S(1)}) custom-call(bf16[32,2048]{1,0:T(8,128)(2,1)S(1)} %copy-done.3, s32[4,8]{1,0:T(4,128)S(1)} %bitcast.12), custom_call_target="tpu_custom_call" | custom-call | flops 10000000 | bytes 1000000 | tf_op jit(solution)/shard_map/pallas_call | solution.py:382
  3.9 15.7 %all-to-all-start = ((bf16[8,4,32,128]{3,2,1,0:T(8,128)(2,1)}), bf16[8,4,32,128]{3,2,1,0:T(8,128)(2,1)S(1)}, u32[]{:S(2)}, u32[]{:S(2)}) async-start(bf16[8,4,32,128]{3,2,1,0:T(8,128)(2,1)} %get-tuple-element.46), calls=%async_computation | async-start | bytes 524288 | tf_op jit(solution)/shard_map/all_to_all | solution.py:334
  21.3 2.0 %copy-done = s32[56,128,128]{2,1,0:T(8,128)S(1)} copy-done((s32[56,128,128]{2,1,0:T(8,128)S(1)}, s32[56,128,128]{2,1,0:T(8,128)}, u32[]{:S(2)}) %copy-start) | copy-done | bytes 3670040
  23.3 1.8 %shard_map.122 = (bf16[56,128,128]{2,1,0:T(8,128)(2,1)S(1)}, f32[16,40,128]{2,1,0:T(8,128)S(1)}) custom-call(bf16[16,32,128]{2,1,0:T(8,128)(2,1)S(1)} %get-tuple-element.47.x_ref, s32[2,56]{1,0:T(2,128)S(1)} %pad_add_fusion.ends_ref, s32[56,128,128]{2,1,0:T(8,128)S(1)} %copy-done), custom_call_target="tpu_custom_call" | custom-call | flops 60000000 | bytes 6000000 | tf_op jit(solution)/shard_map/pallas_call | solution.py:397
  25.1 1.8 %all-to-all-done.b_ref = bf16[8,4,32,128]{3,2,1,0:T(8,128)(2,1)S(1)} async-done(((bf16[8,4,32,128]{3,2,1,0:T(8,128)(2,1)}), bf16[8,4,32,128]{3,2,1,0:T(8,128)(2,1)S(1)}, u32[]{:S(2)}, u32[]{:S(2)}) %all-to-all-start) | async-done | bytes 262176 | tf_op jit(solution)/shard_map/all_to_all | solution.py:334
  27.0 4.8 %all-to-all-start.1 = ((bf16[8,4,32,128]{3,2,1,0:T(8,128)(2,1)}), bf16[8,4,32,128]{3,2,1,0:T(8,128)(2,1)S(1)}, u32[]{:S(2)}, u32[]{:S(2)}) async-start(bf16[8,4,32,128]{3,2,1,0:T(8,128)(2,1)} %get-tuple-element.54), calls=%async_computation.1 | async-start | bytes 524288 | tf_op jit(solution)/shard_map/all_to_all | solution.py:334
  31.8 4.7 %collective-permute-start = (bf16[4,2,2,32,128]{4,3,2,1,0:T(8,128)(2,1)S(1)}, bf16[4,2,2,32,128]{4,3,2,1,0:T(8,128)(2,1)S(1)}, u32[]{:S(2)}, u32[]{:S(2)}) collective-permute-start(bf16[4,2,2,32,128]{4,3,2,1,0:T(8,128)(2,1)S(1)} %get-tuple-element.52), channel_id=1, source_target_pairs={{0,64},{1,65},{2,66},{3,67},{4,68},{5,69},{6,70},{7,71},{8,72},{9,... | collective-permute-start | bytes 393224 | tf_op jit(solution)/shard_map/ppermute | solution.py:360
  36.5 7.0 %collective-permute-start.1 = (bf16[4,2,2,32,128]{4,3,2,1,0:T(8,128)(2,1)S(1)}, bf16[4,2,2,32,128]{4,3,2,1,0:T(8,128)(2,1)S(1)}, u32[]{:S(2)}, u32[]{:S(2)}) collective-permute-start(bf16[4,2,2,32,128]{4,3,2,1,0:T(8,128)(2,1)S(1)} %get-tuple-element.53), channel_id=1, source_target_pairs={{0,65},{1,64},{2,67},{3,66},{4,69},{5,68},{6,71},{7,70},{8,73},{9,... | collective-permute-start | bytes 393224 | tf_op jit(solution)/shard_map/ppermute | solution.py:360
  44.9 3.2 %collective-permute-start.2 = (bf16[4,2,32,128]{3,2,1,0:T(8,128)(2,1)S(1)}, bf16[4,2,32,128]{3,2,1,0:T(8,128)(2,1)S(1)}, u32[]{:S(2)}, u32[]{:S(2)}) collective-permute-start(bf16[4,2,32,128]{3,2,1,0:T(8,128)(2,1)S(1)} %get-tuple-element.58), channel_id=1, source_target_pairs={{0,64},{1,65},{2,66},{3,67},{4,68},{5,69},{6,70},{7,71},{8,72},{9,... | collective-permute-start | bytes 196616 | tf_op jit(solution)/shard_map/ppermute | solution.py:360
  48.1 6.6 %collective-permute-start.3 = (bf16[4,2,32,128]{3,2,1,0:T(8,128)(2,1)S(1)}, bf16[4,2,32,128]{3,2,1,0:T(8,128)(2,1)S(1)}, u32[]{:S(2)}, u32[]{:S(2)}) collective-permute-start(bf16[4,2,32,128]{3,2,1,0:T(8,128)(2,1)S(1)} %get-tuple-element.59), channel_id=1, source_target_pairs={{0,65},{1,64},{2,67},{3,66},{4,69},{5,68},{6,71},{7,70},{8,73},{9,... | collective-permute-start | bytes 196616 | tf_op jit(solution)/shard_map/ppermute | solution.py:360
  55.9 6.2 %collective-permute-done.2.agg_plus_ref = bf16[4,2,32,128]{3,2,1,0:T(8,128)(2,1)S(1)} collective-permute-done((bf16[4,2,32,128]{3,2,1,0:T(8,128)(2,1)S(1)}, bf16[4,2,32,128]{3,2,1,0:T(8,128)(2,1)S(1)}, u32[]{:S(2)}, u32[]{:S(2)}) %collective-permute-start.2) | collective-permute-done | bytes 65568 | tf_op jit(solution)/shard_map/ppermute | solution.py:360
  63.8 4.8 %all-to-all-start.2 = ((bf16[4,3,2,2,32,128]{5,4,3,2,1,0:T(8,128)(2,1)}), bf16[4,3,2,2,32,128]{5,4,3,2,1,0:T(8,128)(2,1)S(1)}, u32[]{:S(2)}, u32[]{:S(2)}) async-start(bf16[4,3,2,2,32,128]{5,4,3,2,1,0:T(8,128)(2,1)} %shard_map.124), calls=%async_computation.2 | async-start | bytes 786432 | tf_op jit(solution)/shard_map/all_to_all | solution.py:343
  68.9 4.9 %all-to-all-done.2.in_ref = bf16[4,3,2,2,32,128]{5,4,3,2,1,0:T(8,128)(2,1)S(1)} async-done(((bf16[4,3,2,2,32,128]{5,4,3,2,1,0:T(8,128)(2,1)}), bf16[4,3,2,2,32,128]{5,4,3,2,1,0:T(8,128)(2,1)S(1)}, u32[]{:S(2)}, u32[]{:S(2)}) %all-to-all-start.2) | async-done | bytes 393248 | tf_op jit(solution)/shard_map/all_to_all | solution.py:343
  74.8 6.7 %collective-permute-start.4 = (bf16[4,2,2,32,128]{4,3,2,1,0:T(8,128)(2,1)S(1)}, bf16[4,2,2,32,128]{4,3,2,1,0:T(8,128)(2,1)S(1)}, u32[]{:S(2)}, u32[]{:S(2)}) collective-permute-start(bf16[4,2,2,32,128]{4,3,2,1,0:T(8,128)(2,1)S(1)} %get-tuple-element.62), channel_id=1, source_target_pairs={{0,64},{1,65},{2,66},{3,67},{4,68},{5,69},{6,70},{7,71},{8,72},{9,... | collective-permute-start | bytes 393224 | tf_op jit(solution)/shard_map/ppermute | solution.py:360
  81.5 3.1 %collective-permute-start.5 = (bf16[4,2,2,32,128]{4,3,2,1,0:T(8,128)(2,1)S(1)}, bf16[4,2,2,32,128]{4,3,2,1,0:T(8,128)(2,1)S(1)}, u32[]{:S(2)}, u32[]{:S(2)}) collective-permute-start(bf16[4,2,2,32,128]{4,3,2,1,0:T(8,128)(2,1)S(1)} %get-tuple-element.63), channel_id=1, source_target_pairs={{0,65},{1,64},{2,67},{3,66},{4,69},{5,68},{6,71},{7,70},{8,73},{9,... | collective-permute-start | bytes 393224 | tf_op jit(solution)/shard_map/ppermute | solution.py:360
  85.6 8.7 %all-to-all-start.3 = ((bf16[32,5,8,128]{3,2,1,0:T(8,128)(2,1)}), bf16[32,5,8,128]{3,2,1,0:T(8,128)(2,1)S(1)}, u32[]{:S(2)}, u32[]{:S(2)}) async-start(bf16[32,5,8,128]{3,2,1,0:T(8,128)(2,1)} %shard_map.126), calls=%async_computation.3 | async-start | bytes 655360 | tf_op jit(solution)/shard_map/all_to_all | solution.py:472
  94.3 8.1 %all-to-all-done.3.part_ref = bf16[32,5,8,128]{3,2,1,0:T(8,128)(2,1)S(1)} async-done(((bf16[32,5,8,128]{3,2,1,0:T(8,128)(2,1)}), bf16[32,5,8,128]{3,2,1,0:T(8,128)(2,1)S(1)}, u32[]{:S(2)}, u32[]{:S(2)}) %all-to-all-start.3) | async-done | bytes 327712 | tf_op jit(solution)/shard_map/all_to_all | solution.py:472
  103.1 9.9 %all-to-all-start.4 = ((bf16[16,3,8,128]{3,2,1,0:T(8,128)(2,1)}), bf16[16,3,8,128]{3,2,1,0:T(8,128)(2,1)S(1)}, u32[]{:S(2)}, u32[]{:S(2)}) async-start(bf16[16,3,8,128]{3,2,1,0:T(8,128)(2,1)} %shard_map.130), calls=%async_computation.4 | async-start | bytes 196608 | tf_op jit(solution)/shard_map/all_to_all | solution.py:478
  113.0 3.7 %collective-permute-start.6 = (bf16[2,2,2,32,128]{4,3,2,1,0:T(8,128)(2,1)S(1)}, bf16[2,2,2,32,128]{4,3,2,1,0:T(8,128)(2,1)S(1)}, u32[]{:S(2)}, u32[]{:S(2)}) collective-permute-start(bf16[2,2,2,32,128]{4,3,2,1,0:T(8,128)(2,1)S(1)} %get-tuple-element.69), channel_id=1, source_target_pairs={{0,2},{1,3},{2,4},{3,5},{4,6},{5,7},{6,0},{7,1},{8,10},{9,11},{10,... | collective-permute-start | bytes 196616 | tf_op jit(solution)/shard_map/ppermute | solution.py:480
  116.7 2.4 %collective-permute-start.7 = (bf16[2,2,2,32,128]{4,3,2,1,0:T(8,128)(2,1)S(1)}, bf16[2,2,2,32,128]{4,3,2,1,0:T(8,128)(2,1)S(1)}, u32[]{:S(2)}, u32[]{:S(2)}) collective-permute-start(bf16[2,2,2,32,128]{4,3,2,1,0:T(8,128)(2,1)S(1)} %get-tuple-element.70), channel_id=1, source_target_pairs={{0,4},{1,5},{2,6},{3,7},{4,0},{5,1},{6,2},{7,3},{8,12},{9,13},{10,... | collective-permute-start | bytes 196616 | tf_op jit(solution)/shard_map/ppermute | solution.py:480
  119.1 2.3 %collective-permute-start.8 = (bf16[2,2,2,32,128]{4,3,2,1,0:T(8,128)(2,1)S(1)}, bf16[2,2,2,32,128]{4,3,2,1,0:T(8,128)(2,1)S(1)}, u32[]{:S(2)}, u32[]{:S(2)}) collective-permute-start(bf16[2,2,2,32,128]{4,3,2,1,0:T(8,128)(2,1)S(1)} %get-tuple-element.71), channel_id=1, source_target_pairs={{0,6},{1,7},{2,0},{3,1},{4,2},{5,3},{6,4},{7,5},{8,14},{9,15},{10,... | collective-permute-start | bytes 196616 | tf_op jit(solution)/shard_map/ppermute | solution.py:480
  121.4 3.0 %collective-permute-done.7.two_ref = bf16[2,2,2,32,128]{4,3,2,1,0:T(8,128)(2,1)S(1)} collective-permute-done((bf16[2,2,2,32,128]{4,3,2,1,0:T(8,128)(2,1)S(1)}, bf16[2,2,2,32,128]{4,3,2,1,0:T(8,128)(2,1)S(1)}, u32[]{:S(2)}, u32[]{:S(2)}) %collective-permute-start.7) | collective-permute-done | bytes 65568 | tf_op jit(solution)/shard_map/ppermute | solution.py:480
  124.4 2.1 %collective-permute-done.8.three_ref = bf16[2,2,2,32,128]{4,3,2,1,0:T(8,128)(2,1)S(1)} collective-permute-done((bf16[2,2,2,32,128]{4,3,2,1,0:T(8,128)(2,1)S(1)}, bf16[2,2,2,32,128]{4,3,2,1,0:T(8,128)(2,1)S(1)}, u32[]{:S(2)}, u32[]{:S(2)}) %collective-permute-start.8) | collective-permute-done | bytes 65568 | tf_op jit(solution)/shard_map/ppermute | solution.py:480
  126.5 1.8 %shard_map.128 = (bf16[8,4,32,128]{3,2,1,0:T(8,128)(2,1)}, bf16[8,4,32,128]{3,2,1,0:T(8,128)(2,1)}, bf16[16,32,128]{2,1,0:T(8,128)(2,1)S(1)}) custom-call(bf16[2,2,2,32,128]{4,3,2,1,0:T(8,128)(2,1)S(1)} %get-tuple-element.68.zero_ref, bf16[2,2,2,32,128]{4,3,2,1,0:T(8,128)(2,1)S(1)} %collective-permute-done.6.one_ref, ...), custom_call_target="tpu_custom_call" | custom-call | flops 10000000 | bytes 1000000 | tf_op jit(solution)/shard_map/pallas_call | solution.py:481
  128.3 11.6 %all-to-all-start.5 = ((bf16[8,4,32,128]{3,2,1,0:T(8,128)(2,1)}), bf16[8,4,32,128]{3,2,1,0:T(8,128)(2,1)S(1)}, u32[]{:S(2)}, u32[]{:S(2)}) async-start(bf16[8,4,32,128]{3,2,1,0:T(8,128)(2,1)} %get-tuple-element.78), calls=%async_computation.5 | async-start | bytes 524288 | tf_op jit(solution)/shard_map/all_to_all | solution.py:334
  139.9 2.0 %collective-permute-start.9 = (f32[1,8,256]{2,1,0:T(8,128)S(1)}, f32[1,8,256]{2,1,0:T(8,128)S(1)}, u32[]{:S(2)}, u32[]{:S(2)}) collective-permute-start(f32[1,8,256]{2,1,0:T(8,128)S(1)} %get-tuple-element.79.one_ref), channel_id=1, source_target_pairs={{0,8},{8,0},{16,24},{24,16},{32,40},{40,32},{48,56},{56,48},{64,72... | collective-permute-start | bytes 24584 | tf_op jit(solution)/shard_map/ppermute | solution.py:338
  142.9 2.7 %collective-permute-start.10 = (f32[2,8,256]{2,1,0:T(8,128)S(1)}, f32[2,8,256]{2,1,0:T(8,128)S(1)}, u32[]{:S(2)}, u32[]{:S(2)}) collective-permute-start(f32[2,8,256]{2,1,0:T(8,128)S(1)} %shard_map.132.one_ref), channel_id=1, source_target_pairs={{0,128},{8,136},{16,144},{24,152},{32,160},{40,168},{48,176},{56,1... | collective-permute-start | bytes 49160 | tf_op jit(solution)/shard_map/ppermute | solution.py:338
  145.7 2.9 %collective-permute-done.10.two_ref = f32[2,8,256]{2,1,0:T(8,128)S(1)} collective-permute-done((f32[2,8,256]{2,1,0:T(8,128)S(1)}, f32[2,8,256]{2,1,0:T(8,128)S(1)}, u32[]{:S(2)}, u32[]{:S(2)}) %collective-permute-start.10) | collective-permute-done | bytes 16416 | tf_op jit(solution)/shard_map/ppermute | solution.py:338
  148.6 5.3 %all-to-all-start.6 = ((bf16[8,4,32,128]{3,2,1,0:T(8,128)(2,1)}), bf16[8,4,32,128]{3,2,1,0:T(8,128)(2,1)S(1)}, u32[]{:S(2)}, u32[]{:S(2)}) async-start(bf16[8,4,32,128]{3,2,1,0:T(8,128)(2,1)} %get-tuple-element.80), calls=%async_computation.6 | async-start | bytes 524288 | tf_op jit(solution)/shard_map/all_to_all | solution.py:334
  154.8 3.4 %collective-permute-start.11 = (f32[4,8,256]{2,1,0:T(8,128)S(1)}, f32[4,8,256]{2,1,0:T(8,128)S(1)}, u32[]{:S(2)}, u32[]{:S(2)}) collective-permute-start(f32[4,8,256]{2,1,0:T(8,128)S(1)} %shard_map.133.near_ref), channel_id=1, source_target_pairs={{0,256},{8,264},{16,272},{24,280},{32,288},{40,296},{48,304},{56,3... | collective-permute-start | bytes 98312 | tf_op jit(solution)/shard_map/ppermute | solution.py:338
  158.8 3.3 %collective-permute-done.11.far_ref = f32[4,8,256]{2,1,0:T(8,128)S(1)} collective-permute-done((f32[4,8,256]{2,1,0:T(8,128)S(1)}, f32[4,8,256]{2,1,0:T(8,128)S(1)}, u32[]{:S(2)}, u32[]{:S(2)}) %collective-permute-start.11) | collective-permute-done | bytes 32800 | tf_op jit(solution)/shard_map/ppermute | solution.py:338
  163.6 1.4 shard_map.134
  (46 shorter events, 14.6 us)
Async XLA Ops:
  0.6 0.9 copy-start.3
  1.5 0.7 copy-start.5
  3.9 23.0 %all-to-all-start = ((bf16[8,4,32,128]{3,2,1,0:T(8,128)(2,1)}), bf16[8,4,32,128]{3,2,1,0:T(8,128)(2,1)S(1)}, u32[]{:S(2)}, u32[]{:S(2)}) async-start(bf16[8,4,32,128]{3,2,1,0:T(8,128)(2,1)} %get-tuple-element.46), calls=%async_computation | async-start | bytes 524288 | tf_op jit(solution)/shard_map/all_to_all | solution.py:334
  19.6 0.9 copy-start.4
  21.3 2.0 %copy-start = (s32[56,128,128]{2,1,0:T(8,128)S(1)}, s32[56,128,128]{2,1,0:T(8,128)}, u32[]{:S(2)}) copy-start(s32[56,128,128]{2,1,0:T(8,128)} %cnt_ref.1) | copy-start | bytes 11010052
  23.3 45.2 %copy-start.2 = (bf16[256,256]{1,0:T(8,128)(2,1)S(1)}, bf16[256,256]{1,0:T(8,128)(2,1)}, u32[]{:S(2)}) copy-start(bf16[256,256]{1,0:T(8,128)(2,1)} %own_w_ref.1) | copy-start | bytes 393220
  23.3 45.3 %copy-start.1 = (bf16[256,256]{1,0:T(8,128)(2,1)S(1)}, bf16[256,256]{1,0:T(8,128)(2,1)}, u32[]{:S(2)}) copy-start(bf16[256,256]{1,0:T(8,128)(2,1)} %neigh_ref.1) | copy-start | bytes 393220
  23.3 45.4 %copy-start.7 = (f32[256]{0:T(256)S(1)}, f32[256]{0:T(256)}, u32[]{:S(2)}) copy-start(f32[256]{0:T(256)} %param.16) | copy-start | bytes 3076
  27.0 16.6 %all-to-all-start.1 = ((bf16[8,4,32,128]{3,2,1,0:T(8,128)(2,1)}), bf16[8,4,32,128]{3,2,1,0:T(8,128)(2,1)S(1)}, u32[]{:S(2)}, u32[]{:S(2)}) async-start(bf16[8,4,32,128]{3,2,1,0:T(8,128)(2,1)} %get-tuple-element.54), calls=%async_computation.1 | async-start | bytes 524288 | tf_op jit(solution)/shard_map/all_to_all | solution.py:334
  31.8 22.9 %collective-permute-start = (bf16[4,2,2,32,128]{4,3,2,1,0:T(8,128)(2,1)S(1)}, bf16[4,2,2,32,128]{4,3,2,1,0:T(8,128)(2,1)S(1)}, u32[]{:S(2)}, u32[]{:S(2)}) collective-permute-start(bf16[4,2,2,32,128]{4,3,2,1,0:T(8,128)(2,1)S(1)} %get-tuple-element.52), channel_id=1, source_target_pairs={{0,64},{1,65},{2,66},{3,67},{4,68},{5,69},{6,70},{7,71},{8,72},{9,... | collective-permute-start | bytes 393224 | tf_op jit(solution)/shard_map/ppermute | solution.py:360
  36.5 19.4 %collective-permute-start.1 = (bf16[4,2,2,32,128]{4,3,2,1,0:T(8,128)(2,1)S(1)}, bf16[4,2,2,32,128]{4,3,2,1,0:T(8,128)(2,1)S(1)}, u32[]{:S(2)}, u32[]{:S(2)}) collective-permute-start(bf16[4,2,2,32,128]{4,3,2,1,0:T(8,128)(2,1)S(1)} %get-tuple-element.53), channel_id=1, source_target_pairs={{0,65},{1,64},{2,67},{3,66},{4,69},{5,68},{6,71},{7,70},{8,73},{9,... | collective-permute-start | bytes 393224 | tf_op jit(solution)/shard_map/ppermute | solution.py:360
  44.9 17.1 %collective-permute-start.2 = (bf16[4,2,32,128]{3,2,1,0:T(8,128)(2,1)S(1)}, bf16[4,2,32,128]{3,2,1,0:T(8,128)(2,1)S(1)}, u32[]{:S(2)}, u32[]{:S(2)}) collective-permute-start(bf16[4,2,32,128]{3,2,1,0:T(8,128)(2,1)S(1)} %get-tuple-element.58), channel_id=1, source_target_pairs={{0,64},{1,65},{2,66},{3,67},{4,68},{5,69},{6,70},{7,71},{8,72},{9,... | collective-permute-start | bytes 196616 | tf_op jit(solution)/shard_map/ppermute | solution.py:360
  48.1 14.9 %collective-permute-start.3 = (bf16[4,2,32,128]{3,2,1,0:T(8,128)(2,1)S(1)}, bf16[4,2,32,128]{3,2,1,0:T(8,128)(2,1)S(1)}, u32[]{:S(2)}, u32[]{:S(2)}) collective-permute-start(bf16[4,2,32,128]{3,2,1,0:T(8,128)(2,1)S(1)} %get-tuple-element.59), channel_id=1, source_target_pairs={{0,65},{1,64},{2,67},{3,66},{4,69},{5,68},{6,71},{7,70},{8,73},{9,... | collective-permute-start | bytes 196616 | tf_op jit(solution)/shard_map/ppermute | solution.py:360
  63.8 10.1 %all-to-all-start.2 = ((bf16[4,3,2,2,32,128]{5,4,3,2,1,0:T(8,128)(2,1)}), bf16[4,3,2,2,32,128]{5,4,3,2,1,0:T(8,128)(2,1)S(1)}, u32[]{:S(2)}, u32[]{:S(2)}) async-start(bf16[4,3,2,2,32,128]{5,4,3,2,1,0:T(8,128)(2,1)} %shard_map.124), calls=%async_computation.2 | async-start | bytes 786432 | tf_op jit(solution)/shard_map/all_to_all | solution.py:343
  74.8 19.5 %collective-permute-start.4 = (bf16[4,2,2,32,128]{4,3,2,1,0:T(8,128)(2,1)S(1)}, bf16[4,2,2,32,128]{4,3,2,1,0:T(8,128)(2,1)S(1)}, u32[]{:S(2)}, u32[]{:S(2)}) collective-permute-start(bf16[4,2,2,32,128]{4,3,2,1,0:T(8,128)(2,1)S(1)} %get-tuple-element.62), channel_id=1, source_target_pairs={{0,64},{1,65},{2,66},{3,67},{4,68},{5,69},{6,70},{7,71},{8,72},{9,... | collective-permute-start | bytes 393224 | tf_op jit(solution)/shard_map/ppermute | solution.py:360
  81.5 12.8 %collective-permute-start.5 = (bf16[4,2,2,32,128]{4,3,2,1,0:T(8,128)(2,1)S(1)}, bf16[4,2,2,32,128]{4,3,2,1,0:T(8,128)(2,1)S(1)}, u32[]{:S(2)}, u32[]{:S(2)}) collective-permute-start(bf16[4,2,2,32,128]{4,3,2,1,0:T(8,128)(2,1)S(1)} %get-tuple-element.63), channel_id=1, source_target_pairs={{0,65},{1,64},{2,67},{3,66},{4,69},{5,68},{6,71},{7,70},{8,73},{9,... | collective-permute-start | bytes 393224 | tf_op jit(solution)/shard_map/ppermute | solution.py:360
  85.6 16.8 %all-to-all-start.3 = ((bf16[32,5,8,128]{3,2,1,0:T(8,128)(2,1)}), bf16[32,5,8,128]{3,2,1,0:T(8,128)(2,1)S(1)}, u32[]{:S(2)}, u32[]{:S(2)}) async-start(bf16[32,5,8,128]{3,2,1,0:T(8,128)(2,1)} %shard_map.126), calls=%async_computation.3 | async-start | bytes 655360 | tf_op jit(solution)/shard_map/all_to_all | solution.py:472
  94.3 69.3 %copy-start.6 = (s32[1,8,4]{1,2,0:T(4,128)S(1)}, s32[1,8,4]{1,2,0:T(4,128)}, u32[]{:S(2)}) copy-start(s32[1,8,4]{1,2,0:T(4,128)} %param.13) | copy-start | bytes 388
  103.1 25.2 %all-to-all-start.4 = ((bf16[16,3,8,128]{3,2,1,0:T(8,128)(2,1)}), bf16[16,3,8,128]{3,2,1,0:T(8,128)(2,1)S(1)}, u32[]{:S(2)}, u32[]{:S(2)}) async-start(bf16[16,3,8,128]{3,2,1,0:T(8,128)(2,1)} %shard_map.130), calls=%async_computation.4 | async-start | bytes 196608 | tf_op jit(solution)/shard_map/all_to_all | solution.py:478
  113.0 8.4 %collective-permute-start.6 = (bf16[2,2,2,32,128]{4,3,2,1,0:T(8,128)(2,1)S(1)}, bf16[2,2,2,32,128]{4,3,2,1,0:T(8,128)(2,1)S(1)}, u32[]{:S(2)}, u32[]{:S(2)}) collective-permute-start(bf16[2,2,2,32,128]{4,3,2,1,0:T(8,128)(2,1)S(1)} %get-tuple-element.69), channel_id=1, source_target_pairs={{0,2},{1,3},{2,4},{3,5},{4,6},{5,7},{6,0},{7,1},{8,10},{9,11},{10,... | collective-permute-start | bytes 196616 | tf_op jit(solution)/shard_map/ppermute | solution.py:480
  116.7 7.7 %collective-permute-start.7 = (bf16[2,2,2,32,128]{4,3,2,1,0:T(8,128)(2,1)S(1)}, bf16[2,2,2,32,128]{4,3,2,1,0:T(8,128)(2,1)S(1)}, u32[]{:S(2)}, u32[]{:S(2)}) collective-permute-start(bf16[2,2,2,32,128]{4,3,2,1,0:T(8,128)(2,1)S(1)} %get-tuple-element.70), channel_id=1, source_target_pairs={{0,4},{1,5},{2,6},{3,7},{4,0},{5,1},{6,2},{7,3},{8,12},{9,13},{10,... | collective-permute-start | bytes 196616 | tf_op jit(solution)/shard_map/ppermute | solution.py:480
  119.1 7.4 %collective-permute-start.8 = (bf16[2,2,2,32,128]{4,3,2,1,0:T(8,128)(2,1)S(1)}, bf16[2,2,2,32,128]{4,3,2,1,0:T(8,128)(2,1)S(1)}, u32[]{:S(2)}, u32[]{:S(2)}) collective-permute-start(bf16[2,2,2,32,128]{4,3,2,1,0:T(8,128)(2,1)S(1)} %get-tuple-element.71), channel_id=1, source_target_pairs={{0,6},{1,7},{2,0},{3,1},{4,2},{5,3},{6,4},{7,5},{8,14},{9,15},{10,... | collective-permute-start | bytes 196616 | tf_op jit(solution)/shard_map/ppermute | solution.py:480
  128.3 20.3 %all-to-all-start.5 = ((bf16[8,4,32,128]{3,2,1,0:T(8,128)(2,1)}), bf16[8,4,32,128]{3,2,1,0:T(8,128)(2,1)S(1)}, u32[]{:S(2)}, u32[]{:S(2)}) async-start(bf16[8,4,32,128]{3,2,1,0:T(8,128)(2,1)} %get-tuple-element.78), calls=%async_computation.5 | async-start | bytes 524288 | tf_op jit(solution)/shard_map/all_to_all | solution.py:334
  139.9 3.1 %collective-permute-start.9 = (f32[1,8,256]{2,1,0:T(8,128)S(1)}, f32[1,8,256]{2,1,0:T(8,128)S(1)}, u32[]{:S(2)}, u32[]{:S(2)}) collective-permute-start(f32[1,8,256]{2,1,0:T(8,128)S(1)} %get-tuple-element.79.one_ref), channel_id=1, source_target_pairs={{0,8},{8,0},{16,24},{24,16},{32,40},{40,32},{48,56},{56,48},{64,72... | collective-permute-start | bytes 24584 | tf_op jit(solution)/shard_map/ppermute | solution.py:338
  142.9 5.6 %collective-permute-start.10 = (f32[2,8,256]{2,1,0:T(8,128)S(1)}, f32[2,8,256]{2,1,0:T(8,128)S(1)}, u32[]{:S(2)}, u32[]{:S(2)}) collective-permute-start(f32[2,8,256]{2,1,0:T(8,128)S(1)} %shard_map.132.one_ref), channel_id=1, source_target_pairs={{0,128},{8,136},{16,144},{24,152},{32,160},{40,168},{48,176},{56,1... | collective-permute-start | bytes 49160 | tf_op jit(solution)/shard_map/ppermute | solution.py:338
  148.6 15.1 %all-to-all-start.6 = ((bf16[8,4,32,128]{3,2,1,0:T(8,128)(2,1)}), bf16[8,4,32,128]{3,2,1,0:T(8,128)(2,1)S(1)}, u32[]{:S(2)}, u32[]{:S(2)}) async-start(bf16[8,4,32,128]{3,2,1,0:T(8,128)(2,1)} %get-tuple-element.80), calls=%async_computation.6 | async-start | bytes 524288 | tf_op jit(solution)/shard_map/all_to_all | solution.py:334
  154.8 7.3 %collective-permute-start.11 = (f32[4,8,256]{2,1,0:T(8,128)S(1)}, f32[4,8,256]{2,1,0:T(8,128)S(1)}, u32[]{:S(2)}, u32[]{:S(2)}) collective-permute-start(f32[4,8,256]{2,1,0:T(8,128)S(1)} %shard_map.133.near_ref), channel_id=1, source_target_pairs={{0,256},{8,264},{16,272},{24,280},{32,288},{40,296},{48,304},{56,3... | collective-permute-start | bytes 98312 | tf_op jit(solution)/shard_map/ppermute | solution.py:338

commit v13 on v12

--- a/solution.py
+++ b/solution.py
@@ -389,7 +389,7 @@
             pltpu.SemaphoreType.DMA((2,)),
         ],
     )(node_feats, table)
-    got_b = swap(send_b, GROUP // 2)
+    got_a = swap(send_a, 0)
     xc_plus, xc_minus = call(
         functools.partial(split_kernel, width), (shape(X, 2, per_col),) * 2, [VMEM] * 2
     )(feats, cotangent)
@@ -415,12 +415,12 @@
             flops=60000000, bytes_accessed=6000000, transcendentals=0
         ),
     )(feats, ends, tile_cnt)
-    send_a, got_b, xc_plus, xc_minus, half, acc = lax.optimization_barrier(
-        (send_a, got_b, xc_plus, xc_minus, half, acc)
+    send_b, got_a, xc_plus, xc_minus, half, acc = lax.optimization_barrier(
+        (send_b, got_a, xc_plus, xc_minus, half, acc)
     )
     xc_plus = along_z(xc_plus, step)
     xc_minus = along_z(xc_minus, -step)
-    got_a = swap(send_a, 0)
+    got_b = swap(send_b, GROUP // 2)
     weight_t = jnp.concatenate([self_weight.T, neigh_weight.T], axis=1)
     bias_col = bias[:, None]
     agg_plus, agg_minus, degree = call(
@@ -492,8 +492,8 @@
     )(part)
     grad_bias = jnp.concatenate([tail[0], tail[4]])
     grad_bias = lax.dynamic_slice_in_dim(grad_bias, lax.axis_index("col") * dim, dim, 0)
-    away_b, rows = lax.optimization_barrier((away_b, rows))
-    back_b = swap(away_b, GROUP // 2)
+    away_a, rows = lax.optimization_barrier((away_a, rows))
+    back_a = swap(away_a, 0)
     for bit in (1, Z_LO * CORE):
         double = jax.ShapeDtypeStruct((2 * rows.shape[0], 8, full), F32)
         rows = call(pair_kernel, double, [VMEM] * 2)(rows, across(rows, bit))
@@ -502,8 +502,8 @@
         jax.ShapeDtypeStruct((blocks, dim, width), F32),
         [VMEM] * 5 + [SMEM, VMEM],
     )(*home, scaled, ends, half)
-    away_a, back_b, rows = lax.optimization_barrier((away_a, back_b, rows))
-    back_a = swap(away_a, 0)
+    away_b, back_a, rows = lax.optimization_barrier((away_b, back_a, rows))
+    back_b = swap(away_b, GROUP // 2)
     grad = jax.ShapeDtypeStruct((dim, full), F32)
     grad_self, grad_neigh = call(order_kernel, (grad, grad), [VMEM] * 2)(
         rows, across(rows, 2 * Z_LO * CORE)

time: 167 us -> 167 us (level)
  waiting for transfers between devices: 36.3 us -> 40.4 us
  starting transfers between devices: 109 us -> 105 us
    all_to_all x4, starting transfers between devices: 37.4 us -> 34.2 us  [swap(): lax.all_to_all(rows, 'blk', 0, 0, axis_index_groups=groups, tiled=False)]
    all_to_all x4, waiting for transfers between devices: 2.76 us -> 5.16 us  [swap(): lax.all_to_all(rows, 'blk', 0, 0, axis_index_groups=groups, tiled=False)]
    all_to_all x1, starting transfers between devices: 9.88 us -> 7.52 us  [per_device(): part = lax.all_to_all(part, both, 0, 0, axis_index_groups=line, tiled=False)]
  transfers between devices with their start and end apart: 19 -> 19, of which waited for: 12 -> 11; matrix products, arithmetic and copies ran while one was open for 1% -> 1% of each run, Pallas kernels for 5% -> 5%
where the time goes in v13:
time: 167 us; the launch traced here: 165 us
  starting transfers between devices  105 us (63%)
  waiting for transfers between devices  40.4 us (24%)
  Pallas kernels  13.1 us (8%)
  local copies, waits for them, and re-layouts  5.46 us (3%)
    all_to_all x4, starting transfers between devices, swap(): lax.all_to_all(rows, 'blk', 0, 0, axis_index_groups=groups, tiled=False)  34.2 us
    ppermute x6, starting transfers between devices, along_z(): return lax.ppermute(rows, ('blk', 'col'), sorted(route))  32.3 us
    all_to_all x1, starting transfers between devices, per_device(): part = lax.all_to_all(part, both, 0, 0, axis_index_groups=flat, tiled=False)  9.87 us
    ppermute x6, waiting for transfers between devices, along_z(): return lax.ppermute(rows, ('blk', 'col'), sorted(route))  9.21 us
    ppermute x3, starting transfers between devices, per_device(): lax.ppermute(home[turn], 'col', route(turn))  8.38 us
    all_to_all x1, waiting for transfers between devices, per_device(): part = lax.all_to_all(part, both, 0, 0, axis_index_groups=flat, tiled=False)  8.07 us
    ppermute x3, waiting for transfers between devices, across(): lax.ppermute(rows, 'blk', [(e, e ^ bit) for e in range(lax.axis_size('blk...  7.96 us
    ppermute x3, starting transfers between devices, across(): lax.ppermute(rows, 'blk', [(e, e ^ bit) for e in range(lax.axis_size('blk...  7.56 us
  transfers between devices with their start and end apart: 19, of which 11 were waited for; matrix products, arithmetic and copies ran while one was open for 1% of the time, Pallas kernels for 5%

profile of v13, /device:TPU:6, one launch (start us, length us, event | category | flops | bytes accessed | tf_op | source)
XLA Modules:
  0.0 165.2 jit_solution(7220897454674278493)
XLA Ops:
  2.2 1.7 %shard_map.120 = (bf16[8,4,32,128]{3,2,1,0:T(8,128)(2,1)}, bf16[8,4,32,128]{3,2,1,0:T(8,128)(2,1)}, bf16[16,32,128]{2,1,0:T(8,128)(2,1)S(1)}) custom-call(bf16[32,2048]{1,0:T(8,128)(2,1)S(1)} %copy-done.3, s32[4,8]{1,0:T(4,128)S(1)} %bitcast.12), custom_call_target="tpu_custom_call" | custom-call | flops 10000000 | bytes 1000000 | tf_op jit(solution)/shard_map/pallas_call | solution.py:382
  3.9 5.9 %all-to-all-start = ((bf16[8,4,32,128]{3,2,1,0:T(8,128)(2,1)}), bf16[8,4,32,128]{3,2,1,0:T(8,128)(2,1)S(1)}, u32[]{:S(2)}, u32[]{:S(2)}) async-start(bf16[8,4,32,128]{3,2,1,0:T(8,128)(2,1)} %get-tuple-element.46), calls=%async_computation | async-start | bytes 524288 | tf_op jit(solution)/shard_map/all_to_all | solution.py:334
  11.5 2.0 %copy-done = s32[56,128,128]{2,1,0:T(8,128)S(1)} copy-done((s32[56,128,128]{2,1,0:T(8,128)S(1)}, s32[56,128,128]{2,1,0:T(8,128)}, u32[]{:S(2)}) %copy-start) | copy-done | bytes 3670040
  13.5 1.8 %shard_map.122 = (bf16[56,128,128]{2,1,0:T(8,128)(2,1)S(1)}, f32[16,40,128]{2,1,0:T(8,128)S(1)}) custom-call(bf16[16,32,128]{2,1,0:T(8,128)(2,1)S(1)} %get-tuple-element.47.x_ref, s32[2,56]{1,0:T(2,128)S(1)} %pad_add_fusion.ends_ref, s32[56,128,128]{2,1,0:T(8,128)S(1)} %copy-done), custom_call_target="tpu_custom_call" | custom-call | flops 60000000 | bytes 6000000 | tf_op jit(solution)/shard_map/pallas_call | solution.py:397
  15.3 4.3 %all-to-all-done.a_ref = bf16[8,4,32,128]{3,2,1,0:T(8,128)(2,1)S(1)} async-done(((bf16[8,4,32,128]{3,2,1,0:T(8,128)(2,1)}), bf16[8,4,32,128]{3,2,1,0:T(8,128)(2,1)S(1)}, u32[]{:S(2)}, u32[]{:S(2)}) %all-to-all-start) | async-done | bytes 262176 | tf_op jit(solution)/shard_map/all_to_all | solution.py:334
  19.6 12.2 %all-to-all-start.1 = ((bf16[8,4,32,128]{3,2,1,0:T(8,128)(2,1)}), bf16[8,4,32,128]{3,2,1,0:T(8,128)(2,1)S(1)}, u32[]{:S(2)}, u32[]{:S(2)}) async-start(bf16[8,4,32,128]{3,2,1,0:T(8,128)(2,1)} %get-tuple-element.55), calls=%async_computation.1 | async-start | bytes 524288 | tf_op jit(solution)/shard_map/all_to_all | solution.py:334
  31.8 2.3 %collective-permute-start = (bf16[4,2,2,32,128]{4,3,2,1,0:T(8,128)(2,1)S(1)}, bf16[4,2,2,32,128]{4,3,2,1,0:T(8,128)(2,1)S(1)}, u32[]{:S(2)}, u32[]{:S(2)}) collective-permute-start(bf16[4,2,2,32,128]{4,3,2,1,0:T(8,128)(2,1)S(1)} %get-tuple-element.52), channel_id=1, source_target_pairs={{0,64},{1,65},{2,66},{3,67},{4,68},{5,69},{6,70},{7,71},{8,72},{9,... | collective-permute-start | bytes 393224 | tf_op jit(solution)/shard_map/ppermute | solution.py:360
  34.1 7.4 %collective-permute-start.1 = (bf16[4,2,2,32,128]{4,3,2,1,0:T(8,128)(2,1)S(1)}, bf16[4,2,2,32,128]{4,3,2,1,0:T(8,128)(2,1)S(1)}, u32[]{:S(2)}, u32[]{:S(2)}) collective-permute-start(bf16[4,2,2,32,128]{4,3,2,1,0:T(8,128)(2,1)S(1)} %get-tuple-element.53), channel_id=1, source_target_pairs={{0,65},{1,64},{2,67},{3,66},{4,69},{5,68},{6,71},{7,70},{8,73},{9,... | collective-permute-start | bytes 393224 | tf_op jit(solution)/shard_map/ppermute | solution.py:360
  42.9 10.9 %collective-permute-start.2 = (bf16[4,2,32,128]{3,2,1,0:T(8,128)(2,1)S(1)}, bf16[4,2,32,128]{3,2,1,0:T(8,128)(2,1)S(1)}, u32[]{:S(2)}, u32[]{:S(2)}) collective-permute-start(bf16[4,2,32,128]{3,2,1,0:T(8,128)(2,1)S(1)} %get-tuple-element.58), channel_id=1, source_target_pairs={{0,64},{1,65},{2,66},{3,67},{4,68},{5,69},{6,70},{7,71},{8,72},{9,... | collective-permute-start | bytes 196616 | tf_op jit(solution)/shard_map/ppermute | solution.py:360
  53.8 1.9 %collective-permute-start.3 = (bf16[4,2,32,128]{3,2,1,0:T(8,128)(2,1)S(1)}, bf16[4,2,32,128]{3,2,1,0:T(8,128)(2,1)S(1)}, u32[]{:S(2)}, u32[]{:S(2)}) collective-permute-start(bf16[4,2,32,128]{3,2,1,0:T(8,128)(2,1)S(1)} %get-tuple-element.59), channel_id=1, source_target_pairs={{0,65},{1,64},{2,67},{3,66},{4,69},{5,68},{6,71},{7,70},{8,73},{9,... | collective-permute-start | bytes 196616 | tf_op jit(solution)/shard_map/ppermute | solution.py:360
  55.8 5.1 %collective-permute-done.2.agg_plus_ref = bf16[4,2,32,128]{3,2,1,0:T(8,128)(2,1)S(1)} collective-permute-done((bf16[4,2,32,128]{3,2,1,0:T(8,128)(2,1)S(1)}, bf16[4,2,32,128]{3,2,1,0:T(8,128)(2,1)S(1)}, u32[]{:S(2)}, u32[]{:S(2)}) %collective-permute-start.2) | collective-permute-done | bytes 65568 | tf_op jit(solution)/shard_map/ppermute | solution.py:360
  60.8 4.1 %collective-permute-done.3.agg_minus_ref = bf16[4,2,32,128]{3,2,1,0:T(8,128)(2,1)S(1)} collective-permute-done((bf16[4,2,32,128]{3,2,1,0:T(8,128)(2,1)S(1)}, bf16[4,2,32,128]{3,2,1,0:T(8,128)(2,1)S(1)}, u32[]{:S(2)}, u32[]{:S(2)}) %collective-permute-start.3) | collective-permute-done | bytes 65568 | tf_op jit(solution)/shard_map/ppermute | solution.py:360
  65.7 4.8 %all-to-all-start.2 = ((bf16[4,3,2,2,32,128]{5,4,3,2,1,0:T(8,128)(2,1)}), bf16[4,3,2,2,32,128]{5,4,3,2,1,0:T(8,128)(2,1)S(1)}, u32[]{:S(2)}, u32[]{:S(2)}) async-start(bf16[4,3,2,2,32,128]{5,4,3,2,1,0:T(8,128)(2,1)} %shard_map.124), calls=%async_computation.2 | async-start | bytes 786432 | tf_op jit(solution)/shard_map/all_to_all | solution.py:343
  70.9 4.9 %all-to-all-done.2.in_ref = bf16[4,3,2,2,32,128]{5,4,3,2,1,0:T(8,128)(2,1)S(1)} async-done(((bf16[4,3,2,2,32,128]{5,4,3,2,1,0:T(8,128)(2,1)}), bf16[4,3,2,2,32,128]{5,4,3,2,1,0:T(8,128)(2,1)S(1)}, u32[]{:S(2)}, u32[]{:S(2)}) %all-to-all-start.2) | async-done | bytes 393248 | tf_op jit(solution)/shard_map/all_to_all | solution.py:343
  76.7 4.6 %collective-permute-start.4 = (bf16[4,2,2,32,128]{4,3,2,1,0:T(8,128)(2,1)S(1)}, bf16[4,2,2,32,128]{4,3,2,1,0:T(8,128)(2,1)S(1)}, u32[]{:S(2)}, u32[]{:S(2)}) collective-permute-start(bf16[4,2,2,32,128]{4,3,2,1,0:T(8,128)(2,1)S(1)} %get-tuple-element.62), channel_id=1, source_target_pairs={{0,64},{1,65},{2,66},{3,67},{4,68},{5,69},{6,70},{7,71},{8,72},{9,... | collective-permute-start | bytes 393224 | tf_op jit(solution)/shard_map/ppermute | solution.py:360
  81.3 5.2 %collective-permute-start.5 = (bf16[4,2,2,32,128]{4,3,2,1,0:T(8,128)(2,1)S(1)}, bf16[4,2,2,32,128]{4,3,2,1,0:T(8,128)(2,1)S(1)}, u32[]{:S(2)}, u32[]{:S(2)}) collective-permute-start(bf16[4,2,2,32,128]{4,3,2,1,0:T(8,128)(2,1)S(1)} %get-tuple-element.63), channel_id=1, source_target_pairs={{0,65},{1,64},{2,67},{3,66},{4,69},{5,68},{6,71},{7,70},{8,73},{9,... | collective-permute-start | bytes 393224 | tf_op jit(solution)/shard_map/ppermute | solution.py:360
  87.5 9.9 %all-to-all-start.3 = ((bf16[32,5,8,128]{3,2,1,0:T(8,128)(2,1)}), bf16[32,5,8,128]{3,2,1,0:T(8,128)(2,1)S(1)}, u32[]{:S(2)}, u32[]{:S(2)}) async-start(bf16[32,5,8,128]{3,2,1,0:T(8,128)(2,1)} %shard_map.126), calls=%async_computation.3 | async-start | bytes 655360 | tf_op jit(solution)/shard_map/all_to_all | solution.py:472
  97.5 8.1 %all-to-all-done.3.part_ref = bf16[32,5,8,128]{3,2,1,0:T(8,128)(2,1)S(1)} async-done(((bf16[32,5,8,128]{3,2,1,0:T(8,128)(2,1)}), bf16[32,5,8,128]{3,2,1,0:T(8,128)(2,1)S(1)}, u32[]{:S(2)}, u32[]{:S(2)}) %all-to-all-start.3) | async-done | bytes 327712 | tf_op jit(solution)/shard_map/all_to_all | solution.py:472
  106.3 7.5 %all-to-all-start.4 = ((bf16[16,3,8,128]{3,2,1,0:T(8,128)(2,1)}), bf16[16,3,8,128]{3,2,1,0:T(8,128)(2,1)S(1)}, u32[]{:S(2)}, u32[]{:S(2)}) async-start(bf16[16,3,8,128]{3,2,1,0:T(8,128)(2,1)} %shard_map.130), calls=%async_computation.4 | async-start | bytes 196608 | tf_op jit(solution)/shard_map/all_to_all | solution.py:478
  113.8 3.7 %collective-permute-start.6 = (bf16[2,2,2,32,128]{4,3,2,1,0:T(8,128)(2,1)S(1)}, bf16[2,2,2,32,128]{4,3,2,1,0:T(8,128)(2,1)S(1)}, u32[]{:S(2)}, u32[]{:S(2)}) collective-permute-start(bf16[2,2,2,32,128]{4,3,2,1,0:T(8,128)(2,1)S(1)} %get-tuple-element.69), channel_id=1, source_target_pairs={{0,2},{1,3},{2,4},{3,5},{4,6},{5,7},{6,0},{7,1},{8,10},{9,11},{10,... | collective-permute-start | bytes 196616 | tf_op jit(solution)/shard_map/ppermute | solution.py:480
  117.5 2.4 %collective-permute-start.7 = (bf16[2,2,2,32,128]{4,3,2,1,0:T(8,128)(2,1)S(1)}, bf16[2,2,2,32,128]{4,3,2,1,0:T(8,128)(2,1)S(1)}, u32[]{:S(2)}, u32[]{:S(2)}) collective-permute-start(bf16[2,2,2,32,128]{4,3,2,1,0:T(8,128)(2,1)S(1)} %get-tuple-element.70), channel_id=1, source_target_pairs={{0,4},{1,5},{2,6},{3,7},{4,0},{5,1},{6,2},{7,3},{8,12},{9,13},{10,... | collective-permute-start | bytes 196616 | tf_op jit(solution)/shard_map/ppermute | solution.py:480
  119.9 2.3 %collective-permute-start.8 = (bf16[2,2,2,32,128]{4,3,2,1,0:T(8,128)(2,1)S(1)}, bf16[2,2,2,32,128]{4,3,2,1,0:T(8,128)(2,1)S(1)}, u32[]{:S(2)}, u32[]{:S(2)}) collective-permute-start(bf16[2,2,2,32,128]{4,3,2,1,0:T(8,128)(2,1)S(1)} %get-tuple-element.71), channel_id=1, source_target_pairs={{0,6},{1,7},{2,0},{3,1},{4,2},{5,3},{6,4},{7,5},{8,14},{9,15},{10,... | collective-permute-start | bytes 196616 | tf_op jit(solution)/shard_map/ppermute | solution.py:480
  122.2 3.0 %collective-permute-done.7.two_ref = bf16[2,2,2,32,128]{4,3,2,1,0:T(8,128)(2,1)S(1)} collective-permute-done((bf16[2,2,2,32,128]{4,3,2,1,0:T(8,128)(2,1)S(1)}, bf16[2,2,2,32,128]{4,3,2,1,0:T(8,128)(2,1)S(1)}, u32[]{:S(2)}, u32[]{:S(2)}) %collective-permute-start.7) | collective-permute-done | bytes 65568 | tf_op jit(solution)/shard_map/ppermute | solution.py:480
  125.2 2.1 %collective-permute-done.8.three_ref = bf16[2,2,2,32,128]{4,3,2,1,0:T(8,128)(2,1)S(1)} collective-permute-done((bf16[2,2,2,32,128]{4,3,2,1,0:T(8,128)(2,1)S(1)}, bf16[2,2,2,32,128]{4,3,2,1,0:T(8,128)(2,1)S(1)}, u32[]{:S(2)}, u32[]{:S(2)}) %collective-permute-start.8) | collective-permute-done | bytes 65568 | tf_op jit(solution)/shard_map/ppermute | solution.py:480
  127.2 1.8 %shard_map.128 = (bf16[8,4,32,128]{3,2,1,0:T(8,128)(2,1)}, bf16[8,4,32,128]{3,2,1,0:T(8,128)(2,1)}, bf16[16,32,128]{2,1,0:T(8,128)(2,1)S(1)}) custom-call(bf16[2,2,2,32,128]{4,3,2,1,0:T(8,128)(2,1)S(1)} %get-tuple-element.68.zero_ref, bf16[2,2,2,32,128]{4,3,2,1,0:T(8,128)(2,1)S(1)} %collective-permute-done.6.one_ref, ...), custom_call_target="tpu_custom_call" | custom-call | flops 10000000 | bytes 1000000 | tf_op jit(solution)/shard_map/pallas_call | solution.py:481
  129.1 5.0 %all-to-all-start.5 = ((bf16[8,4,32,128]{3,2,1,0:T(8,128)(2,1)}), bf16[8,4,32,128]{3,2,1,0:T(8,128)(2,1)S(1)}, u32[]{:S(2)}, u32[]{:S(2)}) async-start(bf16[8,4,32,128]{3,2,1,0:T(8,128)(2,1)} %get-tuple-element.78), calls=%async_computation.5 | async-start | bytes 524288 | tf_op jit(solution)/shard_map/all_to_all | solution.py:334
  134.1 2.4 %collective-permute-start.9 = (f32[1,8,256]{2,1,0:T(8,128)S(1)}, f32[1,8,256]{2,1,0:T(8,128)S(1)}, u32[]{:S(2)}, u32[]{:S(2)}) collective-permute-start(f32[1,8,256]{2,1,0:T(8,128)S(1)} %get-tuple-element.79.one_ref), channel_id=1, source_target_pairs={{0,8},{8,0},{16,24},{24,16},{32,40},{40,32},{48,56},{56,48},{64,72... | collective-permute-start | bytes 24584 | tf_op jit(solution)/shard_map/ppermute | solution.py:338
  137.3 2.4 %collective-permute-start.10 = (f32[2,8,256]{2,1,0:T(8,128)S(1)}, f32[2,8,256]{2,1,0:T(8,128)S(1)}, u32[]{:S(2)}, u32[]{:S(2)}) collective-permute-start(f32[2,8,256]{2,1,0:T(8,128)S(1)} %shard_map.132.one_ref), channel_id=1, source_target_pairs={{0,128},{8,136},{16,144},{24,152},{32,160},{40,168},{48,176},{56,1... | collective-permute-start | bytes 49160 | tf_op jit(solution)/shard_map/ppermute | solution.py:338
  139.7 3.2 %collective-permute-done.10.two_ref = f32[2,8,256]{2,1,0:T(8,128)S(1)} collective-permute-done((f32[2,8,256]{2,1,0:T(8,128)S(1)}, f32[2,8,256]{2,1,0:T(8,128)S(1)}, u32[]{:S(2)}, u32[]{:S(2)}) %collective-permute-start.10) | collective-permute-done | bytes 16416 | tf_op jit(solution)/shard_map/ppermute | solution.py:338
  143.8 11.1 %all-to-all-start.6 = ((bf16[8,4,32,128]{3,2,1,0:T(8,128)(2,1)}), bf16[8,4,32,128]{3,2,1,0:T(8,128)(2,1)S(1)}, u32[]{:S(2)}, u32[]{:S(2)}) async-start(bf16[8,4,32,128]{3,2,1,0:T(8,128)(2,1)} %get-tuple-element.81), calls=%async_computation.6 | async-start | bytes 524288 | tf_op jit(solution)/shard_map/all_to_all | solution.py:334
  155.8 2.8 %collective-permute-start.11 = (f32[4,8,256]{2,1,0:T(8,128)S(1)}, f32[4,8,256]{2,1,0:T(8,128)S(1)}, u32[]{:S(2)}, u32[]{:S(2)}) collective-permute-start(f32[4,8,256]{2,1,0:T(8,128)S(1)} %shard_map.133.near_ref), channel_id=1, source_target_pairs={{0,256},{8,264},{16,272},{24,280},{32,288},{40,296},{48,304},{56,3... | collective-permute-start | bytes 98312 | tf_op jit(solution)/shard_map/ppermute | solution.py:338
  159.2 3.9 %collective-permute-done.11.far_ref = f32[4,8,256]{2,1,0:T(8,128)S(1)} collective-permute-done((f32[4,8,256]{2,1,0:T(8,128)S(1)}, f32[4,8,256]{2,1,0:T(8,128)S(1)}, u32[]{:S(2)}, u32[]{:S(2)}) %collective-permute-start.11) | collective-permute-done | bytes 32800 | tf_op jit(solution)/shard_map/ppermute | solution.py:338
  (46 shorter events, 13.6 us)
Async XLA Ops:
  0.6 0.9 copy-start.3
  1.5 0.7 copy-start.5
  3.9 15.7 %all-to-all-start = ((bf16[8,4,32,128]{3,2,1,0:T(8,128)(2,1)}), bf16[8,4,32,128]{3,2,1,0:T(8,128)(2,1)S(1)}, u32[]{:S(2)}, u32[]{:S(2)}) async-start(bf16[8,4,32,128]{3,2,1,0:T(8,128)(2,1)} %get-tuple-element.46), calls=%async_computation | async-start | bytes 524288 | tf_op jit(solution)/shard_map/all_to_all | solution.py:334
  9.9 0.9 copy-start.4
  11.5 2.0 %copy-start = (s32[56,128,128]{2,1,0:T(8,128)S(1)}, s32[56,128,128]{2,1,0:T(8,128)}, u32[]{:S(2)}) copy-start(s32[56,128,128]{2,1,0:T(8,128)} %cnt_ref.1) | copy-start | bytes 11010052
  13.5 57.0 %copy-start.2 = (bf16[256,256]{1,0:T(8,128)(2,1)S(1)}, bf16[256,256]{1,0:T(8,128)(2,1)}, u32[]{:S(2)}) copy-start(bf16[256,256]{1,0:T(8,128)(2,1)} %own_w_ref.1) | copy-start | bytes 393220
  13.5 57.1 %copy-start.1 = (bf16[256,256]{1,0:T(8,128)(2,1)S(1)}, bf16[256,256]{1,0:T(8,128)(2,1)}, u32[]{:S(2)}) copy-start(bf16[256,256]{1,0:T(8,128)(2,1)} %neigh_ref.1) | copy-start | bytes 393220
  13.5 57.2 %copy-start.7 = (f32[256]{0:T(256)S(1)}, f32[256]{0:T(256)}, u32[]{:S(2)}) copy-start(f32[256]{0:T(256)} %param.16) | copy-start | bytes 3076
  19.6 21.9 %all-to-all-start.1 = ((bf16[8,4,32,128]{3,2,1,0:T(8,128)(2,1)}), bf16[8,4,32,128]{3,2,1,0:T(8,128)(2,1)S(1)}, u32[]{:S(2)}, u32[]{:S(2)}) async-start(bf16[8,4,32,128]{3,2,1,0:T(8,128)(2,1)} %get-tuple-element.55), calls=%async_computation.1 | async-start | bytes 524288 | tf_op jit(solution)/shard_map/all_to_all | solution.py:334
  31.8 24.0 %collective-permute-start = (bf16[4,2,2,32,128]{4,3,2,1,0:T(8,128)(2,1)S(1)}, bf16[4,2,2,32,128]{4,3,2,1,0:T(8,128)(2,1)S(1)}, u32[]{:S(2)}, u32[]{:S(2)}) collective-permute-start(bf16[4,2,2,32,128]{4,3,2,1,0:T(8,128)(2,1)S(1)} %get-tuple-element.52), channel_id=1, source_target_pairs={{0,64},{1,65},{2,66},{3,67},{4,68},{5,69},{6,70},{7,71},{8,72},{9,... | collective-permute-start | bytes 393224 | tf_op jit(solution)/shard_map/ppermute | solution.py:360
  34.1 21.6 %collective-permute-start.1 = (bf16[4,2,2,32,128]{4,3,2,1,0:T(8,128)(2,1)S(1)}, bf16[4,2,2,32,128]{4,3,2,1,0:T(8,128)(2,1)S(1)}, u32[]{:S(2)}, u32[]{:S(2)}) collective-permute-start(bf16[4,2,2,32,128]{4,3,2,1,0:T(8,128)(2,1)S(1)} %get-tuple-element.53), channel_id=1, source_target_pairs={{0,65},{1,64},{2,67},{3,66},{4,69},{5,68},{6,71},{7,70},{8,73},{9,... | collective-permute-start | bytes 393224 | tf_op jit(solution)/shard_map/ppermute | solution.py:360
  42.9 18.0 %collective-permute-start.2 = (bf16[4,2,32,128]{3,2,1,0:T(8,128)(2,1)S(1)}, bf16[4,2,32,128]{3,2,1,0:T(8,128)(2,1)S(1)}, u32[]{:S(2)}, u32[]{:S(2)}) collective-permute-start(bf16[4,2,32,128]{3,2,1,0:T(8,128)(2,1)S(1)} %get-tuple-element.58), channel_id=1, source_target_pairs={{0,64},{1,65},{2,66},{3,67},{4,68},{5,69},{6,70},{7,71},{8,72},{9,... | collective-permute-start | bytes 196616 | tf_op jit(solution)/shard_map/ppermute | solution.py:360
  53.8 11.1 %collective-permute-start.3 = (bf16[4,2,32,128]{3,2,1,0:T(8,128)(2,1)S(1)}, bf16[4,2,32,128]{3,2,1,0:T(8,128)(2,1)S(1)}, u32[]{:S(2)}, u32[]{:S(2)}) collective-permute-start(bf16[4,2,32,128]{3,2,1,0:T(8,128)(2,1)S(1)} %get-tuple-element.59), channel_id=1, source_target_pairs={{0,65},{1,64},{2,67},{3,66},{4,69},{5,68},{6,71},{7,70},{8,73},{9,... | collective-permute-start | bytes 196616 | tf_op jit(solution)/shard_map/ppermute | solution.py:360
  65.7 10.1 %all-to-all-start.2 = ((bf16[4,3,2,2,32,128]{5,4,3,2,1,0:T(8,128)(2,1)}), bf16[4,3,2,2,32,128]{5,4,3,2,1,0:T(8,128)(2,1)S(1)}, u32[]{:S(2)}, u32[]{:S(2)}) async-start(bf16[4,3,2,2,32,128]{5,4,3,2,1,0:T(8,128)(2,1)} %shard_map.124), calls=%async_computation.2 | async-start | bytes 786432 | tf_op jit(solution)/shard_map/all_to_all | solution.py:343
  76.7 20.7 %collective-permute-start.4 = (bf16[4,2,2,32,128]{4,3,2,1,0:T(8,128)(2,1)S(1)}, bf16[4,2,2,32,128]{4,3,2,1,0:T(8,128)(2,1)S(1)}, u32[]{:S(2)}, u32[]{:S(2)}) collective-permute-start(bf16[4,2,2,32,128]{4,3,2,1,0:T(8,128)(2,1)S(1)} %get-tuple-element.62), channel_id=1, source_target_pairs={{0,64},{1,65},{2,66},{3,67},{4,68},{5,69},{6,70},{7,71},{8,72},{9,... | collective-permute-start | bytes 393224 | tf_op jit(solution)/shard_map/ppermute | solution.py:360
  81.3 16.1 %collective-permute-start.5 = (bf16[4,2,2,32,128]{4,3,2,1,0:T(8,128)(2,1)S(1)}, bf16[4,2,2,32,128]{4,3,2,1,0:T(8,128)(2,1)S(1)}, u32[]{:S(2)}, u32[]{:S(2)}) collective-permute-start(bf16[4,2,2,32,128]{4,3,2,1,0:T(8,128)(2,1)S(1)} %get-tuple-element.63), channel_id=1, source_target_pairs={{0,65},{1,64},{2,67},{3,66},{4,69},{5,68},{6,71},{7,70},{8,73},{9,... | collective-permute-start | bytes 393224 | tf_op jit(solution)/shard_map/ppermute | solution.py:360
  87.5 18.0 %all-to-all-start.3 = ((bf16[32,5,8,128]{3,2,1,0:T(8,128)(2,1)}), bf16[32,5,8,128]{3,2,1,0:T(8,128)(2,1)S(1)}, u32[]{:S(2)}, u32[]{:S(2)}) async-start(bf16[32,5,8,128]{3,2,1,0:T(8,128)(2,1)} %shard_map.126), calls=%async_computation.3 | async-start | bytes 655360 | tf_op jit(solution)/shard_map/all_to_all | solution.py:472
  97.5 66.3 %copy-start.6 = (s32[1,8,4]{1,2,0:T(4,128)S(1)}, s32[1,8,4]{1,2,0:T(4,128)}, u32[]{:S(2)}) copy-start(s32[1,8,4]{1,2,0:T(4,128)} %param.13) | copy-start | bytes 388
  106.3 22.8 %all-to-all-start.4 = ((bf16[16,3,8,128]{3,2,1,0:T(8,128)(2,1)}), bf16[16,3,8,128]{3,2,1,0:T(8,128)(2,1)S(1)}, u32[]{:S(2)}, u32[]{:S(2)}) async-start(bf16[16,3,8,128]{3,2,1,0:T(8,128)(2,1)} %shard_map.130), calls=%async_computation.4 | async-start | bytes 196608 | tf_op jit(solution)/shard_map/all_to_all | solution.py:478
  113.8 8.4 %collective-permute-start.6 = (bf16[2,2,2,32,128]{4,3,2,1,0:T(8,128)(2,1)S(1)}, bf16[2,2,2,32,128]{4,3,2,1,0:T(8,128)(2,1)S(1)}, u32[]{:S(2)}, u32[]{:S(2)}) collective-permute-start(bf16[2,2,2,32,128]{4,3,2,1,0:T(8,128)(2,1)S(1)} %get-tuple-element.69), channel_id=1, source_target_pairs={{0,2},{1,3},{2,4},{3,5},{4,6},{5,7},{6,0},{7,1},{8,10},{9,11},{10,... | collective-permute-start | bytes 196616 | tf_op jit(solution)/shard_map/ppermute | solution.py:480
  117.5 7.7 %collective-permute-start.7 = (bf16[2,2,2,32,128]{4,3,2,1,0:T(8,128)(2,1)S(1)}, bf16[2,2,2,32,128]{4,3,2,1,0:T(8,128)(2,1)S(1)}, u32[]{:S(2)}, u32[]{:S(2)}) collective-permute-start(bf16[2,2,2,32,128]{4,3,2,1,0:T(8,128)(2,1)S(1)} %get-tuple-element.70), channel_id=1, source_target_pairs={{0,4},{1,5},{2,6},{3,7},{4,0},{5,1},{6,2},{7,3},{8,12},{9,13},{10,... | collective-permute-start | bytes 196616 | tf_op jit(solution)/shard_map/ppermute | solution.py:480
  119.9 7.4 %collective-permute-start.8 = (bf16[2,2,2,32,128]{4,3,2,1,0:T(8,128)(2,1)S(1)}, bf16[2,2,2,32,128]{4,3,2,1,0:T(8,128)(2,1)S(1)}, u32[]{:S(2)}, u32[]{:S(2)}) collective-permute-start(bf16[2,2,2,32,128]{4,3,2,1,0:T(8,128)(2,1)S(1)} %get-tuple-element.71), channel_id=1, source_target_pairs={{0,6},{1,7},{2,0},{3,1},{4,2},{5,3},{6,4},{7,5},{8,14},{9,15},{10,... | collective-permute-start | bytes 196616 | tf_op jit(solution)/shard_map/ppermute | solution.py:480
  129.1 14.7 %all-to-all-start.5 = ((bf16[8,4,32,128]{3,2,1,0:T(8,128)(2,1)}), bf16[8,4,32,128]{3,2,1,0:T(8,128)(2,1)S(1)}, u32[]{:S(2)}, u32[]{:S(2)}) async-start(bf16[8,4,32,128]{3,2,1,0:T(8,128)(2,1)} %get-tuple-element.78), calls=%async_computation.5 | async-start | bytes 524288 | tf_op jit(solution)/shard_map/all_to_all | solution.py:334
  134.1 3.2 %collective-permute-start.9 = (f32[1,8,256]{2,1,0:T(8,128)S(1)}, f32[1,8,256]{2,1,0:T(8,128)S(1)}, u32[]{:S(2)}, u32[]{:S(2)}) collective-permute-start(f32[1,8,256]{2,1,0:T(8,128)S(1)} %get-tuple-element.79.one_ref), channel_id=1, source_target_pairs={{0,8},{8,0},{16,24},{24,16},{32,40},{40,32},{48,56},{56,48},{64,72... | collective-permute-start | bytes 24584 | tf_op jit(solution)/shard_map/ppermute | solution.py:338
  137.3 5.6 %collective-permute-start.10 = (f32[2,8,256]{2,1,0:T(8,128)S(1)}, f32[2,8,256]{2,1,0:T(8,128)S(1)}, u32[]{:S(2)}, u32[]{:S(2)}) collective-permute-start(f32[2,8,256]{2,1,0:T(8,128)S(1)} %shard_map.132.one_ref), channel_id=1, source_target_pairs={{0,128},{8,136},{16,144},{24,152},{32,160},{40,168},{48,176},{56,1... | collective-permute-start | bytes 49160 | tf_op jit(solution)/shard_map/ppermute | solution.py:338
  143.8 20.0 %all-to-all-start.6 = ((bf16[8,4,32,128]{3,2,1,0:T(8,128)(2,1)}), bf16[8,4,32,128]{3,2,1,0:T(8,128)(2,1)S(1)}, u32[]{:S(2)}, u32[]{:S(2)}) async-start(bf16[8,4,32,128]{3,2,1,0:T(8,128)(2,1)} %get-tuple-element.81), calls=%async_computation.6 | async-start | bytes 524288 | tf_op jit(solution)/shard_map/all_to_all | solution.py:334
  155.8 7.3 %collective-permute-start.11 = (f32[4,8,256]{2,1,0:T(8,128)S(1)}, f32[4,8,256]{2,1,0:T(8,128)S(1)}, u32[]{:S(2)}, u32[]{:S(2)}) collective-permute-start(f32[4,8,256]{2,1,0:T(8,128)S(1)} %shard_map.133.near_ref), channel_id=1, source_target_pairs={{0,256},{8,264},{16,272},{24,280},{32,288},{40,296},{48,304},{56,3... | collective-permute-start | bytes 98312 | tf_op jit(solution)/shard_map/ppermute | solution.py:338

commit v14 on v12

--- a/solution.py
+++ b/solution.py
@@ -29,7 +29,7 @@
     return lax.dot_general(left, right, dims, preferred_element_type=F32)
 
 
-def call(body, out_shape, in_specs, scratch=(), cost=(1e7, 1e6)):
+def call(body, out_shape, in_specs, scratch=(), cost=(1e7, 1e6), room=32):
     outs = jax.tree.map(lambda _: VMEM, out_shape)
     return pl.pallas_call(
         body,
@@ -37,7 +37,7 @@
         in_specs=in_specs,
         out_specs=outs,
         scratch_shapes=scratch,
-        compiler_params=pltpu.CompilerParams(vmem_limit_bytes=32 * 2**20),
+        compiler_params=pltpu.CompilerParams(vmem_limit_bytes=room * 2**20),
         cost_estimate=pl.CostEstimate(
             flops=int(cost[0]), bytes_accessed=int(cost[1]), transcendentals=0
         ),
@@ -388,6 +388,7 @@
             pltpu.SMEM((cap, kinds), jnp.int32),
             pltpu.SemaphoreType.DMA((2,)),
         ],
+        room=60,
     )(node_feats, table)
     got_b = swap(send_b, GROUP // 2)
     xc_plus, xc_minus = call(

time: 167 us -> 166 us (level)
    unnamed x18 -> x16, local copies, waits for them, and re-layouts: 4.73 us -> 4.06 us
where the time goes in v14:
time: 166 us; the launch traced here: 164 us
  starting transfers between devices  109 us (66%)
  waiting for transfers between devices  35.4 us (21%)
  Pallas kernels  13.4 us (8%)
  local copies, waits for them, and re-layouts  4.79 us (3%)
    all_to_all x4, starting transfers between devices, swap(): lax.all_to_all(rows, 'blk', 0, 0, axis_index_groups=groups, tiled=False)  37.4 us
    ppermute x6, starting transfers between devices, along_z(): return lax.ppermute(rows, ('blk', 'col'), sorted(route))  31.2 us
    all_to_all x1, starting transfers between devices, per_device(): part = lax.all_to_all(part, both, 0, 0, axis_index_groups=line, tiled=False)  9.88 us
    all_to_all x1, starting transfers between devices, per_device(): part = lax.all_to_all(part, both, 0, 0, axis_index_groups=flat, tiled=False)  8.69 us
    ppermute x3, starting transfers between devices, per_device(): lax.ppermute(home[turn], 'col', route(turn))  8.38 us
    ppermute x6, waiting for transfers between devices, along_z(): return lax.ppermute(rows, ('blk', 'col'), sorted(route))  8.32 us
    ppermute x3, starting transfers between devices, across(): lax.ppermute(rows, 'blk', [(e, e ^ bit) for e in range(lax.axis_size('blk...  8.2 us
    all_to_all x1, waiting for transfers between devices, per_device(): part = lax.all_to_all(part, both, 0, 0, axis_index_groups=flat, tiled=False)  8.07 us
  transfers between devices with their start and end apart: 19, of which 12 were waited for; matrix products, arithmetic and copies ran while one was open for 1% of the time, Pallas kernels for 5%

profile of v14, /device:TPU:6, one launch (start us, length us, event | category | flops | bytes accessed | tf_op | source)
XLA Modules:
  0.0 163.7 jit_solution(12207825047274041267)
XLA Ops:
  0.6 2.0 %shard_map.120 = (bf16[8,4,32,128]{3,2,1,0:T(8,128)(2,1)}, bf16[8,4,32,128]{3,2,1,0:T(8,128)(2,1)}, bf16[16,32,128]{2,1,0:T(8,128)(2,1)}) custom-call(bf16[32,2048]{1,0:T(8,128)(2,1)} %x_hbm.1, s32[4,8]{1,0:T(4,128)} %bitcast.12), custom_call_target="tpu_custom_call" | custom-call | flops 10000000 | bytes 1000000 | tf_op jit(solution)/shard_map/pallas_call | solution.py:382
  2.6 15.7 %all-to-all-start = ((bf16[8,4,32,128]{3,2,1,0:T(8,128)(2,1)}), bf16[8,4,32,128]{3,2,1,0:T(8,128)(2,1)S(1)}, u32[]{:S(2)}, u32[]{:S(2)}) async-start(bf16[8,4,32,128]{3,2,1,0:T(8,128)(2,1)} %get-tuple-element.46), calls=%async_computation | async-start | bytes 524288 | tf_op jit(solution)/shard_map/all_to_all | solution.py:334
  20.8 2.0 %copy-done = s32[56,128,128]{2,1,0:T(8,128)S(1)} copy-done((s32[56,128,128]{2,1,0:T(8,128)S(1)}, s32[56,128,128]{2,1,0:T(8,128)}, u32[]{:S(2)}) %copy-start) | copy-done | bytes 3670040
  22.9 1.8 %shard_map.122 = (bf16[56,128,128]{2,1,0:T(8,128)(2,1)S(1)}, f32[16,40,128]{2,1,0:T(8,128)S(1)}) custom-call(bf16[16,32,128]{2,1,0:T(8,128)(2,1)S(1)} %copy-done.1, s32[2,56]{1,0:T(2,128)S(1)} %pad_add_fusion.ends_ref, s32[56,128,128]{2,1,0:T(8,128)S(1)} %copy-done), custom_call_target="tpu_custom_call" | custom-call | flops 60000000 | bytes 6000000 | tf_op jit(solution)/shard_map/pallas_call | solution.py:398
  25.6 4.8 %all-to-all-start.1 = ((bf16[8,4,32,128]{3,2,1,0:T(8,128)(2,1)}), bf16[8,4,32,128]{3,2,1,0:T(8,128)(2,1)S(1)}, u32[]{:S(2)}, u32[]{:S(2)}) async-start(bf16[8,4,32,128]{3,2,1,0:T(8,128)(2,1)} %get-tuple-element.54), calls=%async_computation.1 | async-start | bytes 524288 | tf_op jit(solution)/shard_map/all_to_all | solution.py:334
  30.5 4.7 %collective-permute-start = (bf16[4,2,2,32,128]{4,3,2,1,0:T(8,128)(2,1)S(1)}, bf16[4,2,2,32,128]{4,3,2,1,0:T(8,128)(2,1)S(1)}, u32[]{:S(2)}, u32[]{:S(2)}) collective-permute-start(bf16[4,2,2,32,128]{4,3,2,1,0:T(8,128)(2,1)S(1)} %get-tuple-element.52), channel_id=1, source_target_pairs={{0,64},{1,65},{2,66},{3,67},{4,68},{5,69},{6,70},{7,71},{8,72},{9,... | collective-permute-start | bytes 393224 | tf_op jit(solution)/shard_map/ppermute | solution.py:360
  35.2 7.0 %collective-permute-start.1 = (bf16[4,2,2,32,128]{4,3,2,1,0:T(8,128)(2,1)S(1)}, bf16[4,2,2,32,128]{4,3,2,1,0:T(8,128)(2,1)S(1)}, u32[]{:S(2)}, u32[]{:S(2)}) collective-permute-start(bf16[4,2,2,32,128]{4,3,2,1,0:T(8,128)(2,1)S(1)} %get-tuple-element.53), channel_id=1, source_target_pairs={{0,65},{1,64},{2,67},{3,66},{4,69},{5,68},{6,71},{7,70},{8,73},{9,... | collective-permute-start | bytes 393224 | tf_op jit(solution)/shard_map/ppermute | solution.py:360
  42.2 1.3 shard_map.123
  43.6 3.2 %collective-permute-start.2 = (bf16[4,2,32,128]{3,2,1,0:T(8,128)(2,1)S(1)}, bf16[4,2,32,128]{3,2,1,0:T(8,128)(2,1)S(1)}, u32[]{:S(2)}, u32[]{:S(2)}) collective-permute-start(bf16[4,2,32,128]{3,2,1,0:T(8,128)(2,1)S(1)} %get-tuple-element.58), channel_id=1, source_target_pairs={{0,64},{1,65},{2,66},{3,67},{4,68},{5,69},{6,70},{7,71},{8,72},{9,... | collective-permute-start | bytes 196616 | tf_op jit(solution)/shard_map/ppermute | solution.py:360
  46.7 6.6 %collective-permute-start.3 = (bf16[4,2,32,128]{3,2,1,0:T(8,128)(2,1)S(1)}, bf16[4,2,32,128]{3,2,1,0:T(8,128)(2,1)S(1)}, u32[]{:S(2)}, u32[]{:S(2)}) collective-permute-start(bf16[4,2,32,128]{3,2,1,0:T(8,128)(2,1)S(1)} %get-tuple-element.59), channel_id=1, source_target_pairs={{0,65},{1,64},{2,67},{3,66},{4,69},{5,68},{6,71},{7,70},{8,73},{9,... | collective-permute-start | bytes 196616 | tf_op jit(solution)/shard_map/ppermute | solution.py:360
  54.5 6.2 %collective-permute-done.2.agg_plus_ref = bf16[4,2,32,128]{3,2,1,0:T(8,128)(2,1)S(1)} collective-permute-done((bf16[4,2,32,128]{3,2,1,0:T(8,128)(2,1)S(1)}, bf16[4,2,32,128]{3,2,1,0:T(8,128)(2,1)S(1)}, u32[]{:S(2)}, u32[]{:S(2)}) %collective-permute-start.2) | collective-permute-done | bytes 65568 | tf_op jit(solution)/shard_map/ppermute | solution.py:360
  62.4 4.8 %all-to-all-start.2 = ((bf16[4,3,2,2,32,128]{5,4,3,2,1,0:T(8,128)(2,1)}), bf16[4,3,2,2,32,128]{5,4,3,2,1,0:T(8,128)(2,1)S(1)}, u32[]{:S(2)}, u32[]{:S(2)}) async-start(bf16[4,3,2,2,32,128]{5,4,3,2,1,0:T(8,128)(2,1)} %shard_map.124), calls=%async_computation.2 | async-start | bytes 786432 | tf_op jit(solution)/shard_map/all_to_all | solution.py:343
  67.6 4.9 %all-to-all-done.2.in_ref = bf16[4,3,2,2,32,128]{5,4,3,2,1,0:T(8,128)(2,1)S(1)} async-done(((bf16[4,3,2,2,32,128]{5,4,3,2,1,0:T(8,128)(2,1)}), bf16[4,3,2,2,32,128]{5,4,3,2,1,0:T(8,128)(2,1)S(1)}, u32[]{:S(2)}, u32[]{:S(2)}) %all-to-all-start.2) | async-done | bytes 393248 | tf_op jit(solution)/shard_map/all_to_all | solution.py:343
  73.4 6.7 %collective-permute-start.4 = (bf16[4,2,2,32,128]{4,3,2,1,0:T(8,128)(2,1)S(1)}, bf16[4,2,2,32,128]{4,3,2,1,0:T(8,128)(2,1)S(1)}, u32[]{:S(2)}, u32[]{:S(2)}) collective-permute-start(bf16[4,2,2,32,128]{4,3,2,1,0:T(8,128)(2,1)S(1)} %get-tuple-element.62), channel_id=1, source_target_pairs={{0,64},{1,65},{2,66},{3,67},{4,68},{5,69},{6,70},{7,71},{8,72},{9,... | collective-permute-start | bytes 393224 | tf_op jit(solution)/shard_map/ppermute | solution.py:360
  80.1 3.1 %collective-permute-start.5 = (bf16[4,2,2,32,128]{4,3,2,1,0:T(8,128)(2,1)S(1)}, bf16[4,2,2,32,128]{4,3,2,1,0:T(8,128)(2,1)S(1)}, u32[]{:S(2)}, u32[]{:S(2)}) collective-permute-start(bf16[4,2,2,32,128]{4,3,2,1,0:T(8,128)(2,1)S(1)} %get-tuple-element.63), channel_id=1, source_target_pairs={{0,65},{1,64},{2,67},{3,66},{4,69},{5,68},{6,71},{7,70},{8,73},{9,... | collective-permute-start | bytes 393224 | tf_op jit(solution)/shard_map/ppermute | solution.py:360
  84.2 8.7 %all-to-all-start.3 = ((bf16[32,5,8,128]{3,2,1,0:T(8,128)(2,1)}), bf16[32,5,8,128]{3,2,1,0:T(8,128)(2,1)S(1)}, u32[]{:S(2)}, u32[]{:S(2)}) async-start(bf16[32,5,8,128]{3,2,1,0:T(8,128)(2,1)} %shard_map.126), calls=%async_computation.3 | async-start | bytes 655360 | tf_op jit(solution)/shard_map/all_to_all | solution.py:473
  93.0 8.1 %all-to-all-done.3.part_ref = bf16[32,5,8,128]{3,2,1,0:T(8,128)(2,1)S(1)} async-done(((bf16[32,5,8,128]{3,2,1,0:T(8,128)(2,1)}), bf16[32,5,8,128]{3,2,1,0:T(8,128)(2,1)S(1)}, u32[]{:S(2)}, u32[]{:S(2)}) %all-to-all-start.3) | async-done | bytes 327712 | tf_op jit(solution)/shard_map/all_to_all | solution.py:473
  101.8 9.9 %all-to-all-start.4 = ((bf16[16,3,8,128]{3,2,1,0:T(8,128)(2,1)}), bf16[16,3,8,128]{3,2,1,0:T(8,128)(2,1)S(1)}, u32[]{:S(2)}, u32[]{:S(2)}) async-start(bf16[16,3,8,128]{3,2,1,0:T(8,128)(2,1)} %shard_map.130), calls=%async_computation.4 | async-start | bytes 196608 | tf_op jit(solution)/shard_map/all_to_all | solution.py:479
  111.7 3.7 %collective-permute-start.6 = (bf16[2,2,2,32,128]{4,3,2,1,0:T(8,128)(2,1)S(1)}, bf16[2,2,2,32,128]{4,3,2,1,0:T(8,128)(2,1)S(1)}, u32[]{:S(2)}, u32[]{:S(2)}) collective-permute-start(bf16[2,2,2,32,128]{4,3,2,1,0:T(8,128)(2,1)S(1)} %get-tuple-element.69), channel_id=1, source_target_pairs={{0,2},{1,3},{2,4},{3,5},{4,6},{5,7},{6,0},{7,1},{8,10},{9,11},{10,... | collective-permute-start | bytes 196616 | tf_op jit(solution)/shard_map/ppermute | solution.py:481
  115.4 2.4 %collective-permute-start.7 = (bf16[2,2,2,32,128]{4,3,2,1,0:T(8,128)(2,1)S(1)}, bf16[2,2,2,32,128]{4,3,2,1,0:T(8,128)(2,1)S(1)}, u32[]{:S(2)}, u32[]{:S(2)}) collective-permute-start(bf16[2,2,2,32,128]{4,3,2,1,0:T(8,128)(2,1)S(1)} %get-tuple-element.70), channel_id=1, source_target_pairs={{0,4},{1,5},{2,6},{3,7},{4,0},{5,1},{6,2},{7,3},{8,12},{9,13},{10,... | collective-permute-start | bytes 196616 | tf_op jit(solution)/shard_map/ppermute | solution.py:481
  117.8 2.3 %collective-permute-start.8 = (bf16[2,2,2,32,128]{4,3,2,1,0:T(8,128)(2,1)S(1)}, bf16[2,2,2,32,128]{4,3,2,1,0:T(8,128)(2,1)S(1)}, u32[]{:S(2)}, u32[]{:S(2)}) collective-permute-start(bf16[2,2,2,32,128]{4,3,2,1,0:T(8,128)(2,1)S(1)} %get-tuple-element.71), channel_id=1, source_target_pairs={{0,6},{1,7},{2,0},{3,1},{4,2},{5,3},{6,4},{7,5},{8,14},{9,15},{10,... | collective-permute-start | bytes 196616 | tf_op jit(solution)/shard_map/ppermute | solution.py:481
  120.1 3.0 %collective-permute-done.7.two_ref = bf16[2,2,2,32,128]{4,3,2,1,0:T(8,128)(2,1)S(1)} collective-permute-done((bf16[2,2,2,32,128]{4,3,2,1,0:T(8,128)(2,1)S(1)}, bf16[2,2,2,32,128]{4,3,2,1,0:T(8,128)(2,1)S(1)}, u32[]{:S(2)}, u32[]{:S(2)}) %collective-permute-start.7) | collective-permute-done | bytes 65568 | tf_op jit(solution)/shard_map/ppermute | solution.py:481
  123.1 2.1 %collective-permute-done.8.three_ref = bf16[2,2,2,32,128]{4,3,2,1,0:T(8,128)(2,1)S(1)} collective-permute-done((bf16[2,2,2,32,128]{4,3,2,1,0:T(8,128)(2,1)S(1)}, bf16[2,2,2,32,128]{4,3,2,1,0:T(8,128)(2,1)S(1)}, u32[]{:S(2)}, u32[]{:S(2)}) %collective-permute-start.8) | collective-permute-done | bytes 65568 | tf_op jit(solution)/shard_map/ppermute | solution.py:481
  125.1 1.8 %shard_map.128 = (bf16[8,4,32,128]{3,2,1,0:T(8,128)(2,1)}, bf16[8,4,32,128]{3,2,1,0:T(8,128)(2,1)}, bf16[16,32,128]{2,1,0:T(8,128)(2,1)S(1)}) custom-call(bf16[2,2,2,32,128]{4,3,2,1,0:T(8,128)(2,1)S(1)} %get-tuple-element.68.zero_ref, bf16[2,2,2,32,128]{4,3,2,1,0:T(8,128)(2,1)S(1)} %collective-permute-done.6.one_ref, ...), custom_call_target="tpu_custom_call" | custom-call | flops 10000000 | bytes 1000000 | tf_op jit(solution)/shard_map/pallas_call | solution.py:482
  127.0 11.6 %all-to-all-start.5 = ((bf16[8,4,32,128]{3,2,1,0:T(8,128)(2,1)}), bf16[8,4,32,128]{3,2,1,0:T(8,128)(2,1)S(1)}, u32[]{:S(2)}, u32[]{:S(2)}) async-start(bf16[8,4,32,128]{3,2,1,0:T(8,128)(2,1)} %get-tuple-element.78), calls=%async_computation.5 | async-start | bytes 524288 | tf_op jit(solution)/shard_map/all_to_all | solution.py:334
  138.5 2.0 %collective-permute-start.9 = (f32[1,8,256]{2,1,0:T(8,128)S(1)}, f32[1,8,256]{2,1,0:T(8,128)S(1)}, u32[]{:S(2)}, u32[]{:S(2)}) collective-permute-start(f32[1,8,256]{2,1,0:T(8,128)S(1)} %get-tuple-element.79.one_ref), channel_id=1, source_target_pairs={{0,8},{8,0},{16,24},{24,16},{32,40},{40,32},{48,56},{56,48},{64,72... | collective-permute-start | bytes 24584 | tf_op jit(solution)/shard_map/ppermute | solution.py:338
  141.6 2.7 %collective-permute-start.10 = (f32[2,8,256]{2,1,0:T(8,128)S(1)}, f32[2,8,256]{2,1,0:T(8,128)S(1)}, u32[]{:S(2)}, u32[]{:S(2)}) collective-permute-start(f32[2,8,256]{2,1,0:T(8,128)S(1)} %shard_map.132.one_ref), channel_id=1, source_target_pairs={{0,128},{8,136},{16,144},{24,152},{32,160},{40,168},{48,176},{56,1... | collective-permute-start | bytes 49160 | tf_op jit(solution)/shard_map/ppermute | solution.py:338
  144.3 2.9 %collective-permute-done.10.two_ref = f32[2,8,256]{2,1,0:T(8,128)S(1)} collective-permute-done((f32[2,8,256]{2,1,0:T(8,128)S(1)}, f32[2,8,256]{2,1,0:T(8,128)S(1)}, u32[]{:S(2)}, u32[]{:S(2)}) %collective-permute-start.10) | collective-permute-done | bytes 16416 | tf_op jit(solution)/shard_map/ppermute | solution.py:338
  147.2 5.3 %all-to-all-start.6 = ((bf16[8,4,32,128]{3,2,1,0:T(8,128)(2,1)}), bf16[8,4,32,128]{3,2,1,0:T(8,128)(2,1)S(1)}, u32[]{:S(2)}, u32[]{:S(2)}) async-start(bf16[8,4,32,128]{3,2,1,0:T(8,128)(2,1)} %get-tuple-element.80), calls=%async_computation.6 | async-start | bytes 524288 | tf_op jit(solution)/shard_map/all_to_all | solution.py:334
  153.4 3.4 %collective-permute-start.11 = (f32[4,8,256]{2,1,0:T(8,128)S(1)}, f32[4,8,256]{2,1,0:T(8,128)S(1)}, u32[]{:S(2)}, u32[]{:S(2)}) collective-permute-start(f32[4,8,256]{2,1,0:T(8,128)S(1)} %shard_map.133.near_ref), channel_id=1, source_target_pairs={{0,256},{8,264},{16,272},{24,280},{32,288},{40,296},{48,304},{56,3... | collective-permute-start | bytes 98312 | tf_op jit(solution)/shard_map/ppermute | solution.py:338
  157.4 3.3 %collective-permute-done.11.far_ref = f32[4,8,256]{2,1,0:T(8,128)S(1)} collective-permute-done((f32[4,8,256]{2,1,0:T(8,128)S(1)}, f32[4,8,256]{2,1,0:T(8,128)S(1)}, u32[]{:S(2)}, u32[]{:S(2)}) %collective-permute-start.11) | collective-permute-done | bytes 32800 | tf_op jit(solution)/shard_map/ppermute | solution.py:338
  162.3 1.4 shard_map.134
  (44 shorter events, 13.5 us)
Async XLA Ops:
  2.6 23.0 %all-to-all-start = ((bf16[8,4,32,128]{3,2,1,0:T(8,128)(2,1)}), bf16[8,4,32,128]{3,2,1,0:T(8,128)(2,1)S(1)}, u32[]{:S(2)}, u32[]{:S(2)}) async-start(bf16[8,4,32,128]{3,2,1,0:T(8,128)(2,1)} %get-tuple-element.46), calls=%async_computation | async-start | bytes 524288 | tf_op jit(solution)/shard_map/all_to_all | solution.py:334
  18.3 0.9 copy-start.1
  19.2 0.9 copy-start.4
  20.8 2.0 %copy-start = (s32[56,128,128]{2,1,0:T(8,128)S(1)}, s32[56,128,128]{2,1,0:T(8,128)}, u32[]{:S(2)}) copy-start(s32[56,128,128]{2,1,0:T(8,128)} %cnt_ref.1) | copy-start | bytes 11010052
  22.9 44.3 %copy-start.3 = (bf16[256,256]{1,0:T(8,128)(2,1)S(1)}, bf16[256,256]{1,0:T(8,128)(2,1)}, u32[]{:S(2)}) copy-start(bf16[256,256]{1,0:T(8,128)(2,1)} %own_w_ref.1) | copy-start | bytes 393220
  22.9 44.4 %copy-start.2 = (bf16[256,256]{1,0:T(8,128)(2,1)S(1)}, bf16[256,256]{1,0:T(8,128)(2,1)}, u32[]{:S(2)}) copy-start(bf16[256,256]{1,0:T(8,128)(2,1)} %neigh_ref.1) | copy-start | bytes 393220
  22.9 44.5 %copy-start.6 = (f32[256]{0:T(256)S(1)}, f32[256]{0:T(256)}, u32[]{:S(2)}) copy-start(f32[256]{0:T(256)} %param.16) | copy-start | bytes 3076
  25.6 16.6 %all-to-all-start.1 = ((bf16[8,4,32,128]{3,2,1,0:T(8,128)(2,1)}), bf16[8,4,32,128]{3,2,1,0:T(8,128)(2,1)S(1)}, u32[]{:S(2)}, u32[]{:S(2)}) async-start(bf16[8,4,32,128]{3,2,1,0:T(8,128)(2,1)} %get-tuple-element.54), calls=%async_computation.1 | async-start | bytes 524288 | tf_op jit(solution)/shard_map/all_to_all | solution.py:334
  30.5 22.9 %collective-permute-start = (bf16[4,2,2,32,128]{4,3,2,1,0:T(8,128)(2,1)S(1)}, bf16[4,2,2,32,128]{4,3,2,1,0:T(8,128)(2,1)S(1)}, u32[]{:S(2)}, u32[]{:S(2)}) collective-permute-start(bf16[4,2,2,32,128]{4,3,2,1,0:T(8,128)(2,1)S(1)} %get-tuple-element.52), channel_id=1, source_target_pairs={{0,64},{1,65},{2,66},{3,67},{4,68},{5,69},{6,70},{7,71},{8,72},{9,... | collective-permute-start | bytes 393224 | tf_op jit(solution)/shard_map/ppermute | solution.py:360
  35.2 19.4 %collective-permute-start.1 = (bf16[4,2,2,32,128]{4,3,2,1,0:T(8,128)(2,1)S(1)}, bf16[4,2,2,32,128]{4,3,2,1,0:T(8,128)(2,1)S(1)}, u32[]{:S(2)}, u32[]{:S(2)}) collective-permute-start(bf16[4,2,2,32,128]{4,3,2,1,0:T(8,128)(2,1)S(1)} %get-tuple-element.53), channel_id=1, source_target_pairs={{0,65},{1,64},{2,67},{3,66},{4,69},{5,68},{6,71},{7,70},{8,73},{9,... | collective-permute-start | bytes 393224 | tf_op jit(solution)/shard_map/ppermute | solution.py:360
  43.6 17.1 %collective-permute-start.2 = (bf16[4,2,32,128]{3,2,1,0:T(8,128)(2,1)S(1)}, bf16[4,2,32,128]{3,2,1,0:T(8,128)(2,1)S(1)}, u32[]{:S(2)}, u32[]{:S(2)}) collective-permute-start(bf16[4,2,32,128]{3,2,1,0:T(8,128)(2,1)S(1)} %get-tuple-element.58), channel_id=1, source_target_pairs={{0,64},{1,65},{2,66},{3,67},{4,68},{5,69},{6,70},{7,71},{8,72},{9,... | collective-permute-start | bytes 196616 | tf_op jit(solution)/shard_map/ppermute | solution.py:360
  46.7 14.9 %collective-permute-start.3 = (bf16[4,2,32,128]{3,2,1,0:T(8,128)(2,1)S(1)}, bf16[4,2,32,128]{3,2,1,0:T(8,128)(2,1)S(1)}, u32[]{:S(2)}, u32[]{:S(2)}) collective-permute-start(bf16[4,2,32,128]{3,2,1,0:T(8,128)(2,1)S(1)} %get-tuple-element.59), channel_id=1, source_target_pairs={{0,65},{1,64},{2,67},{3,66},{4,69},{5,68},{6,71},{7,70},{8,73},{9,... | collective-permute-start | bytes 196616 | tf_op jit(solution)/shard_map/ppermute | solution.py:360
  62.4 10.1 %all-to-all-start.2 = ((bf16[4,3,2,2,32,128]{5,4,3,2,1,0:T(8,128)(2,1)}), bf16[4,3,2,2,32,128]{5,4,3,2,1,0:T(8,128)(2,1)S(1)}, u32[]{:S(2)}, u32[]{:S(2)}) async-start(bf16[4,3,2,2,32,128]{5,4,3,2,1,0:T(8,128)(2,1)} %shard_map.124), calls=%async_computation.2 | async-start | bytes 786432 | tf_op jit(solution)/shard_map/all_to_all | solution.py:343
  73.4 19.5 %collective-permute-start.4 = (bf16[4,2,2,32,128]{4,3,2,1,0:T(8,128)(2,1)S(1)}, bf16[4,2,2,32,128]{4,3,2,1,0:T(8,128)(2,1)S(1)}, u32[]{:S(2)}, u32[]{:S(2)}) collective-permute-start(bf16[4,2,2,32,128]{4,3,2,1,0:T(8,128)(2,1)S(1)} %get-tuple-element.62), channel_id=1, source_target_pairs={{0,64},{1,65},{2,66},{3,67},{4,68},{5,69},{6,70},{7,71},{8,72},{9,... | collective-permute-start | bytes 393224 | tf_op jit(solution)/shard_map/ppermute | solution.py:360
  80.1 12.8 %collective-permute-start.5 = (bf16[4,2,2,32,128]{4,3,2,1,0:T(8,128)(2,1)S(1)}, bf16[4,2,2,32,128]{4,3,2,1,0:T(8,128)(2,1)S(1)}, u32[]{:S(2)}, u32[]{:S(2)}) collective-permute-start(bf16[4,2,2,32,128]{4,3,2,1,0:T(8,128)(2,1)S(1)} %get-tuple-element.63), channel_id=1, source_target_pairs={{0,65},{1,64},{2,67},{3,66},{4,69},{5,68},{6,71},{7,70},{8,73},{9,... | collective-permute-start | bytes 393224 | tf_op jit(solution)/shard_map/ppermute | solution.py:360
  84.2 16.8 %all-to-all-start.3 = ((bf16[32,5,8,128]{3,2,1,0:T(8,128)(2,1)}), bf16[32,5,8,128]{3,2,1,0:T(8,128)(2,1)S(1)}, u32[]{:S(2)}, u32[]{:S(2)}) async-start(bf16[32,5,8,128]{3,2,1,0:T(8,128)(2,1)} %shard_map.126), calls=%async_computation.3 | async-start | bytes 655360 | tf_op jit(solution)/shard_map/all_to_all | solution.py:473
  93.0 69.3 %copy-start.5 = (s32[1,8,4]{1,2,0:T(4,128)S(1)}, s32[1,8,4]{1,2,0:T(4,128)}, u32[]{:S(2)}) copy-start(s32[1,8,4]{1,2,0:T(4,128)} %param.13) | copy-start | bytes 388
  101.8 25.2 %all-to-all-start.4 = ((bf16[16,3,8,128]{3,2,1,0:T(8,128)(2,1)}), bf16[16,3,8,128]{3,2,1,0:T(8,128)(2,1)S(1)}, u32[]{:S(2)}, u32[]{:S(2)}) async-start(bf16[16,3,8,128]{3,2,1,0:T(8,128)(2,1)} %shard_map.130), calls=%async_computation.4 | async-start | bytes 196608 | tf_op jit(solution)/shard_map/all_to_all | solution.py:479
  111.7 8.4 %collective-permute-start.6 = (bf16[2,2,2,32,128]{4,3,2,1,0:T(8,128)(2,1)S(1)}, bf16[2,2,2,32,128]{4,3,2,1,0:T(8,128)(2,1)S(1)}, u32[]{:S(2)}, u32[]{:S(2)}) collective-permute-start(bf16[2,2,2,32,128]{4,3,2,1,0:T(8,128)(2,1)S(1)} %get-tuple-element.69), channel_id=1, source_target_pairs={{0,2},{1,3},{2,4},{3,5},{4,6},{5,7},{6,0},{7,1},{8,10},{9,11},{10,... | collective-permute-start | bytes 196616 | tf_op jit(solution)/shard_map/ppermute | solution.py:481
  115.4 7.7 %collective-permute-start.7 = (bf16[2,2,2,32,128]{4,3,2,1,0:T(8,128)(2,1)S(1)}, bf16[2,2,2,32,128]{4,3,2,1,0:T(8,128)(2,1)S(1)}, u32[]{:S(2)}, u32[]{:S(2)}) collective-permute-start(bf16[2,2,2,32,128]{4,3,2,1,0:T(8,128)(2,1)S(1)} %get-tuple-element.70), channel_id=1, source_target_pairs={{0,4},{1,5},{2,6},{3,7},{4,0},{5,1},{6,2},{7,3},{8,12},{9,13},{10,... | collective-permute-start | bytes 196616 | tf_op jit(solution)/shard_map/ppermute | solution.py:481
  117.8 7.4 %collective-permute-start.8 = (bf16[2,2,2,32,128]{4,3,2,1,0:T(8,128)(2,1)S(1)}, bf16[2,2,2,32,128]{4,3,2,1,0:T(8,128)(2,1)S(1)}, u32[]{:S(2)}, u32[]{:S(2)}) collective-permute-start(bf16[2,2,2,32,128]{4,3,2,1,0:T(8,128)(2,1)S(1)} %get-tuple-element.71), channel_id=1, source_target_pairs={{0,6},{1,7},{2,0},{3,1},{4,2},{5,3},{6,4},{7,5},{8,14},{9,15},{10,... | collective-permute-start | bytes 196616 | tf_op jit(solution)/shard_map/ppermute | solution.py:481
  127.0 20.3 %all-to-all-start.5 = ((bf16[8,4,32,128]{3,2,1,0:T(8,128)(2,1)}), bf16[8,4,32,128]{3,2,1,0:T(8,128)(2,1)S(1)}, u32[]{:S(2)}, u32[]{:S(2)}) async-start(bf16[8,4,32,128]{3,2,1,0:T(8,128)(2,1)} %get-tuple-element.78), calls=%async_computation.5 | async-start | bytes 524288 | tf_op jit(solution)/shard_map/all_to_all | solution.py:334
  138.5 3.1 %collective-permute-start.9 = (f32[1,8,256]{2,1,0:T(8,128)S(1)}, f32[1,8,256]{2,1,0:T(8,128)S(1)}, u32[]{:S(2)}, u32[]{:S(2)}) collective-permute-start(f32[1,8,256]{2,1,0:T(8,128)S(1)} %get-tuple-element.79.one_ref), channel_id=1, source_target_pairs={{0,8},{8,0},{16,24},{24,16},{32,40},{40,32},{48,56},{56,48},{64,72... | collective-permute-start | bytes 24584 | tf_op jit(solution)/shard_map/ppermute | solution.py:338
  141.6 5.6 %collective-permute-start.10 = (f32[2,8,256]{2,1,0:T(8,128)S(1)}, f32[2,8,256]{2,1,0:T(8,128)S(1)}, u32[]{:S(2)}, u32[]{:S(2)}) collective-permute-start(f32[2,8,256]{2,1,0:T(8,128)S(1)} %shard_map.132.one_ref), channel_id=1, source_target_pairs={{0,128},{8,136},{16,144},{24,152},{32,160},{40,168},{48,176},{56,1... | collective-permute-start | bytes 49160 | tf_op jit(solution)/shard_map/ppermute | solution.py:338
  147.2 15.1 %all-to-all-start.6 = ((bf16[8,4,32,128]{3,2,1,0:T(8,128)(2,1)}), bf16[8,4,32,128]{3,2,1,0:T(8,128)(2,1)S(1)}, u32[]{:S(2)}, u32[]{:S(2)}) async-start(bf16[8,4,32,128]{3,2,1,0:T(8,128)(2,1)} %get-tuple-element.80), calls=%async_computation.6 | async-start | bytes 524288 | tf_op jit(solution)/shard_map/all_to_all | solution.py:334
  153.4 7.3 %collective-permute-start.11 = (f32[4,8,256]{2,1,0:T(8,128)S(1)}, f32[4,8,256]{2,1,0:T(8,128)S(1)}, u32[]{:S(2)}, u32[]{:S(2)}) collective-permute-start(f32[4,8,256]{2,1,0:T(8,128)S(1)} %shard_map.133.near_ref), channel_id=1, source_target_pairs={{0,256},{8,264},{16,272},{24,280},{32,288},{40,296},{48,304},{56,3... | collective-permute-start | bytes 98312 | tf_op jit(solution)/shard_map/ppermute | solution.py:338
